TPU v7x, 32 devices: a whole 2x2x4 slice. The times are simulated.
32 devices in a mesh: replica: 4 (over y, x), fsdp: 8 (over z, core).
Axes of the slice: x: 2, y: 2, z: 4, core: 2. Of those that a mesh axis runs over, the one named last changes fastest.
Arguments:
- tokens: bfloat16 [16384, 2048], P(('replica', 'fsdp')), may hold values from -6 to 6
- segments: int32 [16384], P(('replica', 'fsdp')), may hold values from 0 to 8, as said below
- positions: int32 [16384], P(('replica', 'fsdp')), may hold values from 0 to 2431, as said below
- query_weight: bfloat16 [2048, 2048], P('fsdp'), may hold values from -0.125 to 0.125
- key_weight: bfloat16 [2048, 128], P('fsdp'), may hold values from -0.125 to 0.125
- value_weight: bfloat16 [2048, 128], P('fsdp'), may hold values from -0.125 to 0.125
- output_weight: bfloat16 [2048, 2048], P('fsdp'), may hold values from -2 to 2
- attn_gain: bfloat16 [2048], P('fsdp'), may hold values from 0.5 to 1.5
- gate_weight: bfloat16 [2048, 5632], P(None, 'fsdp'), may hold values from -0.125 to 0.125
- up_weight: bfloat16 [2048, 5632], P(None, 'fsdp'), may hold values from -0.125 to 0.125
- down_weight: bfloat16 [5632, 2048], P('fsdp'), may hold values from -0.078125 to 0.078125
- ffn_gain: bfloat16 [2048], P('fsdp'), may hold values from 0.5 to 1.5
- grad_out: bfloat16 [16384, 2048], P(('replica', 'fsdp')), may hold values from -6 to 6
Outputs:
- layer_out: bfloat16 [16384, 2048], P(('replica', 'fsdp'))
- input_grad: float32 [16384, 2048], P(('replica', 'fsdp'))
- query_grad: float32 [2048, 2048], P('fsdp')
- key_grad: float32 [2048, 128], P('fsdp')
- value_grad: float32 [2048, 128], P('fsdp')
- output_grad: float32 [2048, 2048], P('fsdp')
- attn_gain_grad: float32 [2048], P('fsdp')
- gate_grad: float32 [2048, 5632], P(None, 'fsdp')
- up_grad: float32 [2048, 5632], P(None, 'fsdp')
- down_grad: float32 [5632, 2048], P('fsdp')
- ffn_gain_grad: float32 [2048], P('fsdp')
Inputs may be any that keep to these rules, and one draw needn't show every extreme that they name: `segments`: each aligned block of 4096 tokens is one group: 2048 prompt tokens with segment 0, then continuations 1 to 8 in order, each of 128 to 384 tokens; some continuation of every group has exactly 384 tokens. `positions`: prompt tokens hold 0 to 2047 in order; the tokens of a continuation hold 2048, 2049 and so on.
All inputs are finite; a program needn't handle non-finite values.
Results may differ from a plain program's by a relative error of at most 0.023.
Values may be sent and summed in bfloat16 or wider, within the bound.
A program may use at most 448 MiB of HBM per device.

v0:
```python
import jax
import jax.numpy as jnp
from jax import lax
from jax.sharding import PartitionSpec as P

HEAD_BLOCK = 4
GROUP_TOK = 4096


EPSILON = 1e-05
ROPE_BASE = 10000.0
MASKED = -1e30


def matmul(left, right):
    return jnp.dot(left, right, preferred_element_type=jnp.float32)


def contract(left, right, left_dim, right_dim):
    return lax.dot_general(
        left, right, (((left_dim,), (right_dim,)), ((), ())), preferred_element_type=jnp.float32
    )


def rope_tables(pos_ids, head_dim):
    half_width = head_dim // 2
    frequency = ROPE_BASE ** (-jnp.arange(half_width, dtype=jnp.float32) * 2.0 / head_dim)
    angles = pos_ids.astype(jnp.float32)[:, None] * frequency[None, :]
    return (jnp.cos(angles), jnp.sin(angles))


def rotate(values, cos_table, sin_table):
    half_width = values.shape[-1] // 2
    front_half = values[..., :half_width]
    back_half = values[..., half_width:]
    return jnp.concatenate(
        [
            front_half * cos_table - back_half * sin_table,
            back_half * cos_table + front_half * sin_table,
        ],
        axis=-1,
    )


def norm_forward(values, gain):
    inverse = lax.rsqrt(jnp.mean(values * values, axis=-1, keepdims=True) + EPSILON)
    return (values * inverse * gain, inverse)


def norm_backward(values, inverse, gain, grad):
    scaled = grad * gain
    inner_mean = jnp.mean(scaled * values, axis=-1, keepdims=True)
    return (
        inverse * scaled - values * inverse**3 * inner_mean,
        jnp.sum(grad * values * inverse, axis=0),
    )


def swiglu_back(d_activation, gate_proj, up_proj):
    sigmoid_gate = jax.nn.sigmoid(gate_proj)
    d_gate = (
        d_activation * up_proj * sigmoid_gate * (1.0 + gate_proj * (1.0 - sigmoid_gate))
    ).astype(jnp.bfloat16)
    d_up = (d_activation * gate_proj * sigmoid_gate).astype(jnp.bfloat16)
    return (d_gate, d_up)


def shards(
    tokens,
    segments,
    positions,
    query_weight,
    key_weight,
    value_weight,
    output_weight,
    attn_gain,
    gate_weight,
    up_weight,
    down_weight,
    ffn_gain,
    grad_out,
):
    tok_rows, model_width = tokens.shape
    head_dim = key_weight.shape[1]
    head_count = model_width // head_dim
    block_count = head_count // HEAD_BLOCK
    block_width = HEAD_BLOCK * head_dim
    score_scale = head_dim ** (-0.5)
    fsdp_size = lax.axis_size("fsdp")
    fsdp_index = lax.axis_index("fsdp")
    gathered = (
        lax.all_gather(query_weight, "fsdp", axis=0, tiled=True),
        lax.all_gather(key_weight, "fsdp", axis=0, tiled=True),
        lax.all_gather(value_weight, "fsdp", axis=0, tiled=True),
        lax.all_gather(output_weight, "fsdp", axis=0, tiled=True),
        lax.all_gather(attn_gain, "fsdp", axis=0, tiled=True),
        lax.all_gather(ffn_gain, "fsdp", axis=0, tiled=True),
    )
    w_query, w_key, w_value, w_out, gain_attn, gain_ffn = gathered
    gain_attn = gain_attn.astype(jnp.float32)
    gain_ffn = gain_ffn.astype(jnp.float32)
    inputs = tokens.astype(jnp.float32)
    normed_full, inverse_attn = norm_forward(inputs, gain_attn)
    normed = normed_full.astype(jnp.bfloat16)
    query_raw = matmul(normed, w_query)
    key_raw = matmul(normed, w_key)
    value_rows = matmul(normed, w_value).astype(jnp.bfloat16)
    cos_table, sin_table = rope_tables(positions, head_dim)
    queries = rotate(
        query_raw.reshape(tok_rows, head_count, head_dim), cos_table[:, None], sin_table[:, None]
    ).astype(jnp.bfloat16)
    key_rot = rotate(key_raw, cos_table, sin_table).astype(jnp.bfloat16)
    key_rows, value_all = (
        lax.all_gather(key_rot, "fsdp", axis=0, tiled=True),
        lax.all_gather(value_rows, "fsdp", axis=0, tiled=True),
    )
    seg_all, pos_all = (
        lax.all_gather(segments, "fsdp", axis=0, tiled=True),
        lax.all_gather(positions, "fsdp", axis=0, tiled=True),
    )
    key_width = max(GROUP_TOK, tok_rows)
    window_start = fsdp_index * tok_rows // GROUP_TOK * GROUP_TOK
    key_window = lax.dynamic_slice_in_dim(key_rows, window_start, key_width, 0)
    value_window = lax.dynamic_slice_in_dim(value_all, window_start, key_width, 0)
    seg_window = lax.dynamic_slice_in_dim(seg_all, window_start, key_width, 0)
    pos_window = lax.dynamic_slice_in_dim(pos_all, window_start, key_width, 0)
    key_index = window_start + jnp.arange(key_width, dtype=jnp.int32)
    query_index = fsdp_index * tok_rows + jnp.arange(tok_rows, dtype=jnp.int32)
    visible = (
        (key_index[None, :] // GROUP_TOK == query_index[:, None] // GROUP_TOK)
        & (pos_window[None, :] <= positions[:, None])
        & ((seg_window[None, :] == 0) | (seg_window[None, :] == segments[:, None]))
    )
    query_blocks = queries.reshape(tok_rows, block_count, block_width).transpose(1, 0, 2)

    def block_scores(query_block):
        flat_queries = query_block.reshape(tok_rows * HEAD_BLOCK, head_dim)
        scores = (
            contract(flat_queries, key_window, 1, 1).reshape(tok_rows, HEAD_BLOCK, key_width)
            * score_scale
        )
        return (flat_queries, scores)

    def attend_block(query_block):
        flat_queries, scores = block_scores(query_block)
        scores = jnp.where(visible[:, None, :], scores, MASKED)
        row_max = jnp.max(scores, axis=-1, keepdims=True)
        exp_scores = jnp.exp(scores - row_max)
        totals = jnp.sum(exp_scores, axis=-1, keepdims=True)
        weights = (
            (exp_scores / totals).astype(jnp.bfloat16).reshape(tok_rows * HEAD_BLOCK, key_width)
        )
        mixed_block = matmul(weights, value_window).reshape(tok_rows, block_width)
        return (mixed_block, (row_max + jnp.log(totals))[..., 0])

    mixed_blocks, log_totals = lax.map(attend_block, query_blocks)
    mixed_rows = mixed_blocks.transpose(1, 0, 2).reshape(tok_rows, model_width).astype(jnp.bfloat16)
    hidden = inputs + matmul(mixed_rows, w_out)
    normed_ffn_full, inverse_ffn = norm_forward(hidden, gain_ffn)
    normed_ffn = normed_ffn_full.astype(jnp.bfloat16)
    cotangent = grad_out.astype(jnp.float32)
    w_gate, w_up, w_down = (
        lax.all_gather(gate_weight, "fsdp", axis=1, tiled=True),
        lax.all_gather(up_weight, "fsdp", axis=1, tiled=True),
        lax.all_gather(down_weight, "fsdp", axis=0, tiled=True),
    )
    gate_proj = matmul(normed_ffn, w_gate)
    up_proj = matmul(normed_ffn, w_up)
    activation = (jax.nn.silu(gate_proj) * up_proj).astype(jnp.bfloat16)
    layer_out = (hidden + matmul(activation, w_down)).astype(jnp.bfloat16)
    d_activation = contract(grad_out, w_down, 1, 1)
    d_gate, d_up = swiglu_back(d_activation, gate_proj, up_proj)
    d_normed_ffn = contract(d_gate, w_gate, 1, 1) + contract(d_up, w_up, 1, 1)
    gate_up_part = lax.psum_scatter(
        jnp.concatenate(
            [contract(d_gate, normed_ffn, 0, 0), contract(d_up, normed_ffn, 0, 0)], axis=1
        ).astype(jnp.bfloat16),
        "fsdp",
        scatter_dimension=0,
        tiled=True,
    ).astype(jnp.float32)
    gate_part = gate_up_part[:, :model_width].T
    up_part = gate_up_part[:, model_width:].T
    down_part = lax.psum_scatter(
        contract(activation, grad_out, 0, 0).astype(jnp.bfloat16),
        "fsdp",
        scatter_dimension=0,
        tiled=True,
    )
    resid_ffn, ffn_gain_term = norm_backward(hidden, inverse_ffn, gain_ffn, d_normed_ffn)
    d_hidden = cotangent + resid_ffn
    d_branch = d_hidden.astype(jnp.bfloat16)
    d_mixed = contract(d_branch, w_out, 1, 1).astype(jnp.bfloat16)
    d_mixed_blocks = d_mixed.reshape(tok_rows, block_count, block_width).transpose(1, 0, 2)

    def back_block(totals, block_items):
        query_block, d_block, log_block = block_items
        flat_queries, scores = block_scores(query_block)
        probs = jnp.where(visible[:, None, :], jnp.exp(scores - log_block[..., None]), 0.0)
        d_flat = d_block.reshape(tok_rows * HEAD_BLOCK, head_dim)
        d_probs = contract(d_flat, value_window, 1, 1).reshape(tok_rows, HEAD_BLOCK, key_width)
        row_delta = jnp.sum(probs * d_probs, axis=-1, keepdims=True)
        d_scores = (
            (probs * (d_probs - row_delta))
            .astype(jnp.bfloat16)
            .reshape(tok_rows * HEAD_BLOCK, key_width)
        )
        weights = probs.astype(jnp.bfloat16).reshape(tok_rows * HEAD_BLOCK, key_width)
        d_query_block = matmul(d_scores, key_window) * score_scale
        key_total = totals[0] + contract(d_scores, flat_queries, 0, 0) * score_scale
        value_total = totals[1] + contract(weights, d_flat, 0, 0)
        return ((key_total, value_total), d_query_block.reshape(tok_rows, block_width))

    zero_window = jnp.zeros((key_width, head_dim), jnp.float32)
    window_grads, d_query_blocks = lax.scan(
        back_block, (zero_window, zero_window), (query_blocks, d_mixed_blocks, log_totals)
    )
    d_queries = d_query_blocks.transpose(1, 0, 2).reshape(tok_rows, head_count, head_dim)
    d_query_raw = (
        rotate(d_queries, cos_table[:, None], -sin_table[:, None])
        .astype(jnp.bfloat16)
        .reshape(tok_rows, model_width)
    )
    row_zeros = jnp.zeros((fsdp_size * tok_rows, head_dim), jnp.float32)
    key_term = lax.dynamic_update_slice_in_dim(row_zeros, window_grads[0], window_start, 0)
    value_term = lax.dynamic_update_slice_in_dim(row_zeros, window_grads[1], window_start, 0)
    key_sum, value_sum = (
        lax.psum_scatter(
            key_term.astype(jnp.bfloat16), "fsdp", scatter_dimension=0, tiled=True
        ).astype(jnp.float32),
        lax.psum_scatter(
            value_term.astype(jnp.bfloat16), "fsdp", scatter_dimension=0, tiled=True
        ).astype(jnp.float32),
    )
    d_key_raw = rotate(key_sum, cos_table, -sin_table).astype(jnp.bfloat16)
    d_value = value_sum.astype(jnp.bfloat16)
    d_normed = (
        contract(d_query_raw, w_query, 1, 1)
        + contract(d_key_raw, w_key, 1, 1)
        + contract(d_value, w_value, 1, 1)
    )
    resid_attn, attn_gain_term = norm_backward(inputs, inverse_attn, gain_attn, d_normed)
    input_grad = d_hidden + resid_attn
    attn_part = lax.psum_scatter(
        jnp.concatenate(
            [
                contract(normed, d_query_raw, 0, 0),
                contract(normed, d_key_raw, 0, 0),
                contract(normed, d_value, 0, 0),
                contract(mixed_rows, d_branch, 0, 0),
            ],
            axis=1,
        ).astype(jnp.bfloat16),
        "fsdp",
        scatter_dimension=0,
        tiled=True,
    )
    attn_gain_part, ffn_gain_part = (
        lax.psum_scatter(attn_gain_term, "fsdp", scatter_dimension=0, tiled=True),
        lax.psum_scatter(ffn_gain_term, "fsdp", scatter_dimension=0, tiled=True),
    )
    summed = (
        lax.psum(attn_part, "replica").astype(jnp.float32),
        lax.psum(attn_gain_part.astype(jnp.bfloat16), "replica").astype(jnp.float32),
        lax.psum(ffn_gain_part.astype(jnp.bfloat16), "replica").astype(jnp.float32),
        lax.psum(gate_part.astype(jnp.bfloat16), "replica").astype(jnp.float32),
        lax.psum(up_part.astype(jnp.bfloat16), "replica").astype(jnp.float32),
        lax.psum(down_part, "replica").astype(jnp.float32),
    )
    attn_total, attn_gain_grad, ffn_gain_grad, gate_grad, up_grad, down_grad = summed
    query_grad = attn_total[:, :model_width]
    key_grad = attn_total[:, model_width : model_width + head_dim]
    value_grad = attn_total[:, model_width + head_dim : model_width + 2 * head_dim]
    output_grad = attn_total[:, model_width + 2 * head_dim :]
    return (
        layer_out,
        input_grad,
        query_grad,
        key_grad,
        value_grad,
        output_grad,
        attn_gain_grad,
        gate_grad,
        up_grad,
        down_grad,
        ffn_gain_grad,
    )


def solution(mesh):
    return jax.shard_map(
        shards,
        mesh=mesh,
        in_specs=(
            P(("replica", "fsdp"), None),
            P(("replica", "fsdp")),
            P(("replica", "fsdp")),
            P("fsdp", None),
            P("fsdp", None),
            P("fsdp", None),
            P("fsdp", None),
            P("fsdp"),
            P(None, "fsdp"),
            P(None, "fsdp"),
            P("fsdp", None),
            P("fsdp"),
            P(("replica", "fsdp"), None),
        ),
        out_specs=(
            P(("replica", "fsdp"), None),
            P(("replica", "fsdp"), None),
            P("fsdp", None),
            P("fsdp", None),
            P("fsdp", None),
            P("fsdp", None),
            P("fsdp"),
            P(None, "fsdp"),
            P(None, "fsdp"),
            P("fsdp", None),
            P("fsdp"),
        ),
        check_vma=False,
    )
```

profile of v0, /device:TPU:0, one launch (start us, length us, event | category | flops | bytes accessed | tf_op | source)
XLA Modules:
  0.0 3351.9 jit_solution(6966285076643611045)
XLA Ops:
  7.9 13.4 all-gather.2
  24.1 15.3 all_gather.43
  44.8 16.6 all_gather.45
  80.6 14.5 all-gather.1
  106.3 44.1 %all-gather.12.cloned.1.call-done = bf16[2048,2048]{1,0:T(8,128)(2,1)} async-done(((bf16[256,2048]{1,0:T(8,128)(2,1)}), bf16[2048,2048]{1,0:T(8,128)(2,1)}) %all-gather.12.cloned.1.call-update) | async-done | bytes 8388624 | tf_op jit(solution)/shard_map/all_gather | solution.py:92
  173.2 430.1 %while.30 = (s32[]{:T(128)}, bf16[4,512,512]{1,2,0:T(8,128)(2,1)}, f32[4,512,4]{1,2,0:T(4,128)}, bf16[4,512,512]{1,2,0:T(8,128)(2,1)}, bf16[4096,128]{1,0:T(8,12...) while((s32[]{:T(128)}, bf16[4,512,512]{1,2,0:T(8,128)(2,1)}, ...), condition=%wide.region_4.5_spmd.clone.clone, body=%wide.region_1.4_spmd.clone.sunk.clone | while | flops 4408211456 | bytes 355592384 | solution.py:156
  177.9 15.2 fusion.170
  193.1 16.2 fusion.171
  224.9 22.1 copy.132
  247.0 24.4 reshape.326
  286.2 14.6 fusion.170
  300.8 16.0 fusion.171
  332.5 22.1 copy.132
  354.6 23.9 reshape.326
  393.4 14.4 fusion.170
  407.9 15.9 fusion.171
  439.3 22.1 copy.132
  461.4 24.4 reshape.326
  500.6 14.6 fusion.170
  515.2 16.0 fusion.171
  546.8 22.1 copy.132
  568.9 23.9 reshape.326
  616.2 20.0 fusion.77
  636.2 25.3 all-gather.22.cloned.1.call-done
  661.5 19.2 fusion.78
  680.7 183.3 %all-gather.24.cloned.1.call-done = bf16[5632,2048]{1,0:T(8,128)(2,1)} async-done(((bf16[704,2048]{1,0:T(8,128)(2,1)}), bf16[5632,2048]{1,0:T(8,128)(2,1)}) %all-gather.24.cloned.1.call-update) | async-done | bytes 23068688 | tf_op jit(solution)/shard_map/all_gather | solution.py:165
  864.1 28.1 multiply_convert_fusion.1
  892.2 17.9 convolution_convert_fusion
  910.1 20.1 fusion.79
  930.2 20.2 multiply_reduce_fusion.1
  966.2 765.8 %while.31 = (s32[]{:T(128)}, f32[4096,128]{1,0:T(8,128)}, f32[4096,128]{1,0:T(8,128)}, f32[4,512,512]{1,2,0:T(8,128)}, bf16[4,512,512]{1,2,0:T(8,128)(2,1)}, /*i...) while((s32[]{:T(128)}, f32[4096,128]{1,0:T(8,128)}, ...), condition=%wide.region_9.10_spmd.clone.clone, body=%wide.region_7.9_spmd.clone.sunk.clone | while | flops 13017815040 | bytes 339831072 | solution.py:215
  971.8 19.9 fusion.186
  991.7 39.7 %multiply_convert_fusion.7 = bf16[512,4,4096]{2,0,1:T(8,128)(2,1)} fusion(f32[512,4,4096]{2,0,1:T(8,128)} %get-tuple-element.703, f32[512,4]{0,1:T(4,128)S(1)} %dynamic-slice_bitcast_fusion.5, pred[512,4096]{1,0:T(8,128)(4,1)S(1)} %or_and_fusion.7, bf16[512,4,128]{0,2,1:T(8,128)(2,1)S(1)} %bitcast.161, bf16[4096,128]{1,0:T(8,128)(2,1)} %get-tuple-element.803), kind=kOutput, calls=%fused_computation.14.clone.1.clone | convolution fusion | flops 4378859520 | bytes 54009856 | tf_op jit(solution)/shard_map/while/body/eval_jaxpr/sub | solution.py:204
  1031.4 22.1 copy.134
  1053.5 23.7 reshape.327
  1087.5 22.1 copy.136
  1109.7 23.9 reshape.329
  1162.6 19.9 fusion.186
  1182.5 39.7 %multiply_convert_fusion.7 = bf16[512,4,4096]{2,0,1:T(8,128)(2,1)} fusion(f32[512,4,4096]{2,0,1:T(8,128)} %get-tuple-element.703, f32[512,4]{0,1:T(4,128)S(1)} %dynamic-slice_bitcast_fusion.5, pred[512,4096]{1,0:T(8,128)(4,1)S(1)} %or_and_fusion.7, bf16[512,4,128]{0,2,1:T(8,128)(2,1)S(1)} %bitcast.161, bf16[4096,128]{1,0:T(8,128)(2,1)} %get-tuple-element.803), kind=kOutput, calls=%fused_computation.14.clone.1.clone | convolution fusion | flops 4378859520 | bytes 54009856 | tf_op jit(solution)/shard_map/while/body/eval_jaxpr/sub | solution.py:204
  1222.2 22.1 copy.134
  1244.3 23.7 reshape.327
  1279.0 22.1 copy.136
  1301.1 23.9 reshape.329
  1354.0 19.9 fusion.186
  1374.0 39.7 %multiply_convert_fusion.7 = bf16[512,4,4096]{2,0,1:T(8,128)(2,1)} fusion(f32[512,4,4096]{2,0,1:T(8,128)} %get-tuple-element.703, f32[512,4]{0,1:T(4,128)S(1)} %dynamic-slice_bitcast_fusion.5, pred[512,4096]{1,0:T(8,128)(4,1)S(1)} %or_and_fusion.7, bf16[512,4,128]{0,2,1:T(8,128)(2,1)S(1)} %bitcast.161, bf16[4096,128]{1,0:T(8,128)(2,1)} %get-tuple-element.803), kind=kOutput, calls=%fused_computation.14.clone.1.clone | convolution fusion | flops 4378859520 | bytes 54009856 | tf_op jit(solution)/shard_map/while/body/eval_jaxpr/sub | solution.py:204
  1413.6 22.1 copy.134
  1435.8 23.7 reshape.327
  1470.4 22.1 copy.136
  1492.6 23.9 reshape.329
  1545.5 19.9 fusion.186
  1565.4 39.7 %multiply_convert_fusion.7 = bf16[512,4,4096]{2,0,1:T(8,128)(2,1)} fusion(f32[512,4,4096]{2,0,1:T(8,128)} %get-tuple-element.703, f32[512,4]{0,1:T(4,128)S(1)} %dynamic-slice_bitcast_fusion.5, pred[512,4096]{1,0:T(8,128)(4,1)S(1)} %or_and_fusion.7, bf16[512,4,128]{0,2,1:T(8,128)(2,1)S(1)} %bitcast.161, bf16[4096,128]{1,0:T(8,128)(2,1)} %get-tuple-element.803), kind=kOutput, calls=%fused_computation.14.clone.1.clone | convolution fusion | flops 4378859520 | bytes 54009856 | tf_op jit(solution)/shard_map/while/body/eval_jaxpr/sub | solution.py:204
  1605.1 22.1 copy.134
  1627.2 23.7 reshape.327
  1661.9 22.1 copy.136
  1684.0 23.9 reshape.329
  1737.5 18.0 convolution_convert_fusion.1
  1755.5 31.5 pad_maximum_fusion
  1821.8 19.8 convolution_convert_fusion.2
  1843.5 843.7 %all-reduce.9.cloned.1.call-done = bf16[5632,4096]{0,1:T(8,128)(2,1)} async-done(((bf16[5632,4096]{0,1:T(8,128)(2,1)}), bf16[5632,4096]{0,1:T(8,128)(2,1)}) %all-reduce.9.cloned.1.call-update) | async-done | bytes 46137360
  2697.0 170.6 %reduce-scatter.10.cloned.1.call-done = bf16[256,4352]{0,1:T(8,128)(2,1)} async-done(((bf16[2048,4352]{0,1:T(8,128)(2,1)}), bf16[256,4352]{0,1:T(8,128)(2,1)}) %reduce-scatter.10.cloned.1.call-update) | async-done | bytes 2228240 | tf_op jit(solution)/shard_map/reduce_scatter | solution.py:244
  2867.5 228.0 %reduce-scatter.12.cloned.1.call-done = bf16[704,2048]{1,0:T(8,128)(2,1)} async-done(((bf16[5632,2048]{1,0:T(8,128)(2,1)}), bf16[704,2048]{1,0:T(8,128)(2,1)}) %reduce-scatter.12.cloned.1.call-update) | async-done | bytes 2883600 | tf_op jit(solution)/shard_map/reduce_scatter | solution.py:184
  3096.3 20.0 add_convert_fusion
  3128.9 25.9 all-reduce.3
  3173.0 148.0 %all-reduce.11.cloned.1.call-done = (bf16[256,4352]{0,1:T(8,128)(2,1)}, bf16[2048,704]{1,0:T(8,128)(2,1)}, bf16[2048,704]{1,0:T(8,128)(2,1)}, bf16[704,2048]{1,0:T(8,128)(2,1)}) async-done(((bf16[256,4352]{0,1:T(8,128)(2,1)}, bf16[2048,704]{1,0:T(8,128)(2,1)}, bf16[2048,704]{1,0:T(8,128)(2,1)}, bf16[704,2048]{1,0:T(8,128)(2,1)}), (bf16[256,4352]{0,1:T(8,128)(2,1)}, bf16[2048,704]{1,0:T(8,128)(2,1)}, ...) | async-done | bytes 10878992 | tf_op jit(solution)/shard_map/psum | solution.py:263
  (320 shorter events, 476.6 us)
Async XLA Ops:
  7.2 97.5 %all-gather.14.cloned.1.call-start = ((), (), s32[]{:S(2)}) async-start(), calls=%async_computation.5 | async-start | bytes 1179648 | tf_op jit(solution)/shard_map/all_gather | solution.py:114
  7.2 37.5 %copy-start.47 = (f32[64]{0:T(128)}, f32[64]{0:T(128)S(1)}, u32[]{:S(2)}) copy-start(f32[64]{0:T(128)S(1)} %multiply_power_fusion) | copy-start | bytes 772
  21.3 129.1 %copy-start.36 = (f32[8,1,256]{2,1,0:T(1,128)}, f32[8,1,256]{2,1,0:T(1,128)S(1)}, u32[]{:S(2)}) copy-start(f32[8,1,256]{2,1,0:T(1,128)S(1)} %convert_element_type.154) | copy-start | bytes 24580
  21.4 23.5 copy-start.39
  23.5 38.8 %copy-start.5 = (bf16[512,2048]{1,0:T(8,128)(2,1)S(1)}, bf16[512,2048]{1,0:T(8,128)(2,1)}, u32[]{:S(2)}) copy-start(bf16[512,2048]{1,0:T(8,128)(2,1)} %param.17) | copy-start | bytes 6291460
  24.1 126.3 %copy-start.40 = (f32[512]{0:T(512)}, f32[512]{0:T(512)S(1)}, u32[]{:S(2)}) copy-start(f32[512]{0:T(512)S(1)} %get-tuple-element.460) | copy-start | bytes 6148
  40.1 23.6 copy-start.42
  43.3 115.0 %copy-start.25 = (f32[512,64]{0,1:T(8,128)}, f32[512,64]{0,1:T(8,128)S(1)}, u32[]{:S(2)}) copy-start(f32[512,64]{0,1:T(8,128)S(1)} %get-tuple-element.458) | copy-start | bytes 393220
  44.0 106.4 %all-gather.12.cloned.1.call-start = ((), (), s32[]{:S(2)}) async-start(), calls=%async_computation.4 | async-start | bytes 9437184 | tf_op jit(solution)/shard_map/all_gather | solution.py:92
  44.8 128.5 %all-gather.16.cloned.1.call-start = ((), (), s32[]{:S(2)}) async-start(), calls=%async_computation.6 | async-start | bytes 1179648 | tf_op jit(solution)/shard_map/all_gather | solution.py:115
  63.7 539.7 %all-gather.18.cloned.1.call-start = ((), (), s32[]{:S(2)}) async-start(), calls=%async_computation.7 | async-start | bytes 9437184 | tf_op jit(solution)/shard_map/all_gather | solution.py:95
  64.3 551.9 %all-gather.20.cloned.1.call-start = ((), (), s32[]{:S(2)}) async-start(), calls=%async_computation.8 | async-start | bytes 25952256 | tf_op jit(solution)/shard_map/all_gather | solution.py:163
  64.9 15.7 copy-start.31
  64.9 30.2 copy-start.50
  64.9 596.6 %all-gather.22.cloned.1.call-start = ((), (), s32[]{:S(2)}) async-start(), calls=%async_computation.9 | async-start | bytes 25952256 | tf_op jit(solution)/shard_map/all_gather | solution.py:164
  65.5 798.6 %all-gather.24.cloned.1.call-start = ((), (), s32[]{:S(2)}) async-start(), calls=%async_computation.10 | async-start | bytes 25952256 | tf_op jit(solution)/shard_map/all_gather | solution.py:165
  66.3 1731.4 %reduce-scatter.6.cloned.1.call-start = ((), (), s32[]{:S(2)}) async-start(), calls=%async_computation.11 | async-start | bytes 1179648 | tf_op jit(solution)/shard_map/reduce_scatter | solution.py:228
  193.1 20.9 copy-start
  247.0 24.4 copy-start.49
  300.8 20.9 copy-start
  354.6 23.9 copy-start.49
  407.9 20.6 copy-start
  461.4 24.4 copy-start.49
  515.2 20.7 copy-start
  568.9 23.9 copy-start.49
  603.3 10.3 copy-start.3
  603.4 10.3 copy-start.11
  603.4 10.3 copy-start.21
  603.4 10.3 copy-start.23
  603.4 10.3 copy-start.27
  603.4 10.3 copy-start.33
  603.4 12.3 copy-start.38
  616.2 276.0 %copy-start.13 = (bf16[512,2048]{1,0:T(8,128)(2,1)}, bf16[512,2048]{1,0:T(8,128)(2,1)S(1)}, u32[]{:S(2)}) copy-start(bf16[512,2048]{1,0:T(8,128)(2,1)S(1)} %multiply_convert_fusion.4) | copy-start | bytes 6291460
  910.1 20.1 copy-start.8
  930.2 20.2 copy-start.45
  1109.7 26.3 copy-start.1
  1135.9 8.4 copy-start.4
  1144.4 10.0 copy-start.2
  1301.1 26.3 copy-start.1
  1327.4 8.4 copy-start.4
  1335.8 10.0 copy-start.2
  1492.6 26.3 copy-start.1
  1518.8 8.4 copy-start.4
  1527.3 10.0 copy-start.2
  1684.0 26.3 copy-start.1
  1710.3 8.4 copy-start.4
  1718.7 10.0 copy-start.2
  1732.0 5.5 copy-start.14
  1737.4 67.2 %reduce-scatter.8.cloned.1.call-start = ((), (), s32[]{:S(2)}) async-start(), calls=%async_computation.12 | async-start | bytes 1179648 | tf_op jit(solution)/shard_map/reduce_scatter | solution.py:231
  1755.5 931.6 %all-reduce.9.cloned.1.call-start = ((), (), s32[]{:S(2)}) async-start(), calls=%async_computation.15 | async-start | bytes 92274688
  1787.1 11.5 copy-start.43
  1787.1 11.5 copy-start.48
  1787.1 12.1 copy-start.26
  1787.1 1080.4 %reduce-scatter.10.cloned.1.call-start = ((), (), s32[]{:S(2)}) async-start(), calls=%async_computation.13 | async-start | bytes 20054016 | tf_op jit(solution)/shard_map/reduce_scatter | solution.py:244
  1799.2 4.6 copy-start.6
  1804.7 9.2 slice-start
  1806.6 7.3 slice-start.1
  1821.7 1273.9 %reduce-scatter.12.cloned.1.call-start = ((), (), s32[]{:S(2)}) async-start(), calls=%async_computation.14 | async-start | bytes 25952256 | tf_op jit(solution)/shard_map/reduce_scatter | solution.py:184
  1841.6 1479.4 %all-reduce.11.cloned.1.call-start = ((), (), s32[]{:S(2)}) async-start(), calls=%async_computation.16 | async-start | bytes 22806528 | tf_op jit(solution)/shard_map/psum | solution.py:263
  3096.2 20.0 copy-start.16
  3117.8 7.3 copy-start.18
  3117.8 7.3 copy-start.35
  3125.2 41.3 %copy-start.44 = (f32[512]{0:T(512)S(1)}, f32[512]{0:T(512)}, u32[]{:S(2)}) copy-start(f32[512]{0:T(512)} %get-tuple-element.459) | copy-start | bytes 6148
  3331.2 5.4 copy-start.10
  (18 other events, 43.4 us)
Sparse Core Ops, SparseCore 0:
  44.1 22.8 all-gather.13
  68.7 81.7 all-gather.11
  152.6 20.6 all-gather.15
  174.7 81.6 all-gather.17
  257.9 201.1 all-gather.19
  460.6 200.8 all-gather.21
  663.2 200.8 all-gather.23
  1737.6 30.3 reduce-scatter.5
  1770.9 30.5 reduce-scatter.7
  1803.8 883.2 all-reduce.8
  2689.5 177.9 reduce-scatter.9
  2869.7 225.7 reduce-scatter.11
  3100.1 220.7 all-reduce.10
where the time goes:
time: 3370 us; the launch traced here: 3350 us
  waiting for transfers between devices  1660 us (49%)
  matrix products  689 us (20%)
  local copies, waits for them, and re-layouts  656 us (19%)
  other arithmetic  211 us (6%)
  blocking collectives  118 us (4%)
    unnamed x14, waiting for transfers between devices  847 us
    dot_general x30, matrix products, contract(): lax.dot_general(left, right, (((left_dim,), (right_dim,)), ((), ())), pre...  376 us
    reduce_scatter x1, waiting for transfers between devices, shards(): lax.psum_scatter(contract(activation, grad_out, 0, 0).astype(jnp.bfloat16...  228 us
    all_gather x1, waiting for transfers between devices, shards(): lax.all_gather(down_weight, 'fsdp', axis=0, tiled=True)  183 us
    reduce_scatter x1, waiting for transfers between devices, shards(): lax.psum_scatter(jnp.concatenate([contract(normed, d_query_raw, 0, 0), co...  171 us
    sub x4, matrix products, back_block(): d_probs - row_delta  159 us
    psum x1, waiting for transfers between devices, shards(): lax.psum(attn_part, 'replica').astype(jnp.float32)  148 us
    dot_general x14, matrix products, matmul(): return jnp.dot(left, right, preferred_element_type=jnp.float32)  147 us
  transfers between devices with their start and end apart: 13, of which 8 were waited for; matrix products, arithmetic and copies ran while one was open for 19% of the time, Pallas kernels for 0%

commit v1 on v0

v1 whole, which is shorter than its diff:
```python
import functools

import jax
import jax.numpy as jnp
from jax import lax
from jax.experimental import pallas as pl
from jax.experimental.pallas import tpu as pltpu
from jax.sharding import PartitionSpec as P

GROUP_TOK = 4096
PROMPT = 2048
MAX_CONT = 384
EPSILON = 1e-05
ROPE_BASE = 10000.0
MASKED = -1e30
LOG2E = 1.4426950408889634

TILE = 128
CHUNK = 512
HEAD_GROUP = 4


def matmul(left, right):
    return jnp.dot(left, right, preferred_element_type=jnp.float32)


def contract(left, right, left_dim, right_dim):
    return lax.dot_general(
        left, right, (((left_dim,), (right_dim,)), ((), ())), preferred_element_type=jnp.float32
    )


def rope_tables(pos_ids, head_dim):
    half_width = head_dim // 2
    frequency = ROPE_BASE ** (-jnp.arange(half_width, dtype=jnp.float32) * 2.0 / head_dim)
    angles = pos_ids.astype(jnp.float32)[:, None] * frequency[None, :]
    cos_half, sin_half = jnp.cos(angles), jnp.sin(angles)
    return (
        jnp.concatenate([cos_half, cos_half], axis=1),
        jnp.concatenate([-sin_half, sin_half], axis=1),
    )


def swap_halves(values):
    half_width = values.shape[-1] // 2
    return jnp.concatenate([values[..., half_width:], values[..., :half_width]], axis=-1)


def norm_forward(values, gain):
    inverse = lax.rsqrt(jnp.mean(values * values, axis=-1, keepdims=True) + EPSILON)
    return (values * inverse * gain, inverse)


def norm_backward(values, inverse, gain, grad):
    scaled = grad * gain
    inner_mean = jnp.mean(scaled * values, axis=-1, keepdims=True)
    return (
        inverse * scaled - values * inverse**3 * inner_mean,
        jnp.sum(grad * values * inverse, axis=0),
    )


def swiglu_back(d_activation, gate_proj, up_proj):
    sigmoid_gate = jax.nn.sigmoid(gate_proj)
    d_gate = (
        d_activation * up_proj * sigmoid_gate * (1.0 + gate_proj * (1.0 - sigmoid_gate))
    ).astype(jnp.bfloat16)
    d_up = (d_activation * gate_proj * sigmoid_gate).astype(jnp.bfloat16)
    return (d_gate, d_up)


def stack_heads(block):
    heads = block.shape[1] // 128
    return jnp.concatenate([block[:, h * 128 : (h + 1) * 128] for h in range(heads)], axis=0)


def chunk_plan(base_ref):
    first = base_ref[0] + pl.program_id(0) * TILE
    in_prompt = first < PROMPT
    full = jnp.where(in_prompt, first // CHUNK, PROMPT // CHUNK)
    last = jnp.where(
        in_prompt, first // CHUNK * CHUNK, jnp.maximum(PROMPT, first + TILE - CHUNK)
    )
    return first, full, pl.multiple_of(last, TILE)


def attend_kernel(
    base_ref, q_ref, kv_ref, cos_ref, sin_ref, low_ref, mixed_ref, rot_ref, log_ref, values, top, acc
):
    factor = 128**-0.5 * LOG2E

    @pl.when((pl.program_id(0) == 0) & (pl.program_id(1) == 0))
    def _():
        values[:, :128] = kv_ref[:, 128:]
        values[:, 128:] = jnp.ones_like(values[:, 128:])

    first, full, last = chunk_plan(base_ref)
    cos_table, sin_table = cos_ref[...], sin_ref[...]
    pieces = []
    for h in range(HEAD_GROUP):
        raw = q_ref[:, h * 128 : (h + 1) * 128]
        turned = raw * cos_table + pltpu.roll(raw, 64, 1) * sin_table
        turned = turned.astype(jnp.bfloat16)
        rot_ref[:, h * 128 : (h + 1) * 128] = turned
        pieces.append(turned)
    queries = jnp.concatenate(pieces, axis=0)
    rows = queries.shape[0]
    top[...] = jnp.full_like(top, MASKED)
    acc[...] = jnp.zeros_like(acc)

    def step(start, masked):
        scores = contract(queries, kv_ref[pl.ds(start, CHUNK), :128], 1, 1) * factor
        if masked:
            key_at = start + lax.broadcasted_iota(jnp.int32, (rows, CHUNK), 1)
            row_at = lax.broadcasted_iota(jnp.int32, (rows, 1), 0) % TILE + first
            low = jnp.concatenate([low_ref[:, :1]] * HEAD_GROUP, axis=0)
            scores = jnp.where((key_at <= row_at) & (key_at >= low), scores, MASKED)
        before = top[:, :1]
        after = jnp.maximum(before, jnp.max(scores, axis=1, keepdims=True))
        weights = jnp.exp2(scores - after).astype(jnp.bfloat16)
        acc[...] = acc[...] * jnp.exp2(before - after) + matmul(
            weights, values[pl.ds(start, CHUNK), :]
        )
        top[...] = jnp.broadcast_to(after, top.shape)

    @pl.loop(0, full)
    def _(at):
        step(pl.multiple_of(at * CHUNK, CHUNK), False)

    step(last, True)
    total = acc[:, 128:]
    mixed = acc[:, :128] / total
    for h in range(HEAD_GROUP):
        mixed_ref[:, h * 128 : (h + 1) * 128] = mixed[h * TILE : (h + 1) * TILE].astype(jnp.bfloat16)
    log_ref[0, 0] = (top[...] + jnp.log2(total)).T[:8]


def attend(base, q_raw, kv, cos_table, sin_table, low):
    tok_rows, width = q_raw.shape
    tiles, groups = tok_rows // TILE, width // (128 * HEAD_GROUP)
    lanes, rows = 128 * HEAD_GROUP, TILE * HEAD_GROUP
    tile_spec = pl.BlockSpec((TILE, lanes), lambda i, g, b: (i, g))
    row_spec = pl.BlockSpec((TILE, 128), lambda i, g, b: (i, 0))
    pairs = tok_rows * (width // 128) * 2560
    return pl.pallas_call(
        attend_kernel,
        out_shape=(
            jax.ShapeDtypeStruct((tok_rows, width), jnp.bfloat16),
            jax.ShapeDtypeStruct((tok_rows, width), jnp.bfloat16),
            jax.ShapeDtypeStruct((tiles, groups, 8, rows), jnp.float32),
        ),
        grid_spec=pltpu.PrefetchScalarGridSpec(
            num_scalar_prefetch=1,
            grid=(tiles, groups),
            in_specs=[
                tile_spec,
                pl.BlockSpec(kv.shape, lambda i, g, b: (0, 0)),
                row_spec,
                row_spec,
                row_spec,
            ],
            out_specs=[
                tile_spec,
                tile_spec,
                pl.BlockSpec((1, 1, 8, rows), lambda i, g, b: (i, g, 0, 0)),
            ],
            scratch_shapes=[
                pltpu.VMEM(kv.shape, jnp.bfloat16),
                pltpu.VMEM((rows, 128), jnp.float32),
                pltpu.VMEM((rows, 256), jnp.float32),
            ],
        ),
        compiler_params=pltpu.CompilerParams(vmem_limit_bytes=40 << 20),
        cost_estimate=pl.CostEstimate(
            flops=pairs * 768, transcendentals=pairs, bytes_accessed=16 << 20
        ),
        name="attend",
    )(base, q_raw, kv, cos_table, sin_table, low)


def attend_back_kernel(
    base_ref,
    q_ref,
    kv_ref,
    cos_ref,
    sin_ref,
    low_ref,
    mixed_ref,
    d_mixed_ref,
    log_ref,
    d_q_ref,
    d_kv_ref,
    sums,
    d_q,
):
    scale = 128**-0.5
    factor = scale * LOG2E
    at_start = (pl.program_id(0) == 0) & (pl.program_id(1) == 0)
    at_end = (pl.program_id(0) == pl.num_programs(0) - 1) & (
        pl.program_id(1) == pl.num_programs(1) - 1
    )

    @pl.when(at_start)
    def _():
        sums[...] = jnp.zeros_like(sums)

    first, full, last = chunk_plan(base_ref)
    queries = stack_heads(q_ref[...])
    d_rows = stack_heads(d_mixed_ref[...])
    mixed = stack_heads(mixed_ref[...])
    rows = queries.shape[0]
    products = d_rows.astype(jnp.float32) * mixed.astype(jnp.float32)
    delta = jnp.sum(products.T, axis=0, keepdims=True)
    log_total = log_ref[0, 0, :1]
    d_q[...] = jnp.zeros_like(d_q)

    def step(start, masked):
        keys = kv_ref[pl.ds(start, CHUNK), :128]
        values = kv_ref[pl.ds(start, CHUNK), 128:]
        scores = contract(keys, queries, 1, 1) * factor
        probs = jnp.exp2(scores - log_total)
        if masked:
            key_at = start + lax.broadcasted_iota(jnp.int32, (CHUNK, rows), 0)
            row_at = lax.broadcasted_iota(jnp.int32, (1, rows), 1) % TILE + first
            low = jnp.concatenate([low_ref[:1]] * HEAD_GROUP, axis=1)
            probs = jnp.where((key_at <= row_at) & (key_at >= low), probs, 0.0)
        d_probs = contract(values, d_rows, 1, 1)
        d_scores = (probs * (d_probs - delta)).astype(jnp.bfloat16)
        sums[pl.ds(start, CHUNK), 128:] += matmul(probs.astype(jnp.bfloat16), d_rows)
        sums[pl.ds(start, CHUNK), :128] += matmul(d_scores, queries)
        d_q[...] += contract(d_scores, keys, 0, 0)

    @pl.loop(0, full)
    def _(at):
        step(pl.multiple_of(at * CHUNK, CHUNK), False)

    step(last, True)
    cos_table, sin_table = cos_ref[...] * scale, sin_ref[...] * scale
    for h in range(HEAD_GROUP):
        turned = d_q[h * TILE : (h + 1) * TILE]
        raw = turned * cos_table - pltpu.roll(turned, 64, 1) * sin_table
        d_q_ref[:, h * 128 : (h + 1) * 128] = raw.astype(jnp.bfloat16)

    @pl.when(at_end)
    def _():
        d_kv_ref[:, :128] = (sums[:, :128] * scale).astype(jnp.bfloat16)
        d_kv_ref[:, 128:] = sums[:, 128:].astype(jnp.bfloat16)


def attend_back(base, queries, kv, cos_table, sin_table, low, mixed, d_mixed, logs):
    tok_rows, width = queries.shape
    tiles, groups = tok_rows // TILE, width // (128 * HEAD_GROUP)
    lanes, rows = 128 * HEAD_GROUP, TILE * HEAD_GROUP
    tile_spec = pl.BlockSpec((TILE, lanes), lambda i, g, b: (i, g))
    row_spec = pl.BlockSpec((TILE, 128), lambda i, g, b: (i, 0))
    whole = pl.BlockSpec(kv.shape, lambda i, g, b: (0, 0))
    pairs = tok_rows * (width // 128) * 2560
    return pl.pallas_call(
        attend_back_kernel,
        out_shape=(
            jax.ShapeDtypeStruct((tok_rows, width), jnp.bfloat16),
            jax.ShapeDtypeStruct(kv.shape, jnp.bfloat16),
        ),
        grid_spec=pltpu.PrefetchScalarGridSpec(
            num_scalar_prefetch=1,
            grid=(tiles, groups),
            in_specs=[
                tile_spec,
                whole,
                row_spec,
                row_spec,
                pl.BlockSpec((8, TILE), lambda i, g, b: (0, i)),
                tile_spec,
                tile_spec,
                pl.BlockSpec((1, 1, 8, rows), lambda i, g, b: (i, g, 0, 0)),
            ],
            out_specs=[tile_spec, whole],
            scratch_shapes=[
                pltpu.VMEM(kv.shape, jnp.float32),
                pltpu.VMEM((rows, 128), jnp.float32),
            ],
        ),
        compiler_params=pltpu.CompilerParams(vmem_limit_bytes=48 << 20),
        cost_estimate=pl.CostEstimate(
            flops=pairs * 1280, transcendentals=pairs, bytes_accessed=16 << 20
        ),
        name="attend_back",
    )(base, queries, kv, cos_table, sin_table, low, mixed, d_mixed, logs)


def swap(value, step):
    copies = lax.axis_size("replica")
    return lax.ppermute(value, "replica", [(r, r ^ step) for r in range(copies)])


def gather_copies(block):
    half = block.shape[0] // 2
    beside, across = swap(block, 1), swap(block, 2)
    opposite = jnp.concatenate([swap(beside[:half], 2), swap(across[half:], 1)], axis=0)
    return [block, beside, across, opposite]


def scatter_copies(parts):
    own, beside, across, opposite = parts
    half = opposite.shape[0] // 2
    low = jnp.bfloat16
    first = swap(opposite[:half].astype(low), 1)
    second = swap(opposite[half:].astype(low), 2)
    across = jnp.concatenate(
        [across[:half].astype(jnp.float32) + first.astype(jnp.float32), across[half:]], axis=0
    )
    beside = jnp.concatenate(
        [beside[:half], beside[half:].astype(jnp.float32) + second.astype(jnp.float32)], axis=0
    )
    return (
        own.astype(jnp.float32)
        + swap(beside.astype(low), 1).astype(jnp.float32)
        + swap(across.astype(low), 2).astype(jnp.float32)
    )


def gather_shards(value):
    return lax.all_gather(value, "fsdp", axis=0, tiled=True)


def scatter_shards(value):
    return lax.psum_scatter(value, "fsdp", scatter_dimension=0, tiled=True)


def place(pieces, copy_index):
    out = jnp.zeros((len(pieces),) + pieces[0].shape, pieces[0].dtype)
    for step, piece in enumerate(pieces):
        out = lax.dynamic_update_index_in_dim(out, piece, copy_index ^ step, 0)
    return out


def quarter(shard, copy_index):
    rows = shard.shape[0] // lax.axis_size("replica")
    return lax.dynamic_slice_in_dim(shard, copy_index * rows, rows, 0)


def whole_weight(shard, copy_index):
    rows, width = shard.shape
    copies, fsdp_size = lax.axis_size("replica"), lax.axis_size("fsdp")
    pieces = gather_copies(gather_shards(quarter(shard, copy_index)))
    out = jnp.zeros((fsdp_size, copies, rows // copies, width), shard.dtype)
    for step, piece in enumerate(pieces):
        out = lax.dynamic_update_slice_in_dim(
            out, piece.reshape(fsdp_size, 1, rows // copies, width), copy_index ^ step, 1
        )
    return out.reshape(fsdp_size * rows, width)


def sum_weight_grad(partial, copy_index):
    rows, width = partial.shape
    copies, fsdp_size = lax.axis_size("replica"), lax.axis_size("fsdp")
    fine = rows // (copies * fsdp_size)
    view = partial.reshape(fsdp_size, copies, fine, width)
    parts = [
        lax.dynamic_slice_in_dim(view, copy_index ^ step, 1, 1).reshape(fsdp_size * fine, width)
        for step in range(copies)
    ]
    summed = scatter_shards(scatter_copies(parts).astype(jnp.bfloat16))
    return place(gather_copies(summed), copy_index).reshape(copies * fine, width).astype(jnp.float32)


def shards(
    tokens,
    segments,
    positions,
    query_weight,
    key_weight,
    value_weight,
    output_weight,
    attn_gain,
    gate_weight,
    up_weight,
    down_weight,
    ffn_gain,
    grad_out,
):
    tok_rows, model_width = tokens.shape
    head_dim = key_weight.shape[1]
    fsdp_size = lax.axis_size("fsdp")
    fsdp_index = lax.axis_index("fsdp")
    copy_index = lax.axis_index("replica")
    copies = lax.axis_size("replica")
    low = jnp.bfloat16

    gains = lax.all_gather(jnp.stack([attn_gain, ffn_gain]), "fsdp", axis=1, tiled=True)
    gain_attn = gains[0].astype(jnp.float32)
    gain_ffn = gains[1].astype(jnp.float32)
    w_qkv = whole_weight(
        jnp.concatenate([query_weight, key_weight, value_weight], axis=1), copy_index
    )
    inputs = tokens.astype(jnp.float32)
    normed_full, inverse_attn = norm_forward(inputs, gain_attn)
    normed = normed_full.astype(low)
    qkv = matmul(normed, w_qkv)
    query_raw = qkv[:, :model_width]
    key_raw = qkv[:, model_width : model_width + head_dim]
    value_rows = qkv[:, model_width + head_dim :].astype(low)
    cos_table, sin_table = rope_tables(positions, head_dim)
    key_rot = (key_raw * cos_table + swap_halves(key_raw) * sin_table).astype(low)
    kv_all = gather_shards(jnp.concatenate([key_rot, value_rows], axis=1))
    key_width = max(GROUP_TOK, tok_rows)
    window_start = fsdp_index * tok_rows // key_width * key_width
    one_group = fsdp_size * tok_rows == key_width
    kv = kv_all if one_group else lax.dynamic_slice_in_dim(kv_all, window_start, key_width, 0)

    base = (fsdp_index * tok_rows - window_start).astype(jnp.int32)
    row_at = base + jnp.arange(tok_rows, dtype=jnp.int32)
    lowest = jnp.where(positions < PROMPT, 0, row_at - (positions - PROMPT))
    base = base[None]
    mixed_rows, queries, logs = attend(
        base,
        query_raw,
        kv,
        cos_table,
        sin_table,
        jnp.broadcast_to(lowest[:, None], (tok_rows, 128)),
    )

    w_out = whole_weight(output_weight, copy_index)
    hidden = inputs + matmul(mixed_rows, w_out)
    normed_ffn_full, inverse_ffn = norm_forward(hidden, gain_ffn)
    normed_ffn = normed_ffn_full.astype(low)

    w_gate = gather_shards(quarter(gate_weight.T, copy_index))
    w_up = gather_shards(quarter(up_weight.T, copy_index))
    w_down = gather_shards(quarter(down_weight, copy_index))
    grad_blocks = gather_copies(grad_out)
    grads = jnp.concatenate(grad_blocks, axis=0)
    normed_blocks = gather_copies(normed_ffn)
    normed_all = jnp.concatenate(normed_blocks, axis=0)

    d_activation = contract(grads, w_down, 1, 1)
    gate_proj = contract(normed_all, w_gate, 1, 1)
    up_proj = contract(normed_all, w_up, 1, 1)
    activation = (jax.nn.silu(gate_proj) * up_proj).astype(low)
    d_gate, d_up = swiglu_back(d_activation, gate_proj, up_proj)
    d_normed_parts = matmul(d_gate, w_gate) + matmul(d_up, w_up)
    d_normed_ffn = scatter_copies(jnp.split(d_normed_parts, copies))
    out_parts = matmul(activation, w_down)
    layer_out = (hidden + scatter_copies(jnp.split(out_parts, copies))).astype(low)

    def ffn_grad(partial):
        summed = scatter_shards(partial.astype(low))
        pieces = place(gather_copies(summed), copy_index)
        return pieces.reshape(-1, model_width).astype(jnp.float32)

    gate_grad = ffn_grad(contract(d_gate, normed_all, 0, 0)).T
    up_grad = ffn_grad(contract(d_up, normed_all, 0, 0)).T
    down_grad = ffn_grad(contract(activation, grads, 0, 0))

    cotangent = grad_out.astype(jnp.float32)
    resid_ffn, ffn_gain_term = norm_backward(hidden, inverse_ffn, gain_ffn, d_normed_ffn)
    d_hidden = cotangent + resid_ffn
    d_branch = d_hidden.astype(low)
    d_mixed = contract(d_branch, w_out, 1, 1).astype(low)
    output_grad = sum_weight_grad(contract(mixed_rows, d_branch, 0, 0), copy_index)

    d_query_raw, d_kv = attend_back(
        base,
        queries,
        kv,
        cos_table,
        sin_table,
        jnp.broadcast_to(lowest[None, :], (8, tok_rows)),
        mixed_rows,
        d_mixed,
        logs,
    )
    query_grad = sum_weight_grad(contract(normed, d_query_raw, 0, 0), copy_index)
    if not one_group:
        d_kv = lax.dynamic_update_slice_in_dim(
            jnp.zeros((fsdp_size * tok_rows, 2 * head_dim), low), d_kv, window_start, 0
        )
    d_kv_sum = scatter_shards(d_kv).astype(jnp.float32)
    d_key = d_kv_sum[:, :head_dim]
    d_key_raw = (d_key * cos_table - swap_halves(d_key) * sin_table).astype(low)
    d_kv_raw = jnp.concatenate([d_key_raw, d_kv_sum[:, head_dim:].astype(low)], axis=1)
    kv_grad = sum_weight_grad(contract(normed, d_kv_raw, 0, 0), copy_index)
    d_normed = contract(d_query_raw, w_qkv[:, :model_width], 1, 1) + contract(
        d_kv_raw, w_qkv[:, model_width:], 1, 1
    )
    resid_attn, attn_gain_term = norm_backward(inputs, inverse_attn, gain_attn, d_normed)
    input_grad = d_hidden + resid_attn
    gain_terms = lax.psum(jnp.stack([attn_gain_term, ffn_gain_term]), ("replica", "fsdp"))
    gain_grads = lax.dynamic_slice_in_dim(
        gain_terms, fsdp_index * (model_width // fsdp_size), model_width // fsdp_size, 1
    )
    return (
        layer_out,
        input_grad,
        query_grad,
        kv_grad[:, :head_dim],
        kv_grad[:, head_dim:],
        output_grad,
        gain_grads[0],
        gate_grad,
        up_grad,
        down_grad,
        gain_grads[1],
    )


def solution(mesh):
    return jax.shard_map(
        shards,
        mesh=mesh,
        in_specs=(
            P(("replica", "fsdp"), None),
            P(("replica", "fsdp")),
            P(("replica", "fsdp")),
            P("fsdp", None),
            P("fsdp", None),
            P("fsdp", None),
            P("fsdp", None),
            P("fsdp"),
            P(None, "fsdp"),
            P(None, "fsdp"),
            P("fsdp", None),
            P("fsdp"),
            P(("replica", "fsdp"), None),
        ),
        out_specs=(
            P(("replica", "fsdp"), None),
            P(("replica", "fsdp"), None),
            P("fsdp", None),
            P("fsdp", None),
            P("fsdp", None),
            P("fsdp", None),
            P("fsdp"),
            P(None, "fsdp"),
            P(None, "fsdp"),
            P("fsdp", None),
            P("fsdp"),
        ),
        check_vma=False,
    )
```

time: 3370 us -> 1290 us (0.38)
  waiting for transfers between devices: 1660 us -> 633 us
  local copies, waits for them, and re-layouts: 656 us -> 114 us
  matrix products: 689 us -> 234 us
  other arithmetic: 211 us -> 84.7 us
  starting transfers between devices: 0.52 us -> 71.8 us
  Pallas kernels: 0 us -> 45.1 us
  blocking collectives: 118 us -> 83.3 us
    unnamed x14 -> x13, waiting for transfers between devices: 847 us -> 0.21 us
    ppermute x0 -> x60, waiting for transfers between devices: none -> 371 us  [swap(): lax.ppermute(value, 'replica', [(r, r ^ step) for r in range(copies)])]
    reshape x21 -> x0, local copies, waits for them, and re-layouts: 296 us -> none  [the longest x4 96.6 us: attend_block(): (exp_scores / totals).astype(jnp.bfloat16)]
    convert_element_type x13 -> x0, local copies, waits for them, and re-layouts: 275 us -> none  [the longest x4 88.5 us: back_block(): probs.astype(jnp.bfloat16).reshape(tok_rows * HEAD_BLOCK, key_width)]
    all_gather x7 -> x6, waiting for transfers between devices: 266 us -> 35.4 us  [gather_shards(): return lax.all_gather(value, 'fsdp', axis=0, tiled=True)]
    dot_general x30 -> x12, matrix products: 376 us -> 158 us  [contract(): lax.dot_general(left, right, (((left_dim,), (right_dim,)), ((), ())), pre...]
    reduce_scatter x4 -> x7, waiting for transfers between devices: 399 us -> 227 us  [scatter_shards(): return lax.psum_scatter(value, 'fsdp', scatter_dimension=0, tiled=True)]
    sub x4 -> x0, matrix products: 159 us -> none  [back_block(): d_probs - row_delta]
  transfers between devices with their start and end apart: 13 -> 73, of which waited for: 8 -> 35; matrix products, arithmetic and copies ran while one was open for 19% -> 25% of each run, Pallas kernels for 0% -> 2%
where the time goes in v1:
time: 1290 us; the launch traced here: 1280 us
  waiting for transfers between devices  633 us (49%)
  matrix products  234 us (18%)
  local copies, waits for them, and re-layouts  114 us (9%)
  other arithmetic  84.7 us (7%)
  blocking collectives  83.3 us (6%)
  starting transfers between devices  71.8 us (6%)
  Pallas kernels  45.1 us (3%)
  between operations  15.5 us (1%)
    ppermute x60, waiting for transfers between devices, swap(): lax.ppermute(value, 'replica', [(r, r ^ step) for r in range(copies)])  371 us
    reduce_scatter x7, waiting for transfers between devices, scatter_shards(): return lax.psum_scatter(value, 'fsdp', scatter_dimension=0, tiled=True)  227 us
    dot_general x12, matrix products, contract(): lax.dot_general(left, right, (((left_dim,), (right_dim,)), ((), ())), pre...  158 us
    dot_general x5, matrix products, matmul(): return jnp.dot(left, right, preferred_element_type=jnp.float32)  75.7 us
    psum x1, blocking collectives, shards(): lax.psum(jnp.stack([attn_gain_term, ffn_gain_term]), ('replica', 'fsdp'))  73.3 us
    ppermute x60, starting transfers between devices, swap(): lax.ppermute(value, 'replica', [(r, r ^ step) for r in range(copies)])  70.3 us
    all_gather x6, waiting for transfers between devices, gather_shards(): return lax.all_gather(value, 'fsdp', axis=0, tiled=True)  35.4 us
  transfers between devices with their start and end apart: 73, of which 35 were waited for; matrix products, arithmetic and copies ran while one was open for 25% of the time, Pallas kernels for 2%

profile of v1, /device:TPU:0, one launch (start us, length us, event | category | flops | bytes accessed | tf_op | source)
XLA Modules:
  0.0 1282.0 jit_solution(1817915543004957002)
XLA Ops:
  9.2 35.4 %all-gather.7.cloned.1.call-done = bf16[512,2304]{1,0:T(8,128)(2,1)} async-done(((bf16[64,2304]{1,0:T(8,128)(2,1)}), bf16[512,2304]{1,0:T(8,128)(2,1)}) %all-gather.7.cloned.1.call-update) | async-done | bytes 2359312 | tf_op jit(solution)/shard_map/all_gather | solution.py:323
  50.6 10.0 all_gather.21
  65.2 33.1 %collective-permute-done = bf16[512,2304]{1,0:T(8,128)(2,1)} collective-permute-done((bf16[512,2304]{1,0:T(8,128)(2,1)}, bf16[512,2304]{1,0:T(8,128)(2,1)}, u32[]{:S(2)}, u32[]{:S(2)}) %collective-permute-start) | collective-permute-done | bytes 2359328 | tf_op jit(solution)/shard_map/ppermute | solution.py:293
  109.9 17.1 %collective-permute-done.2 = bf16[256,2304]{1,0:T(8,128)(2,1)S(1)} collective-permute-done((bf16[256,2304]{1,0:T(8,128)(2,1)S(1)}, bf16[256,2304]{1,0:T(8,128)(2,1)S(1)}, u32[]{:S(2)}, u32[]{:S(2)}) %collective-permute-start.2) | collective-permute-done | bytes 1179680 | tf_op jit(solution)/shard_map/ppermute | solution.py:293
  127.0 2.7 collective-permute-done.3
  131.5 5.2 fusion.58
  147.2 44.7 %collective-permute-done.4 = bf16[512,2048]{1,0:T(8,128)(2,1)S(1)} collective-permute-done((bf16[512,2048]{1,0:T(8,128)(2,1)}, bf16[512,2048]{1,0:T(8,128)(2,1)S(1)}, u32[]{:S(2)}, u32[]{:S(2)}) %collective-permute-start.4) | collective-permute-done | bytes 2097184 | tf_op jit(solution)/shard_map/ppermute | solution.py:293
  199.8 4.4 broadcast_in_dim.117
  208.7 49.2 %collective-permute-done.6 = bf16[256,2048]{1,0:T(8,128)(2,1)} collective-permute-done((bf16[256,2048]{1,0:T(8,128)(2,1)}, bf16[256,2048]{1,0:T(8,128)(2,1)}, u32[]{:S(2)}, u32[]{:S(2)}) %collective-permute-start.6) | collective-permute-done | bytes 1048608 | tf_op jit(solution)/shard_map/ppermute | solution.py:293
  261.2 2.6 slice.363.q_ref
  264.0 2.2 copy-done.2
  267.9 21.6 %attend.1 = (bf16[512,2048]{1,0:T(8,128)(2,1)S(1)}, bf16[512,2048]{1,0:T(8,128)(2,1)S(1)}, f32[4,4,8,512]{3,2,1,0:T(8,128)S(1)}) custom-call(s32[1]{0:T(128)} %bitcast.base_ref, f32[512,2048]{1,0:T(8,128)S(1)} %copy-done.2, bf16[4096,256]{1,0:T(8,128)(2,1)S(1)} %copy-done.3, f32[512,128]{1,0:T(8,128)S(1)} %get-tuple-element.70.cos_ref, ...), custom_call_target="tpu_custom_call" | custom-call | flops 16106127360 | bytes 16777216 | tf_op jit(solution)/shard_map/attend/pallas_call | solution.py:145
  289.5 8.6 multiply_reduce_fusion.2
  311.7 21.9 %collective-permute-done.8 = bf16[512,2048]{1,0:T(8,128)(2,1)S(1)} collective-permute-done((bf16[512,2048]{1,0:T(8,128)(2,1)S(1)}, bf16[512,2048]{1,0:T(8,128)(2,1)S(1)}, u32[]{:S(2)}, u32[]{:S(2)}) %collective-permute-start.8) | collective-permute-done | bytes 2097184 | tf_op jit(solution)/shard_map/ppermute | solution.py:293
  334.3 22.6 %collective-permute-done.18 = bf16[256,2048]{1,0:T(8,128)(2,1)S(1)} collective-permute-done((bf16[256,2048]{1,0:T(8,128)(2,1)S(1)}, bf16[256,2048]{1,0:T(8,128)(2,1)S(1)}, u32[]{:S(2)}, u32[]{:S(2)}) %collective-permute-start.18) | collective-permute-done | bytes 1048608 | tf_op jit(solution)/shard_map/ppermute | solution.py:293
  363.2 16.1 %collective-permute-done.10 = bf16[256,2048]{1,0:T(8,128)(2,1)S(1)} collective-permute-done((bf16[256,2048]{1,0:T(8,128)(2,1)S(1)}, bf16[256,2048]{1,0:T(8,128)(2,1)S(1)}, u32[]{:S(2)}, u32[]{:S(2)}) %collective-permute-start.10) | collective-permute-done | bytes 1048608 | tf_op jit(solution)/shard_map/ppermute | solution.py:293
  380.4 2.7 collective-permute-done.11
  384.2 18.7 %fusion.72 = f32[2048,1408]{1,0:T(8,128)} fusion(bf16[2048,2048]{1,0:T(8,128)(2,1)} %constant_dynamic-update-slice_fusion, bf16[1408,2048]{1,0:T(8,128)(2,1)} %all-gather.15.cloned.1.call-done), kind=kOutput, calls=%fused_computation.211 | convolution fusion | flops 11811160064 | bytes 25690112 | tf_op jit(solution)/shard_map/dot_general | solution.py:28
  402.9 19.1 %fusion.71 = f32[2048,1408]{1,0:T(8,128)} fusion(bf16[2048,2048]{1,0:T(8,128)(2,1)} %constant_dynamic-update-slice_fusion, bf16[1408,2048]{1,0:T(8,128)(2,1)} %all-gather.13.cloned.1.call-done), kind=kOutput, calls=%fused_computation.210 | convolution fusion | flops 11811160064 | bytes 25690112 | tf_op jit(solution)/shard_map/dot_general | solution.py:28
  422.0 26.0 %multiply_convert_fusion = (bf16[2048,1408]{1,0:T(8,128)(2,1)}, bf16[2048,1408]{1,0:T(8,128)(2,1)}, bf16[2048,1408]{1,0:T(8,128)(2,1)}) fusion(f32[2048,1408]{1,0:T(8,128)} %fusion.71, f32[2048,1408]{1,0:T(8,128)} %fusion.72, bf16[2048,2048]{1,0:T(8,128)(2,1)} %copy-done.32, bf16[1408,2048]{1,0:T(8,128)(2,1)} %all-gather.17.cloned.1.call-done), kind=kOutput, calls=%fused_computation | convolution fusion | flops 11857297408 | bytes 54525952 | tf_op jit(solution)/shard_map/dot_general | solution.py:28
  448.0 19.2 %fusion.73 = f32[2048,2048]{1,0:T(8,128)} fusion(bf16[2048,1408]{1,0:T(8,128)(2,1)} %get-tuple-element.30, bf16[1408,2048]{1,0:T(8,128)(2,1)} %all-gather.13.cloned.1.call-done), kind=kOutput, calls=%fused_computation.212 | convolution fusion | flops 11811160064 | bytes 28311552 | tf_op jit(solution)/shard_map/dot_general | solution.py:24
  467.2 24.3 %fusion.69 = (bf16[2048,2048]{1,0:T(8,128)(2,1)}, f32[2048,2048]{1,0:T(8,128)}) fusion(f32[2048,2048]{1,0:T(8,128)} %fusion.73, bf16[2048,1408]{1,0:T(8,128)(2,1)} %get-tuple-element.29, bf16[1408,2048]{1,0:T(8,128)(2,1)} %all-gather.15.cloned.1.call-done), kind=kOutput, calls=%fused_computation.208 | convolution fusion | flops 11819548672 | bytes 53477376 | tf_op jit(solution)/shard_map/dot_general | solution.py:24
  491.5 3.5 fusion.60
  496.2 18.5 %fusion.70 = (bf16[2048,2048]{1,0:T(8,128)(2,1)}, f32[2048,2048]{1,0:T(8,128)S(1)}) fusion(bf16[2048,1408]{1,0:T(8,128)(2,1)} %get-tuple-element.31, bf16[1408,2048]{1,0:T(8,128)(2,1)} %all-gather.17.cloned.1.call-done), kind=kOutput, calls=%fused_computation.209 | convolution fusion | flops 11815354368 | bytes 36700160 | tf_op jit(solution)/shard_map/dot_general | solution.py:24
  514.7 5.7 fusion.61
  524.4 3.5 fusion.23
  532.0 3.4 collective-permute-done.12
  542.6 36.9 %collective-permute-done.21 = bf16[512,2048]{1,0:T(8,128)(2,1)} collective-permute-done((bf16[512,2048]{1,0:T(8,128)(2,1)}, bf16[512,2048]{1,0:T(8,128)(2,1)}, u32[]{:S(2)}, u32[]{:S(2)}) %collective-permute-start.21) | collective-permute-done | bytes 2097184 | tf_op jit(solution)/shard_map/ppermute | solution.py:293
  579.5 6.3 multiply_reduce_fusion
  585.8 38.6 %collective-permute-done.13 = bf16[512,2048]{1,0:T(8,128)(2,1)} collective-permute-done((bf16[512,2048]{1,0:T(8,128)(2,1)}, bf16[512,2048]{1,0:T(8,128)(2,1)}, u32[]{:S(2)}, u32[]{:S(2)}) %collective-permute-start.13) | collective-permute-done | bytes 2097184 | tf_op jit(solution)/shard_map/ppermute | solution.py:293
  624.5 8.6 subtract_add_fusion
  633.1 10.7 convolution_convert_fusion.3.d_mixed_ref
  643.9 8.4 fusion.32
  652.3 23.5 %attend_back.1 = (bf16[512,2048]{1,0:T(8,128)(2,1)S(1)}, bf16[4096,256]{1,0:T(8,128)(2,1)}) custom-call(s32[1]{0:T(128)} %bitcast.base_ref, bf16[512,2048]{1,0:T(8,128)(2,1)} %copy-done.6, bf16[4096,256]{1,0:T(8,128)(2,1)} %all-gather.9.cloned.1.call-done.kv_ref, f32[512,128]{1,0:T(8,128)S(1)} %get-tuple-element.70.cos_ref, ...), custom_call_target="tpu_custom_call" | custom-call | flops 26843545600 | bytes 16777216 | tf_op jit(solution)/shard_map/attend_back/pallas_call | solution.py:258
  676.2 6.3 fusion.56
  682.5 6.0 dynamic-slice_convert_fusion
  693.0 2.7 constant_dynamic-slice_fusion.3
  695.7 4.2 dynamic-slice_convert_fusion.3
  701.4 4.7 constant_dynamic-slice_fusion.4
  714.5 145.4 %reduce-scatter.8.cloned.1.call-done = bf16[512,256]{1,0:T(8,128)(2,1)} async-done(((bf16[4096,256]{1,0:T(8,128)(2,1)}), bf16[512,256]{1,0:T(8,128)(2,1)}) %reduce-scatter.8.cloned.1.call-update) | async-done | bytes 262160 | tf_op jit(solution)/shard_map/reduce_scatter | solution.py:327
  863.2 2.6 fusion.50
  875.1 4.8 constant_dynamic-slice_fusion.8
  883.7 5.9 fusion.16
  889.8 12.4 collective-permute-done.24
  902.3 2.3 fusion.29
  910.2 2.5 constant_dynamic-slice_fusion.9
  912.7 37.2 %collective-permute-done.25 = bf16[512,2048]{1,0:T(8,128)(2,1)S(1)} collective-permute-done((bf16[512,2048]{1,0:T(8,128)(2,1)S(1)}, bf16[512,2048]{1,0:T(8,128)(2,1)S(1)}, u32[]{:S(2)}, u32[]{:S(2)}) %collective-permute-start.25) | collective-permute-done | bytes 2097184 | tf_op jit(solution)/shard_map/ppermute | solution.py:293
  951.9 2.4 fusion.18
  954.4 18.0 %convolution_convert_fusion = bf16[1408,2048]{1,0:T(8,128)(2,1)} fusion(bf16[2048,1408]{1,0:T(8,128)(2,1)} %get-tuple-element.31, bf16[2048,2048]{1,0:T(8,128)(2,1)} %copy-done.32), kind=kOutput, calls=%fused_computation.13 | convolution fusion | flops 11814043648 | bytes 19922944 | tf_op jit(solution)/shard_map/dot_general | solution.py:28
  972.4 18.0 %convolution_convert_fusion.1 = bf16[1408,2048]{1,0:T(8,128)(2,1)} fusion(bf16[2048,1408]{1,0:T(8,128)(2,1)} %get-tuple-element.29, bf16[2048,2048]{1,0:T(8,128)(2,1)} %constant_dynamic-update-slice_fusion), kind=kOutput, calls=%fused_computation.14 | convolution fusion | flops 11814043648 | bytes 19922944 | tf_op jit(solution)/shard_map/dot_general | solution.py:28
  990.7 17.9 %convolution_convert_fusion.2 = bf16[1408,2048]{1,0:T(8,128)(2,1)} fusion(bf16[2048,1408]{1,0:T(8,128)(2,1)} %get-tuple-element.30, bf16[2048,2048]{1,0:T(8,128)(2,1)} %constant_dynamic-update-slice_fusion), kind=kOutput, calls=%fused_computation.15 | convolution fusion | flops 11814043648 | bytes 19922944 | tf_op jit(solution)/shard_map/dot_general | solution.py:28
  1010.9 10.6 fusion.10
  1021.5 73.3 %psum.7 = f32[2,2048]{1,0:T(2,128)S(1)} all-reduce(f32[2,2048]{1,0:T(2,128)S(1)} %pad_maximum_fusion.18), channel_id=1, replica_groups=mesh['replica'=4,'fsdp'=8] {'replica','fsdp'}, use_global_device_ids=true, to_apply=%region_10.11 | all-reduce | flops 4096 | bytes 32768 | tf_op jit(solution)/shard_map/psum | solution.py:489
  1095.4 7.1 fusion.7
  1102.5 2.3 collective-permute-start.36
  1119.7 2.9 collective-permute-done.44
  1129.2 2.7 collective-permute-done.30
  1139.3 22.3 %reduce-scatter.18.cloned.1.call-done = bf16[176,2048]{1,0:T(8,128)(2,1)} async-done(((bf16[1408,2048]{1,0:T(8,128)(2,1)}), bf16[176,2048]{1,0:T(8,128)(2,1)}) %reduce-scatter.18.cloned.1.call-update) | async-done | bytes 720912 | tf_op jit(solution)/shard_map/reduce_scatter | solution.py:327
  1168.9 58.9 %reduce-scatter.16.cloned.1.call-done = bf16[176,2048]{1,0:T(8,128)(2,1)} async-done(((bf16[1408,2048]{1,0:T(8,128)(2,1)}), bf16[176,2048]{1,0:T(8,128)(2,1)}) %reduce-scatter.16.cloned.1.call-update) | async-done | bytes 720912 | tf_op jit(solution)/shard_map/reduce_scatter | solution.py:327
  1251.5 6.1 collective-permute-done.58
  1258.3 3.5 bitcast_convert_fusion
  1261.8 3.6 collective-permute-done.54
  1266.3 5.1 convert_bitcast_fusion
  1271.5 3.5 convert_bitcast_fusion.1
  (363 shorter events, 196.4 us)
Async XLA Ops:
  7.2 37.4 %all-gather.7.cloned.1.call-start = ((), (), s32[]{:S(2)}) async-start(), calls=%async_computation.7 | async-start | bytes 2654208 | tf_op jit(solution)/shard_map/all_gather | solution.py:323
  9.1 134.0 %all-gather.11.cloned.1.call-start = ((), (), s32[]{:S(2)}) async-start(), calls=%async_computation.9 | async-start | bytes 2359296 | tf_op jit(solution)/shard_map/all_gather | solution.py:323
  44.6 53.7 %collective-permute-start = (bf16[512,2304]{1,0:T(8,128)(2,1)}, bf16[512,2304]{1,0:T(8,128)(2,1)}, u32[]{:S(2)}, u32[]{:S(2)}) collective-permute-start(bf16[512,2304]{1,0:T(8,128)(2,1)} %all-gather.7.cloned.1.call-done), channel_id=1, source_target_pairs={{0,8},{8,0},{16,24},{24,16},{1,9},{9,1},{17,25},{25,17},{2,10},{10... | collective-permute-start | bytes 7077896 | tf_op jit(solution)/shard_map/ppermute | solution.py:293
  46.1 55.1 %collective-permute-start.1 = (bf16[512,2304]{1,0:T(8,128)(2,1)}, bf16[512,2304]{1,0:T(8,128)(2,1)}, u32[]{:S(2)}, u32[]{:S(2)}) collective-permute-start(bf16[512,2304]{1,0:T(8,128)(2,1)} %all-gather.7.cloned.1.call-done), channel_id=1, source_target_pairs={{0,16},{8,24},{16,0},{24,8},{1,17},{9,25},{17,1},{25,9},{2,18},{10... | collective-permute-start | bytes 7077896 | tf_op jit(solution)/shard_map/ppermute | solution.py:293
  49.2 214.6 %all-gather.9.cloned.1.call-start = ((), (), s32[]{:S(2)}) async-start(), calls=%async_computation.8 | async-start | bytes 2359296 | tf_op jit(solution)/shard_map/all_gather | solution.py:323
  99.7 27.4 %collective-permute-start.2 = (bf16[256,2304]{1,0:T(8,128)(2,1)S(1)}, bf16[256,2304]{1,0:T(8,128)(2,1)S(1)}, u32[]{:S(2)}, u32[]{:S(2)}) collective-permute-start(bf16[256,2304]{1,0:T(8,128)(2,1)S(1)} %slice.361), channel_id=1, source_target_pairs={{0,16},{8,24},{16,0},{24,8},{1,17},{9,25},{17,1},{25,9},{2,18},{10... | collective-permute-start | bytes 3538952 | tf_op jit(solution)/shard_map/ppermute | solution.py:293
  102.6 27.2 %collective-permute-start.3 = (bf16[256,2304]{1,0:T(8,128)(2,1)S(1)}, bf16[256,2304]{1,0:T(8,128)(2,1)}, u32[]{:S(2)}, u32[]{:S(2)}) collective-permute-start(bf16[256,2304]{1,0:T(8,128)(2,1)S(1)} %slice.362), channel_id=1, source_target_pairs={{0,8},{8,0},{16,24},{24,16},{1,9},{9,1},{17,25},{25,17},{2,10},{10... | collective-permute-start | bytes 3538952 | tf_op jit(solution)/shard_map/ppermute | solution.py:293
  139.9 244.3 %all-gather.15.cloned.1.call-start = ((), (), s32[]{:S(2)}) async-start(), calls=%async_computation.11 | async-start | bytes 6488064 | tf_op jit(solution)/shard_map/all_gather | solution.py:323
  140.9 261.9 %all-gather.13.cloned.1.call-start = ((), (), s32[]{:S(2)}) async-start(), calls=%async_computation.10 | async-start | bytes 6488064 | tf_op jit(solution)/shard_map/all_gather | solution.py:323
  143.0 278.9 %all-gather.17.cloned.1.call-start = ((), (), s32[]{:S(2)}) async-start(), calls=%async_computation.12 | async-start | bytes 6488064 | tf_op jit(solution)/shard_map/all_gather | solution.py:323
  143.1 48.8 %collective-permute-start.4 = (bf16[512,2048]{1,0:T(8,128)(2,1)}, bf16[512,2048]{1,0:T(8,128)(2,1)S(1)}, u32[]{:S(2)}, u32[]{:S(2)}) collective-permute-start(bf16[512,2048]{1,0:T(8,128)(2,1)} %all-gather.11.cloned.1.call-done), channel_id=1, source_target_pairs={{0,8},{8,0},{16,24},{24,16},{1,9},{9,1},{17,25},{25,17},{2,10},{10... | collective-permute-start | bytes 6291464 | tf_op jit(solution)/shard_map/ppermute | solution.py:293
  144.7 48.9 %collective-permute-start.5 = (bf16[512,2048]{1,0:T(8,128)(2,1)}, bf16[512,2048]{1,0:T(8,128)(2,1)S(1)}, u32[]{:S(2)}, u32[]{:S(2)}) collective-permute-start(bf16[512,2048]{1,0:T(8,128)(2,1)} %all-gather.11.cloned.1.call-done), channel_id=1, source_target_pairs={{0,16},{8,24},{16,0},{24,8},{1,17},{9,25},{17,1},{25,9},{2,18},{10... | collective-permute-start | bytes 6291464 | tf_op jit(solution)/shard_map/ppermute | solution.py:293
  145.2 156.9 %collective-permute-start.16 = (bf16[512,2048]{1,0:T(8,128)(2,1)}, bf16[512,2048]{1,0:T(8,128)(2,1)}, u32[]{:S(2)}, u32[]{:S(2)}) collective-permute-start(bf16[512,2048]{1,0:T(8,128)(2,1)} %param.24), channel_id=1, source_target_pairs={{0,8},{8,0},{16,24},{24,16},{1,9},{9,1},{17,25},{25,17},{2,10},{10... | collective-permute-start | bytes 6291464 | tf_op jit(solution)/shard_map/ppermute | solution.py:293
  145.8 159.1 %collective-permute-start.17 = (bf16[512,2048]{1,0:T(8,128)(2,1)}, bf16[512,2048]{1,0:T(8,128)(2,1)}, u32[]{:S(2)}, u32[]{:S(2)}) collective-permute-start(bf16[512,2048]{1,0:T(8,128)(2,1)} %param.24), channel_id=1, source_target_pairs={{0,16},{8,24},{16,0},{24,8},{1,17},{9,25},{17,1},{25,9},{2,18},{10... | collective-permute-start | bytes 6291464 | tf_op jit(solution)/shard_map/ppermute | solution.py:293
  193.0 64.8 %collective-permute-start.6 = (bf16[256,2048]{1,0:T(8,128)(2,1)}, bf16[256,2048]{1,0:T(8,128)(2,1)}, u32[]{:S(2)}, u32[]{:S(2)}) collective-permute-start(bf16[256,2048]{1,0:T(8,128)(2,1)} %slice.368), channel_id=1, source_target_pairs={{0,16},{8,24},{16,0},{24,8},{1,17},{9,25},{17,1},{25,9},{2,18},{10... | collective-permute-start | bytes 3145736 | tf_op jit(solution)/shard_map/ppermute | solution.py:293
  196.0 61.9 %collective-permute-start.7 = (bf16[256,2048]{1,0:T(8,128)(2,1)}, bf16[256,2048]{1,0:T(8,128)(2,1)}, u32[]{:S(2)}, u32[]{:S(2)}) collective-permute-start(bf16[256,2048]{1,0:T(8,128)(2,1)} %slice.369), channel_id=1, source_target_pairs={{0,8},{8,0},{16,24},{24,16},{1,9},{9,1},{17,25},{25,17},{2,10},{10... | collective-permute-start | bytes 3145736 | tf_op jit(solution)/shard_map/ppermute | solution.py:293
  199.5 660.5 %reduce-scatter.8.cloned.1.call-start = ((), (), s32[]{:S(2)}) async-start(), calls=%async_computation.13 | async-start | bytes 2359296 | tf_op jit(solution)/shard_map/reduce_scatter | solution.py:327
  300.9 32.6 %collective-permute-start.8 = (bf16[512,2048]{1,0:T(8,128)(2,1)S(1)}, bf16[512,2048]{1,0:T(8,128)(2,1)S(1)}, u32[]{:S(2)}, u32[]{:S(2)}) collective-permute-start(bf16[512,2048]{1,0:T(8,128)(2,1)S(1)} %get-tuple-element.26), channel_id=1, source_target_pairs={{0,8},{8,0},{16,24},{24,16},{1,9},{9,1},{17,25},{25,17},{2,10},{10... | collective-permute-start | bytes 6291464 | tf_op jit(solution)/shard_map/ppermute | solution.py:293
  301.5 55.5 %collective-permute-start.9 = (bf16[512,2048]{1,0:T(8,128)(2,1)S(1)}, bf16[512,2048]{1,0:T(8,128)(2,1)S(1)}, u32[]{:S(2)}, u32[]{:S(2)}) collective-permute-start(bf16[512,2048]{1,0:T(8,128)(2,1)S(1)} %get-tuple-element.26), channel_id=1, source_target_pairs={{0,16},{8,24},{16,0},{24,8},{1,17},{9,25},{17,1},{25,9},{2,18},{10... | collective-permute-start | bytes 6291464 | tf_op jit(solution)/shard_map/ppermute | solution.py:293
  303.4 53.4 %collective-permute-start.18 = (bf16[256,2048]{1,0:T(8,128)(2,1)S(1)}, bf16[256,2048]{1,0:T(8,128)(2,1)S(1)}, u32[]{:S(2)}, u32[]{:S(2)}) collective-permute-start(bf16[256,2048]{1,0:T(8,128)(2,1)S(1)} %slice.379), channel_id=1, source_target_pairs={{0,16},{8,24},{16,0},{24,8},{1,17},{9,25},{17,1},{25,9},{2,18},{10... | collective-permute-start | bytes 3145736 | tf_op jit(solution)/shard_map/ppermute | solution.py:293
  306.2 52.4 %collective-permute-start.19 = (bf16[256,2048]{1,0:T(8,128)(2,1)S(1)}, bf16[256,2048]{1,0:T(8,128)(2,1)S(1)}, u32[]{:S(2)}, u32[]{:S(2)}) collective-permute-start(bf16[256,2048]{1,0:T(8,128)(2,1)S(1)} %slice.380), channel_id=1, source_target_pairs={{0,8},{8,0},{16,24},{24,16},{1,9},{9,1},{17,25},{25,17},{2,10},{10... | collective-permute-start | bytes 3145736 | tf_op jit(solution)/shard_map/ppermute | solution.py:293
  333.6 45.7 %collective-permute-start.10 = (bf16[256,2048]{1,0:T(8,128)(2,1)S(1)}, bf16[256,2048]{1,0:T(8,128)(2,1)S(1)}, u32[]{:S(2)}, u32[]{:S(2)}) collective-permute-start(bf16[256,2048]{1,0:T(8,128)(2,1)S(1)} %slice.371), channel_id=1, source_target_pairs={{0,16},{8,24},{16,0},{24,8},{1,17},{9,25},{17,1},{25,9},{2,18},{10... | collective-permute-start | bytes 3145736 | tf_op jit(solution)/shard_map/ppermute | solution.py:293
  357.1 26.1 %collective-permute-start.11 = (bf16[256,2048]{1,0:T(8,128)(2,1)S(1)}, bf16[256,2048]{1,0:T(8,128)(2,1)S(1)}, u32[]{:S(2)}, u32[]{:S(2)}) collective-permute-start(bf16[256,2048]{1,0:T(8,128)(2,1)S(1)} %slice.372), channel_id=1, source_target_pairs={{0,8},{8,0},{16,24},{24,16},{1,9},{9,1},{17,25},{25,17},{2,10},{10... | collective-permute-start | bytes 3145736 | tf_op jit(solution)/shard_map/ppermute | solution.py:293
  495.0 28.4 %collective-permute-start.20 = (bf16[256,2048]{1,0:T(8,128)(2,1)}, bf16[256,2048]{1,0:T(8,128)(2,1)S(1)}, u32[]{:S(2)}, u32[]{:S(2)}) collective-permute-start(bf16[256,2048]{1,0:T(8,128)(2,1)} %get-tuple-element.47), channel_id=1, source_target_pairs={{0,16},{8,24},{16,0},{24,8},{1,17},{9,25},{17,1},{25,9},{2,18},{10... | collective-permute-start | bytes 3145736 | tf_op jit(solution)/shard_map/ppermute | solution.py:293
  495.6 27.8 %collective-permute-start.22 = (bf16[256,2048]{1,0:T(8,128)(2,1)S(1)}, bf16[256,2048]{1,0:T(8,128)(2,1)}, u32[]{:S(2)}, u32[]{:S(2)}) collective-permute-start(bf16[256,2048]{1,0:T(8,128)(2,1)S(1)} %get-tuple-element.46), channel_id=1, source_target_pairs={{0,8},{8,0},{16,24},{24,16},{1,9},{9,1},{17,25},{25,17},{2,10},{10... | collective-permute-start | bytes 3145736 | tf_op jit(solution)/shard_map/ppermute | solution.py:293
  520.5 14.9 %collective-permute-start.12 = (bf16[256,2048]{1,0:T(8,128)(2,1)S(1)}, bf16[256,2048]{1,0:T(8,128)(2,1)S(1)}, u32[]{:S(2)}, u32[]{:S(2)}) collective-permute-start(bf16[256,2048]{1,0:T(8,128)(2,1)S(1)} %get-tuple-element.51), channel_id=1, source_target_pairs={{0,16},{8,24},{16,0},{24,8},{1,17},{9,25},{17,1},{25,9},{2,18},{10... | collective-permute-start | bytes 3145736 | tf_op jit(solution)/shard_map/ppermute | solution.py:293
  521.9 14.8 %collective-permute-start.14 = (bf16[256,2048]{1,0:T(8,128)(2,1)S(1)}, bf16[256,2048]{1,0:T(8,128)(2,1)S(1)}, u32[]{:S(2)}, u32[]{:S(2)}) collective-permute-start(bf16[256,2048]{1,0:T(8,128)(2,1)S(1)} %get-tuple-element.50), channel_id=1, source_target_pairs={{0,8},{8,0},{16,24},{24,16},{1,9},{9,1},{17,25},{25,17},{2,10},{10... | collective-permute-start | bytes 3145736 | tf_op jit(solution)/shard_map/ppermute | solution.py:293
  529.3 50.2 %collective-permute-start.21 = (bf16[512,2048]{1,0:T(8,128)(2,1)}, bf16[512,2048]{1,0:T(8,128)(2,1)}, u32[]{:S(2)}, u32[]{:S(2)}) collective-permute-start(bf16[512,2048]{1,0:T(8,128)(2,1)} %pad_maximum_fusion.4), channel_id=1, source_target_pairs={{0,8},{8,0},{16,24},{24,16},{1,9},{9,1},{17,25},{25,17},{2,10},{10... | collective-permute-start | bytes 6291464 | tf_op jit(solution)/shard_map/ppermute | solution.py:293
  531.3 48.2 %collective-permute-start.23 = (bf16[512,2048]{1,0:T(8,128)(2,1)}, bf16[512,2048]{1,0:T(8,128)(2,1)}, u32[]{:S(2)}, u32[]{:S(2)}) collective-permute-start(bf16[512,2048]{1,0:T(8,128)(2,1)} %pad_maximum_fusion.5), channel_id=1, source_target_pairs={{0,16},{8,24},{16,0},{24,8},{1,17},{9,25},{17,1},{25,9},{2,18},{10... | collective-permute-start | bytes 6291464 | tf_op jit(solution)/shard_map/ppermute | solution.py:293
  539.0 85.5 %collective-permute-start.13 = (bf16[512,2048]{1,0:T(8,128)(2,1)}, bf16[512,2048]{1,0:T(8,128)(2,1)}, u32[]{:S(2)}, u32[]{:S(2)}) collective-permute-start(bf16[512,2048]{1,0:T(8,128)(2,1)} %pad_maximum_fusion.2), channel_id=1, source_target_pairs={{0,8},{8,0},{16,24},{24,16},{1,9},{9,1},{17,25},{25,17},{2,10},{10... | collective-permute-start | bytes 6291464 | tf_op jit(solution)/shard_map/ppermute | solution.py:293
  542.0 82.4 %collective-permute-start.15 = (bf16[512,2048]{1,0:T(8,128)(2,1)}, bf16[512,2048]{1,0:T(8,128)(2,1)}, u32[]{:S(2)}, u32[]{:S(2)}) collective-permute-start(bf16[512,2048]{1,0:T(8,128)(2,1)} %pad_maximum_fusion.3), channel_id=1, source_target_pairs={{0,16},{8,24},{16,0},{24,8},{1,17},{9,25},{17,1},{25,9},{2,18},{10... | collective-permute-start | bytes 6291464 | tf_op jit(solution)/shard_map/ppermute | solution.py:293
  675.8 426.8 %reduce-scatter.12.cloned.1.call-start = ((), (), s32[]{:S(2)}) async-start(), calls=%async_computation.15 | async-start | bytes 294912 | tf_op jit(solution)/shard_map/reduce_scatter | solution.py:327
  690.1 16.0 %collective-permute-start.40 = (bf16[256,2048]{1,0:T(8,128)(2,1)}, bf16[256,2048]{1,0:T(8,128)(2,1)}, u32[]{:S(2)}, u32[]{:S(2)}) collective-permute-start(bf16[256,2048]{1,0:T(8,128)(2,1)} %bitcast.46), channel_id=1, source_target_pairs={{0,16},{8,24},{16,0},{24,8},{1,17},{9,25},{17,1},{25,9},{2,18},{10... | collective-permute-start | bytes 3145736 | tf_op jit(solution)/shard_map/ppermute | solution.py:293
  690.8 20.1 %collective-permute-start.42 = (bf16[256,2048]{1,0:T(8,128)(2,1)}, bf16[256,2048]{1,0:T(8,128)(2,1)}, u32[]{:S(2)}, u32[]{:S(2)}) collective-permute-start(bf16[256,2048]{1,0:T(8,128)(2,1)} %bitcast.48), channel_id=1, source_target_pairs={{0,8},{8,0},{16,24},{24,16},{1,9},{9,1},{17,25},{25,17},{2,10},{10... | collective-permute-start | bytes 3145736 | tf_op jit(solution)/shard_map/ppermute | solution.py:293
  709.4 174.3 %collective-permute-start.41 = (bf16[512,2048]{1,0:T(8,128)(2,1)}, bf16[512,2048]{1,0:T(8,128)(2,1)}, u32[]{:S(2)}, u32[]{:S(2)}) collective-permute-start(bf16[512,2048]{1,0:T(8,128)(2,1)} %pad_maximum_fusion.8), channel_id=1, source_target_pairs={{0,8},{8,0},{16,24},{24,16},{1,9},{9,1},{17,25},{25,17},{2,10},{10... | collective-permute-start | bytes 6291464 | tf_op jit(solution)/shard_map/ppermute | solution.py:293
  714.1 169.7 %collective-permute-start.43 = (bf16[512,2048]{1,0:T(8,128)(2,1)}, bf16[512,2048]{1,0:T(8,128)(2,1)}, u32[]{:S(2)}, u32[]{:S(2)}) collective-permute-start(bf16[512,2048]{1,0:T(8,128)(2,1)} %pad_maximum_fusion.9), channel_id=1, source_target_pairs={{0,16},{8,24},{16,0},{24,8},{1,17},{9,25},{17,1},{25,9},{2,18},{10... | collective-permute-start | bytes 6291464 | tf_op jit(solution)/shard_map/ppermute | solution.py:293
  871.0 9.6 collective-permute-start.33
  873.7 9.2 collective-permute-start.35
  879.9 22.4 %collective-permute-start.24 = (bf16[256,2048]{1,0:T(8,128)(2,1)}, bf16[256,2048]{1,0:T(8,128)(2,1)}, u32[]{:S(2)}, u32[]{:S(2)}) collective-permute-start(bf16[256,2048]{1,0:T(8,128)(2,1)} %bitcast.19), channel_id=1, source_target_pairs={{0,16},{8,24},{16,0},{24,8},{1,17},{9,25},{17,1},{25,9},{2,18},{10... | collective-permute-start | bytes 3145736 | tf_op jit(solution)/shard_map/ppermute | solution.py:293
  880.6 26.2 %collective-permute-start.26 = (bf16[256,2048]{1,0:T(8,128)(2,1)}, bf16[256,2048]{1,0:T(8,128)(2,1)}, u32[]{:S(2)}, u32[]{:S(2)}) collective-permute-start(bf16[256,2048]{1,0:T(8,128)(2,1)} %bitcast.21), channel_id=1, source_target_pairs={{0,8},{8,0},{16,24},{24,16},{1,9},{9,1},{17,25},{25,17},{2,10},{10... | collective-permute-start | bytes 3145736 | tf_op jit(solution)/shard_map/ppermute | solution.py:293
  883.7 229.8 %reduce-scatter.14.cloned.1.call-start = ((), (), s32[]{:S(2)}) async-start(), calls=%async_computation.16 | async-start | bytes 2359296 | tf_op jit(solution)/shard_map/reduce_scatter | solution.py:327
  889.6 225.9 %reduce-scatter.10.cloned.1.call-start = ((), (), s32[]{:S(2)}) async-start(), calls=%async_computation.14 | async-start | bytes 2359296 | tf_op jit(solution)/shard_map/reduce_scatter | solution.py:327
  906.2 43.7 %collective-permute-start.25 = (bf16[512,2048]{1,0:T(8,128)(2,1)S(1)}, bf16[512,2048]{1,0:T(8,128)(2,1)S(1)}, u32[]{:S(2)}, u32[]{:S(2)}) collective-permute-start(bf16[512,2048]{1,0:T(8,128)(2,1)S(1)} %pad_maximum_fusion.6), channel_id=1, source_target_pairs={{0,8},{8,0},{16,24},{24,16},{1,9},{9,1},{17,25},{25,17},{2,10},{10... | collective-permute-start | bytes 6291464 | tf_op jit(solution)/shard_map/ppermute | solution.py:293
  908.7 43.2 %collective-permute-start.27 = (bf16[512,2048]{1,0:T(8,128)(2,1)S(1)}, bf16[512,2048]{1,0:T(8,128)(2,1)S(1)}, u32[]{:S(2)}, u32[]{:S(2)}) collective-permute-start(bf16[512,2048]{1,0:T(8,128)(2,1)S(1)} %pad_maximum_fusion.7), channel_id=1, source_target_pairs={{0,16},{8,24},{16,0},{24,8},{1,17},{9,25},{17,1},{25,9},{2,18},{10... | collective-permute-start | bytes 6291464 | tf_op jit(solution)/shard_map/ppermute | solution.py:293
  954.3 182.9 %reduce-scatter.20.cloned.1.call-start = ((), (), s32[]{:S(2)}) async-start(), calls=%async_computation.19 | async-start | bytes 6488064 | tf_op jit(solution)/shard_map/reduce_scatter | solution.py:327
  972.4 189.1 %reduce-scatter.18.cloned.1.call-start = ((), (), s32[]{:S(2)}) async-start(), calls=%async_computation.18 | async-start | bytes 6488064 | tf_op jit(solution)/shard_map/reduce_scatter | solution.py:327
  990.5 237.3 %reduce-scatter.16.cloned.1.call-start = ((), (), s32[]{:S(2)}) async-start(), calls=%async_computation.17 | async-start | bytes 6488064 | tf_op jit(solution)/shard_map/reduce_scatter | solution.py:327
  1113.5 9.1 collective-permute-start.44
  1114.8 9.2 collective-permute-start.45
  1115.5 11.3 collective-permute-start.28
  1116.8 11.1 collective-permute-start.29
  1122.6 6.5 collective-permute-start.46
  1137.2 93.5 %collective-permute-start.56 = (bf16[176,2048]{1,0:T(8,128)(2,1)}, bf16[176,2048]{1,0:T(8,128)(2,1)}, u32[]{:S(2)}, u32[]{:S(2)}) collective-permute-start(bf16[176,2048]{1,0:T(8,128)(2,1)} %reduce-scatter.20.cloned.1.call-done), channel_id=1, source_target_pairs={{0,8},{8,0},{16,24},{24,16},{1,9},{9,1},{17,25},{25,17},{2,10},{10... | collective-permute-start | bytes 2162696 | tf_op jit(solution)/shard_map/ppermute | solution.py:293
  1137.9 96.7 %collective-permute-start.57 = (bf16[176,2048]{1,0:T(8,128)(2,1)}, bf16[176,2048]{1,0:T(8,128)(2,1)}, u32[]{:S(2)}, u32[]{:S(2)}) collective-permute-start(bf16[176,2048]{1,0:T(8,128)(2,1)} %reduce-scatter.20.cloned.1.call-done), channel_id=1, source_target_pairs={{0,16},{8,24},{16,0},{24,8},{1,17},{9,25},{17,1},{25,9},{2,18},{10... | collective-permute-start | bytes 2162696 | tf_op jit(solution)/shard_map/ppermute | solution.py:293
  1161.5 75.8 %collective-permute-start.52 = (bf16[176,2048]{1,0:T(8,128)(2,1)}, bf16[176,2048]{1,0:T(8,128)(2,1)}, u32[]{:S(2)}, u32[]{:S(2)}) collective-permute-start(bf16[176,2048]{1,0:T(8,128)(2,1)} %reduce-scatter.18.cloned.1.call-done), channel_id=1, source_target_pairs={{0,8},{8,0},{16,24},{24,16},{1,9},{9,1},{17,25},{25,17},{2,10},{10... | collective-permute-start | bytes 2162696 | tf_op jit(solution)/shard_map/ppermute | solution.py:293
  1163.0 78.1 %collective-permute-start.53 = (bf16[176,2048]{1,0:T(8,128)(2,1)}, bf16[176,2048]{1,0:T(8,128)(2,1)}, u32[]{:S(2)}, u32[]{:S(2)}) collective-permute-start(bf16[176,2048]{1,0:T(8,128)(2,1)} %reduce-scatter.18.cloned.1.call-done), channel_id=1, source_target_pairs={{0,16},{8,24},{16,0},{24,8},{1,17},{9,25},{17,1},{25,9},{2,18},{10... | collective-permute-start | bytes 2162696 | tf_op jit(solution)/shard_map/ppermute | solution.py:293
  1227.8 19.3 %collective-permute-start.48 = (bf16[176,2048]{1,0:T(8,128)(2,1)}, bf16[176,2048]{1,0:T(8,128)(2,1)S(1)}, u32[]{:S(2)}, u32[]{:S(2)}) collective-permute-start(bf16[176,2048]{1,0:T(8,128)(2,1)} %reduce-scatter.16.cloned.1.call-done), channel_id=1, source_target_pairs={{0,8},{8,0},{16,24},{24,16},{1,9},{9,1},{17,25},{25,17},{2,10},{10... | collective-permute-start | bytes 2162696 | tf_op jit(solution)/shard_map/ppermute | solution.py:293
  1230.8 19.1 %collective-permute-start.49 = (bf16[176,2048]{1,0:T(8,128)(2,1)S(1)}, bf16[176,2048]{1,0:T(8,128)(2,1)S(1)}, u32[]{:S(2)}, u32[]{:S(2)}) collective-permute-start(bf16[176,2048]{1,0:T(8,128)(2,1)S(1)} %copy-done.30), channel_id=1, source_target_pairs={{0,16},{8,24},{16,0},{24,8},{1,17},{9,25},{17,1},{25,9},{2,18},{10... | collective-permute-start | bytes 2162696 | tf_op jit(solution)/shard_map/ppermute | solution.py:293
  1234.5 23.1 %collective-permute-start.58 = (bf16[88,2048]{1,0:T(8,128)(2,1)S(1)}, bf16[88,2048]{1,0:T(8,128)(2,1)S(1)}, u32[]{:S(2)}, u32[]{:S(2)}) collective-permute-start(bf16[88,2048]{1,0:T(8,128)(2,1)S(1)} %slice.411), channel_id=1, source_target_pairs={{0,16},{8,24},{16,0},{24,8},{1,17},{9,25},{17,1},{25,9},{2,18},{10... | collective-permute-start | bytes 1081352 | tf_op jit(solution)/shard_map/ppermute | solution.py:293
  1237.4 20.8 %collective-permute-start.59 = (bf16[88,2048]{1,0:T(8,128)(2,1)S(1)}, bf16[88,2048]{1,0:T(8,128)(2,1)S(1)}, u32[]{:S(2)}, u32[]{:S(2)}) collective-permute-start(bf16[88,2048]{1,0:T(8,128)(2,1)S(1)} %slice.412), channel_id=1, source_target_pairs={{0,8},{8,0},{16,24},{24,16},{1,9},{9,1},{17,25},{25,17},{2,10},{10... | collective-permute-start | bytes 1081352 | tf_op jit(solution)/shard_map/ppermute | solution.py:293
  1241.1 24.3 %collective-permute-start.54 = (bf16[88,2048]{1,0:T(8,128)(2,1)S(1)}, bf16[88,2048]{1,0:T(8,128)(2,1)S(1)}, u32[]{:S(2)}, u32[]{:S(2)}) collective-permute-start(bf16[88,2048]{1,0:T(8,128)(2,1)S(1)} %slice.409), channel_id=1, source_target_pairs={{0,16},{8,24},{16,0},{24,8},{1,17},{9,25},{17,1},{25,9},{2,18},{10... | collective-permute-start | bytes 1081352 | tf_op jit(solution)/shard_map/ppermute | solution.py:293
  1247.1 18.3 %collective-permute-start.55 = (bf16[88,2048]{1,0:T(8,128)(2,1)S(1)}, bf16[88,2048]{1,0:T(8,128)(2,1)S(1)}, u32[]{:S(2)}, u32[]{:S(2)}) collective-permute-start(bf16[88,2048]{1,0:T(8,128)(2,1)S(1)} %slice.410), channel_id=1, source_target_pairs={{0,8},{8,0},{16,24},{24,16},{1,9},{9,1},{17,25},{25,17},{2,10},{10... | collective-permute-start | bytes 1081352 | tf_op jit(solution)/shard_map/ppermute | solution.py:293
  1249.9 21.5 %collective-permute-start.50 = (bf16[88,2048]{1,0:T(8,128)(2,1)S(1)}, bf16[88,2048]{1,0:T(8,128)(2,1)S(1)}, u32[]{:S(2)}, u32[]{:S(2)}) collective-permute-start(bf16[88,2048]{1,0:T(8,128)(2,1)S(1)} %slice.407), channel_id=1, source_target_pairs={{0,16},{8,24},{16,0},{24,8},{1,17},{9,25},{17,1},{25,9},{2,18},{10... | collective-permute-start | bytes 1081352 | tf_op jit(solution)/shard_map/ppermute | solution.py:293
  1257.7 13.8 %collective-permute-start.51 = (bf16[88,2048]{1,0:T(8,128)(2,1)S(1)}, bf16[88,2048]{1,0:T(8,128)(2,1)S(1)}, u32[]{:S(2)}, u32[]{:S(2)}) collective-permute-start(bf16[88,2048]{1,0:T(8,128)(2,1)S(1)} %slice.408), channel_id=1, source_target_pairs={{0,8},{8,0},{16,24},{24,16},{1,9},{9,1},{17,25},{25,17},{2,10},{10... | collective-permute-start | bytes 1081352 | tf_op jit(solution)/shard_map/ppermute | solution.py:293
  (58 other events, 1800.4 us)
Sparse Core Ops, SparseCore 0:
  10.3 34.3 all-gather.6
  49.4 26.4 all-gather.10
  140.0 27.2 all-gather.8
  169.4 59.9 all-gather.14
  231.4 59.0 all-gather.12
  292.1 59.0 all-gather.16
  675.9 184.0 reduce-scatter.7
  883.8 70.8 reduce-scatter.11
  957.1 33.9 reduce-scatter.13
  993.9 34.5 reduce-scatter.9
  1030.8 64.5 reduce-scatter.19
  1098.3 63.2 reduce-scatter.17
  1164.5 63.2 reduce-scatter.15

commit v2 on v1

--- a/solution.py
+++ b/solution.py
@@ -140,6 +140,7 @@
     tiles, groups = tok_rows // TILE, width // (128 * HEAD_GROUP)
     lanes, rows = 128 * HEAD_GROUP, TILE * HEAD_GROUP
     tile_spec = pl.BlockSpec((TILE, lanes), lambda i, g, b: (i, g))
+    true_spec = pl.BlockSpec((TILE, lanes), lambda i, g, b: (i, g ^ b[1]))
     row_spec = pl.BlockSpec((TILE, 128), lambda i, g, b: (i, 0))
     pairs = tok_rows * (width // 128) * 2560
     return pl.pallas_call(
@@ -160,7 +161,7 @@
                 row_spec,
             ],
             out_specs=[
-                tile_spec,
+                true_spec,
                 tile_spec,
                 pl.BlockSpec((1, 1, 8, rows), lambda i, g, b: (i, g, 0, 0)),
             ],
@@ -253,6 +254,7 @@
     lanes, rows = 128 * HEAD_GROUP, TILE * HEAD_GROUP
     tile_spec = pl.BlockSpec((TILE, lanes), lambda i, g, b: (i, g))
     row_spec = pl.BlockSpec((TILE, 128), lambda i, g, b: (i, 0))
+    true_spec = pl.BlockSpec((TILE, lanes), lambda i, g, b: (i, g ^ b[1]))
     whole = pl.BlockSpec(kv.shape, lambda i, g, b: (0, 0))
     pairs = tok_rows * (width // 128) * 2560
     return pl.pallas_call(
@@ -270,8 +272,8 @@
                 row_spec,
                 row_spec,
                 pl.BlockSpec((8, TILE), lambda i, g, b: (0, i)),
-                tile_spec,
-                tile_spec,
+                true_spec,
+                true_spec,
                 pl.BlockSpec((1, 1, 8, rows), lambda i, g, b: (i, g, 0, 0)),
             ],
             out_specs=[tile_spec, whole],
@@ -327,41 +329,31 @@
     return lax.psum_scatter(value, "fsdp", scatter_dimension=0, tiled=True)
 
 
-def place(pieces, copy_index):
-    out = jnp.zeros((len(pieces),) + pieces[0].shape, pieces[0].dtype)
-    for step, piece in enumerate(pieces):
-        out = lax.dynamic_update_index_in_dim(out, piece, copy_index ^ step, 0)
-    return out
-
-
-def quarter(shard, copy_index):
-    rows = shard.shape[0] // lax.axis_size("replica")
-    return lax.dynamic_slice_in_dim(shard, copy_index * rows, rows, 0)
-
-
-def whole_weight(shard, copy_index):
-    rows, width = shard.shape
-    copies, fsdp_size = lax.axis_size("replica"), lax.axis_size("fsdp")
-    pieces = gather_copies(gather_shards(quarter(shard, copy_index)))
-    out = jnp.zeros((fsdp_size, copies, rows // copies, width), shard.dtype)
-    for step, piece in enumerate(pieces):
-        out = lax.dynamic_update_slice_in_dim(
-            out, piece.reshape(fsdp_size, 1, rows // copies, width), copy_index ^ step, 1
-        )
-    return out.reshape(fsdp_size * rows, width)
-
-
-def sum_weight_grad(partial, copy_index):
-    rows, width = partial.shape
-    copies, fsdp_size = lax.axis_size("replica"), lax.axis_size("fsdp")
-    fine = rows // (copies * fsdp_size)
-    view = partial.reshape(fsdp_size, copies, fine, width)
-    parts = [
-        lax.dynamic_slice_in_dim(view, copy_index ^ step, 1, 1).reshape(fsdp_size * fine, width)
-        for step in range(copies)
+def reorder(pieces, copy_index):
+    beside = (copy_index & 1) == 1
+    across = (copy_index & 2) == 2
+    a, b, c, d = pieces
+    a, b, c, d = (
+        jnp.where(beside, b, a),
+        jnp.where(beside, a, b),
+        jnp.where(beside, d, c),
+        jnp.where(beside, c, d),
+    )
+    return [
+        jnp.where(across, c, a),
+        jnp.where(across, d, b),
+        jnp.where(across, a, c),
+        jnp.where(across, b, d),
     ]
-    summed = scatter_shards(scatter_copies(parts).astype(jnp.bfloat16))
-    return place(gather_copies(summed), copy_index).reshape(copies * fine, width).astype(jnp.float32)
+
+
+def quarter(shard, copy_index, dim):
+    size = shard.shape[dim] // lax.axis_size("replica")
+    return lax.dynamic_slice_in_dim(shard, copy_index * size, size, dim)
+
+
+def after(value, *others):
+    return lax.optimization_barrier((value, others))[0]
 
 
 def shards(
@@ -386,23 +378,22 @@
     copy_index = lax.axis_index("replica")
     copies = lax.axis_size("replica")
     low = jnp.bfloat16
-
+    lanes = model_width // copies
+
+    w_kv = gather_shards(jnp.concatenate([key_weight, value_weight], axis=1))
+    w_query = gather_copies(gather_shards(after(quarter(query_weight, copy_index, 1), w_kv)))
     gains = lax.all_gather(jnp.stack([attn_gain, ffn_gain]), "fsdp", axis=1, tiled=True)
     gain_attn = gains[0].astype(jnp.float32)
     gain_ffn = gains[1].astype(jnp.float32)
-    w_qkv = whole_weight(
-        jnp.concatenate([query_weight, key_weight, value_weight], axis=1), copy_index
-    )
     inputs = tokens.astype(jnp.float32)
     normed_full, inverse_attn = norm_forward(inputs, gain_attn)
     normed = normed_full.astype(low)
-    qkv = matmul(normed, w_qkv)
-    query_raw = qkv[:, :model_width]
-    key_raw = qkv[:, model_width : model_width + head_dim]
-    value_rows = qkv[:, model_width + head_dim :].astype(low)
+    kv_raw = matmul(normed, w_kv)
+    key_raw = kv_raw[:, :head_dim]
+    value_rows = kv_raw[:, head_dim:].astype(low)
     cos_table, sin_table = rope_tables(positions, head_dim)
     key_rot = (key_raw * cos_table + swap_halves(key_raw) * sin_table).astype(low)
-    kv_all = gather_shards(jnp.concatenate([key_rot, value_rows], axis=1))
+    kv_all = gather_shards(after(jnp.concatenate([key_rot, value_rows], axis=1), w_query[0]))
     key_width = max(GROUP_TOK, tok_rows)
     window_start = fsdp_index * tok_rows // key_width * key_width
     one_group = fsdp_size * tok_rows == key_width
@@ -411,7 +402,14 @@
     base = (fsdp_index * tok_rows - window_start).astype(jnp.int32)
     row_at = base + jnp.arange(tok_rows, dtype=jnp.int32)
     lowest = jnp.where(positions < PROMPT, 0, row_at - (positions - PROMPT))
-    base = base[None]
+    base = jnp.stack([base, copy_index.astype(jnp.int32)])
+    w_out_quarter = gather_shards(after(quarter(output_weight, copy_index, 1), kv_all))
+    w_down = gather_shards(after(quarter(down_weight, copy_index, 0), w_out_quarter))
+    w_gate = gather_shards(after(quarter(gate_weight.T, copy_index, 0), w_down))
+    w_up = gather_shards(after(quarter(up_weight.T, copy_index, 0), w_gate))
+    query_raw = jnp.concatenate([matmul(normed, w) for w in w_query], axis=1)
+    w_out = gather_copies(after(w_out_quarter, query_raw))
+    grads = jnp.concatenate(gather_copies(after(grad_out, w_out[3])), axis=0)
     mixed_rows, queries, logs = attend(
         base,
         query_raw,
@@ -421,45 +419,49 @@
         jnp.broadcast_to(lowest[:, None], (tok_rows, 128)),
     )
 
-    w_out = whole_weight(output_weight, copy_index)
-    hidden = inputs + matmul(mixed_rows, w_out)
+    branch = reorder([matmul(mixed_rows, w) for w in w_out], copy_index)
+    hidden = inputs + jnp.concatenate(branch, axis=1)
     normed_ffn_full, inverse_ffn = norm_forward(hidden, gain_ffn)
     normed_ffn = normed_ffn_full.astype(low)
 
-    w_gate = gather_shards(quarter(gate_weight.T, copy_index))
-    w_up = gather_shards(quarter(up_weight.T, copy_index))
-    w_down = gather_shards(quarter(down_weight, copy_index))
-    grad_blocks = gather_copies(grad_out)
-    grads = jnp.concatenate(grad_blocks, axis=0)
     normed_blocks = gather_copies(normed_ffn)
-    normed_all = jnp.concatenate(normed_blocks, axis=0)
-
-    d_activation = contract(grads, w_down, 1, 1)
+    d_activation = contract(after(grads, normed_ffn), w_down, 1, 1)
+    normed_all = jnp.concatenate(after(normed_blocks, d_activation), axis=0)
     gate_proj = contract(normed_all, w_gate, 1, 1)
     up_proj = contract(normed_all, w_up, 1, 1)
     activation = (jax.nn.silu(gate_proj) * up_proj).astype(low)
     d_gate, d_up = swiglu_back(d_activation, gate_proj, up_proj)
     d_normed_parts = matmul(d_gate, w_gate) + matmul(d_up, w_up)
-    d_normed_ffn = scatter_copies(jnp.split(d_normed_parts, copies))
-    out_parts = matmul(activation, w_down)
-    layer_out = (hidden + scatter_copies(jnp.split(out_parts, copies))).astype(low)
-
-    def ffn_grad(partial):
-        summed = scatter_shards(partial.astype(low))
-        pieces = place(gather_copies(summed), copy_index)
-        return pieces.reshape(-1, model_width).astype(jnp.float32)
-
-    gate_grad = ffn_grad(contract(d_gate, normed_all, 0, 0)).T
-    up_grad = ffn_grad(contract(d_up, normed_all, 0, 0)).T
-    down_grad = ffn_grad(contract(activation, grads, 0, 0))
+    own, beside, across, opposite = jnp.split(d_normed_parts, copies)
+    half = tok_rows // 2
+    first = swap(opposite[:half].astype(low), 1)
+    second = swap(opposite[half:].astype(low), 2)
+    beside_early = swap(beside[:half].astype(low), 1)
+    across_early = swap(across[half:].astype(low), 2)
+    gate_part = contract(d_gate, normed_all, 0, 0).astype(low)
+    first = after(first, gate_part)
+    second = after(second, gate_part)
+    across_late = swap((across[:half] + first.astype(jnp.float32)).astype(low), 2)
+    beside_late = swap((beside[half:] + second.astype(jnp.float32)).astype(low), 1)
+    up_part = contract(after(d_up, gate_part), normed_all, 0, 0).astype(low)
+    down_part = contract(after(activation, up_part), grads, 0, 0).astype(low)
+    beside_late = after(beside_late, down_part)
+    across_late = after(across_late, down_part)
+    d_normed_ffn = (
+        own
+        + jnp.concatenate([beside_early, beside_late], axis=0).astype(jnp.float32)
+        + jnp.concatenate([across_late, across_early], axis=0).astype(jnp.float32)
+    )
 
     cotangent = grad_out.astype(jnp.float32)
     resid_ffn, ffn_gain_term = norm_backward(hidden, inverse_ffn, gain_ffn, d_normed_ffn)
     d_hidden = cotangent + resid_ffn
     d_branch = d_hidden.astype(low)
-    d_mixed = contract(d_branch, w_out, 1, 1).astype(low)
-    output_grad = sum_weight_grad(contract(mixed_rows, d_branch, 0, 0), copy_index)
-
+    d_branch_parts = reorder(jnp.split(d_branch, copies, axis=1), copy_index)
+    d_mixed = sum(contract(d, w, 1, 1) for d, w in zip(d_branch_parts, w_out)).astype(low)
+
+    gate_sum = scatter_shards(gate_part)
+    up_sum = scatter_shards(after(up_part, gate_sum))
     d_query_raw, d_kv = attend_back(
         base,
         queries,
@@ -471,21 +473,43 @@
         d_mixed,
         logs,
     )
-    query_grad = sum_weight_grad(contract(normed, d_query_raw, 0, 0), copy_index)
     if not one_group:
         d_kv = lax.dynamic_update_slice_in_dim(
             jnp.zeros((fsdp_size * tok_rows, 2 * head_dim), low), d_kv, window_start, 0
         )
-    d_kv_sum = scatter_shards(d_kv).astype(jnp.float32)
+    d_kv_sum = scatter_shards(after(d_kv, up_sum))
+    down_sum = scatter_shards(after(down_part, d_kv_sum))
+    d_kv_sum = d_kv_sum.astype(jnp.float32)
+    out_parts = matmul(after(activation, d_mixed), w_down)
+    output_parts = [contract(mixed_rows, d, 0, 0) for d in d_branch_parts]
+    layer_out = (hidden + scatter_copies(jnp.split(out_parts, copies))).astype(low)
+
+    def to_copies(summed, dim):
+        return jnp.concatenate(
+            reorder(gather_copies(summed), copy_index), axis=dim
+        ).astype(jnp.float32)
+
+    query_parts = [
+        contract(normed, d_query_raw[:, i * lanes : (i + 1) * lanes], 0, 0) for i in range(copies)
+    ]
+    output_sum = scatter_shards(after(scatter_copies(output_parts).astype(low), down_sum))
+    query_sum = scatter_shards(after(scatter_copies(query_parts).astype(low), output_sum))
+    gate_grad = to_copies(gate_sum, 0).T
+    up_grad = to_copies(up_sum, 0).T
+    down_grad = to_copies(down_sum, 0)
+
     d_key = d_kv_sum[:, :head_dim]
     d_key_raw = (d_key * cos_table - swap_halves(d_key) * sin_table).astype(low)
     d_kv_raw = jnp.concatenate([d_key_raw, d_kv_sum[:, head_dim:].astype(low)], axis=1)
-    kv_grad = sum_weight_grad(contract(normed, d_kv_raw, 0, 0), copy_index)
-    d_normed = contract(d_query_raw, w_qkv[:, :model_width], 1, 1) + contract(
-        d_kv_raw, w_qkv[:, model_width:], 1, 1
+    kv_sum = scatter_shards(contract(normed, d_kv_raw, 0, 0).astype(low))
+    d_normed = contract(d_kv_raw, w_kv, 1, 1) + sum(
+        contract(d_query_raw[:, i * lanes : (i + 1) * lanes], w_query[i], 1, 1) for i in range(copies)
     )
     resid_attn, attn_gain_term = norm_backward(inputs, inverse_attn, gain_attn, d_normed)
     input_grad = d_hidden + resid_attn
+    kv_grad = lax.psum(kv_sum, "replica").astype(jnp.float32)
+    output_grad = to_copies(output_sum, 1)
+    query_grad = to_copies(query_sum, 1)
     gain_terms = lax.psum(jnp.stack([attn_gain_term, ffn_gain_term]), ("replica", "fsdp"))
     gain_grads = lax.dynamic_slice_in_dim(
         gain_terms, fsdp_index * (model_width // fsdp_size), model_width // fsdp_size, 1

time: 1290 us -> 1350 us (1.047)
  waiting for transfers between devices: 633 us -> 760 us
  local copies, waits for them, and re-layouts: 114 us -> 69.9 us
  matrix products: 234 us -> 261 us
  blocking collectives: 83.3 us -> 56.9 us
    all_gather x6 -> x7, waiting for transfers between devices: 35.4 us -> 151 us  [gather_shards(): return lax.all_gather(value, 'fsdp', axis=0, tiled=True)]
    ppermute x60 -> x54, waiting for transfers between devices: 371 us -> 437 us  [swap(): lax.ppermute(value, 'replica', [(r, r ^ step) for r in range(copies)])]
    reduce_scatter x7, waiting for transfers between devices: 227 us -> 171 us  [scatter_shards(): return lax.psum_scatter(value, 'fsdp', scatter_dimension=0, tiled=True)]
    psum x1, blocking collectives: 73.3 us -> 46.5 us  [shards(): lax.psum(jnp.stack([attn_gain_term, ffn_gain_term]), ('replica', 'fsdp'))]
    dynamic_update_slice x26 -> x0, local copies, waits for them, and re-layouts: 23.2 us -> none  [the longest x18 12.7 us: place(): out = lax.dynamic_update_index_in_dim(out, piece, copy_index ^ step, 0)]
    unnamed x105 -> x188, local copies, waits for them, and re-layouts: 18.5 us -> 34.3 us
    dot_general x12 -> x24, matrix products: 158 us -> 174 us  [contract(): lax.dot_general(left, right, (((left_dim,), (right_dim,)), ((), ())), pre...]
    dot_general x5 -> x12, matrix products: 75.7 us -> 86.9 us  [matmul(): return jnp.dot(left, right, preferred_element_type=jnp.float32)]
  transfers between devices with their start and end apart: 73 -> 69, of which waited for: 35 -> 37; matrix products, arithmetic and copies ran while one was open for 25% -> 24% of each run, Pallas kernels for 2% -> 3%
where the time goes in v2:
time: 1350 us
  waiting for transfers between devices  760 us (56%)
  matrix products  261 us (19%)
  other arithmetic  76.1 us (6%)
  local copies, waits for them, and re-layouts  69.9 us (5%)
  starting transfers between devices  65.8 us (5%)
  blocking collectives  56.9 us (4%)
  Pallas kernels  45.3 us (3%)
  between operations  15.8 us (1%)
    ppermute x54, waiting for transfers between devices, swap(): lax.ppermute(value, 'replica', [(r, r ^ step) for r in range(copies)])  437 us
    dot_general x24, matrix products, contract(): lax.dot_general(left, right, (((left_dim,), (right_dim,)), ((), ())), pre...  174 us
    reduce_scatter x7, waiting for transfers between devices, scatter_shards(): return lax.psum_scatter(value, 'fsdp', scatter_dimension=0, tiled=True)  171 us
    all_gather x7, waiting for transfers between devices, gather_shards(): return lax.all_gather(value, 'fsdp', axis=0, tiled=True)  151 us
    dot_general x12, matrix products, matmul(): return jnp.dot(left, right, preferred_element_type=jnp.float32)  86.9 us
    ppermute x54, starting transfers between devices, swap(): lax.ppermute(value, 'replica', [(r, r ^ step) for r in range(copies)])  64.7 us
    psum x1, blocking collectives, shards(): lax.psum(jnp.stack([attn_gain_term, ffn_gain_term]), ('replica', 'fsdp'))  46.5 us
    unnamed x188, local copies, waits for them, and re-layouts  34.3 us
  transfers between devices with their start and end apart: 69, of which 37 were waited for; matrix products, arithmetic and copies ran while one was open for 24% of the time, Pallas kernels for 3%

profile of v2, /device:TPU:0, one launch (start us, length us, event | category | flops | bytes accessed | tf_op | source)
XLA Modules:
  0.0 1350.6 jit_solution(833286089499006445)
XLA Ops:
  10.7 24.3 %all-gather.8.cloned.1.call-done = bf16[2048,256]{1,0:T(8,128)(2,1)} async-done(((bf16[256,256]{1,0:T(8,128)(2,1)}), bf16[2048,256]{1,0:T(8,128)(2,1)}) %all-gather.8.cloned.1.call-update) | async-done | bytes 1048592 | tf_op jit(solution)/shard_map/all_gather | solution.py:325
  35.2 3.9 copy.23
  39.1 10.5 all_gather.24
  53.4 3.1 fusion.59
  57.7 8.3 all-gather.10.cloned.1.call-done
  67.8 29.0 %all-gather.12.cloned.1.call-done.kv_ref = bf16[4096,256]{1,0:T(8,128)(2,1)} async-done(((bf16[512,256]{1,0:T(8,128)(2,1)}), bf16[4096,256]{1,0:T(8,128)(2,1)}) %all-gather.12.cloned.1.call-update) | async-done | bytes 2097168 | tf_op jit(solution)/shard_map/all_gather | solution.py:325
  97.8 29.6 %all-gather.14.cloned.1.call-done = bf16[2048,512]{1,0:T(8,128)(2,1)} async-done(((bf16[256,512]{1,0:T(8,128)(2,1)}), bf16[2048,512]{1,0:T(8,128)(2,1)}) %all-gather.14.cloned.1.call-update) | async-done | bytes 2097168 | tf_op jit(solution)/shard_map/all_gather | solution.py:325
  129.6 59.9 %all-gather.16.cloned.1.call-done = bf16[1408,2048]{1,0:T(8,128)(2,1)} async-done(((bf16[176,2048]{1,0:T(8,128)(2,1)}), bf16[1408,2048]{1,0:T(8,128)(2,1)}) %all-gather.16.cloned.1.call-update) | async-done | bytes 5767184 | tf_op jit(solution)/shard_map/all_gather | solution.py:325
  193.1 45.0 %collective-permute-done = bf16[2048,512]{1,0:T(8,128)(2,1)S(1)} collective-permute-done((bf16[2048,512]{1,0:T(8,128)(2,1)}, bf16[2048,512]{1,0:T(8,128)(2,1)S(1)}, u32[]{:S(2)}, u32[]{:S(2)}) %collective-permute-start) | collective-permute-done | bytes 2097184 | tf_op jit(solution)/shard_map/ppermute | solution.py:295
  241.3 3.0 fusion.67
  247.2 15.7 %collective-permute-done.2 = bf16[1024,512]{1,0:T(8,128)(2,1)S(1)} collective-permute-done((bf16[1024,512]{1,0:T(8,128)(2,1)S(1)}, bf16[1024,512]{1,0:T(8,128)(2,1)S(1)}, u32[]{:S(2)}, u32[]{:S(2)}) %collective-permute-start.2) | collective-permute-done | bytes 1048608 | tf_op jit(solution)/shard_map/ppermute | solution.py:295
  277.5 22.3 %attend.1 = (bf16[512,2048]{1,0:T(8,128)(2,1)S(1)}, bf16[512,2048]{1,0:T(8,128)(2,1)S(1)}, f32[4,4,8,512]{3,2,1,0:T(8,128)S(1)}) custom-call(s32[2]{0:T(128)S(1)} %pad_add_fusion.base_ref, f32[512,2048]{1,0:T(8,128)S(1)} %copy-done.4, bf16[4096,256]{1,0:T(8,128)(2,1)S(1)} %copy-done.9, f32[512,128]{1,0:T(8,128)S(1)} %get-tuple-element.144.cos_ref, ...), custom_call_target="tpu_custom_call" | custom-call | flops 16106127360 | bytes 16777216 | tf_op jit(solution)/shard_map/attend/pallas_call | solution.py:146
  299.8 15.8 %collective-permute-done.4 = bf16[2048,512]{1,0:T(8,128)(2,1)} collective-permute-done((bf16[2048,512]{1,0:T(8,128)(2,1)}, bf16[2048,512]{1,0:T(8,128)(2,1)}, u32[]{:S(2)}, u32[]{:S(2)}) %collective-permute-start.4) | collective-permute-done | bytes 2097184 | tf_op jit(solution)/shard_map/ppermute | solution.py:295
  322.1 3.9 fusion.82
  326.0 3.9 fusion.81
  332.9 9.7 collective-permute-done.5
  355.1 39.8 %collective-permute-done.12 = bf16[512,2048]{1,0:T(8,128)(2,1)S(1)} collective-permute-done((bf16[512,2048]{1,0:T(8,128)(2,1)S(1)}, bf16[512,2048]{1,0:T(8,128)(2,1)S(1)}, u32[]{:S(2)}, u32[]{:S(2)}) %collective-permute-start.12) | collective-permute-done | bytes 2097184 | tf_op jit(solution)/shard_map/ppermute | solution.py:295
  399.5 40.3 %collective-permute-done.8 = bf16[512,2048]{0,1:T(8,128)(2,1)S(1)} collective-permute-done((bf16[512,2048]{0,1:T(8,128)(2,1)S(1)}, bf16[512,2048]{0,1:T(8,128)(2,1)S(1)}, u32[]{:S(2)}, u32[]{:S(2)}) %collective-permute-start.8) | collective-permute-done | bytes 2097184 | tf_op jit(solution)/shard_map/ppermute | solution.py:295
  444.7 19.9 %collective-permute-done.14 = bf16[256,2048]{1,0:T(8,128)(2,1)S(1)} collective-permute-done((bf16[256,2048]{1,0:T(8,128)(2,1)S(1)}, bf16[256,2048]{1,0:T(8,128)(2,1)S(1)}, u32[]{:S(2)}, u32[]{:S(2)}) %collective-permute-start.14) | collective-permute-done | bytes 1048608 | tf_op jit(solution)/shard_map/ppermute | solution.py:295
  464.7 22.1 %collective-permute-done.10 = bf16[256,2048]{0,1:T(8,128)(2,1)S(1)} collective-permute-done((bf16[256,2048]{0,1:T(8,128)(2,1)S(1)}, bf16[256,2048]{0,1:T(8,128)(2,1)S(1)}, u32[]{:S(2)}, u32[]{:S(2)}) %collective-permute-start.10) | collective-permute-done | bytes 1048608 | tf_op jit(solution)/shard_map/ppermute | solution.py:295
  487.0 16.0 %fusion.83 = f32[2048,1408]{1,0:T(8,128)} fusion(bf16[2048,2048]{1,0:T(8,128)(2,1)S(1)} %constant_dynamic-update-slice_fusion.4, bf16[1408,2048]{1,0:T(8,128)(2,1)S(1)} %bitcast.81), kind=kOutput, calls=%fused_computation.233 | convolution fusion | flops 11811160064 | bytes 25690112 | tf_op jit(solution)/shard_map/dot_general | solution.py:28
  509.2 18.8 %fusion.84 = f32[2048,1408]{1,0:T(8,128)} fusion(bf16[2048,2048]{0,1:T(8,128)(2,1)} %constant_dynamic-update-slice_fusion.9, bf16[1408,2048]{1,0:T(8,128)(2,1)} %all-gather.20.cloned.1.call-done), kind=kOutput, calls=%fused_computation.234 | convolution fusion | flops 11811160064 | bytes 25690112 | tf_op jit(solution)/shard_map/dot_general | solution.py:28
  528.0 28.3 %multiply_convert_fusion = (bf16[2048,1408]{1,0:T(8,128)(2,1)}, bf16[2048,1408]{1,0:T(8,128)(2,1)S(1)}, bf16[2048,1408]{1,0:T(8,128)(2,1)}) fusion(f32[2048,1408]{1,0:T(8,128)} %fusion.83, f32[2048,1408]{1,0:T(8,128)} %fusion.84, bf16[2048,2048]{0,1:T(8,128)(2,1)} %constant_dynamic-update-slice_fusion.9, bf16[1408,2048]{1,0:T(8,128)(2,1)} %all-gather.18.cloned.1.call-done), kind=kOutput, calls=%fused_computation | convolution fusion | flops 11857297408 | bytes 54525952 | tf_op jit(solution)/shard_map/dot_general | solution.py:28
  558.9 16.9 %convolution_convert_fusion.2 = bf16[1408,2048]{1,0:T(8,128)(2,1)} fusion(bf16[2048,1408]{1,0:T(8,128)(2,1)S(1)} %get-tuple-element.92, bf16[2048,2048]{0,1:T(8,128)(2,1)} %constant_dynamic-update-slice_fusion.9), kind=kOutput, calls=%fused_computation.13 | convolution fusion | flops 11814043648 | bytes 19922944 | tf_op jit(solution)/shard_map/dot_general | solution.py:28
  575.8 20.8 %fusion.85 = f32[2048,2048]{0,1:T(8,128)} fusion(bf16[2048,1408]{1,0:T(8,128)(2,1)} %copy-done.82, bf16[1408,2048]{1,0:T(8,128)(2,1)} %all-gather.18.cloned.1.call-done), kind=kOutput, calls=%fused_computation.235 | convolution fusion | flops 11811160064 | bytes 28311552 | tf_op jit(solution)/shard_map/dot_general | solution.py:24
  596.6 18.1 %convolution_convert_fusion.1 = bf16[1408,2048]{1,0:T(8,128)(2,1)} fusion(bf16[2048,1408]{1,0:T(8,128)(2,1)} %get-tuple-element.56, bf16[2048,2048]{0,1:T(8,128)(2,1)} %constant_dynamic-update-slice_fusion.9), kind=kOutput, calls=%fused_computation.12 | convolution fusion | flops 11814043648 | bytes 19922944 | tf_op jit(solution)/shard_map/dot_general | solution.py:28
  614.7 80.8 %reduce-scatter.8.cloned.1.call-done = bf16[176,2048]{1,0:T(8,128)(2,1)} async-done(((bf16[1408,2048]{1,0:T(8,128)(2,1)}), bf16[176,2048]{1,0:T(8,128)(2,1)}) %reduce-scatter.8.cloned.1.call-update) | async-done | bytes 720912 | tf_op jit(solution)/shard_map/reduce_scatter | solution.py:329
  695.5 21.5 %fusion.78 = (bf16[2048,2048]{0,1:T(8,128)(2,1)S(1)}, f32[2048,2048]{0,1:T(8,128)}) fusion(f32[2048,2048]{0,1:T(8,128)} %fusion.85, bf16[2048,1408]{1,0:T(8,128)(2,1)} %get-tuple-element.56, bf16[1408,2048]{1,0:T(8,128)(2,1)} %all-gather.20.cloned.1.call-done), kind=kOutput, calls=%fused_computation.228 | convolution fusion | flops 11819548672 | bytes 53477376 | tf_op jit(solution)/shard_map/dot_general | solution.py:24
  726.2 19.4 %collective-permute-done.19 = bf16[256,2048]{0,1:T(8,128)(2,1)} collective-permute-done((bf16[256,2048]{0,1:T(8,128)(2,1)}, bf16[256,2048]{0,1:T(8,128)(2,1)}, u32[]{:S(2)}, u32[]{:S(2)}) %collective-permute-start.19) | collective-permute-done | bytes 1048608 | tf_op jit(solution)/shard_map/ppermute | solution.py:295
  747.1 4.7 fusion.20
  753.8 18.0 %convolution_convert_fusion = bf16[1408,2048]{1,0:T(8,128)(2,1)} fusion(bf16[2048,1408]{1,0:T(8,128)(2,1)} %get-tuple-element.61, bf16[2048,2048]{1,0:T(8,128)(2,1)} %copy-done.59), kind=kOutput, calls=%fused_computation.11 | convolution fusion | flops 11814043648 | bytes 19922944 | tf_op jit(solution)/shard_map/dot_general | solution.py:28
  771.8 15.4 %collective-permute-done.18 = bf16[256,2048]{0,1:T(8,128)(2,1)} collective-permute-done((bf16[256,2048]{0,1:T(8,128)(2,1)}, bf16[256,2048]{0,1:T(8,128)(2,1)}, u32[]{:S(2)}, u32[]{:S(2)}) %collective-permute-start.18) | collective-permute-done | bytes 1048608 | tf_op jit(solution)/shard_map/ppermute | solution.py:295
  788.4 6.2 multiply_reduce_fusion
  796.8 3.6 fusion.43
  800.5 2.9 fusion.47
  803.4 3.1 fusion.45
  809.3 22.9 %attend_back.1 = (bf16[512,2048]{1,0:T(8,128)(2,1)S(1)}, bf16[4096,256]{1,0:T(8,128)(2,1)S(1)}) custom-call(s32[2]{0:T(128)S(1)} %pad_add_fusion.base_ref, bf16[512,2048]{1,0:T(8,128)(2,1)} %copy-done.10, bf16[4096,256]{1,0:T(8,128)(2,1)} %all-gather.12.cloned.1.call-done.kv_ref, f32[512,128]{1,0:T(8,128)S(1)} %get-tuple-element.144.cos_ref, ...), custom_call_target="tpu_custom_call" | custom-call | flops 26843545600 | bytes 16777216 | tf_op jit(solution)/shard_map/attend_back/pallas_call | solution.py:260
  834.9 90.7 %reduce-scatter.12.cloned.1.call-done = bf16[512,256]{1,0:T(8,128)(2,1)} async-done(((bf16[4096,256]{1,0:T(8,128)(2,1)}), bf16[512,256]{1,0:T(8,128)(2,1)}) %reduce-scatter.12.cloned.1.call-update) | async-done | bytes 262160 | tf_op jit(solution)/shard_map/reduce_scatter | solution.py:329
  936.9 22.1 %fusion.79 = (bf16[2048,2048]{0,1:T(8,128)(2,1)}, f32[2048,2048]{0,1:T(8,128)}) fusion(bf16[2048,1408]{1,0:T(8,128)(2,1)} %get-tuple-element.61, bf16[1408,2048]{1,0:T(8,128)(2,1)} %all-gather.16.cloned.1.call-done), kind=kOutput, calls=%fused_computation.229 | convolution fusion | flops 11815354368 | bytes 36700160 | tf_op jit(solution)/shard_map/dot_general | solution.py:24
  959.1 4.5 fusion.70
  966.6 3.3 fusion.34
  972.9 3.3 fusion.28
  976.2 3.4 fusion.32
  982.6 3.3 fusion.42
  1002.6 4.8 collective-permute-done.28
  1011.1 41.3 %collective-permute-done.31 = bf16[2048,512]{1,0:T(8,128)(2,1)} collective-permute-done((bf16[2048,512]{1,0:T(8,128)(2,1)}, bf16[2048,512]{1,0:T(8,128)(2,1)}, u32[]{:S(2)}, u32[]{:S(2)}) %collective-permute-start.31) | collective-permute-done | bytes 2097184 | tf_op jit(solution)/shard_map/ppermute | solution.py:295
  1054.1 3.4 fusion.36
  1057.5 4.5 add_convert_fusion
  1062.9 11.9 collective-permute-done.24
  1074.8 3.5 fusion.18
  1081.8 53.3 %collective-permute-done.42 = bf16[176,2048]{1,0:T(8,128)(2,1)S(1)} collective-permute-done((bf16[176,2048]{1,0:T(8,128)(2,1)}, bf16[176,2048]{1,0:T(8,128)(2,1)S(1)}, u32[]{:S(2)}, u32[]{:S(2)}) %collective-permute-start.42) | collective-permute-done | bytes 720928 | tf_op jit(solution)/shard_map/ppermute | solution.py:295
  1139.9 4.5 add_convert_fusion.1
  1144.4 42.5 %collective-permute-done.43 = bf16[88,2048]{1,0:T(8,128)(2,1)} collective-permute-done((bf16[88,2048]{1,0:T(8,128)(2,1)}, bf16[88,2048]{1,0:T(8,128)(2,1)}, u32[]{:S(2)}, u32[]{:S(2)}) %collective-permute-start.43) | collective-permute-done | bytes 360480 | tf_op jit(solution)/shard_map/ppermute | solution.py:295
  1193.7 9.6 collective-permute-done.46
  1215.2 4.0 fusion.49
  1219.3 13.1 fusion.8
  1234.5 6.7 fusion.5
  1246.6 5.3 copy.45
  1254.4 46.5 %psum.15 = f32[2,2048]{1,0:T(2,128)S(1)} all-reduce(f32[2,2048]{1,0:T(2,128)S(1)} %pad_maximum_fusion.15), channel_id=1, replica_groups=mesh['replica'=4,'fsdp'=8] {'replica','fsdp'}, use_global_device_ids=true, to_apply=%region_14.15 | all-reduce | flops 4096 | bytes 32768 | tf_op jit(solution)/shard_map/psum | solution.py:513
  1306.5 6.2 collective-permute-done.53
  1316.6 3.1 collective-permute-done.38
  1322.2 2.9 maximum_convert_fusion
  1325.1 3.2 collective-permute-done.41
  1332.1 4.4 collective-permute-done.34
  (417 shorter events, 202.3 us)
Async XLA Ops:
  7.2 27.8 %all-gather.8.cloned.1.call-start = ((), (), s32[]{:S(2)}) async-start(), calls=%async_computation.7 | async-start | bytes 1179648 | tf_op jit(solution)/shard_map/all_gather | solution.py:325
  9.0 57.0 %all-gather.10.cloned.1.call-start = ((), (), s32[]{:S(2)}) async-start(), calls=%async_computation.8 | async-start | bytes 2359296 | tf_op jit(solution)/shard_map/all_gather | solution.py:325
  35.1 61.7 %all-gather.12.cloned.1.call-start = ((), (), s32[]{:S(2)}) async-start(), calls=%async_computation.9 | async-start | bytes 2359296 | tf_op jit(solution)/shard_map/all_gather | solution.py:325
  66.0 61.4 %all-gather.14.cloned.1.call-start = ((), (), s32[]{:S(2)}) async-start(), calls=%async_computation.10 | async-start | bytes 2359296 | tf_op jit(solution)/shard_map/all_gather | solution.py:325
  96.8 92.6 %all-gather.16.cloned.1.call-start = ((), (), s32[]{:S(2)}) async-start(), calls=%async_computation.11 | async-start | bytes 6488064 | tf_op jit(solution)/shard_map/all_gather | solution.py:325
  127.5 202.4 %all-gather.18.cloned.1.call-start = ((), (), s32[]{:S(2)}) async-start(), calls=%async_computation.12 | async-start | bytes 6488064 | tf_op jit(solution)/shard_map/all_gather | solution.py:325
  189.5 319.7 %all-gather.20.cloned.1.call-start = ((), (), s32[]{:S(2)}) async-start(), calls=%async_computation.13 | async-start | bytes 6488064 | tf_op jit(solution)/shard_map/all_gather | solution.py:325
  190.1 48.1 %collective-permute-start = (bf16[2048,512]{1,0:T(8,128)(2,1)}, bf16[2048,512]{1,0:T(8,128)(2,1)S(1)}, u32[]{:S(2)}, u32[]{:S(2)}) collective-permute-start(bf16[2048,512]{1,0:T(8,128)(2,1)} %all-gather.10.cloned.1.call-done), channel_id=1, source_target_pairs={{0,8},{8,0},{16,24},{24,16},{1,9},{9,1},{17,25},{25,17},{2,10},{10... | collective-permute-start | bytes 6291464 | tf_op jit(solution)/shard_map/ppermute | solution.py:295
  191.6 48.1 %collective-permute-start.1 = (bf16[2048,512]{1,0:T(8,128)(2,1)}, bf16[2048,512]{1,0:T(8,128)(2,1)S(1)}, u32[]{:S(2)}, u32[]{:S(2)}) collective-permute-start(bf16[2048,512]{1,0:T(8,128)(2,1)} %all-gather.10.cloned.1.call-done), channel_id=1, source_target_pairs={{0,16},{8,24},{16,0},{24,8},{1,17},{9,25},{17,1},{25,9},{2,18},{10... | collective-permute-start | bytes 6291464 | tf_op jit(solution)/shard_map/ppermute | solution.py:295
  238.2 24.7 %collective-permute-start.2 = (bf16[1024,512]{1,0:T(8,128)(2,1)S(1)}, bf16[1024,512]{1,0:T(8,128)(2,1)S(1)}, u32[]{:S(2)}, u32[]{:S(2)}) collective-permute-start(bf16[1024,512]{1,0:T(8,128)(2,1)S(1)} %slice.279), channel_id=1, source_target_pairs={{0,16},{8,24},{16,0},{24,8},{1,17},{9,25},{17,1},{25,9},{2,18},{10... | collective-permute-start | bytes 3145736 | tf_op jit(solution)/shard_map/ppermute | solution.py:295
  239.8 24.4 %collective-permute-start.3 = (bf16[1024,512]{1,0:T(8,128)(2,1)S(1)}, bf16[1024,512]{1,0:T(8,128)(2,1)S(1)}, u32[]{:S(2)}, u32[]{:S(2)}) collective-permute-start(bf16[1024,512]{1,0:T(8,128)(2,1)S(1)} %slice.280), channel_id=1, source_target_pairs={{0,8},{8,0},{16,24},{24,16},{1,9},{9,1},{17,25},{25,17},{2,10},{10... | collective-permute-start | bytes 3145736 | tf_op jit(solution)/shard_map/ppermute | solution.py:295
  269.4 46.2 %collective-permute-start.4 = (bf16[2048,512]{1,0:T(8,128)(2,1)}, bf16[2048,512]{1,0:T(8,128)(2,1)}, u32[]{:S(2)}, u32[]{:S(2)}) collective-permute-start(bf16[2048,512]{1,0:T(8,128)(2,1)} %all-gather.14.cloned.1.call-done), channel_id=1, source_target_pairs={{0,8},{8,0},{16,24},{24,16},{1,9},{9,1},{17,25},{25,17},{2,10},{10... | collective-permute-start | bytes 6291464 | tf_op jit(solution)/shard_map/ppermute | solution.py:295
  270.9 47.9 %collective-permute-start.6 = (bf16[2048,512]{1,0:T(8,128)(2,1)}, bf16[2048,512]{1,0:T(8,128)(2,1)}, u32[]{:S(2)}, u32[]{:S(2)}) collective-permute-start(bf16[2048,512]{1,0:T(8,128)(2,1)} %all-gather.14.cloned.1.call-done), channel_id=1, source_target_pairs={{0,16},{8,24},{16,0},{24,8},{1,17},{9,25},{17,1},{25,9},{2,18},{10... | collective-permute-start | bytes 6291464 | tf_op jit(solution)/shard_map/ppermute | solution.py:295
  317.8 24.8 %collective-permute-start.5 = (bf16[1024,512]{1,0:T(8,128)(2,1)}, bf16[1024,512]{1,0:T(8,128)(2,1)}, u32[]{:S(2)}, u32[]{:S(2)}) collective-permute-start(bf16[1024,512]{1,0:T(8,128)(2,1)} %slice.285), channel_id=1, source_target_pairs={{0,16},{8,24},{16,0},{24,8},{1,17},{9,25},{17,1},{25,9},{2,18},{10... | collective-permute-start | bytes 3145736 | tf_op jit(solution)/shard_map/ppermute | solution.py:295
  321.1 24.5 %collective-permute-start.7 = (bf16[1024,512]{1,0:T(8,128)(2,1)}, bf16[1024,512]{1,0:T(8,128)(2,1)}, u32[]{:S(2)}, u32[]{:S(2)}) collective-permute-start(bf16[1024,512]{1,0:T(8,128)(2,1)} %slice.286), channel_id=1, source_target_pairs={{0,8},{8,0},{16,24},{24,16},{1,9},{9,1},{17,25},{25,17},{2,10},{10... | collective-permute-start | bytes 3145736 | tf_op jit(solution)/shard_map/ppermute | solution.py:295
  329.9 365.5 %reduce-scatter.8.cloned.1.call-start = ((), (), s32[]{:S(2)}) async-start(), calls=%async_computation.14 | async-start | bytes 6488064 | tf_op jit(solution)/shard_map/reduce_scatter | solution.py:329
  346.9 48.0 %collective-permute-start.12 = (bf16[512,2048]{1,0:T(8,128)(2,1)S(1)}, bf16[512,2048]{1,0:T(8,128)(2,1)S(1)}, u32[]{:S(2)}, u32[]{:S(2)}) collective-permute-start(bf16[512,2048]{1,0:T(8,128)(2,1)S(1)} %copy-done.35), channel_id=1, source_target_pairs={{0,8},{8,0},{16,24},{24,16},{1,9},{9,1},{17,25},{25,17},{2,10},{10... | collective-permute-start | bytes 6291464 | tf_op jit(solution)/shard_map/ppermute | solution.py:295
  348.6 48.6 %collective-permute-start.13 = (bf16[512,2048]{1,0:T(8,128)(2,1)S(1)}, bf16[512,2048]{1,0:T(8,128)(2,1)S(1)}, u32[]{:S(2)}, u32[]{:S(2)}) collective-permute-start(bf16[512,2048]{1,0:T(8,128)(2,1)S(1)} %copy-done.35), channel_id=1, source_target_pairs={{0,16},{8,24},{16,0},{24,8},{1,17},{9,25},{17,1},{25,9},{2,18},{10... | collective-permute-start | bytes 6291464 | tf_op jit(solution)/shard_map/ppermute | solution.py:295
  354.4 85.4 %collective-permute-start.8 = (bf16[512,2048]{0,1:T(8,128)(2,1)S(1)}, bf16[512,2048]{0,1:T(8,128)(2,1)S(1)}, u32[]{:S(2)}, u32[]{:S(2)}) collective-permute-start(bf16[512,2048]{0,1:T(8,128)(2,1)S(1)} %multiply_convert_fusion.3), channel_id=1, source_target_pairs={{0,8},{8,0},{16,24},{24,16},{1,9},{9,1},{17,25},{25,17},{2,10},{10... | collective-permute-start | bytes 6291464 | tf_op jit(solution)/shard_map/ppermute | solution.py:295
  354.5 87.5 %collective-permute-start.9 = (bf16[512,2048]{0,1:T(8,128)(2,1)S(1)}, bf16[512,2048]{0,1:T(8,128)(2,1)S(1)}, u32[]{:S(2)}, u32[]{:S(2)}) collective-permute-start(bf16[512,2048]{0,1:T(8,128)(2,1)S(1)} %multiply_convert_fusion.3), channel_id=1, source_target_pairs={{0,16},{8,24},{16,0},{24,8},{1,17},{9,25},{17,1},{25,9},{2,18},{10... | collective-permute-start | bytes 6291464 | tf_op jit(solution)/shard_map/ppermute | solution.py:295
  395.0 69.5 %collective-permute-start.14 = (bf16[256,2048]{1,0:T(8,128)(2,1)S(1)}, bf16[256,2048]{1,0:T(8,128)(2,1)S(1)}, u32[]{:S(2)}, u32[]{:S(2)}) collective-permute-start(bf16[256,2048]{1,0:T(8,128)(2,1)S(1)} %slice.290), channel_id=1, source_target_pairs={{0,16},{8,24},{16,0},{24,8},{1,17},{9,25},{17,1},{25,9},{2,18},{10... | collective-permute-start | bytes 3145736 | tf_op jit(solution)/shard_map/ppermute | solution.py:295
  397.3 67.3 %collective-permute-start.15 = (bf16[256,2048]{1,0:T(8,128)(2,1)S(1)}, bf16[256,2048]{1,0:T(8,128)(2,1)S(1)}, u32[]{:S(2)}, u32[]{:S(2)}) collective-permute-start(bf16[256,2048]{1,0:T(8,128)(2,1)S(1)} %slice.291), channel_id=1, source_target_pairs={{0,8},{8,0},{16,24},{24,16},{1,9},{9,1},{17,25},{25,17},{2,10},{10... | collective-permute-start | bytes 3145736 | tf_op jit(solution)/shard_map/ppermute | solution.py:295
  439.9 46.9 %collective-permute-start.10 = (bf16[256,2048]{0,1:T(8,128)(2,1)S(1)}, bf16[256,2048]{0,1:T(8,128)(2,1)S(1)}, u32[]{:S(2)}, u32[]{:S(2)}) collective-permute-start(bf16[256,2048]{0,1:T(8,128)(2,1)S(1)} %slice.288), channel_id=1, source_target_pairs={{0,16},{8,24},{16,0},{24,8},{1,17},{9,25},{17,1},{25,9},{2,18},{10... | collective-permute-start | bytes 3145736 | tf_op jit(solution)/shard_map/ppermute | solution.py:295
  442.1 44.7 %collective-permute-start.11 = (bf16[256,2048]{0,1:T(8,128)(2,1)S(1)}, bf16[256,2048]{0,1:T(8,128)(2,1)S(1)}, u32[]{:S(2)}, u32[]{:S(2)}) collective-permute-start(bf16[256,2048]{0,1:T(8,128)(2,1)S(1)} %slice.289), channel_id=1, source_target_pairs={{0,8},{8,0},{16,24},{24,16},{1,9},{9,1},{17,25},{25,17},{2,10},{10... | collective-permute-start | bytes 3145736 | tf_op jit(solution)/shard_map/ppermute | solution.py:295
  575.7 259.1 %reduce-scatter.10.cloned.1.call-start = ((), (), s32[]{:S(2)}) async-start(), calls=%async_computation.15 | async-start | bytes 6488064 | tf_op jit(solution)/shard_map/reduce_scatter | solution.py:329
  695.5 230.1 %reduce-scatter.12.cloned.1.call-start = ((), (), s32[]{:S(2)}) async-start(), calls=%async_computation.16 | async-start | bytes 2359296 | tf_op jit(solution)/shard_map/reduce_scatter | solution.py:329
  719.2 26.4 %collective-permute-start.19 = (bf16[256,2048]{0,1:T(8,128)(2,1)}, bf16[256,2048]{0,1:T(8,128)(2,1)}, u32[]{:S(2)}, u32[]{:S(2)}) collective-permute-start(bf16[256,2048]{0,1:T(8,128)(2,1)} %get-tuple-element.104), channel_id=1, source_target_pairs={{0,8},{8,0},{16,24},{24,16},{1,9},{9,1},{17,25},{25,17},{2,10},{10... | collective-permute-start | bytes 3145736 | tf_op jit(solution)/shard_map/ppermute | solution.py:295
  720.6 26.4 %collective-permute-start.17 = (bf16[256,2048]{0,1:T(8,128)(2,1)}, bf16[256,2048]{0,1:T(8,128)(2,1)}, u32[]{:S(2)}, u32[]{:S(2)}) collective-permute-start(bf16[256,2048]{0,1:T(8,128)(2,1)} %get-tuple-element.105), channel_id=1, source_target_pairs={{0,16},{8,24},{16,0},{24,8},{1,17},{9,25},{17,1},{25,9},{2,18},{10... | collective-permute-start | bytes 3145736 | tf_op jit(solution)/shard_map/ppermute | solution.py:295
  725.0 63.4 %collective-permute-start.16 = (bf16[256,2048]{0,1:T(8,128)(2,1)}, bf16[256,2048]{0,1:T(8,128)(2,1)}, u32[]{:S(2)}, u32[]{:S(2)}) collective-permute-start(bf16[256,2048]{0,1:T(8,128)(2,1)} %get-tuple-element.102), channel_id=1, source_target_pairs={{0,8},{8,0},{16,24},{24,16},{1,9},{9,1},{17,25},{25,17},{2,10},{10... | collective-permute-start | bytes 3145736 | tf_op jit(solution)/shard_map/ppermute | solution.py:295
  725.6 62.8 %collective-permute-start.21 = (bf16[256,2048]{0,1:T(8,128)(2,1)}, bf16[256,2048]{0,1:T(8,128)(2,1)}, u32[]{:S(2)}, u32[]{:S(2)}) collective-permute-start(bf16[256,2048]{0,1:T(8,128)(2,1)} %get-tuple-element.103), channel_id=1, source_target_pairs={{0,16},{8,24},{16,0},{24,8},{1,17},{9,25},{17,1},{25,9},{2,18},{10... | collective-permute-start | bytes 3145736 | tf_op jit(solution)/shard_map/ppermute | solution.py:295
  751.8 35.4 %collective-permute-start.18 = (bf16[256,2048]{0,1:T(8,128)(2,1)}, bf16[256,2048]{0,1:T(8,128)(2,1)}, u32[]{:S(2)}, u32[]{:S(2)}) collective-permute-start(bf16[256,2048]{0,1:T(8,128)(2,1)} %get-tuple-element.96), channel_id=1, source_target_pairs={{0,8},{8,0},{16,24},{24,16},{1,9},{9,1},{17,25},{25,17},{2,10},{10... | collective-permute-start | bytes 3145736 | tf_op jit(solution)/shard_map/ppermute | solution.py:295
  752.4 36.0 %collective-permute-start.20 = (bf16[256,2048]{0,1:T(8,128)(2,1)}, bf16[256,2048]{0,1:T(8,128)(2,1)}, u32[]{:S(2)}, u32[]{:S(2)}) collective-permute-start(bf16[256,2048]{0,1:T(8,128)(2,1)} %get-tuple-element.97), channel_id=1, source_target_pairs={{0,16},{8,24},{16,0},{24,8},{1,17},{9,25},{17,1},{25,9},{2,18},{10... | collective-permute-start | bytes 3145736 | tf_op jit(solution)/shard_map/ppermute | solution.py:295
  834.9 227.7 %reduce-scatter.14.cloned.1.call-start = ((), (), s32[]{:S(2)}) async-start(), calls=%async_computation.17 | async-start | bytes 6488064 | tf_op jit(solution)/shard_map/reduce_scatter | solution.py:329
  925.6 289.5 %reduce-scatter.20.cloned.1.call-start = ((), (), s32[]{:S(2)}) async-start(), calls=%async_computation.20 | async-start | bytes 1179648 | tf_op jit(solution)/shard_map/reduce_scatter | solution.py:329
  929.7 56.2 %collective-permute-start.30 = (bf16[1024,512]{1,0:T(8,128)(2,1)}, bf16[1024,512]{1,0:T(8,128)(2,1)}, u32[]{:S(2)}, u32[]{:S(2)}) collective-permute-start(bf16[1024,512]{1,0:T(8,128)(2,1)} %get-tuple-element.124), channel_id=1, source_target_pairs={{0,16},{8,24},{16,0},{24,8},{1,17},{9,25},{17,1},{25,9},{2,18},{10... | collective-permute-start | bytes 3145736 | tf_op jit(solution)/shard_map/ppermute | solution.py:295
  929.9 60.6 %collective-permute-start.32 = (bf16[1024,512]{1,0:T(8,128)(2,1)}, bf16[1024,512]{1,0:T(8,128)(2,1)}, u32[]{:S(2)}, u32[]{:S(2)}) collective-permute-start(bf16[1024,512]{1,0:T(8,128)(2,1)} %get-tuple-element.125), channel_id=1, source_target_pairs={{0,8},{8,0},{16,24},{24,16},{1,9},{9,1},{17,25},{25,17},{2,10},{10... | collective-permute-start | bytes 3145736 | tf_op jit(solution)/shard_map/ppermute | solution.py:295
  935.2 62.5 %collective-permute-start.26 = (bf16[1024,512]{1,0:T(8,128)(2,1)}, bf16[1024,512]{1,0:T(8,128)(2,1)}, u32[]{:S(2)}, u32[]{:S(2)}) collective-permute-start(bf16[1024,512]{1,0:T(8,128)(2,1)} %get-tuple-element.126), channel_id=1, source_target_pairs={{0,16},{8,24},{16,0},{24,8},{1,17},{9,25},{17,1},{25,9},{2,18},{10... | collective-permute-start | bytes 3145736 | tf_op jit(solution)/shard_map/ppermute | solution.py:295
  963.6 99.1 %collective-permute-start.22 = (bf16[256,2048]{0,1:T(8,128)(2,1)}, bf16[256,2048]{0,1:T(8,128)(2,1)}, u32[]{:S(2)}, u32[]{:S(2)}) collective-permute-start(bf16[256,2048]{0,1:T(8,128)(2,1)} %get-tuple-element.101), channel_id=1, source_target_pairs={{0,16},{8,24},{16,0},{24,8},{1,17},{9,25},{17,1},{25,9},{2,18},{10... | collective-permute-start | bytes 3145736 | tf_op jit(solution)/shard_map/ppermute | solution.py:295
  981.0 26.4 %collective-permute-start.28 = (bf16[1024,512]{1,0:T(8,128)(2,1)}, bf16[1024,512]{1,0:T(8,128)(2,1)}, u32[]{:S(2)}, u32[]{:S(2)}) collective-permute-start(bf16[1024,512]{1,0:T(8,128)(2,1)} %get-tuple-element.127), channel_id=1, source_target_pairs={{0,8},{8,0},{16,24},{24,16},{1,9},{9,1},{17,25},{25,17},{2,10},{10... | collective-permute-start | bytes 3145736 | tf_op jit(solution)/shard_map/ppermute | solution.py:295
  989.0 63.4 %collective-permute-start.31 = (bf16[2048,512]{1,0:T(8,128)(2,1)}, bf16[2048,512]{1,0:T(8,128)(2,1)}, u32[]{:S(2)}, u32[]{:S(2)}) collective-permute-start(bf16[2048,512]{1,0:T(8,128)(2,1)} %pad_maximum_fusion.6), channel_id=1, source_target_pairs={{0,8},{8,0},{16,24},{24,16},{1,9},{9,1},{17,25},{25,17},{2,10},{10... | collective-permute-start | bytes 6291464 | tf_op jit(solution)/shard_map/ppermute | solution.py:295
  993.5 64.0 %collective-permute-start.33 = (bf16[2048,512]{1,0:T(8,128)(2,1)}, bf16[2048,512]{1,0:T(8,128)(2,1)}, u32[]{:S(2)}, u32[]{:S(2)}) collective-permute-start(bf16[2048,512]{1,0:T(8,128)(2,1)} %pad_maximum_fusion.7), channel_id=1, source_target_pairs={{0,16},{8,24},{16,0},{24,8},{1,17},{9,25},{17,1},{25,9},{2,18},{10... | collective-permute-start | bytes 6291464 | tf_op jit(solution)/shard_map/ppermute | solution.py:295
  997.7 221.5 %reduce-scatter.16.cloned.1.call-start = ((), (), s32[]{:S(2)}) async-start(), calls=%async_computation.18 | async-start | bytes 2359296 | tf_op jit(solution)/shard_map/reduce_scatter | solution.py:329
  997.7 77.1 %collective-permute-start.24 = (bf16[256,2048]{0,1:T(8,128)(2,1)}, bf16[256,2048]{0,1:T(8,128)(2,1)}, u32[]{:S(2)}, u32[]{:S(2)}) collective-permute-start(bf16[256,2048]{0,1:T(8,128)(2,1)} %get-tuple-element.100), channel_id=1, source_target_pairs={{0,8},{8,0},{16,24},{24,16},{1,9},{9,1},{17,25},{25,17},{2,10},{10... | collective-permute-start | bytes 3145736 | tf_op jit(solution)/shard_map/ppermute | solution.py:295
  1007.4 131.8 %collective-permute-start.27 = (bf16[2048,512]{1,0:T(8,128)(2,1)}, bf16[2048,512]{1,0:T(8,128)(2,1)}, u32[]{:S(2)}, u32[]{:S(2)}) collective-permute-start(bf16[2048,512]{1,0:T(8,128)(2,1)} %pad_maximum_fusion.4), channel_id=1, source_target_pairs={{0,8},{8,0},{16,24},{24,16},{1,9},{9,1},{17,25},{25,17},{2,10},{10... | collective-permute-start | bytes 6291464 | tf_op jit(solution)/shard_map/ppermute | solution.py:295
  1052.4 87.5 %collective-permute-start.29 = (bf16[2048,512]{1,0:T(8,128)(2,1)}, bf16[2048,512]{1,0:T(8,128)(2,1)}, u32[]{:S(2)}, u32[]{:S(2)}) collective-permute-start(bf16[2048,512]{1,0:T(8,128)(2,1)} %pad_maximum_fusion.5), channel_id=1, source_target_pairs={{0,16},{8,24},{16,0},{24,8},{1,17},{9,25},{17,1},{25,9},{2,18},{10... | collective-permute-start | bytes 6291464 | tf_op jit(solution)/shard_map/ppermute | solution.py:295
  1062.0 73.1 %collective-permute-start.42 = (bf16[176,2048]{1,0:T(8,128)(2,1)}, bf16[176,2048]{1,0:T(8,128)(2,1)S(1)}, u32[]{:S(2)}, u32[]{:S(2)}) collective-permute-start(bf16[176,2048]{1,0:T(8,128)(2,1)} %reduce-scatter.8.cloned.1.call-done), channel_id=1, source_target_pairs={{0,8},{8,0},{16,24},{24,16},{1,9},{9,1},{17,25},{25,17},{2,10},{10... | collective-permute-start | bytes 2162696 | tf_op jit(solution)/shard_map/ppermute | solution.py:295
  1062.6 242.2 %all-reduce.2.cloned.1.call-start = ((), (), s32[]{:S(2)}) async-start(), calls=%async_computation.21 | async-start | bytes 262144 | tf_op jit(solution)/shard_map/psum | solution.py:510
  1062.7 74.9 %collective-permute-start.44 = (bf16[176,2048]{1,0:T(8,128)(2,1)}, bf16[176,2048]{1,0:T(8,128)(2,1)S(1)}, u32[]{:S(2)}, u32[]{:S(2)}) collective-permute-start(bf16[176,2048]{1,0:T(8,128)(2,1)} %reduce-scatter.8.cloned.1.call-done), channel_id=1, source_target_pairs={{0,16},{8,24},{16,0},{24,8},{1,17},{9,25},{17,1},{25,9},{2,18},{10... | collective-permute-start | bytes 2162696 | tf_op jit(solution)/shard_map/ppermute | solution.py:295
  1079.8 154.6 %collective-permute-start.23 = (bf16[512,2048]{0,1:T(8,128)(2,1)}, bf16[512,2048]{0,1:T(8,128)(2,1)}, u32[]{:S(2)}, u32[]{:S(2)}) collective-permute-start(bf16[512,2048]{0,1:T(8,128)(2,1)} %pad_maximum_fusion.2), channel_id=1, source_target_pairs={{0,8},{8,0},{16,24},{24,16},{1,9},{9,1},{17,25},{25,17},{2,10},{10... | collective-permute-start | bytes 6291464 | tf_op jit(solution)/shard_map/ppermute | solution.py:295
  1135.1 99.3 %collective-permute-start.25 = (bf16[512,2048]{0,1:T(8,128)(2,1)}, bf16[512,2048]{0,1:T(8,128)(2,1)}, u32[]{:S(2)}, u32[]{:S(2)}) collective-permute-start(bf16[512,2048]{0,1:T(8,128)(2,1)} %pad_maximum_fusion.3), channel_id=1, source_target_pairs={{0,16},{8,24},{16,0},{24,8},{1,17},{9,25},{17,1},{25,9},{2,18},{10... | collective-permute-start | bytes 6291464 | tf_op jit(solution)/shard_map/ppermute | solution.py:295
  1137.6 49.3 %collective-permute-start.43 = (bf16[88,2048]{1,0:T(8,128)(2,1)}, bf16[88,2048]{1,0:T(8,128)(2,1)}, u32[]{:S(2)}, u32[]{:S(2)}) collective-permute-start(bf16[88,2048]{1,0:T(8,128)(2,1)} %slice.326), channel_id=1, source_target_pairs={{0,16},{8,24},{16,0},{24,8},{1,17},{9,25},{17,1},{25,9},{2,18},{10... | collective-permute-start | bytes 1081352 | tf_op jit(solution)/shard_map/ppermute | solution.py:295
  1139.2 51.7 %collective-permute-start.45 = (bf16[88,2048]{1,0:T(8,128)(2,1)}, bf16[88,2048]{1,0:T(8,128)(2,1)}, u32[]{:S(2)}, u32[]{:S(2)}) collective-permute-start(bf16[88,2048]{1,0:T(8,128)(2,1)} %slice.327), channel_id=1, source_target_pairs={{0,8},{8,0},{16,24},{24,16},{1,9},{9,1},{17,25},{25,17},{2,10},{10... | collective-permute-start | bytes 1081352 | tf_op jit(solution)/shard_map/ppermute | solution.py:295
  1187.9 15.4 %collective-permute-start.46 = (bf16[176,2048]{1,0:T(8,128)(2,1)}, bf16[176,2048]{1,0:T(8,128)(2,1)S(1)}, u32[]{:S(2)}, u32[]{:S(2)}) collective-permute-start(bf16[176,2048]{1,0:T(8,128)(2,1)} %reduce-scatter.10.cloned.1.call-done), channel_id=1, source_target_pairs={{0,8},{8,0},{16,24},{24,16},{1,9},{9,1},{17,25},{25,17},{2,10},{10... | collective-permute-start | bytes 2162696 | tf_op jit(solution)/shard_map/ppermute | solution.py:295
  1188.5 15.9 %collective-permute-start.48 = (bf16[176,2048]{1,0:T(8,128)(2,1)}, bf16[176,2048]{1,0:T(8,128)(2,1)S(1)}, u32[]{:S(2)}, u32[]{:S(2)}) collective-permute-start(bf16[176,2048]{1,0:T(8,128)(2,1)} %reduce-scatter.10.cloned.1.call-done), channel_id=1, source_target_pairs={{0,16},{8,24},{16,0},{24,8},{1,17},{9,25},{17,1},{25,9},{2,18},{10... | collective-permute-start | bytes 2162696 | tf_op jit(solution)/shard_map/ppermute | solution.py:295
  1203.4 7.5 collective-permute-start.47
  1204.4 7.5 collective-permute-start.49
  1215.1 113.3 %reduce-scatter.18.cloned.1.call-start = ((), (), s32[]{:S(2)}) async-start(), calls=%async_computation.19 | async-start | bytes 2359296 | tf_op jit(solution)/shard_map/reduce_scatter | solution.py:329
  1232.3 11.7 collective-permute-start.50
  1234.4 67.1 %collective-permute-start.52 = (bf16[176,2048]{1,0:T(8,128)(2,1)}, bf16[176,2048]{1,0:T(8,128)(2,1)}, u32[]{:S(2)}, u32[]{:S(2)}) collective-permute-start(bf16[176,2048]{1,0:T(8,128)(2,1)} %reduce-scatter.14.cloned.1.call-done), channel_id=1, source_target_pairs={{0,16},{8,24},{16,0},{24,8},{1,17},{9,25},{17,1},{25,9},{2,18},{10... | collective-permute-start | bytes 2162696 | tf_op jit(solution)/shard_map/ppermute | solution.py:295
  1244.9 61.6 %collective-permute-start.51 = (bf16[88,2048]{1,0:T(8,128)(2,1)}, bf16[88,2048]{1,0:T(8,128)(2,1)S(1)}, u32[]{:S(2)}, u32[]{:S(2)}) collective-permute-start(bf16[88,2048]{1,0:T(8,128)(2,1)} %slice.330), channel_id=1, source_target_pairs={{0,16},{8,24},{16,0},{24,8},{1,17},{9,25},{17,1},{25,9},{2,18},{10... | collective-permute-start | bytes 1081352 | tf_op jit(solution)/shard_map/ppermute | solution.py:295
  1302.5 10.1 collective-permute-start.53
  1314.5 7.5 collective-permute-start.40
  1328.4 8.1 collective-permute-start.34
  1328.5 8.6 collective-permute-start.36
  (90 other events, 2603.7 us)
Sparse Core Ops, SparseCore 0:
  10.2 24.7 all-gather.7
  37.2 28.7 all-gather.9
  68.2 28.5 all-gather.11
  98.8 28.5 all-gather.13
  129.5 59.9 all-gather.15
  191.0 59.0 all-gather.17
  330.0 121.8 all-gather.19
  575.9 119.5 reduce-scatter.7
  698.3 63.2 reduce-scatter.9
  835.0 90.5 reduce-scatter.11
  928.5 63.2 reduce-scatter.13
  997.8 28.5 reduce-scatter.19
  1062.7 32.7 reduce-scatter.15
  1215.2 46.0 all-reduce.1
  1263.6 36.0 reduce-scatter.17

commit v3 on v1

--- a/solution.py
+++ b/solution.py
@@ -85,7 +85,7 @@
 
 
 def attend_kernel(
-    base_ref, q_ref, kv_ref, cos_ref, sin_ref, low_ref, mixed_ref, rot_ref, log_ref, values, top, acc
+    base_ref, q_ref, kv_ref, low_ref, mixed_ref, log_ref, values, top, acc
 ):
     factor = 128**-0.5 * LOG2E
 
@@ -95,15 +95,7 @@
         values[:, 128:] = jnp.ones_like(values[:, 128:])
 
     first, full, last = chunk_plan(base_ref)
-    cos_table, sin_table = cos_ref[...], sin_ref[...]
-    pieces = []
-    for h in range(HEAD_GROUP):
-        raw = q_ref[:, h * 128 : (h + 1) * 128]
-        turned = raw * cos_table + pltpu.roll(raw, 64, 1) * sin_table
-        turned = turned.astype(jnp.bfloat16)
-        rot_ref[:, h * 128 : (h + 1) * 128] = turned
-        pieces.append(turned)
-    queries = jnp.concatenate(pieces, axis=0)
+    queries = stack_heads(q_ref[...])
     rows = queries.shape[0]
     top[...] = jnp.full_like(top, MASKED)
     acc[...] = jnp.zeros_like(acc)
@@ -135,8 +127,8 @@
     log_ref[0, 0] = (top[...] + jnp.log2(total)).T[:8]
 
 
-def attend(base, q_raw, kv, cos_table, sin_table, low):
-    tok_rows, width = q_raw.shape
+def attend(base, queries, kv, low):
+    tok_rows, width = queries.shape
     tiles, groups = tok_rows // TILE, width // (128 * HEAD_GROUP)
     lanes, rows = 128 * HEAD_GROUP, TILE * HEAD_GROUP
     tile_spec = pl.BlockSpec((TILE, lanes), lambda i, g, b: (i, g))
@@ -146,7 +138,6 @@
         attend_kernel,
         out_shape=(
             jax.ShapeDtypeStruct((tok_rows, width), jnp.bfloat16),
-            jax.ShapeDtypeStruct((tok_rows, width), jnp.bfloat16),
             jax.ShapeDtypeStruct((tiles, groups, 8, rows), jnp.float32),
         ),
         grid_spec=pltpu.PrefetchScalarGridSpec(
@@ -156,11 +147,8 @@
                 tile_spec,
                 pl.BlockSpec(kv.shape, lambda i, g, b: (0, 0)),
                 row_spec,
-                row_spec,
-                row_spec,
             ],
             out_specs=[
-                tile_spec,
                 tile_spec,
                 pl.BlockSpec((1, 1, 8, rows), lambda i, g, b: (i, g, 0, 0)),
             ],
@@ -175,7 +163,7 @@
             flops=pairs * 768, transcendentals=pairs, bytes_accessed=16 << 20
         ),
         name="attend",
-    )(base, q_raw, kv, cos_table, sin_table, low)
+    )(base, queries, kv, low)
 
 
 def attend_back_kernel(
@@ -288,6 +276,363 @@
     )(base, queries, kv, cos_table, sin_table, low, mixed, d_mixed, logs)
 
 
+MESH = pl.DeviceIdType.MESH
+
+
+def flip(index, bit):
+    return index + bit - 2 * bit * (index // bit % 2)
+
+
+class Chain:
+    def __init__(self, place, count, at, replica, fsdp, sends, recvs):
+        self.place, self.count, self.at = place, count, at
+        self.replica, self.fsdp, self.sends, self.recvs = replica, fsdp, sends, recvs
+
+    def copy(self, shard, way):
+        target = self.fsdp + (2 if way == 0 else -2)
+        return pltpu.make_async_remote_copy(
+            src_ref=self.place(shard),
+            dst_ref=self.place(shard),
+            send_sem=self.sends.at[way, shard],
+            recv_sem=self.recvs.at[way, shard],
+            device_id=(self.replica, target),
+            device_id_type=MESH,
+        )
+
+    def begin(self):
+        @pl.when(self.at < self.count - 1)
+        def _():
+            self.copy(self.at, 0).start()
+
+        @pl.when(self.at > 0)
+        def _():
+            self.copy(self.at, 1).start()
+
+    def step(self, hop, arrived=None):
+        left, right = self.at - hop, self.at + hop
+
+        @pl.when(left >= 0)
+        def _():
+            self.copy(left, 0).wait_recv()
+
+        @pl.when((left >= 0) & (self.at < self.count - 1))
+        def _():
+            self.copy(left, 0).start()
+
+        if arrived is not None:
+
+            @pl.when(left >= 0)
+            def _():
+                arrived(left)
+
+        @pl.when(right < self.count)
+        def _():
+            self.copy(right, 1).wait_recv()
+
+        @pl.when((right < self.count) & (self.at > 0))
+        def _():
+            self.copy(right, 1).start()
+
+        if arrived is not None:
+
+            @pl.when(right < self.count)
+            def _():
+                arrived(right)
+
+    def finish(self):
+        for hop in range(self.count):
+
+            @pl.when((self.at - hop >= 0) & (self.at < self.count - 1))
+            def _(hop=hop):
+                self.copy(self.at - hop, 0).wait_send()
+
+            @pl.when((self.at + hop < self.count) & (self.at > 0))
+            def _(hop=hop):
+                self.copy(self.at + hop, 1).wait_send()
+
+
+class Spread:
+    def __init__(self, buffer, count, at, core, replica, fsdp, sems):
+        self.buffer, self.count, self.at, self.core = buffer, count, at, core
+        self.replica, self.fsdp, self.sems = replica, fsdp, sems
+        self.rows = buffer.shape[1] // 4
+
+    def rows_of(self, shard, copy, half=None):
+        start, size = copy * self.rows, self.rows
+        if half is not None:
+            size = size // 2
+            start = start + half * size
+        return self.buffer.at[2 * shard + self.core, pl.ds(start, size)]
+
+    def copy(self, kind, shard):
+        beside, across = flip(self.replica, 1), flip(self.replica, 2)
+        if kind == 0:
+            ref, target = self.rows_of(shard, self.replica), (beside, self.fsdp)
+        elif kind == 1:
+            ref, target = self.rows_of(shard, self.replica), (across, self.fsdp)
+        elif kind == 2:
+            ref, target = self.rows_of(shard, beside, 0), (across, self.fsdp)
+        elif kind == 3:
+            ref, target = self.rows_of(shard, across, 1), (beside, self.fsdp)
+        else:
+            ref, target = self.buffer.at[2 * shard + self.core], (self.replica, flip(self.fsdp, 1))
+        return pltpu.make_async_remote_copy(
+            src_ref=ref,
+            dst_ref=ref,
+            send_sem=self.sems.at[0, kind, shard],
+            recv_sem=self.sems.at[1, kind, shard],
+            device_id=target,
+            device_id_type=MESH,
+        )
+
+    def recv(self, kind, shard):
+        beside, across = flip(self.replica, 1), flip(self.replica, 2)
+        if kind == 0:
+            ref = self.rows_of(shard, beside)
+        elif kind == 1:
+            ref = self.rows_of(shard, across)
+        elif kind < 4:
+            ref = self.rows_of(shard, flip(beside, 2), kind - 2)
+        else:
+            ref = self.buffer.at[2 * shard + 1 - self.core]
+        return pltpu.make_async_remote_copy(
+            src_ref=ref,
+            dst_ref=ref,
+            send_sem=self.sems.at[0, kind, shard],
+            recv_sem=self.sems.at[1, kind, shard],
+            device_id=(self.replica, flip(self.fsdp, 1)),
+            device_id_type=MESH,
+        )
+
+    def arrived(self, shard):
+        self.copy(0, shard).start()
+        self.copy(1, shard).start()
+
+    def others(self):
+        return [(self.at + hop) % self.count for hop in range(1, self.count)]
+
+    def relay(self):
+        for shard in self.others():
+            self.recv(0, shard).wait_recv()
+            self.copy(2, shard).start()
+            self.recv(1, shard).wait_recv()
+            self.copy(3, shard).start()
+
+    def cores(self):
+        self.copy(4, self.at).start()
+        for shard in self.others():
+            self.recv(2, shard).wait_recv()
+            self.recv(3, shard).wait_recv()
+            self.copy(4, shard).start()
+
+    def finish(self):
+        for shard in self.others() + [self.at]:
+            self.recv(4, shard).wait_recv()
+        for shard in self.others():
+            for kind in range(5):
+                self.copy(kind, shard).wait_send()
+        self.copy(4, self.at).wait_send()
+
+
+def project_kernel(
+    fsdp_size,
+    tokens_ref,
+    wq_ref,
+    wo_ref,
+    kvg_ref,
+    cos_ref,
+    sin_ref,
+    q_ref,
+    normed_ref,
+    gain_ref,
+    wq_all,
+    wo_all,
+    kvg_all,
+    kv_all,
+    wq_vmem,
+    kvg_vmem,
+    kv_vmem,
+    local_sems,
+    kvg_sems,
+    kvg_core,
+    wq_line,
+    wq_sems,
+    wo_line,
+    wo_sems,
+    kv_sems,
+    kv_core,
+):
+    replica, fsdp = lax.axis_index("replica"), lax.axis_index("fsdp")
+    count, at, core = fsdp_size // 2, fsdp // 2, fsdp % 2
+    width = tokens_ref.shape[1]
+    partner = (replica, flip(fsdp, 1))
+
+    barrier = pltpu.get_barrier_semaphore()
+    for target in (partner, (flip(replica, 1), fsdp), (flip(replica, 2), fsdp)):
+        pl.semaphore_signal(barrier, inc=1, device_id=target, device_id_type=MESH)
+
+    @pl.when(at > 0)
+    def _():
+        pl.semaphore_signal(barrier, inc=1, device_id=(replica, fsdp - 2), device_id_type=MESH)
+
+    @pl.when(at < count - 1)
+    def _():
+        pl.semaphore_signal(barrier, inc=1, device_id=(replica, fsdp + 2), device_id_type=MESH)
+
+    own = [
+        pltpu.make_async_copy(kvg_ref, kvg_all.at[fsdp], local_sems.at[0]),
+        pltpu.make_async_copy(wq_ref, wq_all.at[fsdp], local_sems.at[1]),
+        pltpu.make_async_copy(wo_ref, wo_all.at[fsdp], local_sems.at[2]),
+    ]
+    for copy in own:
+        copy.start()
+    inside = (at > 0) & (at < count - 1)
+
+    @pl.when(inside)
+    def _():
+        pl.semaphore_wait(barrier, 5)
+
+    @pl.when(jnp.logical_not(inside))
+    def _():
+        pl.semaphore_wait(barrier, 4)
+
+    def core_copy(buffer, sems, shard, lands=False):
+        ref = buffer.at[2 * shard + (1 - core if lands else core)]
+        return pltpu.make_async_remote_copy(
+            src_ref=ref,
+            dst_ref=ref,
+            send_sem=sems.at[0, shard],
+            recv_sem=sems.at[1, shard],
+            device_id=partner,
+            device_id_type=MESH,
+        )
+
+    def line(place, sems):
+        return Chain(place, count, at, replica, fsdp, sems.at[0], sems.at[1])
+
+    kvg = line(lambda shard: kvg_all.at[2 * shard + core], kvg_sems)
+    kv = line(lambda shard: kv_all.at[2 * shard + core], kv_sems)
+    wq = Spread(wq_all, count, at, core, replica, fsdp, wq_sems)
+    wo = Spread(wo_all, count, at, core, replica, fsdp, wo_sems)
+    wq_chain = line(lambda shard: wq.rows_of(shard, replica), wq_line)
+    wo_chain = line(lambda shard: wo.rows_of(shard, replica), wo_line)
+    own[0].wait()
+    kvg.begin()
+    core_copy(kvg_all, kvg_core, at).start()
+    own[1].wait()
+    wq_chain.begin()
+    own[2].wait()
+    wo_chain.begin()
+
+    inputs = tokens_ref[...].astype(jnp.float32)
+    inverse = lax.rsqrt(jnp.mean(inputs * inputs, axis=1, keepdims=True) + EPSILON)
+
+    for hop in range(1, count):
+        kvg.step(hop, lambda shard: core_copy(kvg_all, kvg_core, shard).start())
+        wq_chain.step(hop, wq.arrived)
+        wo_chain.step(hop, wo.arrived)
+    for shard in range(count):
+        core_copy(kvg_all, kvg_core, shard, True).wait_recv()
+    load = pltpu.make_async_copy(kvg_all, kvg_vmem, local_sems.at[0])
+    load.start()
+    load.wait()
+    table = kvg_vmem[...].reshape(width, kvg_vmem.shape[2])
+    gains = table[:, 256:].astype(jnp.float32).T[:8]
+    gain_ref[...] = gains
+    normed_ref[...] = (inputs * inverse * gains[:1]).astype(jnp.bfloat16)
+    kv_raw = matmul(normed_ref[...], table[:, :256])
+    cos_table, sin_table = cos_ref[...], sin_ref[...]
+    key_raw = kv_raw[:, :128]
+    key_rot = key_raw * cos_table + pltpu.roll(key_raw, 64, 1) * sin_table
+    kv_vmem[:, :128] = key_rot.astype(jnp.bfloat16)
+    kv_vmem[:, 128:] = kv_raw[:, 128:].astype(jnp.bfloat16)
+    store = pltpu.make_async_copy(kv_vmem, kv_all.at[fsdp], local_sems.at[0])
+    store.start()
+    store.wait()
+    kv.begin()
+    core_copy(kv_all, kv_core, at).start()
+    wq.relay()
+    kv.step(1, lambda shard: core_copy(kv_all, kv_core, shard).start())
+    wq.cores()
+    wo.relay()
+    for shard in wq.others() + [at]:
+        wq.recv(4, shard).wait_recv()
+    load = pltpu.make_async_copy(wq_all, wq_vmem, local_sems.at[1])
+    load.start()
+    for hop in range(2, count):
+        kv.step(hop, lambda shard: core_copy(kv_all, kv_core, shard).start())
+    load.wait()
+    weight = wq_vmem.reshape(width, width)
+
+    def columns(block):
+        start = pl.multiple_of(block * 512, 512)
+        raw = matmul(normed_ref[...], weight[:, pl.ds(start, 512)])
+        for h in range(4):
+            head = raw[:, h * 128 : (h + 1) * 128]
+            turned = head * cos_table + pltpu.roll(head, 64, 1) * sin_table
+            q_ref[:, pl.ds(start + h * 128, 128)] = turned.astype(jnp.bfloat16)
+
+    pl.loop(0, width // 512)(columns)
+    wo.cores()
+    for shard in range(count):
+        core_copy(kv_all, kv_core, shard, True).wait_recv()
+    wo.finish()
+    for shard in wq.others():
+        for kind in range(5):
+            wq.copy(kind, shard).wait_send()
+    wq.copy(4, at).wait_send()
+    for shard in range(count):
+        core_copy(kvg_all, kvg_core, shard).wait_send()
+        core_copy(kv_all, kv_core, shard).wait_send()
+    for chain in (kvg, kv, wq_chain, wo_chain):
+        chain.finish()
+
+
+def project(tokens, wq, wo, kvg, cos_table, sin_table):
+    rows, width = tokens.shape
+    shard = wq.shape[0]
+    fsdp_size = lax.axis_size("fsdp")
+    count = fsdp_size // 2
+    low = jnp.bfloat16
+    vmem, hbm = pl.BlockSpec(memory_space=pltpu.VMEM), pl.BlockSpec(memory_space=pl.ANY)
+    dma = pltpu.SemaphoreType.DMA
+    return pl.pallas_call(
+        functools.partial(project_kernel, fsdp_size),
+        out_shape=(
+            jax.ShapeDtypeStruct((rows, width), low),
+            jax.ShapeDtypeStruct((rows, width), low),
+            jax.ShapeDtypeStruct((8, width), jnp.float32),
+            jax.ShapeDtypeStruct((fsdp_size, shard, width), low),
+            jax.ShapeDtypeStruct((fsdp_size, shard, width), low),
+            jax.ShapeDtypeStruct((fsdp_size, shard, kvg.shape[1]), low),
+            jax.ShapeDtypeStruct((fsdp_size, rows, 256), low),
+        ),
+        in_specs=[vmem, hbm, hbm, hbm, vmem, vmem],
+        out_specs=(vmem, vmem, vmem, hbm, hbm, hbm, hbm),
+        scratch_shapes=[
+            pltpu.VMEM((fsdp_size, shard, width), low),
+            pltpu.VMEM((fsdp_size, shard, kvg.shape[1]), low),
+            pltpu.VMEM((rows, 256), low),
+            dma((3,)),
+            dma((2, 2, count)),
+            dma((2, count)),
+            dma((2, 2, count)),
+            dma((2, 5, count)),
+            dma((2, 2, count)),
+            dma((2, 5, count)),
+            dma((2, 2, count)),
+            dma((2, count)),
+        ],
+        compiler_params=pltpu.CompilerParams(
+            collective_id=0, has_side_effects=True, vmem_limit_bytes=48 << 20
+        ),
+        cost_estimate=pl.CostEstimate(
+            flops=2 * rows * width * (width + 256), transcendentals=0, bytes_accessed=40 << 20
+        ),
+        name="project",
+    )(tokens, wq, wo, kvg, cos_table, sin_table)
+
+
 def swap(value, step):
     copies = lax.axis_size("replica")
     return lax.ppermute(value, "replica", [(r, r ^ step) for r in range(copies)])
@@ -337,18 +682,6 @@
 def quarter(shard, copy_index):
     rows = shard.shape[0] // lax.axis_size("replica")
     return lax.dynamic_slice_in_dim(shard, copy_index * rows, rows, 0)
-
-
-def whole_weight(shard, copy_index):
-    rows, width = shard.shape
-    copies, fsdp_size = lax.axis_size("replica"), lax.axis_size("fsdp")
-    pieces = gather_copies(gather_shards(quarter(shard, copy_index)))
-    out = jnp.zeros((fsdp_size, copies, rows // copies, width), shard.dtype)
-    for step, piece in enumerate(pieces):
-        out = lax.dynamic_update_slice_in_dim(
-            out, piece.reshape(fsdp_size, 1, rows // copies, width), copy_index ^ step, 1
-        )
-    return out.reshape(fsdp_size * rows, width)
 
 
 def sum_weight_grad(partial, copy_index):
@@ -387,22 +720,25 @@
     copies = lax.axis_size("replica")
     low = jnp.bfloat16
 
-    gains = lax.all_gather(jnp.stack([attn_gain, ffn_gain]), "fsdp", axis=1, tiled=True)
-    gain_attn = gains[0].astype(jnp.float32)
-    gain_ffn = gains[1].astype(jnp.float32)
-    w_qkv = whole_weight(
-        jnp.concatenate([query_weight, key_weight, value_weight], axis=1), copy_index
-    )
+    cos_table, sin_table = rope_tables(positions, head_dim)
+    gain_columns = jnp.stack([attn_gain, ffn_gain], axis=1)
+    queries, normed, gains, w_query, w_out, w_kvg, kv_all = project(
+        tokens,
+        query_weight,
+        output_weight,
+        jnp.concatenate(
+            [key_weight, value_weight, jnp.pad(gain_columns, ((0, 0), (0, 126)))], axis=1
+        ),
+        cos_table,
+        sin_table,
+    )
+    w_query = w_query.reshape(model_width, model_width)
+    w_out = w_out.reshape(model_width, model_width)
+    w_kv = w_kvg.reshape(model_width, 3 * head_dim)[:, : 2 * head_dim]
+    kv_all = kv_all.reshape(fsdp_size * tok_rows, 2 * head_dim)
+    gain_attn, gain_ffn = gains[0], gains[1]
     inputs = tokens.astype(jnp.float32)
-    normed_full, inverse_attn = norm_forward(inputs, gain_attn)
-    normed = normed_full.astype(low)
-    qkv = matmul(normed, w_qkv)
-    query_raw = qkv[:, :model_width]
-    key_raw = qkv[:, model_width : model_width + head_dim]
-    value_rows = qkv[:, model_width + head_dim :].astype(low)
-    cos_table, sin_table = rope_tables(positions, head_dim)
-    key_rot = (key_raw * cos_table + swap_halves(key_raw) * sin_table).astype(low)
-    kv_all = gather_shards(jnp.concatenate([key_rot, value_rows], axis=1))
+    inverse_attn = lax.rsqrt(jnp.mean(inputs * inputs, axis=-1, keepdims=True) + EPSILON)
     key_width = max(GROUP_TOK, tok_rows)
     window_start = fsdp_index * tok_rows // key_width * key_width
     one_group = fsdp_size * tok_rows == key_width
@@ -412,16 +748,10 @@
     row_at = base + jnp.arange(tok_rows, dtype=jnp.int32)
     lowest = jnp.where(positions < PROMPT, 0, row_at - (positions - PROMPT))
     base = base[None]
-    mixed_rows, queries, logs = attend(
-        base,
-        query_raw,
-        kv,
-        cos_table,
-        sin_table,
-        jnp.broadcast_to(lowest[:, None], (tok_rows, 128)),
-    )
-
-    w_out = whole_weight(output_weight, copy_index)
+    mixed_rows, logs = attend(
+        base, queries, kv, jnp.broadcast_to(lowest[:, None], (tok_rows, 128))
+    )
+
     hidden = inputs + matmul(mixed_rows, w_out)
     normed_ffn_full, inverse_ffn = norm_forward(hidden, gain_ffn)
     normed_ffn = normed_ffn_full.astype(low)
@@ -444,20 +774,26 @@
     out_parts = matmul(activation, w_down)
     layer_out = (hidden + scatter_copies(jnp.split(out_parts, copies))).astype(low)
 
+    gate_part = contract(d_gate, normed_all, 0, 0).astype(low)
+    up_part = contract(d_up, normed_all, 0, 0).astype(low)
+    down_part = contract(activation, grads, 0, 0).astype(low)
+
     def ffn_grad(partial):
-        summed = scatter_shards(partial.astype(low))
+        summed = scatter_shards(partial)
         pieces = place(gather_copies(summed), copy_index)
         return pieces.reshape(-1, model_width).astype(jnp.float32)
-
-    gate_grad = ffn_grad(contract(d_gate, normed_all, 0, 0)).T
-    up_grad = ffn_grad(contract(d_up, normed_all, 0, 0)).T
-    down_grad = ffn_grad(contract(activation, grads, 0, 0))
 
     cotangent = grad_out.astype(jnp.float32)
     resid_ffn, ffn_gain_term = norm_backward(hidden, inverse_ffn, gain_ffn, d_normed_ffn)
     d_hidden = cotangent + resid_ffn
     d_branch = d_hidden.astype(low)
     d_mixed = contract(d_branch, w_out, 1, 1).astype(low)
+    d_mixed, gate_part, up_part, down_part = lax.optimization_barrier(
+        (d_mixed, gate_part, up_part, down_part)
+    )
+    gate_grad = ffn_grad(gate_part).T
+    up_grad = ffn_grad(up_part).T
+    down_grad = ffn_grad(down_part)
     output_grad = sum_weight_grad(contract(mixed_rows, d_branch, 0, 0), copy_index)
 
     d_query_raw, d_kv = attend_back(
@@ -481,8 +817,8 @@
     d_key_raw = (d_key * cos_table - swap_halves(d_key) * sin_table).astype(low)
     d_kv_raw = jnp.concatenate([d_key_raw, d_kv_sum[:, head_dim:].astype(low)], axis=1)
     kv_grad = sum_weight_grad(contract(normed, d_kv_raw, 0, 0), copy_index)
-    d_normed = contract(d_query_raw, w_qkv[:, :model_width], 1, 1) + contract(
-        d_kv_raw, w_qkv[:, model_width:], 1, 1
+    d_normed = contract(d_query_raw, w_query, 1, 1) + contract(
+        d_kv_raw, w_kv, 1, 1
     )
     resid_attn, attn_gain_term = norm_backward(inputs, inverse_attn, gain_attn, d_normed)
     input_grad = d_hidden + resid_attn

time: 1290 us -> 1270 us (0.984)
  Pallas kernels: 45.1 us -> 219 us
  waiting for transfers between devices: 633 us -> 502 us
  local copies, waits for them, and re-layouts: 114 us -> 86.8 us
  matrix products: 234 us -> 216 us
    pallas_call x0 -> x1, Pallas kernels: none -> 177 us  [project(): pl.pallas_call(functools.partial(project_kernel, fsdp_size), out_shape=(j...]
    ppermute x60 -> x52, waiting for transfers between devices: 371 us -> 218 us  [swap(): lax.ppermute(value, 'replica', [(r, r ^ step) for r in range(copies)])]
    reduce_scatter x7, waiting for transfers between devices: 227 us -> 254 us  [scatter_shards(): return lax.psum_scatter(value, 'fsdp', scatter_dimension=0, tiled=True)]
    ppermute x60 -> x52, starting transfers between devices: 70.3 us -> 61.9 us  [swap(): lax.ppermute(value, 'replica', [(r, r ^ step) for r in range(copies)])]
    all_gather x6 -> x3, waiting for transfers between devices: 35.4 us -> 27.5 us  [gather_shards(): return lax.all_gather(value, 'fsdp', axis=0, tiled=True)]
    dot_general x5 -> x4, matrix products: 75.7 us -> 68.3 us  [matmul(): return jnp.dot(left, right, preferred_element_type=jnp.float32)]
  transfers between devices with their start and end apart: 73 -> 62, of which waited for: 35 -> 31; matrix products, arithmetic and copies ran while one was open for 25% -> 20% of each run, Pallas kernels for 2% -> 16%
where the time goes in v3:
time: 1270 us; the launch traced here: 1250 us
  waiting for transfers between devices  502 us (40%)
  Pallas kernels  219 us (17%)
  matrix products  216 us (17%)
  local copies, waits for them, and re-layouts  86.8 us (7%)
  blocking collectives  75.6 us (6%)
  other arithmetic  73.7 us (6%)
  starting transfers between devices  62.7 us (5%)
  between operations  15.8 us (1%)
    reduce_scatter x7, waiting for transfers between devices, scatter_shards(): return lax.psum_scatter(value, 'fsdp', scatter_dimension=0, tiled=True)  254 us
    ppermute x52, waiting for transfers between devices, swap(): lax.ppermute(value, 'replica', [(r, r ^ step) for r in range(copies)])  218 us
    pallas_call x1, Pallas kernels, project(): pl.pallas_call(functools.partial(project_kernel, fsdp_size), out_shape=(j...  177 us
    dot_general x12, matrix products, contract(): lax.dot_general(left, right, (((left_dim,), (right_dim,)), ((), ())), pre...  148 us
    psum x1, blocking collectives, shards(): lax.psum(jnp.stack([attn_gain_term, ffn_gain_term]), ('replica', 'fsdp'))  75.6 us
    dot_general x4, matrix products, matmul(): return jnp.dot(left, right, preferred_element_type=jnp.float32)  68.3 us
    ppermute x52, starting transfers between devices, swap(): lax.ppermute(value, 'replica', [(r, r ^ step) for r in range(copies)])  61.9 us
    all_gather x3, waiting for transfers between devices, gather_shards(): return lax.all_gather(value, 'fsdp', axis=0, tiled=True)  27.5 us
  transfers between devices with their start and end apart: 62, of which 31 were waited for; matrix products, arithmetic and copies ran while one was open for 20% of the time, Pallas kernels for 16%

profile of v3, /device:TPU:0, one launch (start us, length us, event | category | flops | bytes accessed | tf_op | source)
XLA Modules:
  0.0 1251.8 jit_solution(14132806155703430364)
XLA Ops:
  12.2 3.0 collective-permute-start.8
  20.0 176.6 %project.1 = (bf16[512,2048]{1,0:T(8,128)(2,1)}, bf16[512,2048]{1,0:T(8,128)(2,1)}, f32[8,2048]{1,0:T(8,128)S(1)}, bf16[8,256,2048]{2,1,0:T(8,128)(2,1)}, bf16[8...) custom-call(bf16[512,2048]{1,0:T(8,128)(2,1)} %tokens_ref.1, ...), custom_call_target="tpu_custom_call" | custom-call | flops 4831838208 | bytes 41943040 | tf_op jit(solution)/shard_map/project/pallas_call | solution.py:599
  200.0 19.2 %attend.1 = (bf16[512,2048]{1,0:T(8,128)(2,1)S(1)}, f32[4,4,8,512]{3,2,1,0:T(8,128)S(1)}) custom-call(s32[1]{0:T(128)} %bitcast.base_ref, bf16[512,2048]{1,0:T(8,128)(2,1)S(1)} %copy-done.13, bf16[4096,256]{1,0:T(8,128)(2,1)S(1)} %bitcast.183, s32[512,128]{1,0:T(8,128)S(1)} %broadcast_in_dim.105.low_ref), custom_call_target="tpu_custom_call" | custom-call | flops 16106127360 | bytes 16777216 | tf_op jit(solution)/shard_map/attend/pallas_call | solution.py:137
  219.2 4.6 multiply_reduce_fusion.2
  225.5 2.5 constant_dynamic-update-slice_fusion.4
  238.7 19.0 %collective-permute-done.1 = bf16[512,2048]{1,0:T(8,128)(2,1)} collective-permute-done((bf16[512,2048]{1,0:T(8,128)(2,1)}, bf16[512,2048]{1,0:T(8,128)(2,1)}, u32[]{:S(2)}, u32[]{:S(2)}) %collective-permute-start.1) | collective-permute-done | bytes 2097184 | tf_op jit(solution)/shard_map/ppermute | solution.py:638
  265.8 3.2 constant_dynamic-update-slice_fusion.3
  269.0 3.1 constant_dynamic-update-slice_fusion.2
  272.2 7.9 collective-permute-done.10
  281.9 20.6 %collective-permute-done.2 = bf16[256,2048]{1,0:T(8,128)(2,1)S(1)} collective-permute-done((bf16[256,2048]{1,0:T(8,128)(2,1)S(1)}, bf16[256,2048]{1,0:T(8,128)(2,1)S(1)}, u32[]{:S(2)}, u32[]{:S(2)}) %collective-permute-start.2) | collective-permute-done | bytes 1048608 | tf_op jit(solution)/shard_map/ppermute | solution.py:638
  305.4 18.9 %fusion.57 = f32[2048,1408]{1,0:T(8,128)} fusion(bf16[2048,2048]{1,0:T(8,128)(2,1)} %constant_dynamic-update-slice_fusion, bf16[1408,2048]{1,0:T(8,128)(2,1)} %all-gather.6.cloned.1.call-done), kind=kOutput, calls=%fused_computation.182 | convolution fusion | flops 11811160064 | bytes 25690112 | tf_op jit(solution)/shard_map/dot_general | solution.py:28
  324.3 18.6 %fusion.56 = f32[2048,1408]{1,0:T(8,128)} fusion(bf16[2048,2048]{1,0:T(8,128)(2,1)} %constant_dynamic-update-slice_fusion, bf16[1408,2048]{1,0:T(8,128)(2,1)} %all-gather.4.cloned.1.call-done), kind=kOutput, calls=%fused_computation.181 | convolution fusion | flops 11811160064 | bytes 25690112 | tf_op jit(solution)/shard_map/dot_general | solution.py:28
  342.9 27.5 %all-gather.8.cloned.1.call-done = bf16[1408,2048]{1,0:T(8,128)(2,1)} async-done(((bf16[176,2048]{1,0:T(8,128)(2,1)}), bf16[1408,2048]{1,0:T(8,128)(2,1)}) %all-gather.8.cloned.1.call-update) | async-done | bytes 5767184 | tf_op jit(solution)/shard_map/all_gather | solution.py:668
  370.4 26.0 %multiply_convert_fusion = (bf16[2048,1408]{1,0:T(8,128)(2,1)}, bf16[2048,1408]{1,0:T(8,128)(2,1)}, bf16[2048,1408]{1,0:T(8,128)(2,1)}) fusion(f32[2048,1408]{1,0:T(8,128)} %fusion.56, f32[2048,1408]{1,0:T(8,128)} %fusion.57, bf16[2048,2048]{1,0:T(8,128)(2,1)} %copy-done.30, bf16[1408,2048]{1,0:T(8,128)(2,1)} %all-gather.8.cloned.1.call-done), kind=kOutput, calls=%fused_computation | convolution fusion | flops 11857297408 | bytes 54525952 | tf_op jit(solution)/shard_map/dot_general | solution.py:28
  396.4 18.3 %convolution_convert_fusion = bf16[1408,2048]{1,0:T(8,128)(2,1)} fusion(bf16[2048,1408]{1,0:T(8,128)(2,1)} %get-tuple-element.49, bf16[2048,2048]{1,0:T(8,128)(2,1)} %copy-done.30), kind=kOutput, calls=%fused_computation.10 | convolution fusion | flops 11814043648 | bytes 19922944 | tf_op jit(solution)/shard_map/dot_general | solution.py:28
  414.7 19.2 %fusion.58 = f32[2048,2048]{1,0:T(8,128)} fusion(bf16[2048,1408]{1,0:T(8,128)(2,1)} %get-tuple-element.48, bf16[1408,2048]{1,0:T(8,128)(2,1)} %all-gather.4.cloned.1.call-done), kind=kOutput, calls=%fused_computation.183 | convolution fusion | flops 11811160064 | bytes 28311552 | tf_op jit(solution)/shard_map/dot_general | solution.py:24
  434.0 24.1 %fusion.54 = (bf16[2048,2048]{1,0:T(8,128)(2,1)}, f32[2048,2048]{1,0:T(8,128)}) fusion(f32[2048,2048]{1,0:T(8,128)} %fusion.58, bf16[2048,1408]{1,0:T(8,128)(2,1)} %get-tuple-element.47, bf16[1408,2048]{1,0:T(8,128)(2,1)} %all-gather.6.cloned.1.call-done), kind=kOutput, calls=%fused_computation.179 | convolution fusion | flops 11819548672 | bytes 53477376 | tf_op jit(solution)/shard_map/dot_general | solution.py:24
  458.1 4.4 fusion.45
  465.4 20.3 %fusion.55 = (bf16[2048,2048]{1,0:T(8,128)(2,1)}, f32[2048,2048]{1,0:T(8,128)}) fusion(bf16[2048,1408]{1,0:T(8,128)(2,1)} %get-tuple-element.49, bf16[1408,2048]{1,0:T(8,128)(2,1)} %all-gather.8.cloned.1.call-done), kind=kOutput, calls=%fused_computation.180 | convolution fusion | flops 11815354368 | bytes 36700160 | tf_op jit(solution)/shard_map/dot_general | solution.py:24
  485.7 16.7 %convolution_convert_fusion.1 = bf16[1408,2048]{1,0:T(8,128)(2,1)} fusion(bf16[2048,1408]{1,0:T(8,128)(2,1)S(1)} %bitcast.223, bf16[2048,2048]{1,0:T(8,128)(2,1)} %constant_dynamic-update-slice_fusion), kind=kOutput, calls=%fused_computation.11 | convolution fusion | flops 11814043648 | bytes 19922944 | tf_op jit(solution)/shard_map/dot_general | solution.py:28
  502.4 2.7 fusion.46
  506.4 3.6 fusion.16
  516.1 15.2 %collective-permute-done.6 = bf16[256,2048]{1,0:T(8,128)(2,1)S(1)} collective-permute-done((bf16[256,2048]{1,0:T(8,128)(2,1)S(1)}, bf16[256,2048]{1,0:T(8,128)(2,1)S(1)}, u32[]{:S(2)}, u32[]{:S(2)}) %collective-permute-start.6) | collective-permute-done | bytes 1048608 | tf_op jit(solution)/shard_map/ppermute | solution.py:638
  531.9 3.1 fusion.18
  540.2 16.9 %convolution_convert_fusion.2 = bf16[1408,2048]{1,0:T(8,128)(2,1)} fusion(bf16[2048,1408]{1,0:T(8,128)(2,1)S(1)} %bitcast.221, bf16[2048,2048]{1,0:T(8,128)(2,1)} %constant_dynamic-update-slice_fusion), kind=kOutput, calls=%fused_computation.12 | convolution fusion | flops 11814043648 | bytes 19922944 | tf_op jit(solution)/shard_map/dot_general | solution.py:28
  557.1 19.8 %collective-permute-done.15 = bf16[512,2048]{1,0:T(8,128)(2,1)} collective-permute-done((bf16[512,2048]{1,0:T(8,128)(2,1)}, bf16[512,2048]{1,0:T(8,128)(2,1)}, u32[]{:S(2)}, u32[]{:S(2)}) %collective-permute-start.15) | collective-permute-done | bytes 2097184 | tf_op jit(solution)/shard_map/ppermute | solution.py:638
  576.9 5.6 multiply_reduce_fusion
  582.6 38.0 %collective-permute-done.7 = bf16[512,2048]{1,0:T(8,128)(2,1)} collective-permute-done((bf16[512,2048]{1,0:T(8,128)(2,1)}, bf16[512,2048]{1,0:T(8,128)(2,1)}, u32[]{:S(2)}, u32[]{:S(2)}) %collective-permute-start.7) | collective-permute-done | bytes 2097184 | tf_op jit(solution)/shard_map/ppermute | solution.py:638
  620.6 8.7 subtract_add_fusion
  629.3 5.8 convolution_convert_fusion.3.d_mixed_ref
  635.1 8.3 fusion.24
  643.4 23.5 %attend_back.1 = (bf16[512,2048]{1,0:T(8,128)(2,1)S(1)}, bf16[4096,256]{1,0:T(8,128)(2,1)}) custom-call(s32[1]{0:T(128)} %bitcast.base_ref, bf16[512,2048]{1,0:T(8,128)(2,1)} %get-tuple-element.26.q_ref, bf16[4096,256]{1,0:T(8,128)(2,1)} %bitcast.182, f32[512,128]{1,0:T(8,128)S(1)} %copy-done.5, f32[512,128]{1,0:T(8,128)S(1)} %copy-done.3, ...), custom_call_target="tpu_custom_call" | custom-call | flops 26843545600 | bytes 16777216 | tf_op jit(solution)/shard_map/attend_back/pallas_call | solution.py:246
  668.4 2.5 dynamic-slice_convert_fusion
  672.9 4.7 constant_dynamic-slice_fusion.4
  677.6 2.9 constant_dynamic-slice_fusion.3
  681.1 4.7 fusion.60
  685.8 2.8 constant_dynamic-slice_fusion.8
  691.1 4.8 dynamic-slice_convert_fusion.3
  702.1 124.5 %reduce-scatter.8.cloned.1.call-done = bf16[512,256]{1,0:T(8,128)(2,1)} async-done(((bf16[4096,256]{1,0:T(8,128)(2,1)}), bf16[512,256]{1,0:T(8,128)(2,1)}) %reduce-scatter.8.cloned.1.call-update) | async-done | bytes 262160 | tf_op jit(solution)/shard_map/reduce_scatter | solution.py:672
  829.8 2.3 fusion.40
  841.3 3.5 dynamic-slice_convert_fusion.5
  847.4 2.2 collective-permute-done.25
  850.4 5.9 fusion.12
  856.6 10.9 collective-permute-done.18
  867.5 2.3 fusion.21
  874.2 2.5 constant_dynamic-slice_fusion.9
  876.7 36.6 %collective-permute-done.19 = bf16[512,2048]{1,0:T(8,128)(2,1)S(1)} collective-permute-done((bf16[512,2048]{1,0:T(8,128)(2,1)S(1)}, bf16[512,2048]{1,0:T(8,128)(2,1)S(1)}, u32[]{:S(2)}, u32[]{:S(2)}) %collective-permute-start.19) | collective-permute-done | bytes 2097184 | tf_op jit(solution)/shard_map/ppermute | solution.py:638
  915.3 2.4 fusion.14
  922.0 7.8 fusion.59
  929.8 3.5 fusion.6
  933.3 75.6 %psum.7 = f32[2,2048]{1,0:T(2,128)S(1)} all-reduce(f32[2,2048]{1,0:T(2,128)S(1)} %pad_maximum_fusion.15), channel_id=1, replica_groups=mesh['replica'=4,'fsdp'=8] {'replica','fsdp'}, use_global_device_ids=true, to_apply=%region_10.11 | all-reduce | flops 4096 | bytes 32768 | tf_op jit(solution)/shard_map/psum | solution.py:825
  1009.5 7.2 fusion.3
  1016.7 2.4 collective-permute-start.29
  1024.9 2.2 collective-permute-done.30
  1034.1 2.6 collective-permute-done.37
  1050.7 5.0 reduce-scatter.20.cloned.1.call-done
  1058.6 63.1 %reduce-scatter.16.cloned.1.call-done = bf16[176,2048]{1,0:T(8,128)(2,1)} async-done(((bf16[1408,2048]{1,0:T(8,128)(2,1)}), bf16[176,2048]{1,0:T(8,128)(2,1)}) %reduce-scatter.16.cloned.1.call-update) | async-done | bytes 720912 | tf_op jit(solution)/shard_map/reduce_scatter | solution.py:672
  1126.1 61.6 %reduce-scatter.18.cloned.1.call-done = bf16[176,2048]{1,0:T(8,128)(2,1)} async-done(((bf16[1408,2048]{1,0:T(8,128)(2,1)}), bf16[176,2048]{1,0:T(8,128)(2,1)}) %reduce-scatter.18.cloned.1.call-update) | async-done | bytes 720912 | tf_op jit(solution)/shard_map/reduce_scatter | solution.py:672
  1196.6 7.7 collective-permute-done.45
  1214.3 15.6 %collective-permute-done.43 = bf16[88,2048]{1,0:T(8,128)(2,1)S(1)} collective-permute-done((bf16[88,2048]{1,0:T(8,128)(2,1)S(1)}, bf16[88,2048]{1,0:T(8,128)(2,1)S(1)}, u32[]{:S(2)}, u32[]{:S(2)}) %collective-permute-start.43) | collective-permute-done | bytes 360480 | tf_op jit(solution)/shard_map/ppermute | solution.py:638
  1230.5 3.5 convert_bitcast_fusion.1
  1234.0 3.3 collective-permute-done.46
  1237.4 3.5 convert_bitcast_fusion
  1241.0 3.5 bitcast_convert_fusion
  (325 shorter events, 147.7 us)
Async XLA Ops:
  7.2 298.2 %all-gather.6.cloned.1.call-start = ((), (), s32[]{:S(2)}) async-start(), calls=%async_computation.8 | async-start | bytes 6488064 | tf_op jit(solution)/shard_map/all_gather | solution.py:668
  10.0 314.3 %all-gather.4.cloned.1.call-start = ((), (), s32[]{:S(2)}) async-start(), calls=%async_computation.7 | async-start | bytes 6488064 | tf_op jit(solution)/shard_map/all_gather | solution.py:668
  12.2 358.2 %all-gather.8.cloned.1.call-start = ((), (), s32[]{:S(2)}) async-start(), calls=%async_computation.9 | async-start | bytes 6488064 | tf_op jit(solution)/shard_map/all_gather | solution.py:668
  12.2 221.7 %collective-permute-start.8 = (bf16[512,2048]{1,0:T(8,128)(2,1)}, bf16[512,2048]{1,0:T(8,128)(2,1)}, u32[]{:S(2)}, u32[]{:S(2)}) collective-permute-start(bf16[512,2048]{1,0:T(8,128)(2,1)} %param.24), channel_id=1, source_target_pairs={{0,8},{8,0},{16,24},{24,16},{1,9},{9,1},{17,25},{25,17},{2,10},{10... | collective-permute-start | bytes 6291464 | tf_op jit(solution)/shard_map/ppermute | solution.py:638
  15.2 221.6 %collective-permute-start.9 = (bf16[512,2048]{1,0:T(8,128)(2,1)}, bf16[512,2048]{1,0:T(8,128)(2,1)}, u32[]{:S(2)}, u32[]{:S(2)}) collective-permute-start(bf16[512,2048]{1,0:T(8,128)(2,1)} %param.24), channel_id=1, source_target_pairs={{0,16},{8,24},{16,0},{24,8},{1,17},{9,25},{17,1},{25,9},{2,18},{10... | collective-permute-start | bytes 6291464 | tf_op jit(solution)/shard_map/ppermute | solution.py:638
  17.0 179.7 %copy-start.38 = (s32[512]{0:T(512)}, s32[512]{0:T(512)S(1)}, u32[]{:S(2)}) copy-start(s32[512]{0:T(512)S(1)} %get-tuple-element.97) | copy-start | bytes 6148
  18.2 178.4 %copy-start.2 = (f32[512,128]{1,0:T(8,128)}, f32[512,128]{1,0:T(8,128)S(1)}, u32[]{:S(2)}) copy-start(f32[512,128]{1,0:T(8,128)S(1)} %get-tuple-element.107.sin_ref) | copy-start | bytes 786436
  228.0 29.7 %collective-permute-start.1 = (bf16[512,2048]{1,0:T(8,128)(2,1)}, bf16[512,2048]{1,0:T(8,128)(2,1)}, u32[]{:S(2)}, u32[]{:S(2)}) collective-permute-start(bf16[512,2048]{1,0:T(8,128)(2,1)} %get-tuple-element.46), channel_id=1, source_target_pairs={{0,16},{8,24},{16,0},{24,8},{1,17},{9,25},{17,1},{25,9},{2,18},{10... | collective-permute-start | bytes 6291464 | tf_op jit(solution)/shard_map/ppermute | solution.py:638
  229.5 31.0 %collective-permute-start = (bf16[512,2048]{1,0:T(8,128)(2,1)}, bf16[512,2048]{1,0:T(8,128)(2,1)}, u32[]{:S(2)}, u32[]{:S(2)}) collective-permute-start(bf16[512,2048]{1,0:T(8,128)(2,1)} %get-tuple-element.46), channel_id=1, source_target_pairs={{0,8},{8,0},{16,24},{24,16},{1,9},{9,1},{17,25},{25,17},{2,10},{10... | collective-permute-start | bytes 6291464 | tf_op jit(solution)/shard_map/ppermute | solution.py:638
  232.1 594.5 %reduce-scatter.8.cloned.1.call-start = ((), (), s32[]{:S(2)}) async-start(), calls=%async_computation.10 | async-start | bytes 2359296 | tf_op jit(solution)/shard_map/reduce_scatter | solution.py:672
  235.2 44.9 %collective-permute-start.10 = (bf16[256,2048]{1,0:T(8,128)(2,1)S(1)}, bf16[256,2048]{1,0:T(8,128)(2,1)S(1)}, u32[]{:S(2)}, u32[]{:S(2)}) collective-permute-start(bf16[256,2048]{1,0:T(8,128)(2,1)S(1)} %slice.325), channel_id=1, source_target_pairs={{0,16},{8,24},{16,0},{24,8},{1,17},{9,25},{17,1},{25,9},{2,18},{10... | collective-permute-start | bytes 3145736 | tf_op jit(solution)/shard_map/ppermute | solution.py:638
  238.1 43.7 %collective-permute-start.11 = (bf16[256,2048]{1,0:T(8,128)(2,1)S(1)}, bf16[256,2048]{1,0:T(8,128)(2,1)S(1)}, u32[]{:S(2)}, u32[]{:S(2)}) collective-permute-start(bf16[256,2048]{1,0:T(8,128)(2,1)S(1)} %slice.326), channel_id=1, source_target_pairs={{0,8},{8,0},{16,24},{24,16},{1,9},{9,1},{17,25},{25,17},{2,10},{10... | collective-permute-start | bytes 3145736 | tf_op jit(solution)/shard_map/ppermute | solution.py:638
  259.0 45.3 %collective-permute-start.3 = (bf16[256,2048]{1,0:T(8,128)(2,1)S(1)}, bf16[256,2048]{1,0:T(8,128)(2,1)S(1)}, u32[]{:S(2)}, u32[]{:S(2)}) collective-permute-start(bf16[256,2048]{1,0:T(8,128)(2,1)S(1)} %slice.318), channel_id=1, source_target_pairs={{0,8},{8,0},{16,24},{24,16},{1,9},{9,1},{17,25},{25,17},{2,10},{10... | collective-permute-start | bytes 3145736 | tf_op jit(solution)/shard_map/ppermute | solution.py:638
  261.8 40.7 %collective-permute-start.2 = (bf16[256,2048]{1,0:T(8,128)(2,1)S(1)}, bf16[256,2048]{1,0:T(8,128)(2,1)S(1)}, u32[]{:S(2)}, u32[]{:S(2)}) collective-permute-start(bf16[256,2048]{1,0:T(8,128)(2,1)S(1)} %slice.317), channel_id=1, source_target_pairs={{0,16},{8,24},{16,0},{24,8},{1,17},{9,25},{17,1},{25,9},{2,18},{10... | collective-permute-start | bytes 3145736 | tf_op jit(solution)/shard_map/ppermute | solution.py:638
  462.4 43.9 %collective-permute-start.14 = (bf16[256,2048]{1,0:T(8,128)(2,1)}, bf16[256,2048]{1,0:T(8,128)(2,1)}, u32[]{:S(2)}, u32[]{:S(2)}) collective-permute-start(bf16[256,2048]{1,0:T(8,128)(2,1)} %get-tuple-element.64), channel_id=1, source_target_pairs={{0,8},{8,0},{16,24},{24,16},{1,9},{9,1},{17,25},{25,17},{2,10},{10... | collective-permute-start | bytes 3145736 | tf_op jit(solution)/shard_map/ppermute | solution.py:638
  463.9 42.5 %collective-permute-start.12 = (bf16[256,2048]{1,0:T(8,128)(2,1)}, bf16[256,2048]{1,0:T(8,128)(2,1)}, u32[]{:S(2)}, u32[]{:S(2)}) collective-permute-start(bf16[256,2048]{1,0:T(8,128)(2,1)} %get-tuple-element.65), channel_id=1, source_target_pairs={{0,16},{8,24},{16,0},{24,8},{1,17},{9,25},{17,1},{25,9},{2,18},{10... | collective-permute-start | bytes 3145736 | tf_op jit(solution)/shard_map/ppermute | solution.py:638
  505.2 26.1 %collective-permute-start.6 = (bf16[256,2048]{1,0:T(8,128)(2,1)S(1)}, bf16[256,2048]{1,0:T(8,128)(2,1)S(1)}, u32[]{:S(2)}, u32[]{:S(2)}) collective-permute-start(bf16[256,2048]{1,0:T(8,128)(2,1)S(1)} %get-tuple-element.68), channel_id=1, source_target_pairs={{0,8},{8,0},{16,24},{24,16},{1,9},{9,1},{17,25},{25,17},{2,10},{10... | collective-permute-start | bytes 3145736 | tf_op jit(solution)/shard_map/ppermute | solution.py:638
  505.8 26.1 %collective-permute-start.4 = (bf16[256,2048]{1,0:T(8,128)(2,1)S(1)}, bf16[256,2048]{1,0:T(8,128)(2,1)S(1)}, u32[]{:S(2)}, u32[]{:S(2)}) collective-permute-start(bf16[256,2048]{1,0:T(8,128)(2,1)S(1)} %get-tuple-element.69), channel_id=1, source_target_pairs={{0,16},{8,24},{16,0},{24,8},{1,17},{9,25},{17,1},{25,9},{2,18},{10... | collective-permute-start | bytes 3145736 | tf_op jit(solution)/shard_map/ppermute | solution.py:638
  511.6 65.3 %collective-permute-start.15 = (bf16[512,2048]{1,0:T(8,128)(2,1)}, bf16[512,2048]{1,0:T(8,128)(2,1)}, u32[]{:S(2)}, u32[]{:S(2)}) collective-permute-start(bf16[512,2048]{1,0:T(8,128)(2,1)} %pad_maximum_fusion.3), channel_id=1, source_target_pairs={{0,16},{8,24},{16,0},{24,8},{1,17},{9,25},{17,1},{25,9},{2,18},{10... | collective-permute-start | bytes 6291464 | tf_op jit(solution)/shard_map/ppermute | solution.py:638
  514.6 62.3 %collective-permute-start.13 = (bf16[512,2048]{1,0:T(8,128)(2,1)}, bf16[512,2048]{1,0:T(8,128)(2,1)}, u32[]{:S(2)}, u32[]{:S(2)}) collective-permute-start(bf16[512,2048]{1,0:T(8,128)(2,1)} %pad_maximum_fusion.2), channel_id=1, source_target_pairs={{0,8},{8,0},{16,24},{24,16},{1,9},{9,1},{17,25},{25,17},{2,10},{10... | collective-permute-start | bytes 6291464 | tf_op jit(solution)/shard_map/ppermute | solution.py:638
  536.5 84.0 %collective-permute-start.7 = (bf16[512,2048]{1,0:T(8,128)(2,1)}, bf16[512,2048]{1,0:T(8,128)(2,1)}, u32[]{:S(2)}, u32[]{:S(2)}) collective-permute-start(bf16[512,2048]{1,0:T(8,128)(2,1)} %pad_maximum_fusion.1), channel_id=1, source_target_pairs={{0,16},{8,24},{16,0},{24,8},{1,17},{9,25},{17,1},{25,9},{2,18},{10... | collective-permute-start | bytes 6291464 | tf_op jit(solution)/shard_map/ppermute | solution.py:638
  538.7 81.8 %collective-permute-start.5 = (bf16[512,2048]{1,0:T(8,128)(2,1)}, bf16[512,2048]{1,0:T(8,128)(2,1)}, u32[]{:S(2)}, u32[]{:S(2)}) collective-permute-start(bf16[512,2048]{1,0:T(8,128)(2,1)} %pad_maximum_fusion), channel_id=1, source_target_pairs={{0,8},{8,0},{16,24},{24,16},{1,9},{9,1},{17,25},{25,17},{2,10},{10... | collective-permute-start | bytes 6291464 | tf_op jit(solution)/shard_map/ppermute | solution.py:638
  668.2 348.5 %reduce-scatter.12.cloned.1.call-start = ((), (), s32[]{:S(2)}) async-start(), calls=%async_computation.12 | async-start | bytes 294912 | tf_op jit(solution)/shard_map/reduce_scatter | solution.py:672
  671.1 24.8 %collective-permute-start.34 = (bf16[256,2048]{1,0:T(8,128)(2,1)S(1)}, bf16[256,2048]{1,0:T(8,128)(2,1)S(1)}, u32[]{:S(2)}, u32[]{:S(2)}) collective-permute-start(bf16[256,2048]{1,0:T(8,128)(2,1)S(1)} %bitcast.201), channel_id=1, source_target_pairs={{0,8},{8,0},{16,24},{24,16},{1,9},{9,1},{17,25},{25,17},{2,10},{10... | collective-permute-start | bytes 3145736 | tf_op jit(solution)/shard_map/ppermute | solution.py:638
  672.6 27.0 %collective-permute-start.32 = (bf16[256,2048]{1,0:T(8,128)(2,1)S(1)}, bf16[256,2048]{1,0:T(8,128)(2,1)S(1)}, u32[]{:S(2)}, u32[]{:S(2)}) collective-permute-start(bf16[256,2048]{1,0:T(8,128)(2,1)S(1)} %bitcast.200), channel_id=1, source_target_pairs={{0,16},{8,24},{16,0},{24,8},{1,17},{9,25},{17,1},{25,9},{2,18},{10... | collective-permute-start | bytes 3145736 | tf_op jit(solution)/shard_map/ppermute | solution.py:638
  697.9 152.5 %collective-permute-start.35 = (bf16[512,2048]{1,0:T(8,128)(2,1)}, bf16[512,2048]{1,0:T(8,128)(2,1)}, u32[]{:S(2)}, u32[]{:S(2)}) collective-permute-start(bf16[512,2048]{1,0:T(8,128)(2,1)} %pad_maximum_fusion.7), channel_id=1, source_target_pairs={{0,16},{8,24},{16,0},{24,8},{1,17},{9,25},{17,1},{25,9},{2,18},{10... | collective-permute-start | bytes 6291464 | tf_op jit(solution)/shard_map/ppermute | solution.py:638
  701.5 148.9 %collective-permute-start.33 = (bf16[512,2048]{1,0:T(8,128)(2,1)}, bf16[512,2048]{1,0:T(8,128)(2,1)}, u32[]{:S(2)}, u32[]{:S(2)}) collective-permute-start(bf16[512,2048]{1,0:T(8,128)(2,1)} %pad_maximum_fusion.6), channel_id=1, source_target_pairs={{0,8},{8,0},{16,24},{24,16},{1,9},{9,1},{17,25},{25,17},{2,10},{10... | collective-permute-start | bytes 6291464 | tf_op jit(solution)/shard_map/ppermute | solution.py:638
  832.2 5.0 collective-permute-start.26
  833.8 6.4 collective-permute-start.24
  837.3 8.6 collective-permute-start.27
  840.2 9.3 collective-permute-start.25
  844.8 22.7 %collective-permute-start.18 = (bf16[256,2048]{1,0:T(8,128)(2,1)}, bf16[256,2048]{1,0:T(8,128)(2,1)}, u32[]{:S(2)}, u32[]{:S(2)}) collective-permute-start(bf16[256,2048]{1,0:T(8,128)(2,1)} %bitcast.15), channel_id=1, source_target_pairs={{0,8},{8,0},{16,24},{24,16},{1,9},{9,1},{17,25},{25,17},{2,10},{10... | collective-permute-start | bytes 3145736 | tf_op jit(solution)/shard_map/ppermute | solution.py:638
  845.9 24.8 %collective-permute-start.16 = (bf16[256,2048]{1,0:T(8,128)(2,1)}, bf16[256,2048]{1,0:T(8,128)(2,1)}, u32[]{:S(2)}, u32[]{:S(2)}) collective-permute-start(bf16[256,2048]{1,0:T(8,128)(2,1)} %bitcast.13), channel_id=1, source_target_pairs={{0,16},{8,24},{16,0},{24,8},{1,17},{9,25},{17,1},{25,9},{2,18},{10... | collective-permute-start | bytes 3145736 | tf_op jit(solution)/shard_map/ppermute | solution.py:638
  850.4 177.5 %reduce-scatter.14.cloned.1.call-start = ((), (), s32[]{:S(2)}) async-start(), calls=%async_computation.13 | async-start | bytes 2359296 | tf_op jit(solution)/shard_map/reduce_scatter | solution.py:672
  856.4 173.6 %reduce-scatter.10.cloned.1.call-start = ((), (), s32[]{:S(2)}) async-start(), calls=%async_computation.11 | async-start | bytes 2359296 | tf_op jit(solution)/shard_map/reduce_scatter | solution.py:672
  870.1 43.1 %collective-permute-start.19 = (bf16[512,2048]{1,0:T(8,128)(2,1)S(1)}, bf16[512,2048]{1,0:T(8,128)(2,1)S(1)}, u32[]{:S(2)}, u32[]{:S(2)}) collective-permute-start(bf16[512,2048]{1,0:T(8,128)(2,1)S(1)} %pad_maximum_fusion.5), channel_id=1, source_target_pairs={{0,16},{8,24},{16,0},{24,8},{1,17},{9,25},{17,1},{25,9},{2,18},{10... | collective-permute-start | bytes 6291464 | tf_op jit(solution)/shard_map/ppermute | solution.py:638
  872.6 42.7 %collective-permute-start.17 = (bf16[512,2048]{1,0:T(8,128)(2,1)S(1)}, bf16[512,2048]{1,0:T(8,128)(2,1)S(1)}, u32[]{:S(2)}, u32[]{:S(2)}) collective-permute-start(bf16[512,2048]{1,0:T(8,128)(2,1)S(1)} %pad_maximum_fusion.4), channel_id=1, source_target_pairs={{0,8},{8,0},{16,24},{24,16},{1,9},{9,1},{17,25},{25,17},{2,10},{10... | collective-permute-start | bytes 6291464 | tf_op jit(solution)/shard_map/ppermute | solution.py:638
  917.8 137.9 %reduce-scatter.20.cloned.1.call-start = ((), (), s32[]{:S(2)}) async-start(), calls=%async_computation.16 | async-start | bytes 6488064 | tf_op jit(solution)/shard_map/reduce_scatter | solution.py:672
  918.5 203.1 %reduce-scatter.16.cloned.1.call-start = ((), (), s32[]{:S(2)}) async-start(), calls=%async_computation.14 | async-start | bytes 6488064 | tf_op jit(solution)/shard_map/reduce_scatter | solution.py:672
  919.3 268.5 %reduce-scatter.18.cloned.1.call-start = ((), (), s32[]{:S(2)}) async-start(), calls=%async_computation.15 | async-start | bytes 6488064 | tf_op jit(solution)/shard_map/reduce_scatter | solution.py:672
  1016.7 4.5 collective-permute-start.29
  1019.1 4.1 collective-permute-start.28
  1021.2 3.7 collective-permute-start.31
  1023.2 3.9 collective-permute-start.30
  1027.9 8.9 collective-permute-start.37
  1028.1 9.5 collective-permute-start.36
  1029.9 10.6 collective-permute-start.21
  1030.1 12.3 collective-permute-start.20
  1036.8 6.7 collective-permute-start.39
  1037.7 5.8 collective-permute-start.38
  1040.5 5.0 collective-permute-start.23
  1042.4 5.0 collective-permute-start.22
  1055.7 135.5 %collective-permute-start.49 = (bf16[176,2048]{1,0:T(8,128)(2,1)}, bf16[176,2048]{1,0:T(8,128)(2,1)}, u32[]{:S(2)}, u32[]{:S(2)}) collective-permute-start(bf16[176,2048]{1,0:T(8,128)(2,1)} %reduce-scatter.20.cloned.1.call-done), channel_id=1, source_target_pairs={{0,16},{8,24},{16,0},{24,8},{1,17},{9,25},{17,1},{25,9},{2,18},{10... | collective-permute-start | bytes 2162696 | tf_op jit(solution)/shard_map/ppermute | solution.py:638
  1057.1 136.7 %collective-permute-start.48 = (bf16[176,2048]{1,0:T(8,128)(2,1)}, bf16[176,2048]{1,0:T(8,128)(2,1)}, u32[]{:S(2)}, u32[]{:S(2)}) collective-permute-start(bf16[176,2048]{1,0:T(8,128)(2,1)} %reduce-scatter.20.cloned.1.call-done), channel_id=1, source_target_pairs={{0,8},{8,0},{16,24},{24,16},{1,9},{9,1},{17,25},{25,17},{2,10},{10... | collective-permute-start | bytes 2162696 | tf_op jit(solution)/shard_map/ppermute | solution.py:638
  1121.7 84.1 %collective-permute-start.41 = (bf16[176,2048]{1,0:T(8,128)(2,1)}, bf16[176,2048]{1,0:T(8,128)(2,1)}, u32[]{:S(2)}, u32[]{:S(2)}) collective-permute-start(bf16[176,2048]{1,0:T(8,128)(2,1)} %reduce-scatter.16.cloned.1.call-done), channel_id=1, source_target_pairs={{0,16},{8,24},{16,0},{24,8},{1,17},{9,25},{17,1},{25,9},{2,18},{10... | collective-permute-start | bytes 2162696 | tf_op jit(solution)/shard_map/ppermute | solution.py:638
  1123.1 85.2 %collective-permute-start.40 = (bf16[176,2048]{1,0:T(8,128)(2,1)}, bf16[176,2048]{1,0:T(8,128)(2,1)}, u32[]{:S(2)}, u32[]{:S(2)}) collective-permute-start(bf16[176,2048]{1,0:T(8,128)(2,1)} %reduce-scatter.16.cloned.1.call-done), channel_id=1, source_target_pairs={{0,8},{8,0},{16,24},{24,16},{1,9},{9,1},{17,25},{25,17},{2,10},{10... | collective-permute-start | bytes 2162696 | tf_op jit(solution)/shard_map/ppermute | solution.py:638
  1187.7 16.5 %collective-permute-start.45 = (bf16[176,2048]{1,0:T(8,128)(2,1)}, bf16[176,2048]{1,0:T(8,128)(2,1)S(1)}, u32[]{:S(2)}, u32[]{:S(2)}) collective-permute-start(bf16[176,2048]{1,0:T(8,128)(2,1)} %reduce-scatter.18.cloned.1.call-done), channel_id=1, source_target_pairs={{0,16},{8,24},{16,0},{24,8},{1,17},{9,25},{17,1},{25,9},{2,18},{10... | collective-permute-start | bytes 2162696 | tf_op jit(solution)/shard_map/ppermute | solution.py:638
  1191.2 19.9 %collective-permute-start.44 = (bf16[176,2048]{1,0:T(8,128)(2,1)S(1)}, bf16[176,2048]{1,0:T(8,128)(2,1)S(1)}, u32[]{:S(2)}, u32[]{:S(2)}) collective-permute-start(bf16[176,2048]{1,0:T(8,128)(2,1)S(1)} %copy-done.28), channel_id=1, source_target_pairs={{0,8},{8,0},{16,24},{24,16},{1,9},{9,1},{17,25},{25,17},{2,10},{10... | collective-permute-start | bytes 2162696 | tf_op jit(solution)/shard_map/ppermute | solution.py:638
  1193.8 47.1 %collective-permute-start.51 = (bf16[88,2048]{1,0:T(8,128)(2,1)S(1)}, bf16[88,2048]{1,0:T(8,128)(2,1)S(1)}, u32[]{:S(2)}, u32[]{:S(2)}) collective-permute-start(bf16[88,2048]{1,0:T(8,128)(2,1)S(1)} %slice.357), channel_id=1, source_target_pairs={{0,8},{8,0},{16,24},{24,16},{1,9},{9,1},{17,25},{25,17},{2,10},{10... | collective-permute-start | bytes 1081352 | tf_op jit(solution)/shard_map/ppermute | solution.py:638
  1204.2 36.7 %collective-permute-start.50 = (bf16[88,2048]{1,0:T(8,128)(2,1)S(1)}, bf16[88,2048]{1,0:T(8,128)(2,1)S(1)}, u32[]{:S(2)}, u32[]{:S(2)}) collective-permute-start(bf16[88,2048]{1,0:T(8,128)(2,1)S(1)} %slice.356), channel_id=1, source_target_pairs={{0,16},{8,24},{16,0},{24,8},{1,17},{9,25},{17,1},{25,9},{2,18},{10... | collective-permute-start | bytes 1081352 | tf_op jit(solution)/shard_map/ppermute | solution.py:638
  1205.7 28.3 %collective-permute-start.47 = (bf16[88,2048]{1,0:T(8,128)(2,1)S(1)}, bf16[88,2048]{1,0:T(8,128)(2,1)S(1)}, u32[]{:S(2)}, u32[]{:S(2)}) collective-permute-start(bf16[88,2048]{1,0:T(8,128)(2,1)S(1)} %slice.355), channel_id=1, source_target_pairs={{0,8},{8,0},{16,24},{24,16},{1,9},{9,1},{17,25},{25,17},{2,10},{10... | collective-permute-start | bytes 1081352 | tf_op jit(solution)/shard_map/ppermute | solution.py:638
  1208.3 21.6 %collective-permute-start.43 = (bf16[88,2048]{1,0:T(8,128)(2,1)S(1)}, bf16[88,2048]{1,0:T(8,128)(2,1)S(1)}, u32[]{:S(2)}, u32[]{:S(2)}) collective-permute-start(bf16[88,2048]{1,0:T(8,128)(2,1)S(1)} %slice.353), channel_id=1, source_target_pairs={{0,8},{8,0},{16,24},{24,16},{1,9},{9,1},{17,25},{25,17},{2,10},{10... | collective-permute-start | bytes 1081352 | tf_op jit(solution)/shard_map/ppermute | solution.py:638
  1211.1 19.3 %collective-permute-start.42 = (bf16[88,2048]{1,0:T(8,128)(2,1)S(1)}, bf16[88,2048]{1,0:T(8,128)(2,1)S(1)}, u32[]{:S(2)}, u32[]{:S(2)}) collective-permute-start(bf16[88,2048]{1,0:T(8,128)(2,1)S(1)} %slice.352), channel_id=1, source_target_pairs={{0,16},{8,24},{16,0},{24,8},{1,17},{9,25},{17,1},{25,9},{2,18},{10... | collective-permute-start | bytes 1081352 | tf_op jit(solution)/shard_map/ppermute | solution.py:638
  1229.9 7.4 collective-permute-start.46
  (49 other events, 935.7 us)
Sparse Core Ops, SparseCore 0:
  10.3 85.5 all-gather.5
  98.1 81.0 all-gather.3
  232.2 138.1 all-gather.7
  668.3 158.2 reduce-scatter.7
  850.5 63.1 reduce-scatter.11
  915.9 33.8 reduce-scatter.13
  952.8 37.0 reduce-scatter.9
  992.3 63.3 reduce-scatter.19
  1058.7 62.9 reduce-scatter.15
  1124.5 63.1 reduce-scatter.17

commit v4 on v3

--- a/solution.py
+++ b/solution.py
@@ -18,6 +18,7 @@
 TILE = 128
 CHUNK = 512
 HEAD_GROUP = 4
+HEAD_BLOCK = 4
 
 
 def matmul(left, right):
@@ -467,18 +468,6 @@
     width = tokens_ref.shape[1]
     partner = (replica, flip(fsdp, 1))
 
-    barrier = pltpu.get_barrier_semaphore()
-    for target in (partner, (flip(replica, 1), fsdp), (flip(replica, 2), fsdp)):
-        pl.semaphore_signal(barrier, inc=1, device_id=target, device_id_type=MESH)
-
-    @pl.when(at > 0)
-    def _():
-        pl.semaphore_signal(barrier, inc=1, device_id=(replica, fsdp - 2), device_id_type=MESH)
-
-    @pl.when(at < count - 1)
-    def _():
-        pl.semaphore_signal(barrier, inc=1, device_id=(replica, fsdp + 2), device_id_type=MESH)
-
     own = [
         pltpu.make_async_copy(kvg_ref, kvg_all.at[fsdp], local_sems.at[0]),
         pltpu.make_async_copy(wq_ref, wq_all.at[fsdp], local_sems.at[1]),
@@ -486,15 +475,7 @@
     ]
     for copy in own:
         copy.start()
-    inside = (at > 0) & (at < count - 1)
-
-    @pl.when(inside)
-    def _():
-        pl.semaphore_wait(barrier, 5)
-
-    @pl.when(jnp.logical_not(inside))
-    def _():
-        pl.semaphore_wait(barrier, 4)
+    greet(replica, fsdp, at, count)
 
     def core_copy(buffer, sems, shard, lands=False):
         ref = buffer.at[2 * shard + (1 - core if lands else core)]
@@ -633,6 +614,501 @@
     )(tokens, wq, wo, kvg, cos_table, sin_table)
 
 
+def greet(replica, fsdp, at, count):
+    barrier = pltpu.get_barrier_semaphore()
+    for target in (
+        (replica, flip(fsdp, 1)),
+        (flip(replica, 1), fsdp),
+        (flip(replica, 2), fsdp),
+    ):
+        pl.semaphore_signal(barrier, inc=1, device_id=target, device_id_type=MESH)
+
+    @pl.when(at > 0)
+    def _():
+        pl.semaphore_signal(barrier, inc=1, device_id=(replica, fsdp - 2), device_id_type=MESH)
+
+    @pl.when(at < count - 1)
+    def _():
+        pl.semaphore_signal(barrier, inc=1, device_id=(replica, fsdp + 2), device_id_type=MESH)
+
+    inside = (at > 0) & (at < count - 1)
+
+    @pl.when(inside)
+    def _():
+        pl.semaphore_wait(barrier, 5)
+
+    @pl.when(jnp.logical_not(inside))
+    def _():
+        pl.semaphore_wait(barrier, 4)
+
+
+def add_into(ref, index, *others):
+    total = ref[index].astype(jnp.float32)
+    for other in others:
+        total = total + other.astype(jnp.float32)
+    ref[index] = total.astype(ref.dtype)
+
+
+class Collect:
+    def __init__(self, place, grad, core_in, line_in, core_sems, line_sems, copies=None):
+        self.replica, self.fsdp, self.at, self.core, self.count = place
+        self.grad, self.core_in, self.line_in = grad, core_in, line_in
+        self.core_sems, self.line_sems = core_sems, line_sems
+        self.beside, self.across = flip(self.replica, 1), flip(self.replica, 2)
+        self.opposite = flip(self.beside, 2)
+        if copies is None:
+            self.rows = pl.ds(0, grad.shape[1])
+        else:
+            self.diag_in, self.quarter_in, self.full = copies[:3]
+            self.diag_sems, self.quarter_sems, self.full_sems = copies[3:]
+            self.size = grad.shape[1] // 4
+            self.rows = self.quarter(self.replica)
+
+    def quarter(self, copy, half=None):
+        size = self.size if half is None else self.size // 2
+        start = copy * self.size + (0 if half is None else half * size)
+        return pl.ds(pl.multiple_of(start, size), size)
+
+    def remote(self, src, dst, sems, index, target):
+        return pltpu.make_async_remote_copy(
+            src_ref=src,
+            dst_ref=dst,
+            send_sem=sems.at[(0,) + index],
+            recv_sem=sems.at[(1,) + index],
+            device_id=target,
+            device_id_type=MESH,
+        )
+
+    def core_copy(self, shard):
+        return self.remote(
+            self.grad.at[2 * shard + 1 - self.core],
+            self.core_in.at[shard],
+            self.core_sems,
+            (shard,),
+            (self.replica, flip(self.fsdp, 1)),
+        )
+
+    def core_add(self, shard):
+        self.core_copy(shard).wait_recv()
+        add_into(self.grad, 2 * shard + self.core, self.core_in[shard])
+
+    def diag_copy(self, shard, half):
+        return self.remote(
+            self.grad.at[2 * shard + self.core, self.quarter(self.opposite, half)],
+            self.diag_in.at[half, shard],
+            self.diag_sems,
+            (half, shard),
+            (self.beside if half == 0 else self.across, self.fsdp),
+        )
+
+    def diag_start(self, shard):
+        self.diag_copy(shard, 0).start()
+        self.diag_copy(shard, 1).start()
+
+    def quarter_copy(self, shard, way):
+        return self.remote(
+            self.grad.at[2 * shard + self.core, self.quarter(self.across if way else self.beside)],
+            self.quarter_in.at[way, shard],
+            self.quarter_sems,
+            (way, shard),
+            (self.across if way else self.beside, self.fsdp),
+        )
+
+    def quarter_start(self, shard):
+        at = 2 * shard + self.core
+        for half, copy in ((0, self.across), (1, self.beside)):
+            self.diag_copy(shard, half).wait_recv()
+            add_into(self.grad, (at, self.quarter(copy, half)), self.diag_in[half, shard])
+            self.quarter_copy(shard, 1 - half).start()
+
+    def quarter_add(self, shard):
+        self.quarter_copy(shard, 0).wait_recv()
+        self.quarter_copy(shard, 1).wait_recv()
+        add_into(
+            self.grad,
+            (2 * shard + self.core, self.rows),
+            self.quarter_in[0, shard],
+            self.quarter_in[1, shard],
+        )
+
+    def line_copy(self, shard, way):
+        return self.remote(
+            self.grad.at[2 * shard + self.core, self.rows],
+            self.line_in.at[way, shard],
+            self.line_sems,
+            (way, shard),
+            (self.replica, self.fsdp + (2 if way == 0 else -2)),
+        )
+
+    def line_receive(self, shard, way):
+        self.line_copy(shard, way).wait_recv()
+        add_into(self.grad, (2 * shard + self.core, self.rows), self.line_in[way, shard])
+
+    def line_hop(self, hop):
+        for way, shard, there, fed in (
+            (0, self.at + hop, self.at + hop < self.count, self.at > 0),
+            (1, self.at - hop, self.at - hop >= 0, self.at < self.count - 1),
+        ):
+
+            @pl.when(there & fed)
+            def _(shard=shard, way=way):
+                self.line_receive(shard, way)
+
+            @pl.when(there)
+            def _(shard=shard, way=way):
+                self.line_copy(shard, way).start()
+
+    def line_end(self):
+        @pl.when(self.at > 0)
+        def _():
+            self.line_receive(self.at, 0)
+
+        @pl.when(self.at < self.count - 1)
+        def _():
+            self.line_receive(self.at, 1)
+
+    def full_copy(self, kind):
+        own = self.replica
+        rows, target = (
+            (self.quarter(own), self.beside),
+            (self.quarter(own), self.across),
+            (self.quarter(self.beside, 0), self.across),
+            (self.quarter(self.across, 1), self.beside),
+        )[kind]
+        return self.remote(
+            self.full.at[rows],
+            self.full.at[rows],
+            self.full_sems,
+            (kind,),
+            (target, self.fsdp),
+        )
+
+    def full_recv(self, kind):
+        rows = (
+            self.quarter(self.beside),
+            self.quarter(self.across),
+            self.quarter(self.opposite, 0),
+            self.quarter(self.opposite, 1),
+        )[kind]
+        ref = self.full.at[rows]
+        self.remote(ref, ref, self.full_sems, (kind,), (self.beside, self.fsdp)).wait_recv()
+
+    def gather_start(self):
+        self.full[self.rows] = self.grad[2 * self.at + self.core, self.rows]
+        self.full_copy(0).start()
+        self.full_copy(1).start()
+
+    def gather_relay(self):
+        self.full_recv(0)
+        self.full_copy(2).start()
+        self.full_recv(1)
+        self.full_copy(3).start()
+
+    def gather_end(self):
+        self.full_recv(2)
+        self.full_recv(3)
+
+    def drain(self):
+        for shard in range(self.count):
+            self.core_copy(shard).wait_send()
+            if hasattr(self, "size"):
+                for way in (0, 1):
+                    self.diag_copy(shard, way).wait_send()
+                    self.quarter_copy(shard, way).wait_send()
+        for hop in range(1, self.count):
+
+            @pl.when(self.at + hop < self.count)
+            def _(hop=hop):
+                self.line_copy(self.at + hop, 0).wait_send()
+
+            @pl.when(self.at - hop >= 0)
+            def _(hop=hop):
+                self.line_copy(self.at - hop, 1).wait_send()
+
+        if hasattr(self, "size"):
+            for kind in range(4):
+                self.full_copy(kind).wait_send()
+
+
+def collect_scratch(fsdp_size, rows, width, copies=True):
+    count = fsdp_size // 2
+    low, dma = jnp.bfloat16, pltpu.SemaphoreType.DMA
+    size = rows // 4 if copies else rows
+    shapes = [
+        pltpu.VMEM((fsdp_size, rows, width), low),
+        pltpu.VMEM((count, rows, width), low),
+        pltpu.VMEM((2, count, size, width), low),
+        dma((2, count)),
+        dma((2, 2, count)),
+    ]
+    if copies:
+        shapes += [
+            pltpu.VMEM((2, count, size // 2, width), low),
+            pltpu.VMEM((2, count, size, width), low),
+            pltpu.VMEM((rows, width), low),
+            dma((2, 2, count)),
+            dma((2, 2, count)),
+            dma((2, 4)),
+        ]
+    return shapes
+
+
+def make_collect(place, refs, copies=True):
+    return Collect(place, *refs[:5], copies=refs[5:11] if copies else None)
+
+
+def position(fsdp_size):
+    replica, fsdp = lax.axis_index("replica"), lax.axis_index("fsdp")
+    return replica, fsdp, fsdp // 2, fsdp % 2, fsdp_size // 2
+
+
+def outer(collect, left_ref, right_ref, own_core):
+    rows = collect.grad.shape[1]
+    core = collect.core if own_core else 1 - collect.core
+
+    @pl.loop(0, collect.count)
+    def _(shard):
+        start = pl.multiple_of((2 * shard + core) * rows, rows)
+        part = contract(left_ref[:, pl.ds(start, rows)], right_ref[...], 0, 0)
+        collect.grad[2 * shard + core] = part.astype(jnp.bfloat16)
+        if not own_core:
+            collect.core_copy(shard).start()
+
+
+def each(count, step):
+    for shard in range(count):
+        step(shard)
+
+
+def outer_kernel(fsdp_size, left_ref, right_ref, out_ref, *refs):
+    place = position(fsdp_size)
+    greet(*place[:3], place[4])
+    sums = make_collect(place, refs)
+    count = place[4]
+    outer(sums, left_ref, right_ref, False)
+    outer(sums, left_ref, right_ref, True)
+    for shard in range(count):
+        sums.core_add(shard)
+        sums.diag_start(shard)
+    each(count, sums.quarter_start)
+    each(count, sums.quarter_add)
+    for hop in range(count - 1, 0, -1):
+        sums.line_hop(hop)
+    sums.line_end()
+    sums.gather_start()
+    sums.gather_relay()
+    sums.gather_end()
+    out_ref[...] = sums.full[...].astype(jnp.float32)
+    sums.drain()
+
+
+def outer_sum(left, right, collective_id):
+    fsdp_size = lax.axis_size("fsdp")
+    rows, width = left.shape[1] // fsdp_size, right.shape[1]
+    vmem = pl.BlockSpec(memory_space=pltpu.VMEM)
+    return pl.pallas_call(
+        functools.partial(outer_kernel, fsdp_size),
+        out_shape=jax.ShapeDtypeStruct((rows, width), jnp.float32),
+        in_specs=[vmem, vmem],
+        out_specs=vmem,
+        scratch_shapes=collect_scratch(fsdp_size, rows, width),
+        compiler_params=pltpu.CompilerParams(
+            collective_id=collective_id, has_side_effects=True, vmem_limit_bytes=56 << 20
+        ),
+        cost_estimate=pl.CostEstimate(
+            flops=40 * left.shape[0] * left.shape[1] * width, transcendentals=0, bytes_accessed=8 << 20
+        ),
+        name="outer_sum",
+    )(left, right)
+
+
+def finish_kernel(
+    fsdp_size,
+    normed_ref,
+    d_q_ref,
+    tokens_ref,
+    d_hidden_ref,
+    gain_ref,
+    term_ref,
+    cos_ref,
+    sin_ref,
+    d_kv_ref,
+    wq_ref,
+    kvg_ref,
+    ffn_ref,
+    input_grad_ref,
+    q_grad_ref,
+    kv_grad_ref,
+    ffn_all,
+    wq_buf,
+    kvg_vmem,
+    d_kv_raw,
+    term_sum,
+    local_sems,
+    ffn_sems,
+    *refs,
+):
+    place = position(fsdp_size)
+    replica, fsdp, at, core, count = place
+    greet(replica, fsdp, at, count)
+    q_sums = make_collect(place, refs[:11])
+    kv_sums = make_collect(place, refs[11:22])
+    d_kv = make_collect(place, refs[22:27], False)
+    beside, across = flip(replica, 1), flip(replica, 2)
+    width = tokens_ref.shape[1]
+    half = width // 2
+
+    def ffn_copy(kind, lands=False):
+        piece = (replica, replica, beside, across)[kind]
+        if lands:
+            piece = (beside, across, flip(beside, 2), flip(beside, 2))[kind]
+        columns = (slice(None), slice(None), pl.ds(0, half), pl.ds(half, half))[kind]
+        src = ffn_all.at[piece, :, :, columns]
+        return pltpu.make_async_remote_copy(
+            src_ref=src,
+            dst_ref=src,
+            send_sem=ffn_sems.at[0, kind],
+            recv_sem=ffn_sems.at[1, kind],
+            device_id=((beside, across, across, beside)[kind], fsdp),
+            device_id_type=MESH,
+        )
+
+    own_ffn = pltpu.make_async_copy(ffn_ref, ffn_all.at[replica], local_sems.at[0])
+    own_ffn.start()
+    load = pltpu.make_async_copy(d_kv_ref, d_kv.grad, local_sems.at[1])
+    load.start()
+    load_kvg = pltpu.make_async_copy(kvg_ref, kvg_vmem, local_sems.at[2])
+    load_kvg.start()
+    load.wait()
+    each(count, lambda shard: d_kv.core_copy(shard).start())
+    outer(q_sums, normed_ref, d_q_ref, False)
+    each(count, d_kv.core_add)
+    d_kv.line_hop(count - 1)
+    outer(q_sums, normed_ref, d_q_ref, True)
+    for hop in range(count - 2, 0, -1):
+        d_kv.line_hop(hop)
+    for shard in range(count):
+        q_sums.core_add(shard)
+        q_sums.diag_start(shard)
+    d_kv.line_end()
+    each(count, q_sums.quarter_start)
+    own_ffn.wait()
+    ffn_copy(0).start()
+    ffn_copy(1).start()
+
+    summed = d_kv.grad[fsdp].astype(jnp.float32)
+    d_key = summed[:, :128]
+    d_key = d_key * cos_ref[...] - pltpu.roll(d_key, 64, 1) * sin_ref[...]
+    d_kv_raw[:, :128] = d_key.astype(jnp.bfloat16)
+    d_kv_raw[:, 128:] = summed[:, 128:].astype(jnp.bfloat16)
+    load_kvg.wait()
+    rows = kvg_vmem.shape[1]
+
+    def fetch(shard):
+        return pltpu.make_async_copy(wq_ref.at[shard], wq_buf.at[shard % 2], local_sems.at[shard % 2])
+
+    fetch(0).start()
+    for shard in range(fsdp_size):
+        fetch(shard).wait()
+        if shard + 1 < fsdp_size:
+            fetch(shard + 1).start()
+        input_grad_ref[:, shard * rows : (shard + 1) * rows] = contract(
+            d_q_ref[...], wq_buf[shard % 2], 1, 1
+        ) + contract(d_kv_raw[...], kvg_vmem[shard, :, :256], 1, 1)
+    each(count, q_sums.quarter_add)
+    for hop in range(count - 1, 0, -1):
+        q_sums.line_hop(hop)
+
+    term_sum[...] = jnp.zeros_like(term_sum)
+
+    @pl.loop(0, tokens_ref.shape[0] // 128)
+    def _(block):
+        part = pl.ds(pl.multiple_of(block * 128, 128), 128)
+        d_normed = input_grad_ref[part]
+        inputs = tokens_ref[part].astype(jnp.float32)
+        inverse = lax.rsqrt(jnp.mean(inputs * inputs, axis=1, keepdims=True) + EPSILON)
+        scaled = d_normed * gain_ref[:1]
+        inner = jnp.mean(scaled * inputs, axis=1, keepdims=True)
+        term_sum[:1] += jnp.sum(d_normed * inputs * inverse, axis=0, keepdims=True)
+        input_grad_ref[part] = (
+            d_hidden_ref[part] + inverse * scaled - inputs * (inverse**3 * inner)
+        )
+
+    term = term_sum[:1]
+    line = lax.broadcasted_iota(jnp.int32, (128, width), 0)
+    terms = jnp.where(line == 0, term, jnp.where(line == 1, term_ref[:1], 0.0)).T
+    terms = terms.astype(jnp.bfloat16)
+    for shard in range(fsdp_size):
+        left = normed_ref[:, shard * rows : (shard + 1) * rows]
+        kv_sums.grad[shard, :, :256] = contract(left, d_kv_raw[...], 0, 0).astype(jnp.bfloat16)
+        kv_sums.grad[shard, :, 256:] = terms[shard * rows : (shard + 1) * rows]
+    each(count, lambda shard: kv_sums.core_copy(shard).start())
+    q_sums.line_end()
+    q_sums.gather_start()
+    for shard in range(count):
+        kv_sums.core_add(shard)
+        kv_sums.diag_start(shard)
+    each(count, kv_sums.quarter_start)
+    q_sums.gather_relay()
+    each(count, kv_sums.quarter_add)
+    for hop in range(count - 1, 0, -1):
+        kv_sums.line_hop(hop)
+    for kind in (0, 1):
+        ffn_copy(kind, True).wait_recv()
+        ffn_copy(2 + kind).start()
+    kv_sums.line_end()
+    kv_sums.gather_start()
+    q_sums.gather_end()
+    q_grad_ref[...] = q_sums.full[...].astype(jnp.float32)
+    kv_sums.gather_relay()
+    kv_sums.gather_end()
+    kv_grad_ref[...] = kv_sums.full[...].astype(jnp.float32)
+    for kind in (2, 3):
+        ffn_copy(kind, True).wait_recv()
+    for kind in range(4):
+        ffn_copy(kind).wait_send()
+    for sums in (q_sums, kv_sums, d_kv):
+        sums.drain()
+
+
+def finish(
+    normed, d_q, tokens, d_hidden, gains, term, cos_table, sin_table, d_kv, wq_all, kvg_all, ffn
+):
+    fsdp_size, rows, width = wq_all.shape
+    tok_rows = tokens.shape[0]
+    low, dma = jnp.bfloat16, pltpu.SemaphoreType.DMA
+    vmem, hbm = pl.BlockSpec(memory_space=pltpu.VMEM), pl.BlockSpec(memory_space=pl.ANY)
+    return pl.pallas_call(
+        functools.partial(finish_kernel, fsdp_size),
+        out_shape=(
+            jax.ShapeDtypeStruct((tok_rows, width), jnp.float32),
+            jax.ShapeDtypeStruct((rows, width), jnp.float32),
+            jax.ShapeDtypeStruct((rows, 384), jnp.float32),
+            jax.ShapeDtypeStruct((4,) + ffn.shape, low),
+        ),
+        in_specs=[vmem] * 8 + [hbm] * 4,
+        out_specs=(vmem, vmem, vmem, hbm),
+        scratch_shapes=[
+            pltpu.VMEM((2, rows, width), low),
+            pltpu.VMEM((fsdp_size, rows, 384), low),
+            pltpu.VMEM((tok_rows, 256), low),
+            pltpu.VMEM((8, width), jnp.float32),
+            dma((3,)),
+            dma((2, 4)),
+        ]
+        + collect_scratch(fsdp_size, rows, width)
+        + collect_scratch(fsdp_size, rows, 384)
+        + collect_scratch(fsdp_size, tok_rows, 256, False),
+        compiler_params=pltpu.CompilerParams(
+            collective_id=2, has_side_effects=True, vmem_limit_bytes=60 << 20
+        ),
+        cost_estimate=pl.CostEstimate(
+            flops=100 * tok_rows * width * width, transcendentals=0, bytes_accessed=40 << 20
+        ),
+        name="finish",
+    )(normed, d_q, tokens, d_hidden, gains, term, cos_table, sin_table, d_kv, wq_all, kvg_all, ffn)
+
+
 def swap(value, step):
     copies = lax.axis_size("replica")
     return lax.ppermute(value, "replica", [(r, r ^ step) for r in range(copies)])
@@ -672,29 +1148,13 @@
     return lax.psum_scatter(value, "fsdp", scatter_dimension=0, tiled=True)
 
 
-def place(pieces, copy_index):
-    out = jnp.zeros((len(pieces),) + pieces[0].shape, pieces[0].dtype)
-    for step, piece in enumerate(pieces):
-        out = lax.dynamic_update_index_in_dim(out, piece, copy_index ^ step, 0)
-    return out
+def after(value, *others):
+    return lax.optimization_barrier((value, others))[0]
 
 
 def quarter(shard, copy_index):
     rows = shard.shape[0] // lax.axis_size("replica")
     return lax.dynamic_slice_in_dim(shard, copy_index * rows, rows, 0)
-
-
-def sum_weight_grad(partial, copy_index):
-    rows, width = partial.shape
-    copies, fsdp_size = lax.axis_size("replica"), lax.axis_size("fsdp")
-    fine = rows // (copies * fsdp_size)
-    view = partial.reshape(fsdp_size, copies, fine, width)
-    parts = [
-        lax.dynamic_slice_in_dim(view, copy_index ^ step, 1, 1).reshape(fsdp_size * fine, width)
-        for step in range(copies)
-    ]
-    summed = scatter_shards(scatter_copies(parts).astype(jnp.bfloat16))
-    return place(gather_copies(summed), copy_index).reshape(copies * fine, width).astype(jnp.float32)
 
 
 def shards(
@@ -722,7 +1182,7 @@
 
     cos_table, sin_table = rope_tables(positions, head_dim)
     gain_columns = jnp.stack([attn_gain, ffn_gain], axis=1)
-    queries, normed, gains, w_query, w_out, w_kvg, kv_all = project(
+    queries, normed, gains, wq_all, w_out, kvg_all, kv_all = project(
         tokens,
         query_weight,
         output_weight,
@@ -732,13 +1192,10 @@
         cos_table,
         sin_table,
     )
-    w_query = w_query.reshape(model_width, model_width)
     w_out = w_out.reshape(model_width, model_width)
-    w_kv = w_kvg.reshape(model_width, 3 * head_dim)[:, : 2 * head_dim]
     kv_all = kv_all.reshape(fsdp_size * tok_rows, 2 * head_dim)
-    gain_attn, gain_ffn = gains[0], gains[1]
+    gain_ffn = gains[1]
     inputs = tokens.astype(jnp.float32)
-    inverse_attn = lax.rsqrt(jnp.mean(inputs * inputs, axis=-1, keepdims=True) + EPSILON)
     key_width = max(GROUP_TOK, tok_rows)
     window_start = fsdp_index * tok_rows // key_width * key_width
     one_group = fsdp_size * tok_rows == key_width
@@ -771,8 +1228,7 @@
     d_gate, d_up = swiglu_back(d_activation, gate_proj, up_proj)
     d_normed_parts = matmul(d_gate, w_gate) + matmul(d_up, w_up)
     d_normed_ffn = scatter_copies(jnp.split(d_normed_parts, copies))
-    out_parts = matmul(activation, w_down)
-    layer_out = (hidden + scatter_copies(jnp.split(out_parts, copies))).astype(low)
+    out_parts = matmul(activation, w_down).astype(low)
 
     gate_part = contract(d_gate, normed_all, 0, 0).astype(low)
     up_part = contract(d_up, normed_all, 0, 0).astype(low)
@@ -788,14 +1244,16 @@
     d_hidden = cotangent + resid_ffn
     d_branch = d_hidden.astype(low)
     d_mixed = contract(d_branch, w_out, 1, 1).astype(low)
-    d_mixed, gate_part, up_part, down_part = lax.optimization_barrier(
-        (d_mixed, gate_part, up_part, down_part)
-    )
-    gate_grad = ffn_grad(gate_part).T
-    up_grad = ffn_grad(up_part).T
-    down_grad = ffn_grad(down_part)
-    output_grad = sum_weight_grad(contract(mixed_rows, d_branch, 0, 0), copy_index)
-
+    d_mixed = after(d_mixed, gate_part, up_part, down_part)
+    gate_sum = scatter_shards(gate_part)
+    up_sum = scatter_shards(up_part)
+    down_sum = scatter_shards(down_part)
+    output_grad = outer_sum(mixed_rows, d_branch, 1)
+    own_out, *other_outs = jnp.split(after(out_parts, output_grad), copies)
+    layer_out = hidden + own_out.astype(jnp.float32)
+    for step, part in enumerate(other_outs):
+        layer_out = layer_out + swap(part, step + 1).astype(jnp.float32)
+    layer_out = layer_out.astype(low)
     d_query_raw, d_kv = attend_back(
         base,
         queries,
@@ -807,43 +1265,292 @@
         d_mixed,
         logs,
     )
-    query_grad = sum_weight_grad(contract(normed, d_query_raw, 0, 0), copy_index)
     if not one_group:
         d_kv = lax.dynamic_update_slice_in_dim(
             jnp.zeros((fsdp_size * tok_rows, 2 * head_dim), low), d_kv, window_start, 0
         )
-    d_kv_sum = scatter_shards(d_kv).astype(jnp.float32)
-    d_key = d_kv_sum[:, :head_dim]
-    d_key_raw = (d_key * cos_table - swap_halves(d_key) * sin_table).astype(low)
-    d_kv_raw = jnp.concatenate([d_key_raw, d_kv_sum[:, head_dim:].astype(low)], axis=1)
-    kv_grad = sum_weight_grad(contract(normed, d_kv_raw, 0, 0), copy_index)
-    d_normed = contract(d_query_raw, w_query, 1, 1) + contract(
-        d_kv_raw, w_kv, 1, 1
-    )
-    resid_attn, attn_gain_term = norm_backward(inputs, inverse_attn, gain_attn, d_normed)
-    input_grad = d_hidden + resid_attn
-    gain_terms = lax.psum(jnp.stack([attn_gain_term, ffn_gain_term]), ("replica", "fsdp"))
-    gain_grads = lax.dynamic_slice_in_dim(
-        gain_terms, fsdp_index * (model_width // fsdp_size), model_width // fsdp_size, 1
+    input_grad, query_grad, kv_grad, ffn_all = finish(
+        normed,
+        d_query_raw,
+        tokens,
+        d_hidden,
+        gains,
+        jnp.broadcast_to(ffn_gain_term[None], (8, model_width)),
+        cos_table,
+        sin_table,
+        d_kv.reshape(fsdp_size, tok_rows, 2 * head_dim),
+        wq_all,
+        kvg_all,
+        jnp.stack([gate_sum, up_sum, down_sum]),
+    )
+    gate_grad, up_grad, down_grad = (
+        ffn_all[:, i].reshape(-1, model_width).astype(jnp.float32) for i in range(3)
     )
     return (
         layer_out,
         input_grad,
         query_grad,
         kv_grad[:, :head_dim],
-        kv_grad[:, head_dim:],
+        kv_grad[:, head_dim : 2 * head_dim],
         output_grad,
-        gain_grads[0],
+        kv_grad[:, 2 * head_dim],
+        gate_grad.T,
+        up_grad.T,
+        down_grad,
+        kv_grad[:, 2 * head_dim + 1],
+    )
+
+
+def half_tables(pos_ids, head_dim):
+    half_width = head_dim // 2
+    frequency = ROPE_BASE ** (-jnp.arange(half_width, dtype=jnp.float32) * 2.0 / head_dim)
+    angles = pos_ids.astype(jnp.float32)[:, None] * frequency[None, :]
+    return (jnp.cos(angles), jnp.sin(angles))
+
+
+def rotate(values, cos_table, sin_table):
+    half_width = values.shape[-1] // 2
+    front_half = values[..., :half_width]
+    back_half = values[..., half_width:]
+    return jnp.concatenate(
+        [
+            front_half * cos_table - back_half * sin_table,
+            back_half * cos_table + front_half * sin_table,
+        ],
+        axis=-1,
+    )
+
+
+def any_shards(
+    tokens,
+    segments,
+    positions,
+    query_weight,
+    key_weight,
+    value_weight,
+    output_weight,
+    attn_gain,
+    gate_weight,
+    up_weight,
+    down_weight,
+    ffn_gain,
+    grad_out,
+):
+    tok_rows, model_width = tokens.shape
+    head_dim = key_weight.shape[1]
+    head_count = model_width // head_dim
+    block_count = head_count // HEAD_BLOCK
+    block_width = HEAD_BLOCK * head_dim
+    score_scale = head_dim ** (-0.5)
+    fsdp_size = lax.axis_size("fsdp")
+    fsdp_index = lax.axis_index("fsdp")
+    gathered = (
+        lax.all_gather(query_weight, "fsdp", axis=0, tiled=True),
+        lax.all_gather(key_weight, "fsdp", axis=0, tiled=True),
+        lax.all_gather(value_weight, "fsdp", axis=0, tiled=True),
+        lax.all_gather(output_weight, "fsdp", axis=0, tiled=True),
+        lax.all_gather(attn_gain, "fsdp", axis=0, tiled=True),
+        lax.all_gather(ffn_gain, "fsdp", axis=0, tiled=True),
+    )
+    w_query, w_key, w_value, w_out, gain_attn, gain_ffn = gathered
+    gain_attn = gain_attn.astype(jnp.float32)
+    gain_ffn = gain_ffn.astype(jnp.float32)
+    inputs = tokens.astype(jnp.float32)
+    normed_full, inverse_attn = norm_forward(inputs, gain_attn)
+    normed = normed_full.astype(jnp.bfloat16)
+    query_raw = matmul(normed, w_query)
+    key_raw = matmul(normed, w_key)
+    value_rows = matmul(normed, w_value).astype(jnp.bfloat16)
+    cos_table, sin_table = half_tables(positions, head_dim)
+    queries = rotate(
+        query_raw.reshape(tok_rows, head_count, head_dim), cos_table[:, None], sin_table[:, None]
+    ).astype(jnp.bfloat16)
+    key_rot = rotate(key_raw, cos_table, sin_table).astype(jnp.bfloat16)
+    key_rows, value_all = (
+        lax.all_gather(key_rot, "fsdp", axis=0, tiled=True),
+        lax.all_gather(value_rows, "fsdp", axis=0, tiled=True),
+    )
+    seg_all, pos_all = (
+        lax.all_gather(segments, "fsdp", axis=0, tiled=True),
+        lax.all_gather(positions, "fsdp", axis=0, tiled=True),
+    )
+    key_width = max(GROUP_TOK, tok_rows)
+    window_start = fsdp_index * tok_rows // GROUP_TOK * GROUP_TOK
+    key_window = lax.dynamic_slice_in_dim(key_rows, window_start, key_width, 0)
+    value_window = lax.dynamic_slice_in_dim(value_all, window_start, key_width, 0)
+    seg_window = lax.dynamic_slice_in_dim(seg_all, window_start, key_width, 0)
+    pos_window = lax.dynamic_slice_in_dim(pos_all, window_start, key_width, 0)
+    key_index = window_start + jnp.arange(key_width, dtype=jnp.int32)
+    query_index = fsdp_index * tok_rows + jnp.arange(tok_rows, dtype=jnp.int32)
+    visible = (
+        (key_index[None, :] // GROUP_TOK == query_index[:, None] // GROUP_TOK)
+        & (pos_window[None, :] <= positions[:, None])
+        & ((seg_window[None, :] == 0) | (seg_window[None, :] == segments[:, None]))
+    )
+    query_blocks = queries.reshape(tok_rows, block_count, block_width).transpose(1, 0, 2)
+
+    def block_scores(query_block):
+        flat_queries = query_block.reshape(tok_rows * HEAD_BLOCK, head_dim)
+        scores = (
+            contract(flat_queries, key_window, 1, 1).reshape(tok_rows, HEAD_BLOCK, key_width)
+            * score_scale
+        )
+        return (flat_queries, scores)
+
+    def attend_block(query_block):
+        flat_queries, scores = block_scores(query_block)
+        scores = jnp.where(visible[:, None, :], scores, MASKED)
+        row_max = jnp.max(scores, axis=-1, keepdims=True)
+        exp_scores = jnp.exp(scores - row_max)
+        totals = jnp.sum(exp_scores, axis=-1, keepdims=True)
+        weights = (
+            (exp_scores / totals).astype(jnp.bfloat16).reshape(tok_rows * HEAD_BLOCK, key_width)
+        )
+        mixed_block = matmul(weights, value_window).reshape(tok_rows, block_width)
+        return (mixed_block, (row_max + jnp.log(totals))[..., 0])
+
+    mixed_blocks, log_totals = lax.map(attend_block, query_blocks)
+    mixed_rows = mixed_blocks.transpose(1, 0, 2).reshape(tok_rows, model_width).astype(jnp.bfloat16)
+    hidden = inputs + matmul(mixed_rows, w_out)
+    normed_ffn_full, inverse_ffn = norm_forward(hidden, gain_ffn)
+    normed_ffn = normed_ffn_full.astype(jnp.bfloat16)
+    cotangent = grad_out.astype(jnp.float32)
+    w_gate, w_up, w_down = (
+        lax.all_gather(gate_weight, "fsdp", axis=1, tiled=True),
+        lax.all_gather(up_weight, "fsdp", axis=1, tiled=True),
+        lax.all_gather(down_weight, "fsdp", axis=0, tiled=True),
+    )
+    gate_proj = matmul(normed_ffn, w_gate)
+    up_proj = matmul(normed_ffn, w_up)
+    activation = (jax.nn.silu(gate_proj) * up_proj).astype(jnp.bfloat16)
+    layer_out = (hidden + matmul(activation, w_down)).astype(jnp.bfloat16)
+    d_activation = contract(grad_out, w_down, 1, 1)
+    d_gate, d_up = swiglu_back(d_activation, gate_proj, up_proj)
+    d_normed_ffn = contract(d_gate, w_gate, 1, 1) + contract(d_up, w_up, 1, 1)
+    gate_up_part = lax.psum_scatter(
+        jnp.concatenate(
+            [contract(d_gate, normed_ffn, 0, 0), contract(d_up, normed_ffn, 0, 0)], axis=1
+        ).astype(jnp.bfloat16),
+        "fsdp",
+        scatter_dimension=0,
+        tiled=True,
+    ).astype(jnp.float32)
+    gate_part = gate_up_part[:, :model_width].T
+    up_part = gate_up_part[:, model_width:].T
+    down_part = lax.psum_scatter(
+        contract(activation, grad_out, 0, 0).astype(jnp.bfloat16),
+        "fsdp",
+        scatter_dimension=0,
+        tiled=True,
+    )
+    resid_ffn, ffn_gain_term = norm_backward(hidden, inverse_ffn, gain_ffn, d_normed_ffn)
+    d_hidden = cotangent + resid_ffn
+    d_branch = d_hidden.astype(jnp.bfloat16)
+    d_mixed = contract(d_branch, w_out, 1, 1).astype(jnp.bfloat16)
+    d_mixed_blocks = d_mixed.reshape(tok_rows, block_count, block_width).transpose(1, 0, 2)
+
+    def back_block(totals, block_items):
+        query_block, d_block, log_block = block_items
+        flat_queries, scores = block_scores(query_block)
+        probs = jnp.where(visible[:, None, :], jnp.exp(scores - log_block[..., None]), 0.0)
+        d_flat = d_block.reshape(tok_rows * HEAD_BLOCK, head_dim)
+        d_probs = contract(d_flat, value_window, 1, 1).reshape(tok_rows, HEAD_BLOCK, key_width)
+        row_delta = jnp.sum(probs * d_probs, axis=-1, keepdims=True)
+        d_scores = (
+            (probs * (d_probs - row_delta))
+            .astype(jnp.bfloat16)
+            .reshape(tok_rows * HEAD_BLOCK, key_width)
+        )
+        weights = probs.astype(jnp.bfloat16).reshape(tok_rows * HEAD_BLOCK, key_width)
+        d_query_block = matmul(d_scores, key_window) * score_scale
+        key_total = totals[0] + contract(d_scores, flat_queries, 0, 0) * score_scale
+        value_total = totals[1] + contract(weights, d_flat, 0, 0)
+        return ((key_total, value_total), d_query_block.reshape(tok_rows, block_width))
+
+    zero_window = jnp.zeros((key_width, head_dim), jnp.float32)
+    window_grads, d_query_blocks = lax.scan(
+        back_block, (zero_window, zero_window), (query_blocks, d_mixed_blocks, log_totals)
+    )
+    d_queries = d_query_blocks.transpose(1, 0, 2).reshape(tok_rows, head_count, head_dim)
+    d_query_raw = (
+        rotate(d_queries, cos_table[:, None], -sin_table[:, None])
+        .astype(jnp.bfloat16)
+        .reshape(tok_rows, model_width)
+    )
+    row_zeros = jnp.zeros((fsdp_size * tok_rows, head_dim), jnp.float32)
+    key_term = lax.dynamic_update_slice_in_dim(row_zeros, window_grads[0], window_start, 0)
+    value_term = lax.dynamic_update_slice_in_dim(row_zeros, window_grads[1], window_start, 0)
+    key_sum, value_sum = (
+        lax.psum_scatter(
+            key_term.astype(jnp.bfloat16), "fsdp", scatter_dimension=0, tiled=True
+        ).astype(jnp.float32),
+        lax.psum_scatter(
+            value_term.astype(jnp.bfloat16), "fsdp", scatter_dimension=0, tiled=True
+        ).astype(jnp.float32),
+    )
+    d_key_raw = rotate(key_sum, cos_table, -sin_table).astype(jnp.bfloat16)
+    d_value = value_sum.astype(jnp.bfloat16)
+    d_normed = (
+        contract(d_query_raw, w_query, 1, 1)
+        + contract(d_key_raw, w_key, 1, 1)
+        + contract(d_value, w_value, 1, 1)
+    )
+    resid_attn, attn_gain_term = norm_backward(inputs, inverse_attn, gain_attn, d_normed)
+    input_grad = d_hidden + resid_attn
+    attn_part = lax.psum_scatter(
+        jnp.concatenate(
+            [
+                contract(normed, d_query_raw, 0, 0),
+                contract(normed, d_key_raw, 0, 0),
+                contract(normed, d_value, 0, 0),
+                contract(mixed_rows, d_branch, 0, 0),
+            ],
+            axis=1,
+        ).astype(jnp.bfloat16),
+        "fsdp",
+        scatter_dimension=0,
+        tiled=True,
+    )
+    attn_gain_part, ffn_gain_part = (
+        lax.psum_scatter(attn_gain_term, "fsdp", scatter_dimension=0, tiled=True),
+        lax.psum_scatter(ffn_gain_term, "fsdp", scatter_dimension=0, tiled=True),
+    )
+    summed = (
+        lax.psum(attn_part, "replica").astype(jnp.float32),
+        lax.psum(attn_gain_part.astype(jnp.bfloat16), "replica").astype(jnp.float32),
+        lax.psum(ffn_gain_part.astype(jnp.bfloat16), "replica").astype(jnp.float32),
+        lax.psum(gate_part.astype(jnp.bfloat16), "replica").astype(jnp.float32),
+        lax.psum(up_part.astype(jnp.bfloat16), "replica").astype(jnp.float32),
+        lax.psum(down_part, "replica").astype(jnp.float32),
+    )
+    attn_total, attn_gain_grad, ffn_gain_grad, gate_grad, up_grad, down_grad = summed
+    query_grad = attn_total[:, :model_width]
+    key_grad = attn_total[:, model_width : model_width + head_dim]
+    value_grad = attn_total[:, model_width + head_dim : model_width + 2 * head_dim]
+    output_grad = attn_total[:, model_width + 2 * head_dim :]
+    return (
+        layer_out,
+        input_grad,
+        query_grad,
+        key_grad,
+        value_grad,
+        output_grad,
+        attn_gain_grad,
         gate_grad,
         up_grad,
         down_grad,
-        gain_grads[1],
-    )
+        ffn_gain_grad,
+    )
+
+
+def suits(mesh):
+    fsdp_size = mesh.shape["fsdp"]
+    return mesh.shape["replica"] == 4 and fsdp_size % 2 == 0 and 2048 % (128 * fsdp_size) == 0
 
 
 def solution(mesh):
     return jax.shard_map(
-        shards,
+        shards if suits(mesh) else any_shards,
         mesh=mesh,
         in_specs=(
             P(("replica", "fsdp"), None),

time: 1270 us -> 1080 us (0.85)
  Pallas kernels: 219 us -> 569 us
  waiting for transfers between devices: 502 us -> 166 us
  blocking collectives: 75.6 us -> 0 us
  starting transfers between devices: 62.7 us -> 18.7 us
  other arithmetic: 73.7 us -> 34.5 us
  matrix products: 216 us -> 194 us
  local copies, waits for them, and re-layouts: 86.8 us -> 67.7 us
    pallas_call x0 -> x2, Pallas kernels: none -> 350 us  [the longest x1 184 us: outer_sum(): pl.pallas_call(functools.partial(outer_kernel, fsdp_size), out_shape=jax....]
    reduce_scatter x7 -> x3, waiting for transfers between devices: 254 us -> 0.01 us  [scatter_shards(): return lax.psum_scatter(value, 'fsdp', scatter_dimension=0, tiled=True)]
    psum x1 -> x0, blocking collectives: 75.6 us -> none  [shards(): lax.psum(jnp.stack([attn_gain_term, ffn_gain_term]), ('replica', 'fsdp'))]
    ppermute x52 -> x15, waiting for transfers between devices: 218 us -> 165 us  [swap(): lax.ppermute(value, 'replica', [(r, r ^ step) for r in range(copies)])]
    ppermute x52 -> x15, starting transfers between devices: 61.9 us -> 18.5 us  [swap(): lax.ppermute(value, 'replica', [(r, r ^ step) for r in range(copies)])]
    all_gather x3, waiting for transfers between devices: 27.5 us -> 0.01 us  [gather_shards(): return lax.all_gather(value, 'fsdp', axis=0, tiled=True)]
    dot_general x12 -> x7, matrix products: 148 us -> 128 us  [contract(): lax.dot_general(left, right, (((left_dim,), (right_dim,)), ((), ())), pre...]
    add x2 -> x0, other arithmetic: 15.9 us -> none  [the longest x1 8.72 us: shards(): d_hidden = cotangent + resid_ffn]
  transfers between devices with their start and end apart: 62 -> 21, of which waited for: 31 -> 7; matrix products, arithmetic and copies ran while one was open for 20% -> 20% of each run, Pallas kernels for 16% -> 38%
where the time goes in v4:
time: 1080 us; the launch traced here: 1060 us
  Pallas kernels  569 us (53%)
  matrix products  194 us (18%)
  waiting for transfers between devices  166 us (15%)
  local copies, waits for them, and re-layouts  67.7 us (6%)
  other arithmetic  34.5 us (3%)
  starting transfers between devices  18.7 us (2%)
  between operations  15.1 us (1%)
    pallas_call x1, Pallas kernels, outer_sum(): pl.pallas_call(functools.partial(outer_kernel, fsdp_size), out_shape=jax....  184 us
    pallas_call x1, Pallas kernels, project(): pl.pallas_call(functools.partial(project_kernel, fsdp_size), out_shape=(j...  177 us
    pallas_call x1, Pallas kernels, finish(): pl.pallas_call(functools.partial(finish_kernel, fsdp_size), out_shape=(ja...  166 us
    ppermute x15, waiting for transfers between devices, swap(): lax.ppermute(value, 'replica', [(r, r ^ step) for r in range(copies)])  165 us
    dot_general x7, matrix products, contract(): lax.dot_general(left, right, (((left_dim,), (right_dim,)), ((), ())), pre...  128 us
    dot_general x4, matrix products, matmul(): return jnp.dot(left, right, preferred_element_type=jnp.float32)  66.7 us
    unnamed x82, local copies, waits for them, and re-layouts  35.7 us
    pallas_call x1, Pallas kernels, attend_back(): pl.pallas_call(attend_back_kernel, out_shape=(jax.ShapeDtypeStruct((tok_r...  22.2 us
  transfers between devices with their start and end apart: 21, of which 7 were waited for; matrix products, arithmetic and copies ran while one was open for 20% of the time, Pallas kernels for 38%

profile of v4, /device:TPU:0, one launch (start us, length us, event | category | flops | bytes accessed | tf_op | source)
XLA Modules:
  0.0 1064.8 jit_solution(1293254575279039837)
XLA Ops:
  7.2 1.8 copy-done
  10.0 2.0 dynamic-slice_bitcast_fusion.1
  16.5 1.4 copy-done.7
  19.2 177.4 %project.1 = (bf16[512,2048]{1,0:T(8,128)(2,1)}, bf16[512,2048]{1,0:T(8,128)(2,1)}, f32[8,2048]{1,0:T(8,128)S(1)}, bf16[8,256,2048]{2,1,0:T(8,128)(2,1)}, bf16[8...) custom-call(bf16[512,2048]{1,0:T(8,128)(2,1)} %tokens_ref.3, ...), custom_call_target="tpu_custom_call" | custom-call | flops 4831838208 | bytes 41943040 | tf_op jit(solution)/shard_map/project/pallas_call | solution.py:580
  196.8 2.0 copy-done.9
  198.8 1.6 copy-done.11
  200.4 19.2 %attend.1 = (bf16[512,2048]{1,0:T(8,128)(2,1)S(1)}, f32[4,4,8,512]{3,2,1,0:T(8,128)S(1)}) custom-call(s32[1]{0:T(128)} %bitcast.base_ref, bf16[512,2048]{1,0:T(8,128)(2,1)S(1)} %copy-done.11, bf16[4096,256]{1,0:T(8,128)(2,1)S(1)} %bitcast.48, s32[512,128]{1,0:T(8,128)S(1)} %broadcast_in_dim.14.low_ref), custom_call_target="tpu_custom_call" | custom-call | flops 16106127360 | bytes 16777216 | tf_op jit(solution)/shard_map/attend/pallas_call | solution.py:138
  219.6 4.6 multiply_reduce_fusion.2
  224.9 1.5 copy-done.15
  226.4 2.5 constant_dynamic-update-slice_fusion.4
  228.9 1.5 collective-permute-start
  230.4 1.5 collective-permute-start.1
  233.0 2.0 constant_dynamic-slice_fusion
  235.1 1.6 constant_dynamic-update-slice_fusion.9
  236.7 21.9 %collective-permute-done = bf16[512,2048]{1,0:T(8,128)(2,1)} collective-permute-done((bf16[512,2048]{1,0:T(8,128)(2,1)}, bf16[512,2048]{1,0:T(8,128)(2,1)}, u32[]{:S(2)}, u32[]{:S(2)}) %collective-permute-start) | collective-permute-done | bytes 2097184 | tf_op jit(solution)/shard_map/ppermute | solution.py:1114
  259.8 1.5 collective-permute-start.2
  262.7 1.5 collective-permute-start.3
  264.2 39.3 %collective-permute-done.4 = bf16[512,2048]{1,0:T(8,128)(2,1)} collective-permute-done((bf16[512,2048]{1,0:T(8,128)(2,1)S(1)}, bf16[512,2048]{1,0:T(8,128)(2,1)}, u32[]{:S(2)}, u32[]{:S(2)}) %collective-permute-start.4) | collective-permute-done | bytes 2097184 | tf_op jit(solution)/shard_map/ppermute | solution.py:1114
  304.8 1.5 collective-permute-start.6
  306.3 1.3 slice.85
  307.6 1.5 collective-permute-start.7
  309.2 3.1 constant_dynamic-update-slice_fusion.3
  312.3 3.2 constant_dynamic-update-slice_fusion.2
  315.5 3.2 constant_dynamic-update-slice_fusion.8
  318.7 3.2 constant_dynamic-update-slice_fusion.7
  321.9 5.7 collective-permute-done.2
  329.7 20.4 %collective-permute-done.6 = bf16[256,2048]{1,0:T(8,128)(2,1)S(1)} collective-permute-done((bf16[256,2048]{1,0:T(8,128)(2,1)S(1)}, bf16[256,2048]{1,0:T(8,128)(2,1)S(1)}, u32[]{:S(2)}, u32[]{:S(2)}) %collective-permute-start.6) | collective-permute-done | bytes 1048608 | tf_op jit(solution)/shard_map/ppermute | solution.py:1114
  352.3 19.1 %fusion.13 = f32[2048,1408]{1,0:T(8,128)} fusion(bf16[2048,2048]{1,0:T(8,128)(2,1)} %constant_dynamic-update-slice_fusion, bf16[1408,2048]{1,0:T(8,128)(2,1)} %all-gather.6.cloned.1.call-done), kind=kOutput, calls=%fused_computation.65 | convolution fusion | flops 11811160064 | bytes 25690112 | tf_op jit(solution)/shard_map/dot_general | solution.py:29
  371.4 18.7 %fusion.12 = f32[2048,1408]{1,0:T(8,128)} fusion(bf16[2048,2048]{1,0:T(8,128)(2,1)} %constant_dynamic-update-slice_fusion, bf16[1408,2048]{1,0:T(8,128)(2,1)} %all-gather.4.cloned.1.call-done), kind=kOutput, calls=%fused_computation.64 | convolution fusion | flops 11811160064 | bytes 25690112 | tf_op jit(solution)/shard_map/dot_general | solution.py:29
  390.1 26.0 %multiply_convert_fusion = (bf16[2048,1408]{1,0:T(8,128)(2,1)}, bf16[2048,1408]{1,0:T(8,128)(2,1)}, bf16[2048,1408]{1,0:T(8,128)(2,1)}) fusion(f32[2048,1408]{1,0:T(8,128)} %fusion.12, f32[2048,1408]{1,0:T(8,128)} %fusion.13, bf16[2048,2048]{1,0:T(8,128)(2,1)} %constant_dynamic-update-slice_fusion.5, bf16[1408,2048]{1,0:T(8,128)(2,1)} %all-gather.8.cloned.1.call-done), kind=kOutput, calls=%fused_computation | convolution fusion | flops 11857297408 | bytes 54525952 | tf_op jit(solution)/shard_map/dot_general | solution.py:29
  416.1 18.1 %convolution_convert_fusion.3 = bf16[1408,2048]{1,0:T(8,128)(2,1)} fusion(bf16[2048,1408]{1,0:T(8,128)(2,1)} %get-tuple-element.54, bf16[2048,2048]{1,0:T(8,128)(2,1)} %constant_dynamic-update-slice_fusion), kind=kOutput, calls=%fused_computation.8 | convolution fusion | flops 11814043648 | bytes 19922944 | tf_op jit(solution)/shard_map/dot_general | solution.py:29
  434.3 18.0 %convolution_convert_fusion.2 = bf16[1408,2048]{1,0:T(8,128)(2,1)} fusion(bf16[2048,1408]{1,0:T(8,128)(2,1)} %get-tuple-element.53, bf16[2048,2048]{1,0:T(8,128)(2,1)} %constant_dynamic-update-slice_fusion), kind=kOutput, calls=%fused_computation.7 | convolution fusion | flops 11814043648 | bytes 19922944 | tf_op jit(solution)/shard_map/dot_general | solution.py:29
  452.3 19.4 %fusion.14 = f32[2048,2048]{1,0:T(8,128)} fusion(bf16[2048,1408]{1,0:T(8,128)(2,1)} %get-tuple-element.54, bf16[1408,2048]{1,0:T(8,128)(2,1)} %all-gather.4.cloned.1.call-done), kind=kOutput, calls=%fused_computation.66 | convolution fusion | flops 11811160064 | bytes 28311552 | tf_op jit(solution)/shard_map/dot_general | solution.py:25
  471.7 23.9 %fusion.11 = (bf16[2048,2048]{1,0:T(8,128)(2,1)}, f32[2048,2048]{1,0:T(8,128)}) fusion(f32[2048,2048]{1,0:T(8,128)} %fusion.14, bf16[2048,1408]{1,0:T(8,128)(2,1)} %get-tuple-element.53, bf16[1408,2048]{1,0:T(8,128)(2,1)} %all-gather.6.cloned.1.call-done), kind=kOutput, calls=%fused_computation.63 | convolution fusion | flops 11819548672 | bytes 53477376 | tf_op jit(solution)/shard_map/dot_general | solution.py:25
  495.6 4.1 fusion.9
  500.2 1.5 collective-permute-start.8
  501.6 18.3 %convolution_convert_fusion.1 = bf16[1408,2048]{1,0:T(8,128)(2,1)} fusion(bf16[2048,1408]{1,0:T(8,128)(2,1)} %get-tuple-element.55, bf16[2048,2048]{1,0:T(8,128)(2,1)} %constant_dynamic-update-slice_fusion.5), kind=kOutput, calls=%fused_computation.6 | convolution fusion | flops 11814043648 | bytes 19922944 | tf_op jit(solution)/shard_map/dot_general | solution.py:29
  520.0 3.5 fusion.2
  523.6 1.6 collective-permute-start.9
  526.1 18.8 %convolution_convert_fusion = bf16[2048,2048]{1,0:T(8,128)(2,1)} fusion(bf16[2048,1408]{1,0:T(8,128)(2,1)} %get-tuple-element.55, bf16[1408,2048]{1,0:T(8,128)(2,1)} %all-gather.8.cloned.1.call-done), kind=kOutput, calls=%fused_computation.5 | convolution fusion | flops 11815354368 | bytes 19922944 | tf_op jit(solution)/shard_map/dot_general | solution.py:25
  544.9 20.6 %collective-permute-done.9 = bf16[512,2048]{1,0:T(8,128)(2,1)S(1)} collective-permute-done((bf16[512,2048]{1,0:T(8,128)(2,1)S(1)}, bf16[512,2048]{1,0:T(8,128)(2,1)S(1)}, u32[]{:S(2)}, u32[]{:S(2)}) %collective-permute-start.9) | collective-permute-done | bytes 2097184 | tf_op jit(solution)/shard_map/ppermute | solution.py:1114
  565.5 2.0 multiply_reduce_fusion
  567.5 3.5 fusion.6
  571.0 1.3 copy-done.22
  572.3 9.3 convolution_convert_fusion.4.d_mixed_ref
  581.7 184.0 %outer_sum.1 = f32[256,2048]{1,0:T(8,128)} custom-call(bf16[512,2048]{1,0:T(8,128)(2,1)} %copy-done.12, bf16[512,2048]{1,0:T(8,128)(2,1)} %copy-done.22), custom_call_target="tpu_custom_call" | custom-call | flops 85899345920 | bytes 8388608 | tf_op jit(solution)/shard_map/outer_sum/pallas_call | solution.py:909
  765.7 5.9 fusion.8
  771.6 2.6 collective-permute-start.12
  774.2 1.5 collective-permute-start.14
  775.7 22.2 %attend_back.1 = (bf16[512,2048]{1,0:T(8,128)(2,1)S(1)}, bf16[4096,256]{1,0:T(8,128)(2,1)S(1)}) custom-call(s32[1]{0:T(128)} %bitcast.base_ref, bf16[512,2048]{1,0:T(8,128)(2,1)} %get-tuple-element.28.q_ref, bf16[4096,256]{1,0:T(8,128)(2,1)} %bitcast.47, f32[512,128]{1,0:T(8,128)S(1)} %copy-done.3, f32[512,128]{1,0:T(8,128)S(1)} %copy-done.5, ...), custom_call_target="tpu_custom_call" | custom-call | flops 26843545600 | bytes 16777216 | tf_op jit(solution)/shard_map/attend_back/pallas_call | solution.py:247
  800.5 20.4 %collective-permute-done.12 = bf16[512,2048]{1,0:T(8,128)(2,1)S(1)} collective-permute-done((bf16[512,2048]{1,0:T(8,128)(2,1)}, bf16[512,2048]{1,0:T(8,128)(2,1)S(1)}, u32[]{:S(2)}, u32[]{:S(2)}) %collective-permute-start.12) | collective-permute-done | bytes 2097184 | tf_op jit(solution)/shard_map/ppermute | solution.py:1114
  820.9 37.2 %collective-permute-done.13 = bf16[512,2048]{1,0:T(8,128)(2,1)S(1)} collective-permute-done((bf16[512,2048]{1,0:T(8,128)(2,1)}, bf16[512,2048]{1,0:T(8,128)(2,1)S(1)}, u32[]{:S(2)}, u32[]{:S(2)}) %collective-permute-start.13) | collective-permute-done | bytes 2097184 | tf_op jit(solution)/shard_map/ppermute | solution.py:1114
  858.2 5.7 add_convert_fusion
  863.9 3.1 pad_maximum_fusion.ffn_ref
  867.6 166.2 %finish.1 = (f32[512,2048]{1,0:T(8,128)}, f32[256,2048]{1,0:T(8,128)}, f32[256,384]{1,0:T(8,128)}, bf16[4,3,176,2048]{3,2,1,0:T(8,128)(2,1)}) custom-call(bf16[512,2048]{1,0:T(8,128)(2,1)} %get-tuple-element.34.normed_ref, bf16[512,2048]{1,0:T(8,128)(2,1)} %copy-done.14, bf16[512,2048]{1,0:T(8,128)(2,1)} %tokens_ref.3, ...), custom_call_target="tpu_custom_call" | custom-call | flops 214748364800 | bytes 41943040 | tf_op jit(solution)/shard_map/finish/pallas_call | solution.py:1081
  1033.9 1.7 fusion.10
  1035.5 1.8 slice_reduce_fusion
  1037.3 4.0 fusion.7
  1041.3 3.5 bitcast_convert_fusion
  1044.8 3.5 convert_bitcast_fusion
  1048.3 3.5 convert_bitcast_fusion.1
  1051.8 2.1 copy.37
  1054.8 1.3 copy.38
  1056.2 1.3 copy.39
  (123 shorter events, 22.6 us)
Async XLA Ops:
  7.2 1.8 copy-start
  7.2 345.1 %all-gather.6.cloned.1.call-start = ((), (), s32[]{:S(2)}) async-start(), calls=%async_computation.4 | async-start | bytes 6488064 | tf_op jit(solution)/shard_map/all_gather | solution.py:1144
  10.0 361.4 %all-gather.4.cloned.1.call-start = ((), (), s32[]{:S(2)}) async-start(), calls=%async_computation.3 | async-start | bytes 6488064 | tf_op jit(solution)/shard_map/all_gather | solution.py:1144
  12.1 378.0 %all-gather.8.cloned.1.call-start = ((), (), s32[]{:S(2)}) async-start(), calls=%async_computation.5 | async-start | bytes 6488064 | tf_op jit(solution)/shard_map/all_gather | solution.py:1144
  15.3 181.4 %copy-start.27 = (s32[512]{0:T(512)}, s32[512]{0:T(512)S(1)}, u32[]{:S(2)}) copy-start(s32[512]{0:T(512)S(1)} %get-tuple-element.75) | copy-start | bytes 6148
  16.5 180.1 %copy-start.2 = (f32[512,128]{1,0:T(8,128)}, f32[512,128]{1,0:T(8,128)S(1)}, u32[]{:S(2)}) copy-start(f32[512,128]{1,0:T(8,128)S(1)} %get-tuple-element.81.cos_ref) | copy-start | bytes 786436
  16.5 180.1 %copy-start.4 = (f32[512,128]{1,0:T(8,128)}, f32[512,128]{1,0:T(8,128)S(1)}, u32[]{:S(2)}) copy-start(f32[512,128]{1,0:T(8,128)S(1)} %get-tuple-element.82.sin_ref) | copy-start | bytes 786436
  16.5 1.4 copy-start.7
  17.9 1.2 copy-start.8
  196.6 23.0 %copy-start.6 = (f32[8,2048]{1,0:T(8,128)}, f32[8,2048]{1,0:T(8,128)S(1)}, u32[]{:S(2)}) copy-start(f32[8,2048]{1,0:T(8,128)S(1)} %get-tuple-element.32.gain_ref) | copy-start | bytes 196612
  196.6 23.0 %copy-start.13 = (bf16[8,256,384]{2,1,0:T(8,128)(2,1)}, bf16[8,256,384]{2,1,0:T(8,128)(2,1)S(1)}, u32[]{:S(2)}) copy-start(bf16[8,256,384]{2,1,0:T(8,128)(2,1)S(1)} %get-tuple-element.40.kvg_ref) | copy-start | bytes 4718596
  196.7 28.3 %copy-start.23 = (f32[1,2048]{1,0:T(1,128)}, f32[1,2048]{1,0:T(1,128)S(1)}, u32[]{:S(2)}) copy-start(f32[1,2048]{1,0:T(1,128)S(1)} %slice.64) | copy-start | bytes 24580
  196.8 2.0 copy-start.9
  198.8 1.6 copy-start.11
  200.4 19.2 %copy-start.30 = (bf16[512,2048]{1,0:T(8,128)(2,1)S(1)}, bf16[512,2048]{1,0:T(8,128)(2,1)}, u32[]{:S(2)}) copy-start(bf16[512,2048]{1,0:T(8,128)(2,1)} %tokens_ref.3) | copy-start | bytes 6291460
  200.4 19.2 %copy-start.31 = (bf16[8,256,2048]{2,1,0:T(8,128)(2,1)S(1)}, bf16[8,256,2048]{2,1,0:T(8,128)(2,1)}, u32[]{:S(2)}) copy-start(bf16[8,256,2048]{2,1,0:T(8,128)(2,1)} %get-tuple-element.31) | copy-start | bytes 25165828
  219.6 4.7 copy-start.12
  224.3 2.1 copy-start.15
  224.3 7.6 copy-start.17
  224.9 11.8 %copy-start.25 = (f32[512]{0:T(512)}, f32[512]{0:T(512)S(1)}, u32[]{:S(2)}) copy-start(f32[512]{0:T(512)S(1)} %get-tuple-element.74) | copy-start | bytes 6148
  228.9 29.6 %collective-permute-start = (bf16[512,2048]{1,0:T(8,128)(2,1)}, bf16[512,2048]{1,0:T(8,128)(2,1)}, u32[]{:S(2)}, u32[]{:S(2)}) collective-permute-start(bf16[512,2048]{1,0:T(8,128)(2,1)} %get-tuple-element.52), channel_id=1, source_target_pairs={{0,8},{8,0},{16,24},{24,16},{1,9},{9,1},{17,25},{25,17},{2,10},{10... | collective-permute-start | bytes 6291464 | tf_op jit(solution)/shard_map/ppermute | solution.py:1114
  230.4 31.0 %collective-permute-start.1 = (bf16[512,2048]{1,0:T(8,128)(2,1)}, bf16[512,2048]{1,0:T(8,128)(2,1)}, u32[]{:S(2)}, u32[]{:S(2)}) collective-permute-start(bf16[512,2048]{1,0:T(8,128)(2,1)} %get-tuple-element.52), channel_id=1, source_target_pairs={{0,16},{8,24},{16,0},{24,8},{1,17},{9,25},{17,1},{25,9},{2,18},{10... | collective-permute-start | bytes 6291464 | tf_op jit(solution)/shard_map/ppermute | solution.py:1114
  231.8 71.6 %collective-permute-start.4 = (bf16[512,2048]{1,0:T(8,128)(2,1)S(1)}, bf16[512,2048]{1,0:T(8,128)(2,1)}, u32[]{:S(2)}, u32[]{:S(2)}) collective-permute-start(bf16[512,2048]{1,0:T(8,128)(2,1)S(1)} %copy-done.17), channel_id=1, source_target_pairs={{0,8},{8,0},{16,24},{24,16},{1,9},{9,1},{17,25},{25,17},{2,10},{10... | collective-permute-start | bytes 6291464 | tf_op jit(solution)/shard_map/ppermute | solution.py:1114
  232.4 73.9 %collective-permute-start.5 = (bf16[512,2048]{1,0:T(8,128)(2,1)S(1)}, bf16[512,2048]{1,0:T(8,128)(2,1)}, u32[]{:S(2)}, u32[]{:S(2)}) collective-permute-start(bf16[512,2048]{1,0:T(8,128)(2,1)S(1)} %copy-done.17), channel_id=1, source_target_pairs={{0,16},{8,24},{16,0},{24,8},{1,17},{9,25},{17,1},{25,9},{2,18},{10... | collective-permute-start | bytes 6291464 | tf_op jit(solution)/shard_map/ppermute | solution.py:1114
  235.0 628.9 %reduce-scatter.4.cloned.1.call-start = ((), (), s32[]{:S(2)}) async-start(), calls=%async_computation.6 | async-start | bytes 6488064 | tf_op jit(solution)/shard_map/reduce_scatter | solution.py:1148
  259.8 67.8 %collective-permute-start.2 = (bf16[256,2048]{1,0:T(8,128)(2,1)S(1)}, bf16[256,2048]{1,0:T(8,128)(2,1)S(1)}, u32[]{:S(2)}, u32[]{:S(2)}) collective-permute-start(bf16[256,2048]{1,0:T(8,128)(2,1)S(1)} %slice.82), channel_id=1, source_target_pairs={{0,16},{8,24},{16,0},{24,8},{1,17},{9,25},{17,1},{25,9},{2,18},{10... | collective-permute-start | bytes 3145736 | tf_op jit(solution)/shard_map/ppermute | solution.py:1114
  262.7 65.9 %collective-permute-start.3 = (bf16[256,2048]{1,0:T(8,128)(2,1)S(1)}, bf16[256,2048]{1,0:T(8,128)(2,1)S(1)}, u32[]{:S(2)}, u32[]{:S(2)}) collective-permute-start(bf16[256,2048]{1,0:T(8,128)(2,1)S(1)} %slice.83), channel_id=1, source_target_pairs={{0,8},{8,0},{16,24},{24,16},{1,9},{9,1},{17,25},{25,17},{2,10},{10... | collective-permute-start | bytes 3145736 | tf_op jit(solution)/shard_map/ppermute | solution.py:1114
  304.8 45.3 %collective-permute-start.6 = (bf16[256,2048]{1,0:T(8,128)(2,1)S(1)}, bf16[256,2048]{1,0:T(8,128)(2,1)S(1)}, u32[]{:S(2)}, u32[]{:S(2)}) collective-permute-start(bf16[256,2048]{1,0:T(8,128)(2,1)S(1)} %slice.84), channel_id=1, source_target_pairs={{0,16},{8,24},{16,0},{24,8},{1,17},{9,25},{17,1},{25,9},{2,18},{10... | collective-permute-start | bytes 3145736 | tf_op jit(solution)/shard_map/ppermute | solution.py:1114
  307.6 43.5 %collective-permute-start.7 = (bf16[256,2048]{1,0:T(8,128)(2,1)S(1)}, bf16[256,2048]{1,0:T(8,128)(2,1)S(1)}, u32[]{:S(2)}, u32[]{:S(2)}) collective-permute-start(bf16[256,2048]{1,0:T(8,128)(2,1)S(1)} %slice.85), channel_id=1, source_target_pairs={{0,8},{8,0},{16,24},{24,16},{1,9},{9,1},{17,25},{25,17},{2,10},{10... | collective-permute-start | bytes 3145736 | tf_op jit(solution)/shard_map/ppermute | solution.py:1114
  434.2 429.7 %reduce-scatter.6.cloned.1.call-start = ((), (), s32[]{:S(2)}) async-start(), calls=%async_computation.7 | async-start | bytes 6488064 | tf_op jit(solution)/shard_map/reduce_scatter | solution.py:1148
  452.3 411.6 %reduce-scatter.8.cloned.1.call-start = ((), (), s32[]{:S(2)}) async-start(), calls=%async_computation.8 | async-start | bytes 6488064 | tf_op jit(solution)/shard_map/reduce_scatter | solution.py:1148
  499.7 20.3 %collective-permute-start.10 = (bf16[256,2048]{1,0:T(8,128)(2,1)}, bf16[256,2048]{1,0:T(8,128)(2,1)}, u32[]{:S(2)}, u32[]{:S(2)}) collective-permute-start(bf16[256,2048]{1,0:T(8,128)(2,1)} %get-tuple-element.66), channel_id=1, source_target_pairs={{0,8},{8,0},{16,24},{24,16},{1,9},{9,1},{17,25},{25,17},{2,10},{10... | collective-permute-start | bytes 3145736 | tf_op jit(solution)/shard_map/ppermute | solution.py:1114
  500.2 19.8 %collective-permute-start.8 = (bf16[256,2048]{1,0:T(8,128)(2,1)}, bf16[256,2048]{1,0:T(8,128)(2,1)}, u32[]{:S(2)}, u32[]{:S(2)}) collective-permute-start(bf16[256,2048]{1,0:T(8,128)(2,1)} %get-tuple-element.67), channel_id=1, source_target_pairs={{0,16},{8,24},{16,0},{24,8},{1,17},{9,25},{17,1},{25,9},{2,18},{10... | collective-permute-start | bytes 3145736 | tf_op jit(solution)/shard_map/ppermute | solution.py:1114
  523.6 41.8 %collective-permute-start.9 = (bf16[512,2048]{1,0:T(8,128)(2,1)S(1)}, bf16[512,2048]{1,0:T(8,128)(2,1)S(1)}, u32[]{:S(2)}, u32[]{:S(2)}) collective-permute-start(bf16[512,2048]{1,0:T(8,128)(2,1)S(1)} %pad_maximum_fusion.1), channel_id=1, source_target_pairs={{0,8},{8,0},{16,24},{24,16},{1,9},{9,1},{17,25},{25,17},{2,10},{10... | collective-permute-start | bytes 6291464 | tf_op jit(solution)/shard_map/ppermute | solution.py:1114
  525.3 40.2 %slice-start = ((s8[16777216]{0:T(1024)(128)(4,1)}), s8[4194304]{0:T(1024)(128)(4,1)S(1)}, s32[]{:S(2)}) async-start(s8[16777216]{0:T(1024)(128)(4,1)} %bitcast.50), calls=%async_computation.9 | async-start | bytes 8388608
  525.4 40.1 %copy-start.16 = (f32[512,2048]{1,0:T(8,128)S(1)}, f32[512,2048]{1,0:T(8,128)}, u32[]{:S(2)}) copy-start(f32[512,2048]{1,0:T(8,128)} %copy-done.15) | copy-start | bytes 12582916
  525.4 40.1 %slice-start.1 = ((s8[16777216]{0:T(1024)(128)(4,1)}), s8[4194304]{0:T(1024)(128)(4,1)S(1)}, s32[]{:S(2)}) async-start(s8[16777216]{0:T(1024)(128)(4,1)} %bitcast.50), calls=%async_computation.10 | async-start | bytes 8388608
  525.4 40.1 %slice-start.2 = ((s8[16777216]{0:T(1024)(128)(4,1)}), s8[4194304]{0:T(1024)(128)(4,1)S(1)}, s32[]{:S(2)}) async-start(s8[16777216]{0:T(1024)(128)(4,1)} %bitcast.50), calls=%async_computation.11 | async-start | bytes 8388608
  525.5 40.1 %slice-start.3 = ((s8[16777216]{0:T(1024)(128)(4,1)}), s8[4194304]{0:T(1024)(128)(4,1)S(1)}, s32[]{:S(2)}) async-start(s8[16777216]{0:T(1024)(128)(4,1)} %bitcast.50), calls=%async_computation.12 | async-start | bytes 8388608
  525.5 40.1 %copy-start.24 = (f32[1,2048]{1,0:T(1,128)S(1)}, f32[1,2048]{1,0:T(1,128)}, u32[]{:S(2)}) copy-start(f32[1,2048]{1,0:T(1,128)} %copy-done.23) | copy-start | bytes 24580
  525.5 40.1 %copy-start.26 = (f32[512]{0:T(512)S(1)}, f32[512]{0:T(512)}, u32[]{:S(2)}) copy-start(f32[512]{0:T(512)} %copy-done.25) | copy-start | bytes 6148
  525.5 40.0 %collective-permute-start.11 = (bf16[512,2048]{1,0:T(8,128)(2,1)S(1)}, bf16[512,2048]{1,0:T(8,128)(2,1)S(1)}, u32[]{:S(2)}, u32[]{:S(2)}) collective-permute-start(bf16[512,2048]{1,0:T(8,128)(2,1)S(1)} %pad_maximum_fusion.2), channel_id=1, source_target_pairs={{0,16},{8,24},{16,0},{24,8},{1,17},{9,25},{17,1},{25,9},{2,18},{10... | collective-permute-start | bytes 6291464 | tf_op jit(solution)/shard_map/ppermute | solution.py:1114
  544.9 22.7 %copy-start.18 = (bf16[512,2048]{1,0:T(8,128)(2,1)S(1)}, bf16[512,2048]{1,0:T(8,128)(2,1)}, u32[]{:S(2)}) copy-start(bf16[512,2048]{1,0:T(8,128)(2,1)} %param.24) | copy-start | bytes 6291460
  544.9 22.7 %copy-start.29 = (f32[512]{0:T(512)S(1)}, f32[512]{0:T(512)}, u32[]{:S(2)}) copy-start(f32[512]{0:T(512)} %get-tuple-element.73) | copy-start | bytes 6148
  571.0 1.3 copy-start.22
  765.7 10.0 copy-start.28
  765.7 10.0 copy-start.3
  765.7 10.0 copy-start.5
  771.6 49.4 %collective-permute-start.12 = (bf16[512,2048]{1,0:T(8,128)(2,1)}, bf16[512,2048]{1,0:T(8,128)(2,1)S(1)}, u32[]{:S(2)}, u32[]{:S(2)}) collective-permute-start(bf16[512,2048]{1,0:T(8,128)(2,1)} %get-tuple-element.61), channel_id=1, source_target_pairs={{0,8},{8,0},{16,24},{24,16},{1,9},{9,1},{17,25},{25,17},{2,10},{10... | collective-permute-start | bytes 6291464 | tf_op jit(solution)/shard_map/ppermute | solution.py:1114
  774.2 84.0 %collective-permute-start.13 = (bf16[512,2048]{1,0:T(8,128)(2,1)}, bf16[512,2048]{1,0:T(8,128)(2,1)S(1)}, u32[]{:S(2)}, u32[]{:S(2)}) collective-permute-start(bf16[512,2048]{1,0:T(8,128)(2,1)} %get-tuple-element.63), channel_id=1, source_target_pairs={{0,16},{8,24},{16,0},{24,8},{1,17},{9,25},{17,1},{25,9},{2,18},{10... | collective-permute-start | bytes 6291464 | tf_op jit(solution)/shard_map/ppermute | solution.py:1114
  774.2 84.0 %collective-permute-start.14 = (bf16[512,2048]{1,0:T(8,128)(2,1)}, bf16[512,2048]{1,0:T(8,128)(2,1)}, u32[]{:S(2)}, u32[]{:S(2)}) collective-permute-start(bf16[512,2048]{1,0:T(8,128)(2,1)} %get-tuple-element.62), channel_id=1, source_target_pairs={{0,24},{8,16},{16,8},{24,0},{1,25},{9,17},{17,9},{25,1},{2,26},{10... | collective-permute-start | bytes 6291464 | tf_op jit(solution)/shard_map/ppermute | solution.py:1114
  797.9 1.3 copy-start.10
  799.2 1.3 copy-start.14
  1048.3 3.5 copy-start.19
  1051.8 3.1 copy-start.21
  1051.8 4.4 copy-start.20
  1051.8 5.7 copy-start.1
Sparse Core Ops, SparseCore 0:
  10.2 85.1 all-gather.5
  97.6 80.0 all-gather.3
  235.1 139.0 all-gather.7
  434.3 160.4 reduce-scatter.3
  597.0 63.2 reduce-scatter.5
  663.0 69.3 reduce-scatter.7

commit v5 on v4

--- a/solution.py
+++ b/solution.py
@@ -18,6 +18,7 @@
 TILE = 128
 CHUNK = 512
 HEAD_GROUP = 4
+FFN_ROWS = 256
 HEAD_BLOCK = 4
 
 
@@ -70,13 +71,209 @@
     return (d_gate, d_up)
 
 
+MESH = pl.DeviceIdType.MESH
+
+
+def flip(index, bit):
+    return index + bit - 2 * bit * (index // bit % 2)
+
+
+class Exchange:
+    def __init__(self, buffer, sems):
+        self.replica, self.fsdp = lax.axis_index("replica"), lax.axis_index("fsdp")
+        self.buffer, self.sems = buffer, sems
+        self.beside, self.across = flip(self.replica, 1), flip(self.replica, 2)
+        self.half = buffer.shape[1] // 2
+
+    def greet(self):
+        barrier = pltpu.get_barrier_semaphore()
+        for target in (self.beside, self.across):
+            pl.semaphore_signal(
+                barrier, inc=1, device_id=(target, self.fsdp), device_id_type=MESH
+            )
+        pl.semaphore_wait(barrier, 2)
+
+    def copy(self, kind):
+        first, second = pl.ds(0, self.half), pl.ds(self.half, self.half)
+        source, dest, target = (
+            (self.buffer.at[0], self.buffer.at[1], self.beside),
+            (self.buffer.at[0], self.buffer.at[2], self.across),
+            (self.buffer.at[1, first], self.buffer.at[3, first], self.across),
+            (self.buffer.at[2, second], self.buffer.at[3, second], self.beside),
+        )[kind]
+        return pltpu.make_async_remote_copy(
+            src_ref=source,
+            dst_ref=dest,
+            send_sem=self.sems.at[0, kind],
+            recv_sem=self.sems.at[1, kind],
+            device_id=(target, self.fsdp),
+            device_id_type=MESH,
+        )
+
+    def begin(self):
+        self.copy(0).start()
+        self.copy(1).start()
+
+    def relay(self):
+        self.copy(0).wait_recv()
+        self.copy(2).start()
+        self.copy(1).wait_recv()
+        self.copy(3).start()
+
+    def end(self):
+        self.copy(2).wait_recv()
+        self.copy(3).wait_recv()
+
+    def drain(self):
+        for kind in range(4):
+            self.copy(kind).wait_send()
+
+
+def ffn_kernel(
+    x_ref,
+    grads_ref,
+    gate_ref,
+    up_ref,
+    down_ref,
+    x_all,
+    act_all,
+    d_gate_all,
+    d_up_all,
+    d_x_all,
+    gate_w,
+    up_w,
+    down_w,
+    block,
+    d_act,
+    act,
+    d_gate,
+    d_up,
+    d_x,
+    load_sems,
+    store_sems,
+    x_sems,
+):
+    exchange = Exchange(x_all, x_sems)
+    exchange.greet()
+    own = pltpu.make_async_copy(x_ref, x_all.at[0], load_sems.at[0])
+    own.start()
+    loads = [
+        pltpu.make_async_copy(src, dst, load_sems.at[1 + i])
+        for i, (src, dst) in enumerate(
+            ((down_ref, down_w), (gate_ref, gate_w), (up_ref, up_w))
+        )
+    ]
+    for load in loads:
+        load.start()
+
+    def fetch(source, at, slot):
+        return pltpu.make_async_copy(source.at[at], block.at[slot], load_sems.at[4 + slot])
+
+    fetch(grads_ref, 0, 0).start()
+    own.wait()
+    exchange.begin()
+    loads[0].wait()
+    rows = d_act.shape[1]
+    parts = rows // FFN_ROWS
+    for at in range(4):
+        fetch(grads_ref, at, at % 2).wait()
+        if at < 3:
+            fetch(grads_ref, at + 1, (at + 1) % 2).start()
+
+        @pl.loop(0, parts)
+        def _(part, at=at):
+            some = pl.ds(pl.multiple_of(part * FFN_ROWS, FFN_ROWS), FFN_ROWS)
+            d_act[at, some] = contract(block[at % 2, some], down_w[...], 1, 1).astype(jnp.bfloat16)
+
+    loads[1].wait()
+    loads[2].wait()
+
+    def stores(at):
+        return [
+            pltpu.make_async_copy(src, dst.at[at], store_sems.at[i])
+            for i, (src, dst) in enumerate(
+                ((act, act_all), (d_gate, d_gate_all), (d_up, d_up_all), (d_x, d_x_all))
+            )
+        ]
+
+    for at in range(4):
+        if at == 1:
+            exchange.relay()
+        if at == 3:
+            exchange.end()
+        load = fetch(x_all, at, 0)
+        load.start()
+        load.wait()
+        if at > 0:
+            for store in stores(at - 1):
+                store.wait()
+
+        @pl.loop(0, parts)
+        def _(part, at=at):
+            some = pl.ds(pl.multiple_of(part * FFN_ROWS, FFN_ROWS), FFN_ROWS)
+            x = block[0, some]
+            gate = contract(x, gate_w[...], 1, 1)
+            up = contract(x, up_w[...], 1, 1)
+            slope = jax.nn.sigmoid(gate)
+            d = d_act[at, some].astype(jnp.float32)
+            swish = gate * slope
+            act[some] = (swish * up).astype(jnp.bfloat16)
+            by_gate = (d * up * (slope + swish * (1.0 - slope))).astype(jnp.bfloat16)
+            by_up = (d * swish).astype(jnp.bfloat16)
+            d_gate[some] = by_gate
+            d_up[some] = by_up
+            d_x[some] = (matmul(by_gate, gate_w[...]) + matmul(by_up, up_w[...])).astype(
+                jnp.bfloat16
+            )
+
+        for store in stores(at):
+            store.start()
+    for store in stores(3):
+        store.wait()
+    exchange.drain()
+
+
+def feed_forward(x, grads, w_gate, w_up, w_down):
+    rows, width = x.shape
+    hidden = w_gate.shape[0]
+    low, dma = jnp.bfloat16, pltpu.SemaphoreType.DMA
+    hbm = pl.BlockSpec(memory_space=pl.ANY)
+    wide = jax.ShapeDtypeStruct((4, rows, width), low)
+    thin = jax.ShapeDtypeStruct((4, rows, hidden), low)
+    return pl.pallas_call(
+        ffn_kernel,
+        out_shape=(wide, thin, thin, thin, wide),
+        in_specs=[hbm] * 5,
+        out_specs=(hbm,) * 5,
+        scratch_shapes=[pltpu.VMEM((hidden, width), low)] * 3
+        + [
+            pltpu.VMEM((2, rows, width), low),
+            pltpu.VMEM((4, rows, hidden), low),
+            pltpu.VMEM((rows, hidden), low),
+            pltpu.VMEM((rows, hidden), low),
+            pltpu.VMEM((rows, hidden), low),
+            pltpu.VMEM((rows, width), low),
+            dma((6,)),
+            dma((4,)),
+            dma((2, 4)),
+        ],
+        compiler_params=pltpu.CompilerParams(
+            collective_id=3, has_side_effects=True, vmem_limit_bytes=50 << 20
+        ),
+        cost_estimate=pl.CostEstimate(
+            flops=40 * rows * width * hidden, transcendentals=0, bytes_accessed=40 << 20
+        ),
+        name="feed_forward",
+    )(x, grads, w_gate, w_up, w_down)
+
+
 def stack_heads(block):
     heads = block.shape[1] // 128
     return jnp.concatenate([block[:, h * 128 : (h + 1) * 128] for h in range(heads)], axis=0)
 
 
-def chunk_plan(base_ref):
-    first = base_ref[0] + pl.program_id(0) * TILE
+def chunk_plan(tok_rows):
+    first = lax.axis_index("fsdp") * tok_rows % GROUP_TOK + pl.program_id(0) * TILE
     in_prompt = first < PROMPT
     full = jnp.where(in_prompt, first // CHUNK, PROMPT // CHUNK)
     last = jnp.where(
@@ -86,16 +283,39 @@
 
 
 def attend_kernel(
-    base_ref, q_ref, kv_ref, low_ref, mixed_ref, log_ref, values, top, acc
+    tok_rows,
+    q_ref,
+    kv_ref,
+    low_ref,
+    grads_ref,
+    mixed_ref,
+    log_ref,
+    grads_all,
+    values,
+    top,
+    acc,
+    sems,
+    own_sem,
 ):
     factor = 128**-0.5 * LOG2E
 
+    exchange = Exchange(grads_all, sems)
+    own = pltpu.make_async_copy(grads_ref, grads_all.at[0], own_sem)
+
     @pl.when((pl.program_id(0) == 0) & (pl.program_id(1) == 0))
     def _():
+        own.start()
+        exchange.greet()
+        own.wait()
+        exchange.begin()
         values[:, :128] = kv_ref[:, 128:]
         values[:, 128:] = jnp.ones_like(values[:, 128:])
 
-    first, full, last = chunk_plan(base_ref)
+    @pl.when((pl.program_id(0) == pl.num_programs(0) // 2) & (pl.program_id(1) == 0))
+    def _():
+        exchange.relay()
+
+    first, full, last = chunk_plan(tok_rows)
     queries = stack_heads(q_ref[...])
     rows = queries.shape[0]
     top[...] = jnp.full_like(top, MASKED)
@@ -127,48 +347,59 @@
         mixed_ref[:, h * 128 : (h + 1) * 128] = mixed[h * TILE : (h + 1) * TILE].astype(jnp.bfloat16)
     log_ref[0, 0] = (top[...] + jnp.log2(total)).T[:8]
 
-
-def attend(base, queries, kv, low):
+    @pl.when(
+        (pl.program_id(0) == pl.num_programs(0) - 1) & (pl.program_id(1) == pl.num_programs(1) - 1)
+    )
+    def _():
+        exchange.end()
+        exchange.drain()
+
+
+def attend(queries, kv, low, grads):
     tok_rows, width = queries.shape
     tiles, groups = tok_rows // TILE, width // (128 * HEAD_GROUP)
     lanes, rows = 128 * HEAD_GROUP, TILE * HEAD_GROUP
-    tile_spec = pl.BlockSpec((TILE, lanes), lambda i, g, b: (i, g))
-    row_spec = pl.BlockSpec((TILE, 128), lambda i, g, b: (i, 0))
+    tile_spec = pl.BlockSpec((TILE, lanes), lambda i, g: (i, g))
+    hbm = pl.BlockSpec(memory_space=pl.ANY)
     pairs = tok_rows * (width // 128) * 2560
     return pl.pallas_call(
-        attend_kernel,
+        functools.partial(attend_kernel, tok_rows),
         out_shape=(
             jax.ShapeDtypeStruct((tok_rows, width), jnp.bfloat16),
             jax.ShapeDtypeStruct((tiles, groups, 8, rows), jnp.float32),
+            jax.ShapeDtypeStruct((4,) + grads.shape, jnp.bfloat16),
         ),
-        grid_spec=pltpu.PrefetchScalarGridSpec(
-            num_scalar_prefetch=1,
-            grid=(tiles, groups),
-            in_specs=[
-                tile_spec,
-                pl.BlockSpec(kv.shape, lambda i, g, b: (0, 0)),
-                row_spec,
-            ],
-            out_specs=[
-                tile_spec,
-                pl.BlockSpec((1, 1, 8, rows), lambda i, g, b: (i, g, 0, 0)),
-            ],
-            scratch_shapes=[
-                pltpu.VMEM(kv.shape, jnp.bfloat16),
-                pltpu.VMEM((rows, 128), jnp.float32),
-                pltpu.VMEM((rows, 256), jnp.float32),
-            ],
+        grid=(tiles, groups),
+        in_specs=[
+            tile_spec,
+            pl.BlockSpec(kv.shape, lambda i, g: (0, 0)),
+            pl.BlockSpec((TILE, 128), lambda i, g: (i, 0)),
+            hbm,
+        ],
+        out_specs=[
+            tile_spec,
+            pl.BlockSpec((1, 1, 8, rows), lambda i, g: (i, g, 0, 0)),
+            hbm,
+        ],
+        scratch_shapes=[
+            pltpu.VMEM(kv.shape, jnp.bfloat16),
+            pltpu.VMEM((rows, 128), jnp.float32),
+            pltpu.VMEM((rows, 256), jnp.float32),
+            pltpu.SemaphoreType.DMA((2, 4)),
+            pltpu.SemaphoreType.DMA,
+        ],
+        compiler_params=pltpu.CompilerParams(
+            collective_id=4, has_side_effects=True, vmem_limit_bytes=40 << 20
         ),
-        compiler_params=pltpu.CompilerParams(vmem_limit_bytes=40 << 20),
         cost_estimate=pl.CostEstimate(
-            flops=pairs * 768, transcendentals=pairs, bytes_accessed=16 << 20
+            flops=pairs * 3000, transcendentals=pairs, bytes_accessed=16 << 20
         ),
         name="attend",
-    )(base, queries, kv, low)
+    )(queries, kv, low, grads)
 
 
 def attend_back_kernel(
-    base_ref,
+    tok_rows,
     q_ref,
     kv_ref,
     cos_ref,
@@ -193,7 +424,7 @@
     def _():
         sums[...] = jnp.zeros_like(sums)
 
-    first, full, last = chunk_plan(base_ref)
+    first, full, last = chunk_plan(tok_rows)
     queries = stack_heads(q_ref[...])
     d_rows = stack_heads(d_mixed_ref[...])
     mixed = stack_heads(mixed_ref[...])
@@ -236,52 +467,42 @@
         d_kv_ref[:, 128:] = sums[:, 128:].astype(jnp.bfloat16)
 
 
-def attend_back(base, queries, kv, cos_table, sin_table, low, mixed, d_mixed, logs):
+def attend_back(queries, kv, cos_table, sin_table, low, mixed, d_mixed, logs):
     tok_rows, width = queries.shape
     tiles, groups = tok_rows // TILE, width // (128 * HEAD_GROUP)
     lanes, rows = 128 * HEAD_GROUP, TILE * HEAD_GROUP
-    tile_spec = pl.BlockSpec((TILE, lanes), lambda i, g, b: (i, g))
-    row_spec = pl.BlockSpec((TILE, 128), lambda i, g, b: (i, 0))
-    whole = pl.BlockSpec(kv.shape, lambda i, g, b: (0, 0))
+    tile_spec = pl.BlockSpec((TILE, lanes), lambda i, g: (i, g))
+    row_spec = pl.BlockSpec((TILE, 128), lambda i, g: (i, 0))
+    whole = pl.BlockSpec(kv.shape, lambda i, g: (0, 0))
     pairs = tok_rows * (width // 128) * 2560
     return pl.pallas_call(
-        attend_back_kernel,
+        functools.partial(attend_back_kernel, tok_rows),
         out_shape=(
             jax.ShapeDtypeStruct((tok_rows, width), jnp.bfloat16),
             jax.ShapeDtypeStruct(kv.shape, jnp.bfloat16),
         ),
-        grid_spec=pltpu.PrefetchScalarGridSpec(
-            num_scalar_prefetch=1,
-            grid=(tiles, groups),
-            in_specs=[
-                tile_spec,
-                whole,
-                row_spec,
-                row_spec,
-                pl.BlockSpec((8, TILE), lambda i, g, b: (0, i)),
-                tile_spec,
-                tile_spec,
-                pl.BlockSpec((1, 1, 8, rows), lambda i, g, b: (i, g, 0, 0)),
-            ],
-            out_specs=[tile_spec, whole],
-            scratch_shapes=[
-                pltpu.VMEM(kv.shape, jnp.float32),
-                pltpu.VMEM((rows, 128), jnp.float32),
-            ],
-        ),
+        grid=(tiles, groups),
+        in_specs=[
+            tile_spec,
+            whole,
+            row_spec,
+            row_spec,
+            pl.BlockSpec((8, TILE), lambda i, g: (0, i)),
+            tile_spec,
+            tile_spec,
+            pl.BlockSpec((1, 1, 8, rows), lambda i, g: (i, g, 0, 0)),
+        ],
+        out_specs=[tile_spec, whole],
+        scratch_shapes=[
+            pltpu.VMEM(kv.shape, jnp.float32),
+            pltpu.VMEM((rows, 128), jnp.float32),
+        ],
         compiler_params=pltpu.CompilerParams(vmem_limit_bytes=48 << 20),
         cost_estimate=pl.CostEstimate(
-            flops=pairs * 1280, transcendentals=pairs, bytes_accessed=16 << 20
+            flops=pairs * 3000, transcendentals=pairs, bytes_accessed=16 << 20
         ),
         name="attend_back",
-    )(base, queries, kv, cos_table, sin_table, low, mixed, d_mixed, logs)
-
-
-MESH = pl.DeviceIdType.MESH
-
-
-def flip(index, bit):
-    return index + bit - 2 * bit * (index // bit % 2)
+    )(queries, kv, cos_table, sin_table, low, mixed, d_mixed, logs)
 
 
 class Chain:
@@ -913,7 +1134,7 @@
         out_specs=vmem,
         scratch_shapes=collect_scratch(fsdp_size, rows, width),
         compiler_params=pltpu.CompilerParams(
-            collective_id=collective_id, has_side_effects=True, vmem_limit_bytes=56 << 20
+            collective_id=collective_id, has_side_effects=True, vmem_limit_bytes=50 << 20
         ),
         cost_estimate=pl.CostEstimate(
             flops=40 * left.shape[0] * left.shape[1] * width, transcendentals=0, bytes_accessed=8 << 20
@@ -944,6 +1165,7 @@
     kvg_vmem,
     d_kv_raw,
     term_sum,
+    hidden_buf,
     local_sems,
     ffn_sems,
     *refs,
@@ -1024,15 +1246,17 @@
     @pl.loop(0, tokens_ref.shape[0] // 128)
     def _(block):
         part = pl.ds(pl.multiple_of(block * 128, 128), 128)
+        fetch_hidden = pltpu.make_async_copy(d_hidden_ref.at[part], hidden_buf, local_sems.at[0])
+        fetch_hidden.start()
         d_normed = input_grad_ref[part]
         inputs = tokens_ref[part].astype(jnp.float32)
         inverse = lax.rsqrt(jnp.mean(inputs * inputs, axis=1, keepdims=True) + EPSILON)
         scaled = d_normed * gain_ref[:1]
         inner = jnp.mean(scaled * inputs, axis=1, keepdims=True)
         term_sum[:1] += jnp.sum(d_normed * inputs * inverse, axis=0, keepdims=True)
-        input_grad_ref[part] = (
-            d_hidden_ref[part] + inverse * scaled - inputs * (inverse**3 * inner)
-        )
+        step = inverse * scaled - inputs * (inverse**3 * inner)
+        fetch_hidden.wait()
+        input_grad_ref[part] = hidden_buf[...] + step
 
     term = term_sum[:1]
     line = lax.broadcasted_iota(jnp.int32, (128, width), 0)
@@ -1086,13 +1310,14 @@
             jax.ShapeDtypeStruct((rows, 384), jnp.float32),
             jax.ShapeDtypeStruct((4,) + ffn.shape, low),
         ),
-        in_specs=[vmem] * 8 + [hbm] * 4,
+        in_specs=[vmem] * 3 + [hbm] + [vmem] * 4 + [hbm] * 4,
         out_specs=(vmem, vmem, vmem, hbm),
         scratch_shapes=[
             pltpu.VMEM((2, rows, width), low),
             pltpu.VMEM((fsdp_size, rows, 384), low),
             pltpu.VMEM((tok_rows, 256), low),
             pltpu.VMEM((8, width), jnp.float32),
+            pltpu.VMEM((128, width), jnp.float32),
             dma((3,)),
             dma((2, 4)),
         ]
@@ -1100,7 +1325,7 @@
         + collect_scratch(fsdp_size, rows, 384)
         + collect_scratch(fsdp_size, tok_rows, 256, False),
         compiler_params=pltpu.CompilerParams(
-            collective_id=2, has_side_effects=True, vmem_limit_bytes=60 << 20
+            collective_id=2, has_side_effects=True, vmem_limit_bytes=54 << 20
         ),
         cost_estimate=pl.CostEstimate(
             flops=100 * tok_rows * width * width, transcendentals=0, bytes_accessed=40 << 20
@@ -1201,43 +1426,30 @@
     one_group = fsdp_size * tok_rows == key_width
     kv = kv_all if one_group else lax.dynamic_slice_in_dim(kv_all, window_start, key_width, 0)
 
-    base = (fsdp_index * tok_rows - window_start).astype(jnp.int32)
-    row_at = base + jnp.arange(tok_rows, dtype=jnp.int32)
+    row_at = fsdp_index * tok_rows - window_start + jnp.arange(tok_rows, dtype=jnp.int32)
     lowest = jnp.where(positions < PROMPT, 0, row_at - (positions - PROMPT))
-    base = base[None]
-    mixed_rows, logs = attend(
-        base, queries, kv, jnp.broadcast_to(lowest[:, None], (tok_rows, 128))
+    w_gate = gather_shards(after(quarter(gate_weight.T, copy_index), normed))
+    w_up = gather_shards(after(quarter(up_weight.T, copy_index), normed))
+    w_down = gather_shards(after(quarter(down_weight, copy_index), normed))
+    mixed_rows, logs, grads = attend(
+        queries, kv, jnp.broadcast_to(lowest[:, None], (tok_rows, 128)), grad_out
     )
 
     hidden = inputs + matmul(mixed_rows, w_out)
     normed_ffn_full, inverse_ffn = norm_forward(hidden, gain_ffn)
     normed_ffn = normed_ffn_full.astype(low)
 
-    w_gate = gather_shards(quarter(gate_weight.T, copy_index))
-    w_up = gather_shards(quarter(up_weight.T, copy_index))
-    w_down = gather_shards(quarter(down_weight, copy_index))
-    grad_blocks = gather_copies(grad_out)
-    grads = jnp.concatenate(grad_blocks, axis=0)
-    normed_blocks = gather_copies(normed_ffn)
-    normed_all = jnp.concatenate(normed_blocks, axis=0)
-
-    d_activation = contract(grads, w_down, 1, 1)
-    gate_proj = contract(normed_all, w_gate, 1, 1)
-    up_proj = contract(normed_all, w_up, 1, 1)
-    activation = (jax.nn.silu(gate_proj) * up_proj).astype(low)
-    d_gate, d_up = swiglu_back(d_activation, gate_proj, up_proj)
-    d_normed_parts = matmul(d_gate, w_gate) + matmul(d_up, w_up)
-    d_normed_ffn = scatter_copies(jnp.split(d_normed_parts, copies))
+    x_all, activation, d_gate, d_up, d_normed_parts = feed_forward(
+        normed_ffn, grads, w_gate, w_up, w_down
+    )
+    d_normed_ffn = scatter_copies(list(d_normed_parts))
+    all_rows = copies * tok_rows
+    x_all, grads = x_all.reshape(all_rows, -1), grads.reshape(all_rows, -1)
+    activation = activation.reshape(all_rows, -1)
+    gate_part = contract(d_gate.reshape(all_rows, -1), x_all, 0, 0).astype(low)
+    up_part = contract(d_up.reshape(all_rows, -1), x_all, 0, 0).astype(low)
+    down_part = contract(activation, grads, 0, 0).astype(low)
     out_parts = matmul(activation, w_down).astype(low)
-
-    gate_part = contract(d_gate, normed_all, 0, 0).astype(low)
-    up_part = contract(d_up, normed_all, 0, 0).astype(low)
-    down_part = contract(activation, grads, 0, 0).astype(low)
-
-    def ffn_grad(partial):
-        summed = scatter_shards(partial)
-        pieces = place(gather_copies(summed), copy_index)
-        return pieces.reshape(-1, model_width).astype(jnp.float32)
 
     cotangent = grad_out.astype(jnp.float32)
     resid_ffn, ffn_gain_term = norm_backward(hidden, inverse_ffn, gain_ffn, d_normed_ffn)
@@ -1255,7 +1467,6 @@
         layer_out = layer_out + swap(part, step + 1).astype(jnp.float32)
     layer_out = layer_out.astype(low)
     d_query_raw, d_kv = attend_back(
-        base,
         queries,
         kv,
         cos_table,

time: 1080 us -> 925 us (0.86)
  matrix products: 194 us -> 86.1 us
  local copies, waits for them, and re-layouts: 67.7 us -> 39.3 us
  Pallas kernels: 569 us -> 549 us
  waiting for transfers between devices: 166 us -> 186 us
    pallas_call x2 -> x3, Pallas kernels: 41.3 us -> 195 us  [the longest x1 99.2 us: feed_forward(): pl.pallas_call(ffn_kernel, out_shape=(wide, thin, thin, thin, wide), in_s...]
    all_gather x3, waiting for transfers between devices: 0.01 us -> 93.8 us  [gather_shards(): return lax.all_gather(value, 'fsdp', axis=0, tiled=True)]
    pallas_call x1, Pallas kernels: 184 us -> 94.8 us  [outer_sum(): pl.pallas_call(functools.partial(outer_kernel, fsdp_size), out_shape=jax....]
    pallas_call x1, Pallas kernels: 177 us -> 93.8 us  [project(): pl.pallas_call(functools.partial(project_kernel, fsdp_size), out_shape=(j...]
    ppermute x15 -> x7, waiting for transfers between devices: 165 us -> 91.6 us  [swap(): lax.ppermute(value, 'replica', [(r, r ^ step) for r in range(copies)])]
    dot_general x7 -> x4, matrix products: 128 us -> 64.4 us  [contract(): lax.dot_general(left, right, (((left_dim,), (right_dim,)), ((), ())), pre...]
    dot_general x4 -> x2, matrix products: 66.7 us -> 21.6 us  [matmul(): return jnp.dot(left, right, preferred_element_type=jnp.float32)]
    unnamed x82 -> x73, local copies, waits for them, and re-layouts: 35.7 us -> 18.6 us
  transfers between devices with their start and end apart: 21 -> 13, of which waited for: 7 -> 7; matrix products, arithmetic and copies ran while one was open for 20% -> 10% of each run, Pallas kernels for 38% -> 21%
where the time goes in v5:
time: 925 us; the launch traced here: 918 us
  Pallas kernels  549 us (59%)
  waiting for transfers between devices  186 us (20%)
  matrix products  86.1 us (9%)
  local copies, waits for them, and re-layouts  39.3 us (4%)
  other arithmetic  34.4 us (4%)
  between operations  14.7 us (2%)
    pallas_call x1, Pallas kernels, finish(): pl.pallas_call(functools.partial(finish_kernel, fsdp_size), out_shape=(ja...  165 us
    pallas_call x1, Pallas kernels, feed_forward(): pl.pallas_call(ffn_kernel, out_shape=(wide, thin, thin, thin, wide), in_s...  99.2 us
    pallas_call x1, Pallas kernels, outer_sum(): pl.pallas_call(functools.partial(outer_kernel, fsdp_size), out_shape=jax....  94.8 us
    all_gather x3, waiting for transfers between devices, gather_shards(): return lax.all_gather(value, 'fsdp', axis=0, tiled=True)  93.8 us
    pallas_call x1, Pallas kernels, project(): pl.pallas_call(functools.partial(project_kernel, fsdp_size), out_shape=(j...  93.8 us
    ppermute x7, waiting for transfers between devices, swap(): lax.ppermute(value, 'replica', [(r, r ^ step) for r in range(copies)])  91.6 us
    pallas_call x1, Pallas kernels, attend(): pl.pallas_call(functools.partial(attend_kernel, tok_rows), out_shape=(jax...  73.9 us
    dot_general x4, matrix products, contract(): lax.dot_general(left, right, (((left_dim,), (right_dim,)), ((), ())), pre...  64.4 us
  transfers between devices with their start and end apart: 13, of which 7 were waited for; matrix products, arithmetic and copies ran while one was open for 10% of the time, Pallas kernels for 21%

profile of v5, /device:TPU:0, one launch (start us, length us, event | category | flops | bytes accessed | tf_op | source)
XLA Modules:
  0.0 918.3 jit_solution(10776667296214958720)
XLA Ops:
  7.3 0.8 stack.21
  8.1 0.7 stack.22
  8.9 0.8 subtract_select_fusion
  9.7 1.8 fusion.5
  11.4 1.4 pad_maximum_fusion.3
  12.8 1.1 fusion.4.kvg_ref
  13.9 2.6 dynamic-slice_bitcast_fusion
  16.5 93.8 %project.1 = (bf16[512,2048]{1,0:T(8,128)(2,1)}, bf16[512,2048]{1,0:T(8,128)(2,1)}, f32[8,2048]{1,0:T(8,128)S(1)}, bf16[8,256,2048]{2,1,0:T(8,128)(2,1)}, bf16[8...) custom-call(bf16[512,2048]{1,0:T(8,128)(2,1)} %tokens_ref.3, ...), custom_call_target="tpu_custom_call" | custom-call | flops 4831838208 | bytes 41943040 | tf_op jit(solution)/shard_map/project/pallas_call | solution.py:801
  110.3 1.1 copy-done.17
  111.5 0.7 all-gather.6.cloned.1.call-update
  112.3 0.9 constant_dynamic-slice_fusion
  113.2 0.6 reduce-scatter.6.cloned.1.call-start
  114.0 1.6 copy-done.2
  115.6 1.6 copy-done.13
  117.2 1.8 copy-done.15
  119.0 73.9 %attend.1 = (bf16[512,2048]{1,0:T(8,128)(2,1)S(1)}, f32[4,4,8,512]{3,2,1,0:T(8,128)S(1)}, bf16[4,512,2048]{2,1,0:T(8,128)(2,1)}) custom-call(bf16[512,2048]{1,0:T(8,128)(2,1)S(1)} %copy-done.15, bf16[4096,256]{1,0:T(8,128)(2,1)S(1)} %bitcast.68, s32[512,128]{1,0:T(8,128)S(1)} %broadcast_in_dim.11.low_ref, bf16[512,2048]{1,0:T(8,128)(2,1)S(1)} %copy-done.2), custom_call_target="tpu_custom_call" | custom-call | flops 62914560000 | bytes 16777216 | tf_op jit(solution)/shard_map/attend/pallas_call | solution.py:365
  192.9 4.6 multiply_reduce_fusion.2
  197.6 2.0 copy-done.19
  199.6 0.4 multiply_convert_fusion.x_ref
  200.1 32.4 %all-gather.6.cloned.1.call-done.up_ref = bf16[1408,2048]{1,0:T(8,128)(2,1)} async-done(((bf16[176,2048]{1,0:T(8,128)(2,1)}), bf16[1408,2048]{1,0:T(8,128)(2,1)}) %all-gather.6.cloned.1.call-update) | async-done | bytes 5767184 | tf_op jit(solution)/shard_map/all_gather | solution.py:1369
  232.4 61.4 %all-gather.8.cloned.1.call-done.down_ref = bf16[1408,2048]{1,0:T(8,128)(2,1)} async-done(((bf16[176,2048]{1,0:T(8,128)(2,1)}), bf16[1408,2048]{1,0:T(8,128)(2,1)}) %all-gather.8.cloned.1.call-update) | async-done | bytes 5767184 | tf_op jit(solution)/shard_map/all_gather | solution.py:1369
  293.8 99.2 %feed_forward.1 = (bf16[4,512,2048]{2,1,0:T(8,128)(2,1)}, bf16[4,512,1408]{2,1,0:T(8,128)(2,1)}, bf16[4,512,1408]{2,1,0:T(8,128)(2,1)}, bf16[4,512,1408]{2,1,0:T(8,128)(2,1)}, bf16[4,512,2048]{2,1,0:T(8,128)(2,1)}) custom-call(bf16[512,2048]{1,0:T(8,128)(2,1)S(1)} %multiply_convert_fusion.x_ref, bf16[4,512,2048]{2,1,0:T(8,128)(2,1)} %get-tuple-element.42.grads_ref, ...), custom_call_target="tpu_custom_call" | custom-call | flops 59055800320 | bytes 41943040 | tf_op jit(solution)/shard_map/feed_forward/pallas_call | solution.py:243
  393.1 18.3 %bitcast_convert_fusion.1 = bf16[1408,2048]{1,0:T(8,128)(2,1)} fusion(bf16[4,512,1408]{2,1,0:T(8,128)(2,1)} %get-tuple-element.52, bf16[4,512,2048]{2,1,0:T(8,128)(2,1)} %get-tuple-element.51), kind=kOutput, calls=%fused_computation.1 | convolution fusion | flops 11814043648 | bytes 19922944 | tf_op jit(solution)/shard_map/dot_general | solution.py:30
  411.5 18.0 %bitcast_convert_fusion.2 = bf16[1408,2048]{1,0:T(8,128)(2,1)} fusion(bf16[4,512,1408]{2,1,0:T(8,128)(2,1)} %get-tuple-element.50, bf16[4,512,2048]{2,1,0:T(8,128)(2,1)} %get-tuple-element.51), kind=kOutput, calls=%fused_computation.2 | convolution fusion | flops 11814043648 | bytes 19922944 | tf_op jit(solution)/shard_map/dot_general | solution.py:30
  429.5 4.0 slice_bitcast_fusion.3
  433.6 0.5 collective-permute-start
  434.1 1.5 collective-permute-start.2
  435.6 18.1 %bitcast_convert_fusion = bf16[1408,2048]{1,0:T(8,128)(2,1)} fusion(bf16[4,512,1408]{2,1,0:T(8,128)(2,1)} %get-tuple-element.47, bf16[4,512,2048]{2,1,0:T(8,128)(2,1)} %get-tuple-element.42.grads_ref), kind=kOutput, calls=%fused_computation | convolution fusion | flops 11814043648 | bytes 19922944 | tf_op jit(solution)/shard_map/dot_general | solution.py:30
  453.8 4.5 collective-permute-done
  458.2 1.0 copy-done.27
  459.2 3.0 fusion.2
  462.4 0.9 collective-permute-start.1
  463.3 0.2 pad_maximum_fusion.2
  463.5 1.2 collective-permute-start.3
  464.7 17.0 %convolution_convert_fusion = bf16[2048,2048]{1,0:T(8,128)(2,1)S(1)} fusion(bf16[2048,1408]{1,0:T(8,128)(2,1)} %bitcast.80, bf16[1408,2048]{1,0:T(8,128)(2,1)} %all-gather.8.cloned.1.call-done.down_ref), kind=kOutput, calls=%fused_computation.3 | convolution fusion | flops 11815354368 | bytes 19922944 | tf_op jit(solution)/shard_map/dot_general | solution.py:26
  481.7 26.8 %collective-permute-done.1 = bf16[512,2048]{1,0:T(8,128)(2,1)S(1)} collective-permute-done((bf16[512,2048]{1,0:T(8,128)(2,1)S(1)}, bf16[512,2048]{1,0:T(8,128)(2,1)S(1)}, u32[]{:S(2)}, u32[]{:S(2)}) %collective-permute-start.1) | collective-permute-done | bytes 2097184 | tf_op jit(solution)/shard_map/ppermute | solution.py:1339
  508.5 0.5 collective-permute-done.3
  509.1 2.8 multiply_reduce_fusion
  511.8 3.6 fusion.6
  515.5 10.0 %convolution_convert_fusion.1.d_mixed_ref = bf16[512,2048]{1,0:T(8,128)(2,1)} fusion(bf16[512,2048]{1,0:T(8,128)(2,1)S(1)} %get-tuple-element.67.right_ref, bf16[2048,2048]{1,0:T(8,128)(2,1)} %bitcast.78), kind=kOutput, calls=%fused_computation.15 | convolution fusion | flops 4296015872 | bytes 12582912 | tf_op jit(solution)/shard_map/dot_general | solution.py:30
  525.4 94.8 %outer_sum.1 = f32[256,2048]{1,0:T(8,128)S(1)} custom-call(bf16[512,2048]{1,0:T(8,128)(2,1)} %copy-done.16, bf16[512,2048]{1,0:T(8,128)(2,1)} %copy-done.25), custom_call_target="tpu_custom_call" | custom-call | flops 85899345920 | bytes 8388608 | tf_op jit(solution)/shard_map/outer_sum/pallas_call | solution.py:1130
  620.3 3.3 fusion.8
  623.6 2.0 collective-permute-start.5
  625.6 1.5 collective-permute-start.6
  627.1 22.3 %attend_back.1 = (bf16[512,2048]{1,0:T(8,128)(2,1)S(1)}, bf16[4096,256]{1,0:T(8,128)(2,1)S(1)}) custom-call(bf16[512,2048]{1,0:T(8,128)(2,1)} %get-tuple-element.37.q_ref, bf16[4096,256]{1,0:T(8,128)(2,1)} %bitcast.67, f32[512,128]{1,0:T(8,128)S(1)} %copy-done.7, f32[512,128]{1,0:T(8,128)S(1)} %copy-done.9, s32[8,512]{1,0:T(8,128)S(1)} %broadcast_in_dim.12.low_ref, ...), custom_call_target="tpu_custom_call" | custom-call | flops 62914560000 | bytes 16777216 | tf_op jit(solution)/shard_map/attend_back/pallas_call | solution.py:478
  649.4 1.3 copy-done.14
  650.7 1.3 copy-done.18
  652.0 20.3 %collective-permute-done.4 = bf16[512,2048]{1,0:T(8,128)(2,1)S(1)} collective-permute-done((bf16[512,2048]{1,0:T(8,128)(2,1)}, bf16[512,2048]{1,0:T(8,128)(2,1)S(1)}, u32[]{:S(2)}, u32[]{:S(2)}) %collective-permute-start.4) | collective-permute-done | bytes 2097184 | tf_op jit(solution)/shard_map/ppermute | solution.py:1339
  672.4 39.4 %collective-permute-done.5 = bf16[512,2048]{1,0:T(8,128)(2,1)S(1)} collective-permute-done((bf16[512,2048]{1,0:T(8,128)(2,1)}, bf16[512,2048]{1,0:T(8,128)(2,1)S(1)}, u32[]{:S(2)}, u32[]{:S(2)}) %collective-permute-start.5) | collective-permute-done | bytes 2097184 | tf_op jit(solution)/shard_map/ppermute | solution.py:1339
  711.8 5.7 add_convert_fusion
  717.5 3.1 pad_maximum_fusion.ffn_ref
  720.7 0.6 broadcast_in_dim.13.term_ref
  721.3 165.3 %finish.1 = (f32[512,2048]{1,0:T(8,128)}, f32[256,2048]{1,0:T(8,128)}, f32[256,384]{1,0:T(8,128)}, bf16[4,3,176,2048]{3,2,1,0:T(8,128)(2,1)}) custom-call(bf16[512,2048]{1,0:T(8,128)(2,1)} %get-tuple-element.43.normed_ref, bf16[512,2048]{1,0:T(8,128)(2,1)} %copy-done.18, bf16[512,2048]{1,0:T(8,128)(2,1)} %tokens_ref.3, ...), custom_call_target="tpu_custom_call" | custom-call | flops 214748364800 | bytes 41943040 | tf_op jit(solution)/shard_map/finish/pallas_call | solution.py:1305
  886.6 1.7 fusion.9
  888.3 1.8 slice_reduce_fusion
  890.1 4.0 fusion.7
  894.0 3.5 bitcast_convert_fusion.3
  897.5 3.5 convert_bitcast_fusion
  901.0 3.5 convert_bitcast_fusion.1
  904.5 2.1 copy.41
  906.6 1.0 copy-done.26
  907.6 1.3 copy.42
  908.9 1.0 copy-done.5
  909.9 1.3 copy.43
  (87 shorter events, 0.9 us)
Async XLA Ops:
  7.2 105.1 %copy-start = (bf16[704,2048]{1,0:T(8,128)(2,1)S(1)}, bf16[704,2048]{1,0:T(8,128)(2,1)}, u32[]{:S(2)}) copy-start(bf16[704,2048]{1,0:T(8,128)(2,1)} %param.22) | copy-start | bytes 8650756
  7.2 192.9 %all-gather.4.cloned.1.call-start = ((), (), s32[]{:S(2)}) async-start(), calls=%async_computation.3 | async-start | bytes 6488064 | tf_op jit(solution)/shard_map/all_gather | solution.py:1369
  9.7 104.2 %copy-start.29 = (s32[512]{0:T(512)}, s32[512]{0:T(512)S(1)}, u32[]{:S(2)}) copy-start(s32[512]{0:T(512)S(1)} %get-tuple-element.88) | copy-start | bytes 6148
  11.4 5.1 copy-start.11
  11.4 5.1 copy-start.12
  12.8 97.5 %copy-start.6 = (f32[512,128]{1,0:T(8,128)}, f32[512,128]{1,0:T(8,128)S(1)}, u32[]{:S(2)}) copy-start(f32[512,128]{1,0:T(8,128)S(1)} %get-tuple-element.92.cos_ref) | copy-start | bytes 786436
  12.8 97.5 %copy-start.8 = (f32[512,128]{1,0:T(8,128)}, f32[512,128]{1,0:T(8,128)S(1)}, u32[]{:S(2)}) copy-start(f32[512,128]{1,0:T(8,128)S(1)} %get-tuple-element.93.sin_ref) | copy-start | bytes 786436
  110.3 1.1 copy-start.17
  111.4 81.5 %copy-start.10 = (f32[8,2048]{1,0:T(8,128)}, f32[8,2048]{1,0:T(8,128)S(1)}, u32[]{:S(2)}) copy-start(f32[8,2048]{1,0:T(8,128)S(1)} %get-tuple-element.41.gain_ref) | copy-start | bytes 196612
  111.5 121.0 %all-gather.6.cloned.1.call-start = ((), (), s32[]{:S(2)}) async-start(), calls=%async_computation.4 | async-start | bytes 6488064 | tf_op jit(solution)/shard_map/all_gather | solution.py:1369
  112.2 181.6 %all-gather.8.cloned.1.call-start = ((), (), s32[]{:S(2)}) async-start(), calls=%async_computation.5 | async-start | bytes 6488064 | tf_op jit(solution)/shard_map/all_gather | solution.py:1369
  113.2 604.3 %reduce-scatter.6.cloned.1.call-start = ((), (), s32[]{:S(2)}) async-start(), calls=%async_computation.7 | async-start | bytes 6488064 | tf_op jit(solution)/shard_map/reduce_scatter | solution.py:1373
  114.0 1.6 copy-start.2
  115.6 1.6 copy-start.13
  117.2 1.8 copy-start.15
  119.0 73.9 %copy-start.31 = (bf16[512,2048]{1,0:T(8,128)(2,1)S(1)}, bf16[512,2048]{1,0:T(8,128)(2,1)}, u32[]{:S(2)}) copy-start(bf16[512,2048]{1,0:T(8,128)(2,1)} %tokens_ref.3) | copy-start | bytes 6291460
  119.0 73.9 %copy-start.32 = (bf16[8,256,2048]{2,1,0:T(8,128)(2,1)S(1)}, bf16[8,256,2048]{2,1,0:T(8,128)(2,1)}, u32[]{:S(2)}) copy-start(bf16[8,256,2048]{2,1,0:T(8,128)(2,1)} %get-tuple-element.40) | copy-start | bytes 25165828
  192.9 4.7 copy-start.16
  197.6 2.0 copy-start.19
  411.4 306.1 %reduce-scatter.4.cloned.1.call-start = ((), (), s32[]{:S(2)}) async-start(), calls=%async_computation.6 | async-start | bytes 6488064 | tf_op jit(solution)/shard_map/reduce_scatter | solution.py:1373
  429.5 288.1 %reduce-scatter.8.cloned.1.call-start = ((), (), s32[]{:S(2)}) async-start(), calls=%async_computation.8 | async-start | bytes 6488064 | tf_op jit(solution)/shard_map/reduce_scatter | solution.py:1373
  433.6 24.7 %collective-permute-start = (bf16[256,2048]{1,0:T(8,128)(2,1)}, bf16[256,2048]{1,0:T(8,128)(2,1)S(1)}, u32[]{:S(2)}, u32[]{:S(2)}) collective-permute-start(bf16[256,2048]{1,0:T(8,128)(2,1)} %get-tuple-element.78), channel_id=1, source_target_pairs={{0,16},{8,24},{16,0},{24,8},{1,17},{9,25},{17,1},{25,9},{2,18},{10... | collective-permute-start | bytes 3145736 | tf_op jit(solution)/shard_map/ppermute | solution.py:1339
  434.1 25.1 %collective-permute-start.2 = (bf16[256,2048]{1,0:T(8,128)(2,1)}, bf16[256,2048]{1,0:T(8,128)(2,1)}, u32[]{:S(2)}, u32[]{:S(2)}) collective-permute-start(bf16[256,2048]{1,0:T(8,128)(2,1)} %get-tuple-element.77), channel_id=1, source_target_pairs={{0,8},{8,0},{16,24},{24,16},{1,9},{9,1},{17,25},{25,17},{2,10},{10... | collective-permute-start | bytes 3145736 | tf_op jit(solution)/shard_map/ppermute | solution.py:1339
  453.7 9.5 %copy-start.24 = (bf16[256,2048]{1,0:T(8,128)(2,1)S(1)}, bf16[256,2048]{1,0:T(8,128)(2,1)}, u32[]{:S(2)}) copy-start(bf16[256,2048]{1,0:T(8,128)(2,1)} %get-tuple-element.76) | copy-start | bytes 3145732
  458.2 1.0 copy-start.27
  462.4 46.2 %collective-permute-start.1 = (bf16[512,2048]{1,0:T(8,128)(2,1)S(1)}, bf16[512,2048]{1,0:T(8,128)(2,1)S(1)}, u32[]{:S(2)}, u32[]{:S(2)}) collective-permute-start(bf16[512,2048]{1,0:T(8,128)(2,1)S(1)} %pad_maximum_fusion.1), channel_id=1, source_target_pairs={{0,8},{8,0},{16,24},{24,16},{1,9},{9,1},{17,25},{25,17},{2,10},{10... | collective-permute-start | bytes 6291464 | tf_op jit(solution)/shard_map/ppermute | solution.py:1339
  463.3 45.8 %slice-start = ((s8[8388608]{0:T(1024)(128)(4,1)}), s8[4194304]{0:T(1024)(128)(4,1)S(1)}, s32[]{:S(2)}) async-start(s8[8388608]{0:T(1024)(128)(4,1)} %bitcast.70), calls=%async_computation.9 | async-start | bytes 8388608
  463.5 45.6 %collective-permute-start.3 = (bf16[512,2048]{1,0:T(8,128)(2,1)S(1)}, bf16[512,2048]{1,0:T(8,128)(2,1)S(1)}, u32[]{:S(2)}, u32[]{:S(2)}) collective-permute-start(bf16[512,2048]{1,0:T(8,128)(2,1)S(1)} %pad_maximum_fusion.2), channel_id=1, source_target_pairs={{0,16},{8,24},{16,0},{24,8},{1,17},{9,25},{17,1},{25,9},{2,18},{10... | collective-permute-start | bytes 6291464 | tf_op jit(solution)/shard_map/ppermute | solution.py:1339
  464.7 44.4 %copy-start.20 = (f32[512,2048]{1,0:T(8,128)S(1)}, f32[512,2048]{1,0:T(8,128)}, u32[]{:S(2)}) copy-start(f32[512,2048]{1,0:T(8,128)} %copy-done.19) | copy-start | bytes 12582916
  464.7 44.4 %slice-start.1 = ((s8[8388608]{0:T(1024)(128)(4,1)}), s8[4194304]{0:T(1024)(128)(4,1)S(1)}, s32[]{:S(2)}) async-start(s8[8388608]{0:T(1024)(128)(4,1)} %bitcast.70), calls=%async_computation.10 | async-start | bytes 8388608
  481.7 138.6 %copy-start.22 = (bf16[2048,2048]{1,0:T(8,128)(2,1)}, bf16[2048,2048]{1,0:T(8,128)(2,1)S(1)}, u32[]{:S(2)}) copy-start(bf16[2048,2048]{1,0:T(8,128)(2,1)S(1)} %convolution_convert_fusion) | copy-start | bytes 25165828
  481.7 30.1 %copy-start.3 = (bf16[512,2048]{1,0:T(8,128)(2,1)S(1)}, bf16[512,2048]{1,0:T(8,128)(2,1)}, u32[]{:S(2)}) copy-start(bf16[512,2048]{1,0:T(8,128)(2,1)} %grads_ref.1) | copy-start | bytes 6291460
  515.5 10.0 %copy-start.25 = (bf16[512,2048]{1,0:T(8,128)(2,1)}, bf16[512,2048]{1,0:T(8,128)(2,1)S(1)}, u32[]{:S(2)}) copy-start(bf16[512,2048]{1,0:T(8,128)(2,1)S(1)} %get-tuple-element.67.right_ref) | copy-start | bytes 6291460
  620.3 3.3 copy-start.4
  620.3 6.8 copy-start.30
  620.3 6.8 copy-start.7
  620.3 6.8 copy-start.9
  623.6 48.8 %collective-permute-start.4 = (bf16[512,2048]{1,0:T(8,128)(2,1)}, bf16[512,2048]{1,0:T(8,128)(2,1)S(1)}, u32[]{:S(2)}, u32[]{:S(2)}) collective-permute-start(bf16[512,2048]{1,0:T(8,128)(2,1)} %get-tuple-element.72), channel_id=1, source_target_pairs={{0,8},{8,0},{16,24},{24,16},{1,9},{9,1},{17,25},{25,17},{2,10},{10... | collective-permute-start | bytes 6291464 | tf_op jit(solution)/shard_map/ppermute | solution.py:1339
  623.6 88.2 %collective-permute-start.5 = (bf16[512,2048]{1,0:T(8,128)(2,1)}, bf16[512,2048]{1,0:T(8,128)(2,1)S(1)}, u32[]{:S(2)}, u32[]{:S(2)}) collective-permute-start(bf16[512,2048]{1,0:T(8,128)(2,1)} %get-tuple-element.74), channel_id=1, source_target_pairs={{0,16},{8,24},{16,0},{24,8},{1,17},{9,25},{17,1},{25,9},{2,18},{10... | collective-permute-start | bytes 6291464 | tf_op jit(solution)/shard_map/ppermute | solution.py:1339
  625.6 86.2 %collective-permute-start.6 = (bf16[512,2048]{1,0:T(8,128)(2,1)}, bf16[512,2048]{1,0:T(8,128)(2,1)}, u32[]{:S(2)}, u32[]{:S(2)}) collective-permute-start(bf16[512,2048]{1,0:T(8,128)(2,1)} %get-tuple-element.73), channel_id=1, source_target_pairs={{0,24},{8,16},{16,8},{24,0},{1,25},{9,17},{17,9},{25,1},{2,26},{10... | collective-permute-start | bytes 6291464 | tf_op jit(solution)/shard_map/ppermute | solution.py:1339
  627.1 84.7 %copy-start.21 = (f32[512,2048]{1,0:T(8,128)S(1)}, f32[512,2048]{1,0:T(8,128)}, u32[]{:S(2)}) copy-start(f32[512,2048]{1,0:T(8,128)} %copy-done.19) | copy-start | bytes 12582916
  649.4 1.3 copy-start.14
  650.7 1.3 copy-start.18
  717.5 3.1 copy-start.28
  901.0 3.5 copy-start.23
  904.5 3.1 copy-start.26
  904.5 6.8 copy-start.1
  907.6 2.3 copy-start.5
Sparse Core Ops, SparseCore 0:
  111.6 59.4 all-gather.3
  173.3 59.1 all-gather.5
  234.7 59.1 all-gather.7
  411.5 62.5 reduce-scatter.5
  476.9 63.2 reduce-scatter.3
  542.9 80.0 reduce-scatter.7

commit v6 on v5

--- a/solution.py
+++ b/solution.py
@@ -139,7 +139,10 @@
     act_all,
     d_gate_all,
     d_up_all,
-    d_x_all,
+    d_x_own,
+    d_x_beside,
+    d_x_across,
+    d_x_got,
     gate_w,
     up_w,
     down_w,
@@ -152,6 +155,7 @@
     load_sems,
     store_sems,
     x_sems,
+    far_sems,
 ):
     exchange = Exchange(x_all, x_sems)
     exchange.greet()
@@ -189,14 +193,27 @@
     loads[2].wait()
 
     def stores(at):
+        pairs = [(act, act_all.at[at]), (d_gate, d_gate_all.at[at]), (d_up, d_up_all.at[at])]
+        if at < 3:
+            pairs.append((d_x, (d_x_own, d_x_beside, d_x_across)[at]))
         return [
-            pltpu.make_async_copy(src, dst.at[at], store_sems.at[i])
-            for i, (src, dst) in enumerate(
-                ((act, act_all), (d_gate, d_gate_all), (d_up, d_up_all), (d_x, d_x_all))
-            )
+            pltpu.make_async_copy(src, dst, store_sems.at[i])
+            for i, (src, dst) in enumerate(pairs)
         ]
 
-    for at in range(4):
+    def far(half):
+        size = rows // 2
+        return pltpu.make_async_remote_copy(
+            src_ref=block.at[1, pl.ds(half * size, size)],
+            dst_ref=d_x_got.at[half],
+            send_sem=far_sems.at[0, half],
+            recv_sem=far_sems.at[1, half],
+            device_id=((exchange.beside, exchange.across)[half], exchange.fsdp),
+            device_id_type=MESH,
+        )
+
+    order = (0, 1, 3, 2)
+    for turn, at in enumerate(order):
         if at == 1:
             exchange.relay()
         if at == 3:
@@ -204,8 +221,8 @@
         load = fetch(x_all, at, 0)
         load.start()
         load.wait()
-        if at > 0:
-            for store in stores(at - 1):
+        if turn > 0:
+            for store in stores(order[turn - 1]):
                 store.wait()
 
         @pl.loop(0, parts)
@@ -222,14 +239,19 @@
             by_up = (d * swish).astype(jnp.bfloat16)
             d_gate[some] = by_gate
             d_up[some] = by_up
-            d_x[some] = (matmul(by_gate, gate_w[...]) + matmul(by_up, up_w[...])).astype(
-                jnp.bfloat16
-            )
+            (block.at[1] if at == 3 else d_x)[some] = (
+                matmul(by_gate, gate_w[...]) + matmul(by_up, up_w[...])
+            ).astype(jnp.bfloat16)
 
         for store in stores(at):
             store.start()
-    for store in stores(3):
+        if at == 3:
+            far(0).start()
+            far(1).start()
+    for store in stores(order[3]):
         store.wait()
+    far(0).wait()
+    far(1).wait()
     exchange.drain()
 
 
@@ -238,13 +260,15 @@
     hidden = w_gate.shape[0]
     low, dma = jnp.bfloat16, pltpu.SemaphoreType.DMA
     hbm = pl.BlockSpec(memory_space=pl.ANY)
+    block = jax.ShapeDtypeStruct((rows, width), low)
+    halves = jax.ShapeDtypeStruct((2, rows // 2, width), low)
     wide = jax.ShapeDtypeStruct((4, rows, width), low)
     thin = jax.ShapeDtypeStruct((4, rows, hidden), low)
     return pl.pallas_call(
         ffn_kernel,
-        out_shape=(wide, thin, thin, thin, wide),
+        out_shape=(wide, thin, thin, thin, block, block, block, halves),
         in_specs=[hbm] * 5,
-        out_specs=(hbm,) * 5,
+        out_specs=(hbm,) * 8,
         scratch_shapes=[pltpu.VMEM((hidden, width), low)] * 3
         + [
             pltpu.VMEM((2, rows, width), low),
@@ -256,6 +280,7 @@
             dma((6,)),
             dma((4,)),
             dma((2, 4)),
+            dma((2, 2)),
         ],
         compiler_params=pltpu.CompilerParams(
             collective_id=3, has_side_effects=True, vmem_limit_bytes=50 << 20
@@ -399,6 +424,7 @@
 
 
 def attend_back_kernel(
+    fsdp_size,
     tok_rows,
     q_ref,
     kv_ref,
@@ -408,21 +434,60 @@
     mixed_ref,
     d_mixed_ref,
     log_ref,
+    rows_ref,
+    branch_ref,
     d_q_ref,
     d_kv_ref,
+    output_ref,
     sums,
     d_q,
+    *refs,
 ):
     scale = 128**-0.5
     factor = scale * LOG2E
-    at_start = (pl.program_id(0) == 0) & (pl.program_id(1) == 0)
     at_end = (pl.program_id(0) == pl.num_programs(0) - 1) & (
         pl.program_id(1) == pl.num_programs(1) - 1
     )
 
-    @pl.when(at_start)
-    def _():
+    place = position(fsdp_size)
+    grad = make_collect(place, refs)
+    count = place[4]
+
+    def begin():
         sums[...] = jnp.zeros_like(sums)
+        greet(*place[:3], count)
+        outer(grad, rows_ref, branch_ref, False)
+        outer(grad, rows_ref, branch_ref, True)
+
+    def cores():
+        for shard in range(count):
+            grad.core_add(shard)
+            grad.diag_start(shard)
+
+    def sum_quarters():
+        each(count, grad.quarter_add)
+        grad.line_hop(count - 1)
+
+    def hops():
+        for hop in range(count - 2, 0, -1):
+            grad.line_hop(hop)
+
+    def gather():
+        grad.line_end()
+        grad.gather_start()
+
+    stages = {
+        0: begin,
+        1: cores,
+        5: lambda: each(count, grad.quarter_start),
+        10: sum_quarters,
+        11: hops,
+        12: gather,
+        14: grad.gather_relay,
+    }
+    now = pl.program_id(0) * pl.num_programs(1) + pl.program_id(1)
+    for step_at, stage in stages.items():
+        pl.when(now == step_at)(stage)
 
     first, full, last = chunk_plan(tok_rows)
     queries = stack_heads(q_ref[...])
@@ -465,10 +530,15 @@
     def _():
         d_kv_ref[:, :128] = (sums[:, :128] * scale).astype(jnp.bfloat16)
         d_kv_ref[:, 128:] = sums[:, 128:].astype(jnp.bfloat16)
-
-
-def attend_back(queries, kv, cos_table, sin_table, low, mixed, d_mixed, logs):
+        grad.gather_end()
+        output_ref[...] = grad.full[...].astype(jnp.float32)
+        grad.drain()
+
+
+def attend_back(queries, kv, cos_table, sin_table, low, mixed, d_mixed, logs, d_branch):
     tok_rows, width = queries.shape
+    fsdp_size = lax.axis_size("fsdp")
+    shard = width // fsdp_size
     tiles, groups = tok_rows // TILE, width // (128 * HEAD_GROUP)
     lanes, rows = 128 * HEAD_GROUP, TILE * HEAD_GROUP
     tile_spec = pl.BlockSpec((TILE, lanes), lambda i, g: (i, g))
@@ -476,10 +546,11 @@
     whole = pl.BlockSpec(kv.shape, lambda i, g: (0, 0))
     pairs = tok_rows * (width // 128) * 2560
     return pl.pallas_call(
-        functools.partial(attend_back_kernel, tok_rows),
+        functools.partial(attend_back_kernel, fsdp_size, tok_rows),
         out_shape=(
             jax.ShapeDtypeStruct((tok_rows, width), jnp.bfloat16),
             jax.ShapeDtypeStruct(kv.shape, jnp.bfloat16),
+            jax.ShapeDtypeStruct((shard, width), jnp.float32),
         ),
         grid=(tiles, groups),
         in_specs=[
@@ -491,18 +562,23 @@
             tile_spec,
             tile_spec,
             pl.BlockSpec((1, 1, 8, rows), lambda i, g: (i, g, 0, 0)),
+            pl.BlockSpec(mixed.shape, lambda i, g: (0, 0)),
+            pl.BlockSpec(mixed.shape, lambda i, g: (0, 0)),
         ],
-        out_specs=[tile_spec, whole],
+        out_specs=[tile_spec, whole, pl.BlockSpec((shard, width), lambda i, g: (0, 0))],
         scratch_shapes=[
             pltpu.VMEM(kv.shape, jnp.float32),
             pltpu.VMEM((rows, 128), jnp.float32),
-        ],
-        compiler_params=pltpu.CompilerParams(vmem_limit_bytes=48 << 20),
+        ]
+        + collect_scratch(fsdp_size, shard, width),
+        compiler_params=pltpu.CompilerParams(
+            collective_id=1, has_side_effects=True, vmem_limit_bytes=50 << 20
+        ),
         cost_estimate=pl.CostEstimate(
             flops=pairs * 3000, transcendentals=pairs, bytes_accessed=16 << 20
         ),
         name="attend_back",
-    )(queries, kv, cos_table, sin_table, low, mixed, d_mixed, logs)
+    )(queries, kv, cos_table, sin_table, low, mixed, d_mixed, logs, mixed, d_branch)
 
 
 class Chain:
@@ -1101,48 +1177,6 @@
         step(shard)
 
 
-def outer_kernel(fsdp_size, left_ref, right_ref, out_ref, *refs):
-    place = position(fsdp_size)
-    greet(*place[:3], place[4])
-    sums = make_collect(place, refs)
-    count = place[4]
-    outer(sums, left_ref, right_ref, False)
-    outer(sums, left_ref, right_ref, True)
-    for shard in range(count):
-        sums.core_add(shard)
-        sums.diag_start(shard)
-    each(count, sums.quarter_start)
-    each(count, sums.quarter_add)
-    for hop in range(count - 1, 0, -1):
-        sums.line_hop(hop)
-    sums.line_end()
-    sums.gather_start()
-    sums.gather_relay()
-    sums.gather_end()
-    out_ref[...] = sums.full[...].astype(jnp.float32)
-    sums.drain()
-
-
-def outer_sum(left, right, collective_id):
-    fsdp_size = lax.axis_size("fsdp")
-    rows, width = left.shape[1] // fsdp_size, right.shape[1]
-    vmem = pl.BlockSpec(memory_space=pltpu.VMEM)
-    return pl.pallas_call(
-        functools.partial(outer_kernel, fsdp_size),
-        out_shape=jax.ShapeDtypeStruct((rows, width), jnp.float32),
-        in_specs=[vmem, vmem],
-        out_specs=vmem,
-        scratch_shapes=collect_scratch(fsdp_size, rows, width),
-        compiler_params=pltpu.CompilerParams(
-            collective_id=collective_id, has_side_effects=True, vmem_limit_bytes=50 << 20
-        ),
-        cost_estimate=pl.CostEstimate(
-            flops=40 * left.shape[0] * left.shape[1] * width, transcendentals=0, bytes_accessed=8 << 20
-        ),
-        name="outer_sum",
-    )(left, right)
-
-
 def finish_kernel(
     fsdp_size,
     normed_ref,
@@ -1203,6 +1237,9 @@
     load_kvg.start()
     load.wait()
     each(count, lambda shard: d_kv.core_copy(shard).start())
+    own_ffn.wait()
+    ffn_copy(0).start()
+    ffn_copy(1).start()
     outer(q_sums, normed_ref, d_q_ref, False)
     each(count, d_kv.core_add)
     d_kv.line_hop(count - 1)
@@ -1214,9 +1251,6 @@
         q_sums.diag_start(shard)
     d_kv.line_end()
     each(count, q_sums.quarter_start)
-    own_ffn.wait()
-    ffn_copy(0).start()
-    ffn_copy(1).start()
 
     summed = d_kv.grad[fsdp].astype(jnp.float32)
     d_key = summed[:, :128]
@@ -1237,6 +1271,9 @@
         input_grad_ref[:, shard * rows : (shard + 1) * rows] = contract(
             d_q_ref[...], wq_buf[shard % 2], 1, 1
         ) + contract(d_kv_raw[...], kvg_vmem[shard, :, :256], 1, 1)
+    for kind in (0, 1):
+        ffn_copy(kind, True).wait_recv()
+        ffn_copy(2 + kind).start()
     each(count, q_sums.quarter_add)
     for hop in range(count - 1, 0, -1):
         q_sums.line_hop(hop)
@@ -1277,9 +1314,6 @@
     each(count, kv_sums.quarter_add)
     for hop in range(count - 1, 0, -1):
         kv_sums.line_hop(hop)
-    for kind in (0, 1):
-        ffn_copy(kind, True).wait_recv()
-        ffn_copy(2 + kind).start()
     kv_sums.line_end()
     kv_sums.gather_start()
     q_sums.gather_end()
@@ -1339,30 +1373,13 @@
     return lax.ppermute(value, "replica", [(r, r ^ step) for r in range(copies)])
 
 
-def gather_copies(block):
-    half = block.shape[0] // 2
-    beside, across = swap(block, 1), swap(block, 2)
-    opposite = jnp.concatenate([swap(beside[:half], 2), swap(across[half:], 1)], axis=0)
-    return [block, beside, across, opposite]
-
-
-def scatter_copies(parts):
-    own, beside, across, opposite = parts
-    half = opposite.shape[0] // 2
-    low = jnp.bfloat16
-    first = swap(opposite[:half].astype(low), 1)
-    second = swap(opposite[half:].astype(low), 2)
-    across = jnp.concatenate(
-        [across[:half].astype(jnp.float32) + first.astype(jnp.float32), across[half:]], axis=0
-    )
-    beside = jnp.concatenate(
-        [beside[:half], beside[half:].astype(jnp.float32) + second.astype(jnp.float32)], axis=0
-    )
-    return (
-        own.astype(jnp.float32)
-        + swap(beside.astype(low), 1).astype(jnp.float32)
-        + swap(across.astype(low), 2).astype(jnp.float32)
-    )
+def pass_on(beside, across, got):
+    half = got.shape[1]
+    low, wide = jnp.bfloat16, jnp.float32
+    got = got.astype(wide)
+    across = jnp.concatenate([across[:half].astype(wide) + got[0], across[half:].astype(wide)])
+    beside = jnp.concatenate([beside[:half].astype(wide), beside[half:].astype(wide) + got[1]])
+    return beside.astype(low), across.astype(low)
 
 
 def gather_shards(value):
@@ -1405,6 +1422,7 @@
     copies = lax.axis_size("replica")
     low = jnp.bfloat16
 
+    w_down = gather_shards(quarter(down_weight, copy_index))
     cos_table, sin_table = rope_tables(positions, head_dim)
     gain_columns = jnp.stack([attn_gain, ffn_gain], axis=1)
     queries, normed, gains, wq_all, w_out, kvg_all, kv_all = project(
@@ -1430,23 +1448,30 @@
     lowest = jnp.where(positions < PROMPT, 0, row_at - (positions - PROMPT))
     w_gate = gather_shards(after(quarter(gate_weight.T, copy_index), normed))
     w_up = gather_shards(after(quarter(up_weight.T, copy_index), normed))
-    w_down = gather_shards(after(quarter(down_weight, copy_index), normed))
     mixed_rows, logs, grads = attend(
-        queries, kv, jnp.broadcast_to(lowest[:, None], (tok_rows, 128)), grad_out
+        queries, kv, jnp.broadcast_to(lowest[:, None], (tok_rows, 128)), after(grad_out, w_down)
     )
 
     hidden = inputs + matmul(mixed_rows, w_out)
     normed_ffn_full, inverse_ffn = norm_forward(hidden, gain_ffn)
     normed_ffn = normed_ffn_full.astype(low)
 
-    x_all, activation, d_gate, d_up, d_normed_parts = feed_forward(
+    x_all, activation, d_gate, d_up, *d_normed_parts = feed_forward(
         normed_ffn, grads, w_gate, w_up, w_down
     )
-    d_normed_ffn = scatter_copies(list(d_normed_parts))
+    own_part, *other_parts = d_normed_parts
+    beside, across = pass_on(*other_parts)
     all_rows = copies * tok_rows
     x_all, grads = x_all.reshape(all_rows, -1), grads.reshape(all_rows, -1)
     activation = activation.reshape(all_rows, -1)
+    d_gate = after(d_gate, beside, across)
     gate_part = contract(d_gate.reshape(all_rows, -1), x_all, 0, 0).astype(low)
+    d_up, activation = after((d_up, activation), gate_part)
+    d_normed_ffn = (
+        own_part.astype(jnp.float32)
+        + swap(beside, 1).astype(jnp.float32)
+        + swap(across, 2).astype(jnp.float32)
+    )
     up_part = contract(d_up.reshape(all_rows, -1), x_all, 0, 0).astype(low)
     down_part = contract(activation, grads, 0, 0).astype(low)
     out_parts = matmul(activation, w_down).astype(low)
@@ -1460,13 +1485,9 @@
     gate_sum = scatter_shards(gate_part)
     up_sum = scatter_shards(up_part)
     down_sum = scatter_shards(down_part)
-    output_grad = outer_sum(mixed_rows, d_branch, 1)
-    own_out, *other_outs = jnp.split(after(out_parts, output_grad), copies)
-    layer_out = hidden + own_out.astype(jnp.float32)
-    for step, part in enumerate(other_outs):
-        layer_out = layer_out + swap(part, step + 1).astype(jnp.float32)
-    layer_out = layer_out.astype(low)
-    d_query_raw, d_kv = attend_back(
+    own_out, *other_outs = jnp.split(after(out_parts, d_mixed), copies)
+    other_outs = [swap(part, step + 1) for step, part in enumerate(other_outs)]
+    d_query_raw, d_kv, output_grad = attend_back(
         queries,
         kv,
         cos_table,
@@ -1475,7 +1496,12 @@
         mixed_rows,
         d_mixed,
         logs,
-    )
+        d_branch,
+    )
+    layer_out = hidden + own_out.astype(jnp.float32)
+    for part in after(other_outs, d_kv):
+        layer_out = layer_out + part.astype(jnp.float32)
+    layer_out = layer_out.astype(low)
     if not one_group:
         d_kv = lax.dynamic_update_slice_in_dim(
             jnp.zeros((fsdp_size * tok_rows, 2 * head_dim), low), d_kv, window_start, 0

time: 925 us -> 1010 us (1.092)
  Pallas kernels: 549 us -> 763 us
  waiting for transfers between devices: 186 us -> 62 us
    pallas_call x3 -> x2, Pallas kernels: 216 us -> 334 us  [the longest x1 177 us: feed_forward(): pl.pallas_call(ffn_kernel, out_shape=(wide, thin, thin, thin, block, bloc...]
    ppermute x7 -> x5, waiting for transfers between devices: 91.6 us -> 26.9 us  [swap(): lax.ppermute(value, 'replica', [(r, r ^ step) for r in range(copies)])]
    all_gather x3, waiting for transfers between devices: 93.8 us -> 34.3 us  [gather_shards(): return lax.all_gather(value, 'fsdp', axis=0, tiled=True)]
    pallas_call x1, Pallas kernels: 165 us -> 214 us  [finish(): pl.pallas_call(functools.partial(finish_kernel, fsdp_size), out_shape=(ja...]
    pallas_call x1, Pallas kernels: 93.8 us -> 141 us  [project(): pl.pallas_call(functools.partial(project_kernel, fsdp_size), out_shape=(j...]
  transfers between devices with their start and end apart: 13 -> 11, of which waited for: 7 -> 3; matrix products, arithmetic and copies ran while one was open for 10% -> 8% of each run, Pallas kernels for 21% -> 37%
where the time goes in v6:
time: 1010 us; the launch traced here: 1000 us
  Pallas kernels  763 us (76%)
  matrix products  82 us (8%)
  waiting for transfers between devices  62 us (6%)
  other arithmetic  39.8 us (4%)
  local copies, waits for them, and re-layouts  35.9 us (4%)
  between operations  14.7 us (1%)
    pallas_call x1, Pallas kernels, finish(): pl.pallas_call(functools.partial(finish_kernel, fsdp_size), out_shape=(ja...  214 us
    pallas_call x1, Pallas kernels, feed_forward(): pl.pallas_call(ffn_kernel, out_shape=(wide, thin, thin, thin, block, bloc...  177 us
    pallas_call x1, Pallas kernels, attend_back(): pl.pallas_call(functools.partial(attend_back_kernel, fsdp_size, tok_rows)...  157 us
    pallas_call x1, Pallas kernels, project(): pl.pallas_call(functools.partial(project_kernel, fsdp_size), out_shape=(j...  141 us
    pallas_call x1, Pallas kernels, attend(): pl.pallas_call(functools.partial(attend_kernel, tok_rows), out_shape=(jax...  74 us
    dot_general x4, matrix products, contract(): lax.dot_general(left, right, (((left_dim,), (right_dim,)), ((), ())), pre...  60.1 us
    all_gather x3, waiting for transfers between devices, gather_shards(): return lax.all_gather(value, 'fsdp', axis=0, tiled=True)  34.3 us
    ppermute x5, waiting for transfers between devices, swap(): lax.ppermute(value, 'replica', [(r, r ^ step) for r in range(copies)])  26.9 us
  transfers between devices with their start and end apart: 11, of which 3 were waited for; matrix products, arithmetic and copies ran while one was open for 8% of the time, Pallas kernels for 37%

profile of v6, /device:TPU:0, one launch (start us, length us, event | category | flops | bytes accessed | tf_op | source)
XLA Modules:
  0.0 1003.4 jit_solution(14757380949990283470)
XLA Ops:
  7.2 1.8 copy-done
  9.0 0.9 constant_dynamic-slice_fusion
  10.0 0.7 stack.21
  10.7 0.7 stack.22
  11.4 0.1 copy.29
  11.6 1.0 fusion.5.kvg_ref
  12.6 0.8 subtract_select_fusion
  13.3 1.0 fusion.6
  14.3 0.2 pad_maximum_fusion.3
  14.5 2.8 dynamic-slice_bitcast_fusion
  17.3 140.8 %project.1 = (bf16[512,2048]{1,0:T(8,128)(2,1)}, bf16[512,2048]{1,0:T(8,128)(2,1)}, f32[8,2048]{1,0:T(8,128)S(1)}, bf16[8,256,2048]{2,1,0:T(8,128)(2,1)}, bf16[8...) custom-call(bf16[512,2048]{1,0:T(8,128)(2,1)} %tokens_ref.3, ...), custom_call_target="tpu_custom_call" | custom-call | flops 4831838208 | bytes 41943040 | tf_op jit(solution)/shard_map/project/pallas_call | solution.py:877
  158.2 1.2 copy-done.14
  159.5 0.7 all-gather.8.cloned.1.call-update
  160.2 0.5 reduce-scatter.8.cloned.1.call-start
  160.8 0.1 broadcast_in_dim.11.low_ref
  160.9 1.6 copy-done.11
  162.5 1.6 copy-done.12
  164.1 74.0 %attend.1 = (bf16[512,2048]{1,0:T(8,128)(2,1)S(1)}, f32[4,4,8,512]{3,2,1,0:T(8,128)S(1)}, bf16[4,512,2048]{2,1,0:T(8,128)(2,1)}) custom-call(bf16[512,2048]{1,0:T(8,128)(2,1)S(1)} %copy-done.12, bf16[4096,256]{1,0:T(8,128)(2,1)S(1)} %bitcast.55, s32[512,128]{1,0:T(8,128)S(1)} %broadcast_in_dim.11.low_ref, bf16[512,2048]{1,0:T(8,128)(2,1)S(1)} %copy-done.2), custom_call_target="tpu_custom_call" | custom-call | flops 62914560000 | bytes 16777216 | tf_op jit(solution)/shard_map/attend/pallas_call | solution.py:390
  238.2 4.6 multiply_reduce_fusion.2
  242.8 2.0 copy-done.16
  244.8 1.7 multiply_convert_fusion.x_ref
  246.6 34.2 %all-gather.8.cloned.1.call-done.up_ref = bf16[1408,2048]{1,0:T(8,128)(2,1)} async-done(((bf16[176,2048]{1,0:T(8,128)(2,1)}), bf16[1408,2048]{1,0:T(8,128)(2,1)}) %all-gather.8.cloned.1.call-update) | async-done | bytes 5767184 | tf_op jit(solution)/shard_map/all_gather | solution.py:1386
  280.8 177.1 %feed_forward.1 = (bf16[4,512,2048]{2,1,0:T(8,128)(2,1)}, bf16[4,512,1408]{2,1,0:T(8,128)(2,1)}, bf16[4,512,1408]{2,1,0:T(8,128)(2,1)}, bf16[4,512,1408]{2,1,0:T...) custom-call(bf16[512,2048]{1,0:T(8,128)(2,1)} %multiply_convert_fusi, ...), custom_call_target="tpu_custom_call" | custom-call | flops 59055800320 | bytes 41943040 | tf_op jit(solution)/shard_map/feed_forward/pallas_call | solution.py:267
  457.9 2.3 convert_element_type.87
  460.2 0.1 slice.48
  460.3 0.5 copy-done.23
  460.9 0.7 fusion.1
  461.6 1.6 pad_maximum_fusion.2
  463.2 1.6 pad_maximum_fusion.1
  464.8 1.0 slice-done
  465.8 0.4 slice-done.3
  466.2 1.4 slice-done.1
  467.6 14.3 %bitcast_convert_fusion.1 = bf16[1408,2048]{1,0:T(8,128)(2,1)} fusion(bf16[4,512,1408]{2,1,0:T(8,128)(2,1)S(1)} %bitcast.71, bf16[4,512,2048]{2,1,0:T(8,128)(2,1)S(1)} %bitcast.69), kind=kOutput, calls=%fused_computation.1 | convolution fusion | flops 11814043648 | bytes 19922944 | tf_op jit(solution)/shard_map/dot_general | solution.py:30
  481.9 17.9 %convolution_convert_fusion.1 = bf16[1408,2048]{1,0:T(8,128)(2,1)} fusion(bf16[2048,1408]{1,0:T(8,128)(2,1)} %bitcast.65, bf16[2048,2048]{1,0:T(8,128)(2,1)} %bitcast.64), kind=kOutput, calls=%fused_computation.3 | convolution fusion | flops 11814043648 | bytes 19922944 | tf_op jit(solution)/shard_map/dot_general | solution.py:30
  499.9 18.0 %bitcast_convert_fusion = bf16[1408,2048]{1,0:T(8,128)(2,1)} fusion(bf16[4,512,1408]{2,1,0:T(8,128)(2,1)} %get-tuple-element.67, bf16[4,512,2048]{2,1,0:T(8,128)(2,1)} %get-tuple-element.64), kind=kOutput, calls=%fused_computation | convolution fusion | flops 11814043648 | bytes 19922944 | tf_op jit(solution)/shard_map/dot_general | solution.py:30
  517.9 0.6 collective-permute-start.1
  518.5 1.5 collective-permute-start
  520.0 17.3 %convolution_convert_fusion = bf16[2048,2048]{1,0:T(8,128)(2,1)S(1)} fusion(bf16[2048,1408]{1,0:T(8,128)(2,1)} %bitcast.66, bf16[1408,2048]{1,0:T(8,128)(2,1)} %all-gather.4.cloned.1.call-done.down_ref), kind=kOutput, calls=%fused_computation.2 | convolution fusion | flops 11815354368 | bytes 19922944 | tf_op jit(solution)/shard_map/dot_general | solution.py:26
  537.3 26.6 %collective-permute-done.1 = bf16[512,2048]{1,0:T(8,128)(2,1)} collective-permute-done((bf16[512,2048]{1,0:T(8,128)(2,1)}, bf16[512,2048]{1,0:T(8,128)(2,1)}, u32[]{:S(2)}, u32[]{:S(2)}) %collective-permute-start.1) | collective-permute-done | bytes 2097184 | tf_op jit(solution)/shard_map/ppermute | solution.py:1373
  564.0 0.3 collective-permute-done
  564.3 4.0 multiply_reduce_fusion
  568.3 5.2 fusion.7
  573.5 9.9 convolution_convert_fusion.2.d_mixed_ref
  583.4 2.8 fusion.9
  586.3 1.3 collective-permute-start.2
  587.6 0.5 collective-permute-start.3
  588.0 1.7 collective-permute-start.4
  589.8 156.9 %attend_back.1 = (bf16[512,2048]{1,0:T(8,128)(2,1)S(1)}, bf16[4096,256]{1,0:T(8,128)(2,1)}, f32[256,2048]{1,0:T(8,128)}) custom-call(bf16[512,2048]{1,0:T(8,128)(2,1)} %get-tuple-element.47.q_ref, bf16[4096,256]{1,0:T(8,128)(2,1)} %bitcast.54, f32[512,128]{1,0:T(8,128)S(1)} %copy-done.5, f32[512,128]{1,0:T(8,128)S(1)} %copy-done.7, ...), custom_call_target="tpu_custom_call" | custom-call | flops 62914560000 | bytes 16777216 | tf_op jit(solution)/shard_map/attend_back/pallas_call | solution.py:548
  746.7 1.3 copy-done.15
  748.0 6.1 add_convert_fusion
  754.2 3.1 pad_maximum_fusion.ffn_ref
  757.3 0.6 broadcast_in_dim.13.term_ref
  757.9 213.9 %finish.1 = (f32[512,2048]{1,0:T(8,128)}, f32[256,2048]{1,0:T(8,128)}, f32[256,384]{1,0:T(8,128)}, bf16[4,3,176,2048]{3,2,1,0:T(8,128)(2,1)}) custom-call(bf16[512,2048]{1,0:T(8,128)(2,1)} %get-tuple-element.54.normed_ref, bf16[512,2048]{1,0:T(8,128)(2,1)} %copy-done.15, bf16[512,2048]{1,0:T(8,128)(2,1)} %tokens_ref.3, ...), custom_call_target="tpu_custom_call" | custom-call | flops 214748364800 | bytes 41943040 | tf_op jit(solution)/shard_map/finish/pallas_call | solution.py:1339
  971.8 1.7 fusion.10
  973.5 1.8 slice_reduce_fusion
  975.3 3.9 fusion.8
  979.1 3.5 bitcast_convert_fusion.2
  982.6 3.5 convert_bitcast_fusion
  986.1 3.5 convert_bitcast_fusion.1
  989.6 2.1 copy.37
  991.7 1.0 copy-done.22
  992.7 1.3 copy.38
  994.0 1.0 copy-done.21
  995.1 1.3 copy.39
  (81 shorter events, 0.6 us)
Async XLA Ops:
  7.2 1.8 copy-start
  7.2 153.6 %all-gather.4.cloned.1.call-start = ((), (), s32[]{:S(2)}) async-start(), calls=%async_computation.3 | async-start | bytes 6488064 | tf_op jit(solution)/shard_map/all_gather | solution.py:1386
  9.9 7.4 copy-start.9
  9.9 236.6 %all-gather.6.cloned.1.call-start = ((), (), s32[]{:S(2)}) async-start(), calls=%async_computation.4 | async-start | bytes 6488064 | tf_op jit(solution)/shard_map/all_gather | solution.py:1386
  11.5 5.8 copy-start.10
  13.3 147.4 %copy-start.25 = (s32[512]{0:T(512)}, s32[512]{0:T(512)S(1)}, u32[]{:S(2)}) copy-start(s32[512]{0:T(512)S(1)} %get-tuple-element.104) | copy-start | bytes 6148
  14.5 143.6 %copy-start.4 = (f32[512,128]{1,0:T(8,128)}, f32[512,128]{1,0:T(8,128)S(1)}, u32[]{:S(2)}) copy-start(f32[512,128]{1,0:T(8,128)S(1)} %get-tuple-element.108.cos_ref) | copy-start | bytes 786436
  14.5 143.6 %copy-start.6 = (f32[512,128]{1,0:T(8,128)}, f32[512,128]{1,0:T(8,128)S(1)}, u32[]{:S(2)}) copy-start(f32[512,128]{1,0:T(8,128)S(1)} %get-tuple-element.109.sin_ref) | copy-start | bytes 786436
  17.3 143.6 %copy-start.2 = (bf16[512,2048]{1,0:T(8,128)(2,1)S(1)}, bf16[512,2048]{1,0:T(8,128)(2,1)}, u32[]{:S(2)}) copy-start(bf16[512,2048]{1,0:T(8,128)(2,1)} %grads_ref) | copy-start | bytes 6291460
  158.2 1.3 copy-start.14
  159.4 78.7 %copy-start.8 = (f32[8,2048]{1,0:T(8,128)}, f32[8,2048]{1,0:T(8,128)S(1)}, u32[]{:S(2)}) copy-start(f32[8,2048]{1,0:T(8,128)S(1)} %get-tuple-element.52.gain_ref) | copy-start | bytes 196612
  159.5 121.3 %all-gather.8.cloned.1.call-start = ((), (), s32[]{:S(2)}) async-start(), calls=%async_computation.5 | async-start | bytes 6488064 | tf_op jit(solution)/shard_map/all_gather | solution.py:1386
  160.2 594.0 %reduce-scatter.8.cloned.1.call-start = ((), (), s32[]{:S(2)}) async-start(), calls=%async_computation.8 | async-start | bytes 6488064 | tf_op jit(solution)/shard_map/reduce_scatter | solution.py:1390
  160.9 1.6 copy-start.11
  162.5 1.6 copy-start.12
  164.1 74.0 %copy-start.27 = (bf16[512,2048]{1,0:T(8,128)(2,1)S(1)}, bf16[512,2048]{1,0:T(8,128)(2,1)}, u32[]{:S(2)}) copy-start(bf16[512,2048]{1,0:T(8,128)(2,1)} %tokens_ref.3) | copy-start | bytes 6291460
  164.1 74.0 %copy-start.28 = (bf16[8,256,2048]{2,1,0:T(8,128)(2,1)S(1)}, bf16[8,256,2048]{2,1,0:T(8,128)(2,1)}, u32[]{:S(2)}) copy-start(bf16[8,256,2048]{2,1,0:T(8,128)(2,1)} %get-tuple-element.51) | copy-start | bytes 25165828
  238.1 4.7 copy-start.13
  242.8 2.0 copy-start.16
  457.9 2.3 copy-start.24
  457.9 2.8 copy-start.23
  460.8 4.0 slice-start.2
  460.9 4.9 slice-start
  460.9 5.3 slice-start.3
  461.6 6.0 slice-start.1
  499.8 254.3 %reduce-scatter.6.cloned.1.call-start = ((), (), s32[]{:S(2)}) async-start(), calls=%async_computation.7 | async-start | bytes 6488064 | tf_op jit(solution)/shard_map/reduce_scatter | solution.py:1390
  517.9 236.3 %reduce-scatter.4.cloned.1.call-start = ((), (), s32[]{:S(2)}) async-start(), calls=%async_computation.6 | async-start | bytes 6488064 | tf_op jit(solution)/shard_map/reduce_scatter | solution.py:1390
  517.9 46.0 %collective-permute-start.1 = (bf16[512,2048]{1,0:T(8,128)(2,1)}, bf16[512,2048]{1,0:T(8,128)(2,1)}, u32[]{:S(2)}, u32[]{:S(2)}) collective-permute-start(bf16[512,2048]{1,0:T(8,128)(2,1)} %pad_maximum_fusion.2), channel_id=1, source_target_pairs={{0,16},{8,24},{16,0},{24,8},{1,17},{9,25},{17,1},{25,9},{2,18},{10... | collective-permute-start | bytes 6291464 | tf_op jit(solution)/shard_map/ppermute | solution.py:1373
  518.5 45.7 %collective-permute-start = (bf16[512,2048]{1,0:T(8,128)(2,1)}, bf16[512,2048]{1,0:T(8,128)(2,1)}, u32[]{:S(2)}, u32[]{:S(2)}) collective-permute-start(bf16[512,2048]{1,0:T(8,128)(2,1)} %pad_maximum_fusion.1), channel_id=1, source_target_pairs={{0,8},{8,0},{16,24},{24,16},{1,9},{9,1},{17,25},{25,17},{2,10},{10... | collective-permute-start | bytes 6291464 | tf_op jit(solution)/shard_map/ppermute | solution.py:1373
  520.0 44.3 %copy-start.17 = (f32[512,2048]{1,0:T(8,128)S(1)}, f32[512,2048]{1,0:T(8,128)}, u32[]{:S(2)}) copy-start(f32[512,2048]{1,0:T(8,128)} %copy-done.16) | copy-start | bytes 12582916
  537.3 46.1 %copy-start.18 = (bf16[2048,2048]{1,0:T(8,128)(2,1)}, bf16[2048,2048]{1,0:T(8,128)(2,1)S(1)}, u32[]{:S(2)}) copy-start(bf16[2048,2048]{1,0:T(8,128)(2,1)S(1)} %convolution_convert_fusion) | copy-start | bytes 25165828
  564.3 4.0 copy-start.3
  573.5 9.9 copy-start.20
  583.4 6.4 copy-start.26
  583.4 6.4 copy-start.5
  583.4 6.3 copy-start.7
  586.3 161.7 %collective-permute-start.2 = (bf16[512,2048]{1,0:T(8,128)(2,1)}, bf16[512,2048]{1,0:T(8,128)(2,1)S(1)}, u32[]{:S(2)}, u32[]{:S(2)}) collective-permute-start(bf16[512,2048]{1,0:T(8,128)(2,1)} %get-tuple-element.94), channel_id=1, source_target_pairs={{0,8},{8,0},{16,24},{24,16},{1,9},{9,1},{17,25},{25,17},{2,10},{10... | collective-permute-start | bytes 6291464 | tf_op jit(solution)/shard_map/ppermute | solution.py:1373
  587.6 160.5 %collective-permute-start.3 = (bf16[512,2048]{1,0:T(8,128)(2,1)}, bf16[512,2048]{1,0:T(8,128)(2,1)}, u32[]{:S(2)}, u32[]{:S(2)}) collective-permute-start(bf16[512,2048]{1,0:T(8,128)(2,1)} %get-tuple-element.93), channel_id=1, source_target_pairs={{0,16},{8,24},{16,0},{24,8},{1,17},{9,25},{17,1},{25,9},{2,18},{10... | collective-permute-start | bytes 6291464 | tf_op jit(solution)/shard_map/ppermute | solution.py:1373
  588.0 160.0 %collective-permute-start.4 = (bf16[512,2048]{1,0:T(8,128)(2,1)}, bf16[512,2048]{1,0:T(8,128)(2,1)}, u32[]{:S(2)}, u32[]{:S(2)}) collective-permute-start(bf16[512,2048]{1,0:T(8,128)(2,1)} %get-tuple-element.92), channel_id=1, source_target_pairs={{0,24},{8,16},{16,8},{24,0},{1,25},{9,17},{17,9},{25,1},{2,26},{10... | collective-permute-start | bytes 6291464 | tf_op jit(solution)/shard_map/ppermute | solution.py:1373
  746.7 1.3 copy-start.15
  986.1 3.5 copy-start.19
  989.6 3.1 copy-start.22
  989.6 6.8 copy-start.1
  992.7 2.3 copy-start.21
Sparse Core Ops, SparseCore 0:
  10.2 85.7 all-gather.3
  159.6 59.8 all-gather.5
  221.7 59.0 all-gather.7
  500.0 62.6 reduce-scatter.7
  565.3 63.2 reduce-scatter.5
  631.3 63.2 reduce-scatter.3

commit v7 on v6

--- a/solution.py
+++ b/solution.py
@@ -79,9 +79,9 @@
 
 
 class Exchange:
-    def __init__(self, buffer, sems):
+    def __init__(self, source, buffer, sems):
         self.replica, self.fsdp = lax.axis_index("replica"), lax.axis_index("fsdp")
-        self.buffer, self.sems = buffer, sems
+        self.source, self.buffer, self.sems = source, buffer, sems
         self.beside, self.across = flip(self.replica, 1), flip(self.replica, 2)
         self.half = buffer.shape[1] // 2
 
@@ -96,8 +96,8 @@
     def copy(self, kind):
         first, second = pl.ds(0, self.half), pl.ds(self.half, self.half)
         source, dest, target = (
-            (self.buffer.at[0], self.buffer.at[1], self.beside),
-            (self.buffer.at[0], self.buffer.at[2], self.across),
+            (self.source, self.buffer.at[1], self.beside),
+            (self.source, self.buffer.at[2], self.across),
             (self.buffer.at[1, first], self.buffer.at[3, first], self.across),
             (self.buffer.at[2, second], self.buffer.at[3, second], self.beside),
         )[kind]
@@ -157,10 +157,9 @@
     x_sems,
     far_sems,
 ):
-    exchange = Exchange(x_all, x_sems)
+    exchange = Exchange(x_ref, x_all, x_sems)
     exchange.greet()
-    own = pltpu.make_async_copy(x_ref, x_all.at[0], load_sems.at[0])
-    own.start()
+    exchange.begin()
     loads = [
         pltpu.make_async_copy(src, dst, load_sems.at[1 + i])
         for i, (src, dst) in enumerate(
@@ -174,8 +173,6 @@
         return pltpu.make_async_copy(source.at[at], block.at[slot], load_sems.at[4 + slot])
 
     fetch(grads_ref, 0, 0).start()
-    own.wait()
-    exchange.begin()
     loads[0].wait()
     rows = d_act.shape[1]
     parts = rows // FFN_ROWS
@@ -218,9 +215,16 @@
             exchange.relay()
         if at == 3:
             exchange.end()
-        load = fetch(x_all, at, 0)
+        load = (
+            fetch(x_all, at, 0)
+            if at
+            else pltpu.make_async_copy(x_ref, block.at[0], load_sems.at[0])
+        )
         load.start()
         load.wait()
+        if at == 0:
+            keep = pltpu.make_async_copy(block.at[0], x_all.at[0], load_sems.at[0])
+            keep.start()
         if turn > 0:
             for store in stores(order[turn - 1]):
                 store.wait()
@@ -245,6 +249,8 @@
 
         for store in stores(at):
             store.start()
+        if at == 0:
+            keep.wait()
         if at == 3:
             far(0).start()
             far(1).start()
@@ -319,20 +325,23 @@
     values,
     top,
     acc,
+    own_rows,
     sems,
     own_sem,
 ):
     factor = 128**-0.5 * LOG2E
 
-    exchange = Exchange(grads_all, sems)
-    own = pltpu.make_async_copy(grads_ref, grads_all.at[0], own_sem)
+    exchange = Exchange(grads_ref, grads_all, sems)
+    load_own = pltpu.make_async_copy(grads_ref, own_rows, own_sem)
+    keep_own = pltpu.make_async_copy(own_rows, grads_all.at[0], own_sem)
 
     @pl.when((pl.program_id(0) == 0) & (pl.program_id(1) == 0))
     def _():
-        own.start()
+        load_own.start()
         exchange.greet()
-        own.wait()
         exchange.begin()
+        load_own.wait()
+        keep_own.start()
         values[:, :128] = kv_ref[:, 128:]
         values[:, 128:] = jnp.ones_like(values[:, 128:])
 
@@ -376,6 +385,7 @@
         (pl.program_id(0) == pl.num_programs(0) - 1) & (pl.program_id(1) == pl.num_programs(1) - 1)
     )
     def _():
+        keep_own.wait()
         exchange.end()
         exchange.drain()
 
@@ -410,6 +420,7 @@
             pltpu.VMEM(kv.shape, jnp.bfloat16),
             pltpu.VMEM((rows, 128), jnp.float32),
             pltpu.VMEM((rows, 256), jnp.float32),
+            pltpu.VMEM(grads.shape, jnp.bfloat16),
             pltpu.SemaphoreType.DMA((2, 4)),
             pltpu.SemaphoreType.DMA,
         ],
@@ -765,12 +776,21 @@
     width = tokens_ref.shape[1]
     partner = (replica, flip(fsdp, 1))
 
+    spare = flip(fsdp, 1)
+    load_own = [
+        pltpu.make_async_copy(kvg_ref, kvg_vmem.at[fsdp], local_sems.at[0]),
+        pltpu.make_async_copy(wq_ref, wq_vmem.at[fsdp], local_sems.at[1]),
+        pltpu.make_async_copy(wo_ref, wq_vmem.at[spare], local_sems.at[2]),
+    ]
     own = [
-        pltpu.make_async_copy(kvg_ref, kvg_all.at[fsdp], local_sems.at[0]),
-        pltpu.make_async_copy(wq_ref, wq_all.at[fsdp], local_sems.at[1]),
-        pltpu.make_async_copy(wo_ref, wo_all.at[fsdp], local_sems.at[2]),
+        pltpu.make_async_copy(kvg_vmem.at[fsdp], kvg_all.at[fsdp], local_sems.at[0]),
+        pltpu.make_async_copy(wq_vmem.at[fsdp], wq_all.at[fsdp], local_sems.at[1]),
+        pltpu.make_async_copy(wq_vmem.at[spare], wo_all.at[fsdp], local_sems.at[2]),
     ]
-    for copy in own:
+    for copy in load_own:
+        copy.start()
+    for load, copy in zip(load_own, own):
+        load.wait()
         copy.start()
     greet(replica, fsdp, at, count)
 
@@ -1219,28 +1239,38 @@
         if lands:
             piece = (beside, across, flip(beside, 2), flip(beside, 2))[kind]
         columns = (slice(None), slice(None), pl.ds(0, half), pl.ds(half, half))[kind]
-        src = ffn_all.at[piece, :, :, columns]
+        dst = ffn_all.at[piece, :, :, columns]
         return pltpu.make_async_remote_copy(
-            src_ref=src,
-            dst_ref=src,
+            src_ref=ffn_ref if kind < 2 and not lands else dst,
+            dst_ref=dst,
             send_sem=ffn_sems.at[0, kind],
             recv_sem=ffn_sems.at[1, kind],
             device_id=((beside, across, across, beside)[kind], fsdp),
             device_id_type=MESH,
         )
 
-    own_ffn = pltpu.make_async_copy(ffn_ref, ffn_all.at[replica], local_sems.at[0])
-    own_ffn.start()
+    ffn_copy(0).start()
+    ffn_copy(1).start()
+    ffn_rows = ffn_ref.shape[1]
+
+    def keep_ffn(part, slot, out):
+        held = wq_buf.at[slot, pl.ds(0, ffn_rows)]
+        place_at = ffn_all.at[replica, part]
+        return pltpu.make_async_copy(
+            held if out else ffn_ref.at[part], place_at if out else held, local_sems.at[0]
+        )
+
     load = pltpu.make_async_copy(d_kv_ref, d_kv.grad, local_sems.at[1])
     load.start()
     load_kvg = pltpu.make_async_copy(kvg_ref, kvg_vmem, local_sems.at[2])
     load_kvg.start()
     load.wait()
     each(count, lambda shard: d_kv.core_copy(shard).start())
-    own_ffn.wait()
-    ffn_copy(0).start()
-    ffn_copy(1).start()
     outer(q_sums, normed_ref, d_q_ref, False)
+    for part in range(3):
+        for out in (False, True):
+            keep_ffn(part, 0, out).start()
+            keep_ffn(part, 0, out).wait()
     each(count, d_kv.core_add)
     d_kv.line_hop(count - 1)
     outer(q_sums, normed_ref, d_q_ref, True)

time: 1010 us -> 878 us (0.87)
  Pallas kernels: 763 us -> 630 us
    pallas_call x1, Pallas kernels: 214 us -> 147 us  [finish(): pl.pallas_call(functools.partial(finish_kernel, fsdp_size), out_shape=(ja...]
    pallas_call x1, Pallas kernels: 177 us -> 112 us  [feed_forward(): pl.pallas_call(ffn_kernel, out_shape=(wide, thin, thin, thin, block, bloc...]
  transfers between devices with their start and end apart: 11 -> 11, of which waited for: 3 -> 3; matrix products, arithmetic and copies ran while one was open for 8% -> 9% of each run, Pallas kernels for 37% -> 42%
where the time goes in v7:
time: 878 us; the launch traced here: 872 us
  Pallas kernels  630 us (72%)
  matrix products  82 us (9%)
  waiting for transfers between devices  63.4 us (7%)
  other arithmetic  39.7 us (5%)
  local copies, waits for them, and re-layouts  35.9 us (4%)
  between operations  14.7 us (2%)
    pallas_call x1, Pallas kernels, attend_back(): pl.pallas_call(functools.partial(attend_back_kernel, fsdp_size, tok_rows)...  157 us
    pallas_call x1, Pallas kernels, finish(): pl.pallas_call(functools.partial(finish_kernel, fsdp_size), out_shape=(ja...  147 us
    pallas_call x1, Pallas kernels, project(): pl.pallas_call(functools.partial(project_kernel, fsdp_size), out_shape=(j...  141 us
    pallas_call x1, Pallas kernels, feed_forward(): pl.pallas_call(ffn_kernel, out_shape=(wide, thin, thin, thin, block, bloc...  112 us
    pallas_call x1, Pallas kernels, attend(): pl.pallas_call(functools.partial(attend_kernel, tok_rows), out_shape=(jax...  72.4 us
    dot_general x4, matrix products, contract(): lax.dot_general(left, right, (((left_dim,), (right_dim,)), ((), ())), pre...  60 us
    all_gather x3, waiting for transfers between devices, gather_shards(): return lax.all_gather(value, 'fsdp', axis=0, tiled=True)  35.7 us
    ppermute x5, waiting for transfers between devices, swap(): lax.ppermute(value, 'replica', [(r, r ^ step) for r in range(copies)])  26.9 us
  transfers between devices with their start and end apart: 11, of which 3 were waited for; matrix products, arithmetic and copies ran while one was open for 9% of the time, Pallas kernels for 42%

profile of v7, /device:TPU:0, one launch (start us, length us, event | category | flops | bytes accessed | tf_op | source)
XLA Modules:
  0.0 872.4 jit_solution(10336685557267415235)
XLA Ops:
  7.2 1.8 copy-done
  9.0 0.9 constant_dynamic-slice_fusion
  10.0 0.7 stack.21
  10.7 0.7 stack.22
  11.4 0.1 copy.29
  11.6 1.0 fusion.5.kvg_ref
  12.6 0.8 subtract_select_fusion
  13.3 1.0 fusion.6
  14.3 0.2 pad_maximum_fusion.3
  14.5 2.8 dynamic-slice_bitcast_fusion
  17.3 141.2 %project.1 = (bf16[512,2048]{1,0:T(8,128)(2,1)}, bf16[512,2048]{1,0:T(8,128)(2,1)}, f32[8,2048]{1,0:T(8,128)S(1)}, bf16[8,256,2048]{2,1,0:T(8,128)(2,1)}, bf16[8...) custom-call(bf16[512,2048]{1,0:T(8,128)(2,1)} %tokens_ref.3, ...), custom_call_target="tpu_custom_call" | custom-call | flops 4831838208 | bytes 41943040 | tf_op jit(solution)/shard_map/project/pallas_call | solution.py:897
  158.6 1.2 copy-done.14
  159.9 0.7 all-gather.8.cloned.1.call-update
  160.6 0.5 reduce-scatter.8.cloned.1.call-start
  161.2 0.1 broadcast_in_dim.11.low_ref
  161.3 1.6 copy-done.11
  162.9 1.6 copy-done.12
  164.5 72.4 %attend.1 = (bf16[512,2048]{1,0:T(8,128)(2,1)S(1)}, f32[4,4,8,512]{3,2,1,0:T(8,128)S(1)}, bf16[4,512,2048]{2,1,0:T(8,128)(2,1)}) custom-call(bf16[512,2048]{1,0:T(8,128)(2,1)S(1)} %copy-done.12, bf16[4096,256]{1,0:T(8,128)(2,1)S(1)} %bitcast.55, s32[512,128]{1,0:T(8,128)S(1)} %broadcast_in_dim.11.low_ref, bf16[512,2048]{1,0:T(8,128)(2,1)S(1)} %copy-done.2), custom_call_target="tpu_custom_call" | custom-call | flops 62914560000 | bytes 16777216 | tf_op jit(solution)/shard_map/attend/pallas_call | solution.py:400
  236.9 4.6 multiply_reduce_fusion.2
  241.6 2.0 copy-done.16
  243.6 1.7 multiply_convert_fusion.x_ref
  245.3 35.7 %all-gather.8.cloned.1.call-done.up_ref = bf16[1408,2048]{1,0:T(8,128)(2,1)} async-done(((bf16[176,2048]{1,0:T(8,128)(2,1)}), bf16[1408,2048]{1,0:T(8,128)(2,1)}) %all-gather.8.cloned.1.call-update) | async-done | bytes 5767184 | tf_op jit(solution)/shard_map/all_gather | solution.py:1416
  281.0 112.5 %feed_forward.1 = (bf16[4,512,2048]{2,1,0:T(8,128)(2,1)}, bf16[4,512,1408]{2,1,0:T(8,128)(2,1)}, bf16[4,512,1408]{2,1,0:T(8,128)(2,1)}, bf16[4,512,1408]{2,1,0:T...) custom-call(bf16[512,2048]{1,0:T(8,128)(2,1)} %multiply_convert_fusi, ...), custom_call_target="tpu_custom_call" | custom-call | flops 59055800320 | bytes 41943040 | tf_op jit(solution)/shard_map/feed_forward/pallas_call | solution.py:273
  393.5 2.3 convert_element_type.87
  395.8 0.1 slice.48
  395.9 0.5 copy-done.23
  396.5 0.7 fusion.1
  397.2 1.6 pad_maximum_fusion.2
  398.8 1.6 pad_maximum_fusion.1
  400.4 1.0 slice-done
  401.4 0.4 slice-done.3
  401.8 1.4 slice-done.1
  403.2 14.3 %bitcast_convert_fusion.1 = bf16[1408,2048]{1,0:T(8,128)(2,1)} fusion(bf16[4,512,1408]{2,1,0:T(8,128)(2,1)S(1)} %bitcast.71, bf16[4,512,2048]{2,1,0:T(8,128)(2,1)S(1)} %bitcast.69), kind=kOutput, calls=%fused_computation.1 | convolution fusion | flops 11814043648 | bytes 19922944 | tf_op jit(solution)/shard_map/dot_general | solution.py:30
  417.5 17.9 %convolution_convert_fusion.1 = bf16[1408,2048]{1,0:T(8,128)(2,1)} fusion(bf16[2048,1408]{1,0:T(8,128)(2,1)} %bitcast.65, bf16[2048,2048]{1,0:T(8,128)(2,1)} %bitcast.64), kind=kOutput, calls=%fused_computation.3 | convolution fusion | flops 11814043648 | bytes 19922944 | tf_op jit(solution)/shard_map/dot_general | solution.py:30
  435.4 17.9 %bitcast_convert_fusion = bf16[1408,2048]{1,0:T(8,128)(2,1)} fusion(bf16[4,512,1408]{2,1,0:T(8,128)(2,1)} %get-tuple-element.67, bf16[4,512,2048]{2,1,0:T(8,128)(2,1)} %get-tuple-element.64), kind=kOutput, calls=%fused_computation | convolution fusion | flops 11814043648 | bytes 19922944 | tf_op jit(solution)/shard_map/dot_general | solution.py:30
  453.5 0.6 collective-permute-start.1
  454.1 1.5 collective-permute-start
  455.6 17.3 %convolution_convert_fusion = bf16[2048,2048]{1,0:T(8,128)(2,1)S(1)} fusion(bf16[2048,1408]{1,0:T(8,128)(2,1)} %bitcast.66, bf16[1408,2048]{1,0:T(8,128)(2,1)} %all-gather.4.cloned.1.call-done.down_ref), kind=kOutput, calls=%fused_computation.2 | convolution fusion | flops 11815354368 | bytes 19922944 | tf_op jit(solution)/shard_map/dot_general | solution.py:26
  472.9 26.7 %collective-permute-done.1 = bf16[512,2048]{1,0:T(8,128)(2,1)} collective-permute-done((bf16[512,2048]{1,0:T(8,128)(2,1)}, bf16[512,2048]{1,0:T(8,128)(2,1)}, u32[]{:S(2)}, u32[]{:S(2)}) %collective-permute-start.1) | collective-permute-done | bytes 2097184 | tf_op jit(solution)/shard_map/ppermute | solution.py:1403
  499.5 0.3 collective-permute-done
  499.8 4.0 multiply_reduce_fusion
  503.8 5.1 fusion.7
  509.0 9.9 %convolution_convert_fusion.2.d_mixed_ref = bf16[512,2048]{1,0:T(8,128)(2,1)} fusion(bf16[512,2048]{1,0:T(8,128)(2,1)S(1)} %get-tuple-element.87.branch_ref, bf16[2048,2048]{1,0:T(8,128)(2,1)} %bitcast.62), kind=kOutput, calls=%fused_computation.14 | convolution fusion | flops 4296015872 | bytes 12582912 | tf_op jit(solution)/shard_map/dot_general | solution.py:30
  518.9 2.8 fusion.9
  521.7 1.4 collective-permute-start.2
  523.1 0.5 collective-permute-start.3
  523.6 1.6 collective-permute-start.4
  525.2 157.0 %attend_back.1 = (bf16[512,2048]{1,0:T(8,128)(2,1)S(1)}, bf16[4096,256]{1,0:T(8,128)(2,1)}, f32[256,2048]{1,0:T(8,128)}) custom-call(bf16[512,2048]{1,0:T(8,128)(2,1)} %get-tuple-element.47.q_ref, bf16[4096,256]{1,0:T(8,128)(2,1)} %bitcast.54, f32[512,128]{1,0:T(8,128)S(1)} %copy-done.5, f32[512,128]{1,0:T(8,128)S(1)} %copy-done.7, ...), custom_call_target="tpu_custom_call" | custom-call | flops 62914560000 | bytes 16777216 | tf_op jit(solution)/shard_map/attend_back/pallas_call | solution.py:559
  682.3 1.3 copy-done.15
  683.6 6.1 add_convert_fusion
  689.7 3.1 pad_maximum_fusion.ffn_ref
  692.9 0.6 broadcast_in_dim.13.term_ref
  693.5 147.2 %finish.1 = (f32[512,2048]{1,0:T(8,128)}, f32[256,2048]{1,0:T(8,128)}, f32[256,384]{1,0:T(8,128)}, bf16[4,3,176,2048]{3,2,1,0:T(8,128)(2,1)}) custom-call(bf16[512,2048]{1,0:T(8,128)(2,1)} %get-tuple-element.54.normed_ref, bf16[512,2048]{1,0:T(8,128)(2,1)} %copy-done.15, bf16[512,2048]{1,0:T(8,128)(2,1)} %tokens_ref.3, ...), custom_call_target="tpu_custom_call" | custom-call | flops 214748364800 | bytes 41943040 | tf_op jit(solution)/shard_map/finish/pallas_call | solution.py:1369
  840.8 1.7 fusion.10
  842.4 1.8 slice_reduce_fusion
  844.2 3.9 fusion.8
  848.1 3.5 bitcast_convert_fusion.2
  851.6 3.5 convert_bitcast_fusion
  855.1 3.5 convert_bitcast_fusion.1
  858.6 2.1 copy.37
  860.7 1.0 copy-done.22
  861.7 1.3 copy.38
  863.0 1.0 copy-done.21
  864.0 1.3 copy.39
  (81 shorter events, 0.6 us)
Async XLA Ops:
  7.2 1.8 copy-start
  7.2 153.9 %all-gather.4.cloned.1.call-start = ((), (), s32[]{:S(2)}) async-start(), calls=%async_computation.3 | async-start | bytes 6488064 | tf_op jit(solution)/shard_map/all_gather | solution.py:1416
  9.9 7.4 copy-start.9
  9.9 235.4 %all-gather.6.cloned.1.call-start = ((), (), s32[]{:S(2)}) async-start(), calls=%async_computation.4 | async-start | bytes 6488064 | tf_op jit(solution)/shard_map/all_gather | solution.py:1416
  11.5 5.8 copy-start.10
  13.3 147.8 %copy-start.25 = (s32[512]{0:T(512)}, s32[512]{0:T(512)S(1)}, u32[]{:S(2)}) copy-start(s32[512]{0:T(512)S(1)} %get-tuple-element.104) | copy-start | bytes 6148
  14.5 144.0 %copy-start.4 = (f32[512,128]{1,0:T(8,128)}, f32[512,128]{1,0:T(8,128)S(1)}, u32[]{:S(2)}) copy-start(f32[512,128]{1,0:T(8,128)S(1)} %get-tuple-element.108.cos_ref) | copy-start | bytes 786436
  14.5 144.0 %copy-start.6 = (f32[512,128]{1,0:T(8,128)}, f32[512,128]{1,0:T(8,128)S(1)}, u32[]{:S(2)}) copy-start(f32[512,128]{1,0:T(8,128)S(1)} %get-tuple-element.109.sin_ref) | copy-start | bytes 786436
  17.3 144.0 %copy-start.2 = (bf16[512,2048]{1,0:T(8,128)(2,1)S(1)}, bf16[512,2048]{1,0:T(8,128)(2,1)}, u32[]{:S(2)}) copy-start(bf16[512,2048]{1,0:T(8,128)(2,1)} %grads_ref) | copy-start | bytes 6291460
  158.6 1.3 copy-start.14
  159.8 77.1 %copy-start.8 = (f32[8,2048]{1,0:T(8,128)}, f32[8,2048]{1,0:T(8,128)S(1)}, u32[]{:S(2)}) copy-start(f32[8,2048]{1,0:T(8,128)S(1)} %get-tuple-element.52.gain_ref) | copy-start | bytes 196612
  159.9 121.1 %all-gather.8.cloned.1.call-start = ((), (), s32[]{:S(2)}) async-start(), calls=%async_computation.5 | async-start | bytes 6488064 | tf_op jit(solution)/shard_map/all_gather | solution.py:1416
  160.6 529.1 %reduce-scatter.8.cloned.1.call-start = ((), (), s32[]{:S(2)}) async-start(), calls=%async_computation.8 | async-start | bytes 6488064 | tf_op jit(solution)/shard_map/reduce_scatter | solution.py:1420
  161.3 1.6 copy-start.11
  162.9 1.6 copy-start.12
  164.5 72.4 %copy-start.27 = (bf16[512,2048]{1,0:T(8,128)(2,1)S(1)}, bf16[512,2048]{1,0:T(8,128)(2,1)}, u32[]{:S(2)}) copy-start(bf16[512,2048]{1,0:T(8,128)(2,1)} %tokens_ref.3) | copy-start | bytes 6291460
  164.5 72.4 %copy-start.28 = (bf16[8,256,2048]{2,1,0:T(8,128)(2,1)S(1)}, bf16[8,256,2048]{2,1,0:T(8,128)(2,1)}, u32[]{:S(2)}) copy-start(bf16[8,256,2048]{2,1,0:T(8,128)(2,1)} %get-tuple-element.51) | copy-start | bytes 25165828
  236.9 4.7 copy-start.13
  241.6 2.0 copy-start.16
  393.5 2.3 copy-start.24
  393.5 2.8 copy-start.23
  396.3 4.0 slice-start.2
  396.5 4.9 slice-start
  396.5 5.3 slice-start.3
  397.2 6.0 slice-start.1
  435.4 254.3 %reduce-scatter.6.cloned.1.call-start = ((), (), s32[]{:S(2)}) async-start(), calls=%async_computation.7 | async-start | bytes 6488064 | tf_op jit(solution)/shard_map/reduce_scatter | solution.py:1420
  453.4 236.3 %reduce-scatter.4.cloned.1.call-start = ((), (), s32[]{:S(2)}) async-start(), calls=%async_computation.6 | async-start | bytes 6488064 | tf_op jit(solution)/shard_map/reduce_scatter | solution.py:1420
  453.5 46.1 %collective-permute-start.1 = (bf16[512,2048]{1,0:T(8,128)(2,1)}, bf16[512,2048]{1,0:T(8,128)(2,1)}, u32[]{:S(2)}, u32[]{:S(2)}) collective-permute-start(bf16[512,2048]{1,0:T(8,128)(2,1)} %pad_maximum_fusion.2), channel_id=1, source_target_pairs={{0,16},{8,24},{16,0},{24,8},{1,17},{9,25},{17,1},{25,9},{2,18},{10... | collective-permute-start | bytes 6291464 | tf_op jit(solution)/shard_map/ppermute | solution.py:1403
  454.1 45.7 %collective-permute-start = (bf16[512,2048]{1,0:T(8,128)(2,1)}, bf16[512,2048]{1,0:T(8,128)(2,1)}, u32[]{:S(2)}, u32[]{:S(2)}) collective-permute-start(bf16[512,2048]{1,0:T(8,128)(2,1)} %pad_maximum_fusion.1), channel_id=1, source_target_pairs={{0,8},{8,0},{16,24},{24,16},{1,9},{9,1},{17,25},{25,17},{2,10},{10... | collective-permute-start | bytes 6291464 | tf_op jit(solution)/shard_map/ppermute | solution.py:1403
  455.6 44.3 %copy-start.17 = (f32[512,2048]{1,0:T(8,128)S(1)}, f32[512,2048]{1,0:T(8,128)}, u32[]{:S(2)}) copy-start(f32[512,2048]{1,0:T(8,128)} %copy-done.16) | copy-start | bytes 12582916
  472.9 46.0 %copy-start.18 = (bf16[2048,2048]{1,0:T(8,128)(2,1)}, bf16[2048,2048]{1,0:T(8,128)(2,1)S(1)}, u32[]{:S(2)}) copy-start(bf16[2048,2048]{1,0:T(8,128)(2,1)S(1)} %convolution_convert_fusion) | copy-start | bytes 25165828
  499.8 4.0 copy-start.3
  508.9 9.9 %copy-start.20 = (bf16[512,2048]{1,0:T(8,128)(2,1)}, bf16[512,2048]{1,0:T(8,128)(2,1)S(1)}, u32[]{:S(2)}) copy-start(bf16[512,2048]{1,0:T(8,128)(2,1)S(1)} %get-tuple-element.87.branch_ref) | copy-start | bytes 6291460
  518.9 6.4 copy-start.26
  518.9 6.4 copy-start.5
  518.9 6.3 copy-start.7
  521.7 161.9 %collective-permute-start.2 = (bf16[512,2048]{1,0:T(8,128)(2,1)}, bf16[512,2048]{1,0:T(8,128)(2,1)S(1)}, u32[]{:S(2)}, u32[]{:S(2)}) collective-permute-start(bf16[512,2048]{1,0:T(8,128)(2,1)} %get-tuple-element.94), channel_id=1, source_target_pairs={{0,8},{8,0},{16,24},{24,16},{1,9},{9,1},{17,25},{25,17},{2,10},{10... | collective-permute-start | bytes 6291464 | tf_op jit(solution)/shard_map/ppermute | solution.py:1403
  523.1 160.5 %collective-permute-start.3 = (bf16[512,2048]{1,0:T(8,128)(2,1)}, bf16[512,2048]{1,0:T(8,128)(2,1)}, u32[]{:S(2)}, u32[]{:S(2)}) collective-permute-start(bf16[512,2048]{1,0:T(8,128)(2,1)} %get-tuple-element.93), channel_id=1, source_target_pairs={{0,16},{8,24},{16,0},{24,8},{1,17},{9,25},{17,1},{25,9},{2,18},{10... | collective-permute-start | bytes 6291464 | tf_op jit(solution)/shard_map/ppermute | solution.py:1403
  523.6 160.0 %collective-permute-start.4 = (bf16[512,2048]{1,0:T(8,128)(2,1)}, bf16[512,2048]{1,0:T(8,128)(2,1)}, u32[]{:S(2)}, u32[]{:S(2)}) collective-permute-start(bf16[512,2048]{1,0:T(8,128)(2,1)} %get-tuple-element.92), channel_id=1, source_target_pairs={{0,24},{8,16},{16,8},{24,0},{1,25},{9,17},{17,9},{25,1},{2,26},{10... | collective-permute-start | bytes 6291464 | tf_op jit(solution)/shard_map/ppermute | solution.py:1403
  682.3 1.3 copy-start.15
  855.1 3.5 copy-start.19
  858.6 3.1 copy-start.22
  858.6 6.8 copy-start.1
  861.7 2.3 copy-start.21
Sparse Core Ops, SparseCore 0:
  10.2 85.6 all-gather.3
  160.0 59.6 all-gather.5
  221.9 59.0 all-gather.7
  435.5 62.7 reduce-scatter.7
  501.0 63.2 reduce-scatter.5
  567.0 63.2 reduce-scatter.3

commit v8 on v7

--- a/solution.py
+++ b/solution.py
@@ -143,6 +143,10 @@
     d_x_beside,
     d_x_across,
     d_x_got,
+    out_own,
+    out_beside,
+    out_across,
+    out_got,
     gate_w,
     up_w,
     down_w,
@@ -152,6 +156,8 @@
     d_gate,
     d_up,
     d_x,
+    out,
+    out_far,
     load_sems,
     store_sems,
     x_sems,
@@ -193,18 +199,20 @@
         pairs = [(act, act_all.at[at]), (d_gate, d_gate_all.at[at]), (d_up, d_up_all.at[at])]
         if at < 3:
             pairs.append((d_x, (d_x_own, d_x_beside, d_x_across)[at]))
+            pairs.append((out, (out_own, out_beside, out_across)[at]))
         return [
             pltpu.make_async_copy(src, dst, store_sems.at[i])
             for i, (src, dst) in enumerate(pairs)
         ]
 
-    def far(half):
-        size = rows // 2
+    def far(kind):
+        size, half = rows // 2, kind % 2
+        source = block.at[1] if kind < 2 else out_far
         return pltpu.make_async_remote_copy(
-            src_ref=block.at[1, pl.ds(half * size, size)],
-            dst_ref=d_x_got.at[half],
-            send_sem=far_sems.at[0, half],
-            recv_sem=far_sems.at[1, half],
+            src_ref=source.at[pl.ds(half * size, size)],
+            dst_ref=(d_x_got if kind < 2 else out_got).at[half],
+            send_sem=far_sems.at[0, kind],
+            recv_sem=far_sems.at[1, kind],
             device_id=((exchange.beside, exchange.across)[half], exchange.fsdp),
             device_id_type=MESH,
         )
@@ -243,6 +251,9 @@
             by_up = (d * swish).astype(jnp.bfloat16)
             d_gate[some] = by_gate
             d_up[some] = by_up
+            (out_far if at == 3 else out)[some] = matmul(act[some], down_w[...]).astype(
+                jnp.bfloat16
+            )
             (block.at[1] if at == 3 else d_x)[some] = (
                 matmul(by_gate, gate_w[...]) + matmul(by_up, up_w[...])
             ).astype(jnp.bfloat16)
@@ -252,12 +263,12 @@
         if at == 0:
             keep.wait()
         if at == 3:
-            far(0).start()
-            far(1).start()
+            for kind in range(4):
+                far(kind).start()
     for store in stores(order[3]):
         store.wait()
-    far(0).wait()
-    far(1).wait()
+    for kind in range(4):
+        far(kind).wait()
     exchange.drain()
 
 
@@ -272,9 +283,9 @@
     thin = jax.ShapeDtypeStruct((4, rows, hidden), low)
     return pl.pallas_call(
         ffn_kernel,
-        out_shape=(wide, thin, thin, thin, block, block, block, halves),
+        out_shape=(wide, thin, thin, thin, block, block, block, halves, block, block, block, halves),
         in_specs=[hbm] * 5,
-        out_specs=(hbm,) * 8,
+        out_specs=(hbm,) * 12,
         scratch_shapes=[pltpu.VMEM((hidden, width), low)] * 3
         + [
             pltpu.VMEM((2, rows, width), low),
@@ -283,10 +294,12 @@
             pltpu.VMEM((rows, hidden), low),
             pltpu.VMEM((rows, hidden), low),
             pltpu.VMEM((rows, width), low),
+            pltpu.VMEM((rows, width), low),
+            pltpu.VMEM((rows, width), low),
             dma((6,)),
-            dma((4,)),
+            dma((5,)),
             dma((2, 4)),
-            dma((2, 2)),
+            dma((2, 4)),
         ],
         compiler_params=pltpu.CompilerParams(
             collective_id=3, has_side_effects=True, vmem_limit_bytes=50 << 20
@@ -1486,11 +1499,11 @@
     normed_ffn_full, inverse_ffn = norm_forward(hidden, gain_ffn)
     normed_ffn = normed_ffn_full.astype(low)
 
-    x_all, activation, d_gate, d_up, *d_normed_parts = feed_forward(
+    x_all, activation, d_gate, d_up, *parts = feed_forward(
         normed_ffn, grads, w_gate, w_up, w_down
     )
-    own_part, *other_parts = d_normed_parts
-    beside, across = pass_on(*other_parts)
+    own_part, own_out = parts[0], parts[4]
+    beside, across = pass_on(*parts[1:4])
     all_rows = copies * tok_rows
     x_all, grads = x_all.reshape(all_rows, -1), grads.reshape(all_rows, -1)
     activation = activation.reshape(all_rows, -1)
@@ -1504,7 +1517,6 @@
     )
     up_part = contract(d_up.reshape(all_rows, -1), x_all, 0, 0).astype(low)
     down_part = contract(activation, grads, 0, 0).astype(low)
-    out_parts = matmul(activation, w_down).astype(low)
 
     cotangent = grad_out.astype(jnp.float32)
     resid_ffn, ffn_gain_term = norm_backward(hidden, inverse_ffn, gain_ffn, d_normed_ffn)
@@ -1515,8 +1527,9 @@
     gate_sum = scatter_shards(gate_part)
     up_sum = scatter_shards(up_part)
     down_sum = scatter_shards(down_part)
-    own_out, *other_outs = jnp.split(after(out_parts, d_mixed), copies)
-    other_outs = [swap(part, step + 1) for step, part in enumerate(other_outs)]
+    out_beside, out_across = pass_on(*after(parts[5:8], down_part))
+    out_beside, out_across = after((out_beside, out_across), d_mixed)
+    other_outs = [swap(out_beside, 1), swap(out_across, 2)]
     d_query_raw, d_kv, output_grad = attend_back(
         queries,
         kv,

time: 878 us -> 869 us (0.990)
  matrix products: 82 us -> 61.1 us
  waiting for transfers between devices: 63.4 us -> 74.2 us
    pallas_call x1, Pallas kernels: 112 us -> 138 us  [feed_forward(): pl.pallas_call(ffn_kernel, out_shape=(wide, thin, thin, thin, block, bloc...]
    pallas_call x1, Pallas kernels: 157 us -> 133 us  [attend_back(): pl.pallas_call(functools.partial(attend_back_kernel, fsdp_size, tok_rows)...]
    dot_general x2 -> x1, matrix products: 21.9 us -> 4.65 us  [matmul(): return jnp.dot(left, right, preferred_element_type=jnp.float32)]
    ppermute x5 -> x4, waiting for transfers between devices: 26.9 us -> 37.6 us  [swap(): lax.ppermute(value, 'replica', [(r, r ^ step) for r in range(copies)])]
    unnamed x69 -> x77, local copies, waits for them, and re-layouts: 19.6 us -> 20.1 us
  transfers between devices with their start and end apart: 11 -> 10, of which waited for: 3 -> 3; matrix products, arithmetic and copies ran while one was open for 9% -> 7% of each run, Pallas kernels for 42% -> 40%
where the time goes in v8:
time: 869 us; the launch traced here: 864 us
  Pallas kernels  631 us (73%)
  waiting for transfers between devices  74.2 us (9%)
  matrix products  61.1 us (7%)
  other arithmetic  45.2 us (5%)
  local copies, waits for them, and re-layouts  33.7 us (4%)
  between operations  14.9 us (2%)
    pallas_call x1, Pallas kernels, finish(): pl.pallas_call(functools.partial(finish_kernel, fsdp_size), out_shape=(ja...  146 us
    pallas_call x1, Pallas kernels, project(): pl.pallas_call(functools.partial(project_kernel, fsdp_size), out_shape=(j...  141 us
    pallas_call x1, Pallas kernels, feed_forward(): pl.pallas_call(ffn_kernel, out_shape=(wide, thin, thin, thin, block, bloc...  138 us
    pallas_call x1, Pallas kernels, attend_back(): pl.pallas_call(functools.partial(attend_back_kernel, fsdp_size, tok_rows)...  133 us
    pallas_call x1, Pallas kernels, attend(): pl.pallas_call(functools.partial(attend_kernel, tok_rows), out_shape=(jax...  72.4 us
    dot_general x4, matrix products, contract(): lax.dot_general(left, right, (((left_dim,), (right_dim,)), ((), ())), pre...  56.4 us
    ppermute x4, waiting for transfers between devices, swap(): lax.ppermute(value, 'replica', [(r, r ^ step) for r in range(copies)])  37.6 us
    all_gather x3, waiting for transfers between devices, gather_shards(): return lax.all_gather(value, 'fsdp', axis=0, tiled=True)  35.9 us
  transfers between devices with their start and end apart: 10, of which 3 were waited for; matrix products, arithmetic and copies ran while one was open for 7% of the time, Pallas kernels for 40%

profile of v8, /device:TPU:0, one launch (start us, length us, event | category | flops | bytes accessed | tf_op | source)
XLA Modules:
  0.0 864.1 jit_solution(479807621619364764)
XLA Ops:
  7.2 1.8 copy-done
  9.0 0.9 constant_dynamic-slice_fusion
  10.0 0.7 stack.21
  10.7 0.7 stack.22
  11.4 0.1 copy.29
  11.6 1.0 fusion.9.kvg_ref
  12.6 0.8 subtract_select_fusion
  13.3 1.0 fusion.10
  14.3 0.2 pad_maximum_fusion.5
  14.5 2.8 dynamic-slice_bitcast_fusion
  17.3 141.3 %project.1 = (bf16[512,2048]{1,0:T(8,128)(2,1)}, bf16[512,2048]{1,0:T(8,128)(2,1)}, f32[8,2048]{1,0:T(8,128)S(1)}, bf16[8,256,2048]{2,1,0:T(8,128)(2,1)}, bf16[8...) custom-call(bf16[512,2048]{1,0:T(8,128)(2,1)} %tokens_ref.3, ...), custom_call_target="tpu_custom_call" | custom-call | flops 4831838208 | bytes 41943040 | tf_op jit(solution)/shard_map/project/pallas_call | solution.py:910
  158.7 1.2 copy-done.14
  159.9 0.7 all-gather.8.cloned.1.call-update
  160.6 0.2 reduce-scatter.6.cloned.1.call-start
  161.0 1.6 copy-done.11
  162.6 1.6 copy-done.12
  164.2 72.4 %attend.1 = (bf16[512,2048]{1,0:T(8,128)(2,1)S(1)}, f32[4,4,8,512]{3,2,1,0:T(8,128)S(1)}, bf16[4,512,2048]{2,1,0:T(8,128)(2,1)}) custom-call(bf16[512,2048]{1,0:T(8,128)(2,1)S(1)} %copy-done.12, bf16[4096,256]{1,0:T(8,128)(2,1)S(1)} %bitcast.65, s32[512,128]{1,0:T(8,128)S(1)} %broadcast_in_dim.11.low_ref, bf16[512,2048]{1,0:T(8,128)(2,1)S(1)} %copy-done.2), custom_call_target="tpu_custom_call" | custom-call | flops 62914560000 | bytes 16777216 | tf_op jit(solution)/shard_map/attend/pallas_call | solution.py:413
  236.7 4.6 multiply_reduce_fusion.2
  241.3 2.0 copy-done.16
  243.3 1.7 multiply_convert_fusion.x_ref
  245.1 35.9 %all-gather.8.cloned.1.call-done.up_ref = bf16[1408,2048]{1,0:T(8,128)(2,1)} async-done(((bf16[176,2048]{1,0:T(8,128)(2,1)}), bf16[1408,2048]{1,0:T(8,128)(2,1)}) %all-gather.8.cloned.1.call-update) | async-done | bytes 5767184 | tf_op jit(solution)/shard_map/all_gather | solution.py:1429
  280.9 138.2 %feed_forward.1 = (bf16[4,512,2048]{2,1,0:T(8,128)(2,1)}, bf16[4,512,1408]{2,1,0:T(8,128)(2,1)}, bf16[4,512,1408]{2,1,0:T(8,128)(2,1)}, bf16[4,512,1408]{2,1,0:T...) custom-call(bf16[512,2048]{1,0:T(8,128)(2,1)} %multiply_convert_fusi, ...), custom_call_target="tpu_custom_call" | custom-call | flops 59055800320 | bytes 41943040 | tf_op jit(solution)/shard_map/feed_forward/pallas_call | solution.py:284
  419.2 2.3 convert_element_type.95
  421.6 0.5 copy-done.25
  422.1 0.7 fusion.5
  422.9 1.6 pad_maximum_fusion.2
  424.5 1.6 pad_maximum_fusion.1
  426.1 1.0 slice-done.2
  427.0 0.4 slice-done.5
  427.4 1.4 slice-done.3
  428.9 14.1 %bitcast_convert_fusion.1 = bf16[1408,2048]{1,0:T(8,128)(2,1)} fusion(bf16[4,512,1408]{2,1,0:T(8,128)(2,1)S(1)} %bitcast.82, bf16[4,512,2048]{2,1,0:T(8,128)(2,1)S(1)} %bitcast.80), kind=kOutput, calls=%fused_computation.1 | convolution fusion | flops 11814043648 | bytes 19922944 | tf_op jit(solution)/shard_map/dot_general | solution.py:30
  443.0 18.3 %bitcast_convert_fusion = bf16[1408,2048]{1,0:T(8,128)(2,1)} fusion(bf16[4,512,1408]{2,1,0:T(8,128)(2,1)} %get-tuple-element.81, bf16[4,512,2048]{2,1,0:T(8,128)(2,1)} %get-tuple-element.75), kind=kOutput, calls=%fused_computation | convolution fusion | flops 11814043648 | bytes 19922944 | tf_op jit(solution)/shard_map/dot_general | solution.py:30
  461.3 18.0 %convolution_convert_fusion = bf16[1408,2048]{1,0:T(8,128)(2,1)} fusion(bf16[2048,1408]{1,0:T(8,128)(2,1)} %bitcast.77, bf16[2048,2048]{1,0:T(8,128)(2,1)} %bitcast.76), kind=kOutput, calls=%fused_computation.2 | convolution fusion | flops 11814043648 | bytes 19922944 | tf_op jit(solution)/shard_map/dot_general | solution.py:30
  479.4 0.6 collective-permute-start.1
  480.0 1.5 collective-permute-start
  481.5 2.3 convert_element_type.100
  483.8 0.6 copy-done.23
  484.5 0.7 fusion.1
  485.2 1.5 pad_maximum_fusion.4
  486.7 1.5 pad_maximum_fusion.3
  488.1 37.3 %collective-permute-done.1 = bf16[512,2048]{1,0:T(8,128)(2,1)} collective-permute-done((bf16[512,2048]{1,0:T(8,128)(2,1)}, bf16[512,2048]{1,0:T(8,128)(2,1)}, u32[]{:S(2)}, u32[]{:S(2)}) %collective-permute-start.1) | collective-permute-done | bytes 2097184 | tf_op jit(solution)/shard_map/ppermute | solution.py:1416
  525.4 0.3 collective-permute-done
  525.7 4.0 multiply_reduce_fusion
  529.7 5.8 fusion.11
  535.6 6.0 convolution_convert_fusion.1.d_mixed_ref
  541.6 1.2 collective-permute-start.2
  542.8 0.4 collective-permute-start.3
  543.2 132.6 %attend_back.1 = (bf16[512,2048]{1,0:T(8,128)(2,1)S(1)}, bf16[4096,256]{1,0:T(8,128)(2,1)}, f32[256,2048]{1,0:T(8,128)}) custom-call(bf16[512,2048]{1,0:T(8,128)(2,1)} %get-tuple-element.54.q_ref, bf16[4096,256]{1,0:T(8,128)(2,1)} %bitcast.64, f32[512,128]{1,0:T(8,128)S(1)} %copy-done.5, f32[512,128]{1,0:T(8,128)S(1)} %copy-done.7, ...), custom_call_target="tpu_custom_call" | custom-call | flops 62914560000 | bytes 16777216 | tf_op jit(solution)/shard_map/attend_back/pallas_call | solution.py:572
  675.8 1.3 copy-done.15
  677.1 5.0 add_convert_fusion
  682.1 3.1 pad_maximum_fusion.ffn_ref
  685.3 0.6 broadcast_in_dim.13.term_ref
  685.9 146.5 %finish.1 = (f32[512,2048]{1,0:T(8,128)}, f32[256,2048]{1,0:T(8,128)}, f32[256,384]{1,0:T(8,128)}, bf16[4,3,176,2048]{3,2,1,0:T(8,128)(2,1)}) custom-call(bf16[512,2048]{1,0:T(8,128)(2,1)} %get-tuple-element.61.normed_ref, bf16[512,2048]{1,0:T(8,128)(2,1)} %copy-done.15, bf16[512,2048]{1,0:T(8,128)(2,1)} %tokens_ref.3, ...), custom_call_target="tpu_custom_call" | custom-call | flops 214748364800 | bytes 41943040 | tf_op jit(solution)/shard_map/finish/pallas_call | solution.py:1382
  832.4 1.7 fusion.13
  834.1 1.8 slice_reduce_fusion
  835.9 3.9 fusion.12
  839.7 3.5 bitcast_convert_fusion.2
  843.2 3.5 convert_bitcast_fusion
  846.7 3.5 convert_bitcast_fusion.1
  850.2 2.1 copy.37
  852.3 1.0 copy-done.21
  853.3 1.3 copy.38
  854.6 1.0 copy-done.20
  855.6 1.3 copy.39
  (92 shorter events, 1.0 us)
Async XLA Ops:
  7.2 1.8 copy-start
  7.2 153.7 %all-gather.4.cloned.1.call-start = ((), (), s32[]{:S(2)}) async-start(), calls=%async_computation.3 | async-start | bytes 6488064 | tf_op jit(solution)/shard_map/all_gather | solution.py:1429
  9.9 7.4 copy-start.9
  9.9 235.1 %all-gather.6.cloned.1.call-start = ((), (), s32[]{:S(2)}) async-start(), calls=%async_computation.4 | async-start | bytes 6488064 | tf_op jit(solution)/shard_map/all_gather | solution.py:1429
  11.5 5.8 copy-start.10
  13.3 147.6 %copy-start.27 = (s32[512]{0:T(512)}, s32[512]{0:T(512)S(1)}, u32[]{:S(2)}) copy-start(s32[512]{0:T(512)S(1)} %get-tuple-element.117) | copy-start | bytes 6148
  14.5 144.1 %copy-start.4 = (f32[512,128]{1,0:T(8,128)}, f32[512,128]{1,0:T(8,128)S(1)}, u32[]{:S(2)}) copy-start(f32[512,128]{1,0:T(8,128)S(1)} %get-tuple-element.121.cos_ref) | copy-start | bytes 786436
  14.5 144.1 %copy-start.6 = (f32[512,128]{1,0:T(8,128)}, f32[512,128]{1,0:T(8,128)S(1)}, u32[]{:S(2)}) copy-start(f32[512,128]{1,0:T(8,128)S(1)} %get-tuple-element.122.sin_ref) | copy-start | bytes 786436
  17.3 143.7 %copy-start.2 = (bf16[512,2048]{1,0:T(8,128)(2,1)S(1)}, bf16[512,2048]{1,0:T(8,128)(2,1)}, u32[]{:S(2)}) copy-start(bf16[512,2048]{1,0:T(8,128)(2,1)} %grads_ref) | copy-start | bytes 6291460
  158.7 1.2 copy-start.14
  159.9 76.8 %copy-start.8 = (f32[8,2048]{1,0:T(8,128)}, f32[8,2048]{1,0:T(8,128)S(1)}, u32[]{:S(2)}) copy-start(f32[8,2048]{1,0:T(8,128)S(1)} %get-tuple-element.59.gain_ref) | copy-start | bytes 196612
  159.9 121.1 %all-gather.8.cloned.1.call-start = ((), (), s32[]{:S(2)}) async-start(), calls=%async_computation.5 | async-start | bytes 6488064 | tf_op jit(solution)/shard_map/all_gather | solution.py:1429
  160.6 521.5 %reduce-scatter.6.cloned.1.call-start = ((), (), s32[]{:S(2)}) async-start(), calls=%async_computation.7 | async-start | bytes 6488064 | tf_op jit(solution)/shard_map/reduce_scatter | solution.py:1433
  161.0 1.6 copy-start.11
  162.6 1.6 copy-start.12
  164.2 72.4 %copy-start.29 = (bf16[512,2048]{1,0:T(8,128)(2,1)S(1)}, bf16[512,2048]{1,0:T(8,128)(2,1)}, u32[]{:S(2)}) copy-start(bf16[512,2048]{1,0:T(8,128)(2,1)} %tokens_ref.3) | copy-start | bytes 6291460
  164.2 72.4 %copy-start.30 = (bf16[8,256,2048]{2,1,0:T(8,128)(2,1)S(1)}, bf16[8,256,2048]{2,1,0:T(8,128)(2,1)}, u32[]{:S(2)}) copy-start(bf16[8,256,2048]{2,1,0:T(8,128)(2,1)} %get-tuple-element.58) | copy-start | bytes 25165828
  236.6 4.7 copy-start.13
  241.3 2.0 copy-start.16
  419.2 2.3 copy-start.26
  419.2 2.8 copy-start.25
  422.0 4.1 slice-start.4
  422.1 4.9 slice-start.2
  422.1 5.3 slice-start.5
  422.9 6.0 slice-start.3
  461.3 220.8 %reduce-scatter.8.cloned.1.call-start = ((), (), s32[]{:S(2)}) async-start(), calls=%async_computation.8 | async-start | bytes 6488064 | tf_op jit(solution)/shard_map/reduce_scatter | solution.py:1433
  479.4 202.8 %reduce-scatter.4.cloned.1.call-start = ((), (), s32[]{:S(2)}) async-start(), calls=%async_computation.6 | async-start | bytes 6488064 | tf_op jit(solution)/shard_map/reduce_scatter | solution.py:1433
  479.4 46.0 %collective-permute-start.1 = (bf16[512,2048]{1,0:T(8,128)(2,1)}, bf16[512,2048]{1,0:T(8,128)(2,1)}, u32[]{:S(2)}, u32[]{:S(2)}) collective-permute-start(bf16[512,2048]{1,0:T(8,128)(2,1)} %pad_maximum_fusion.2), channel_id=1, source_target_pairs={{0,16},{8,24},{16,0},{24,8},{1,17},{9,25},{17,1},{25,9},{2,18},{10... | collective-permute-start | bytes 6291464 | tf_op jit(solution)/shard_map/ppermute | solution.py:1416
  480.0 45.7 %collective-permute-start = (bf16[512,2048]{1,0:T(8,128)(2,1)}, bf16[512,2048]{1,0:T(8,128)(2,1)}, u32[]{:S(2)}, u32[]{:S(2)}) collective-permute-start(bf16[512,2048]{1,0:T(8,128)(2,1)} %pad_maximum_fusion.1), channel_id=1, source_target_pairs={{0,8},{8,0},{16,24},{24,16},{1,9},{9,1},{17,25},{25,17},{2,10},{10... | collective-permute-start | bytes 6291464 | tf_op jit(solution)/shard_map/ppermute | solution.py:1416
  481.5 2.3 copy-start.24
  481.5 2.9 copy-start.23
  485.2 40.5 %copy-start.17 = (f32[512,2048]{1,0:T(8,128)S(1)}, f32[512,2048]{1,0:T(8,128)}, u32[]{:S(2)}) copy-start(f32[512,2048]{1,0:T(8,128)} %copy-done.16) | copy-start | bytes 12582916
  525.7 4.0 copy-start.3
  525.7 9.8 %slice-start = ((s8[8388608]{0:T(1024)(128)(4,1)}), s8[4194304]{0:T(1024)(128)(4,1)S(1)}, s32[]{:S(2)}) async-start(s8[8388608]{0:T(1024)(128)(4,1)} %bitcast.73), calls=%async_computation.9 | async-start | bytes 8388608
  529.7 5.8 slice-start.1
  535.5 6.1 copy-start.19
  535.6 7.7 copy-start.28
  535.6 7.6 copy-start.5
  535.6 7.6 copy-start.7
  541.6 135.5 %collective-permute-start.2 = (bf16[512,2048]{1,0:T(8,128)(2,1)}, bf16[512,2048]{1,0:T(8,128)(2,1)}, u32[]{:S(2)}, u32[]{:S(2)}) collective-permute-start(bf16[512,2048]{1,0:T(8,128)(2,1)} %pad_maximum_fusion.3), channel_id=1, source_target_pairs={{0,8},{8,0},{16,24},{24,16},{1,9},{9,1},{17,25},{25,17},{2,10},{10... | collective-permute-start | bytes 6291464 | tf_op jit(solution)/shard_map/ppermute | solution.py:1416
  542.8 134.3 %collective-permute-start.3 = (bf16[512,2048]{1,0:T(8,128)(2,1)}, bf16[512,2048]{1,0:T(8,128)(2,1)}, u32[]{:S(2)}, u32[]{:S(2)}) collective-permute-start(bf16[512,2048]{1,0:T(8,128)(2,1)} %pad_maximum_fusion.4), channel_id=1, source_target_pairs={{0,16},{8,24},{16,0},{24,8},{1,17},{9,25},{17,1},{25,9},{2,18},{10... | collective-permute-start | bytes 6291464 | tf_op jit(solution)/shard_map/ppermute | solution.py:1416
  543.2 133.9 %copy-start.22 = (bf16[512,2048]{1,0:T(8,128)(2,1)S(1)}, bf16[512,2048]{1,0:T(8,128)(2,1)}, u32[]{:S(2)}) copy-start(bf16[512,2048]{1,0:T(8,128)(2,1)} %get-tuple-element.64) | copy-start | bytes 6291460
  675.8 1.3 copy-start.15
  846.7 3.5 copy-start.18
  850.2 3.1 copy-start.21
  850.2 6.8 copy-start.1
  853.3 2.3 copy-start.20
Sparse Core Ops, SparseCore 0:
  10.2 85.6 all-gather.3
  160.0 59.5 all-gather.5
  221.9 59.0 all-gather.7
  461.4 62.6 reduce-scatter.5
  526.8 63.2 reduce-scatter.7
  592.8 80.0 reduce-scatter.3

commit v9 on v8

--- a/solution.py
+++ b/solution.py
@@ -1509,11 +1509,10 @@
     activation = activation.reshape(all_rows, -1)
     d_gate = after(d_gate, beside, across)
     gate_part = contract(d_gate.reshape(all_rows, -1), x_all, 0, 0).astype(low)
-    d_up, activation = after((d_up, activation), gate_part)
+    beside, across = swap(beside, 1), swap(across, 2)
+    d_up, activation = after((d_up, activation), gate_part, beside, across)
     d_normed_ffn = (
-        own_part.astype(jnp.float32)
-        + swap(beside, 1).astype(jnp.float32)
-        + swap(across, 2).astype(jnp.float32)
+        own_part.astype(jnp.float32) + beside.astype(jnp.float32) + across.astype(jnp.float32)
     )
     up_part = contract(d_up.reshape(all_rows, -1), x_all, 0, 0).astype(low)
     down_part = contract(activation, grads, 0, 0).astype(low)

time: 869 us -> 866 us (level)
  Pallas kernels: 631 us -> 621 us
    pallas_call x1, Pallas kernels: 133 us -> 121 us  [attend_back(): pl.pallas_call(functools.partial(attend_back_kernel, fsdp_size, tok_rows)...]
    unnamed x77 -> x75, local copies, waits for them, and re-layouts: 20.1 us -> 19.2 us
  transfers between devices with their start and end apart: 10 -> 10, of which waited for: 3 -> 3; matrix products, arithmetic and copies ran while one was open for 7% -> 9% of each run, Pallas kernels for 40% -> 39%
where the time goes in v9:
time: 866 us; the launch traced here: 861 us
  Pallas kernels  621 us (72%)
  waiting for transfers between devices  79.3 us (9%)
  matrix products  62.7 us (7%)
  other arithmetic  45.7 us (5%)
  local copies, waits for them, and re-layouts  32.9 us (4%)
  between operations  14.9 us (2%)
    pallas_call x1, Pallas kernels, finish(): pl.pallas_call(functools.partial(finish_kernel, fsdp_size), out_shape=(ja...  148 us
    pallas_call x1, Pallas kernels, project(): pl.pallas_call(functools.partial(project_kernel, fsdp_size), out_shape=(j...  141 us
    pallas_call x1, Pallas kernels, feed_forward(): pl.pallas_call(ffn_kernel, out_shape=(wide, thin, thin, thin, block, bloc...  138 us
    pallas_call x1, Pallas kernels, attend_back(): pl.pallas_call(functools.partial(attend_back_kernel, fsdp_size, tok_rows)...  121 us
    pallas_call x1, Pallas kernels, attend(): pl.pallas_call(functools.partial(attend_kernel, tok_rows), out_shape=(jax...  72.4 us
    dot_general x4, matrix products, contract(): lax.dot_general(left, right, (((left_dim,), (right_dim,)), ((), ())), pre...  56.6 us
    ppermute x4, waiting for transfers between devices, swap(): lax.ppermute(value, 'replica', [(r, r ^ step) for r in range(copies)])  44.3 us
    all_gather x3, waiting for transfers between devices, gather_shards(): return lax.all_gather(value, 'fsdp', axis=0, tiled=True)  34.2 us
  transfers between devices with their start and end apart: 10, of which 3 were waited for; matrix products, arithmetic and copies ran while one was open for 9% of the time, Pallas kernels for 39%

profile of v9, /device:TPU:0, one launch (start us, length us, event | category | flops | bytes accessed | tf_op | source)
XLA Modules:
  0.0 860.9 jit_solution(15560008333972427919)
XLA Ops:
  7.2 1.8 copy-done
  9.0 0.9 constant_dynamic-slice_fusion
  10.0 0.7 stack.21
  10.7 0.7 stack.22
  11.4 0.1 copy.29
  11.6 1.0 fusion.9.kvg_ref
  12.6 0.8 subtract_select_fusion
  13.3 1.0 fusion.10
  14.3 0.2 pad_maximum_fusion.5
  14.5 2.8 dynamic-slice_bitcast_fusion
  17.3 141.3 %project.1 = (bf16[512,2048]{1,0:T(8,128)(2,1)}, bf16[512,2048]{1,0:T(8,128)(2,1)}, f32[8,2048]{1,0:T(8,128)S(1)}, bf16[8,256,2048]{2,1,0:T(8,128)(2,1)}, bf16[8...) custom-call(bf16[512,2048]{1,0:T(8,128)(2,1)} %tokens_ref.3, ...), custom_call_target="tpu_custom_call" | custom-call | flops 4831838208 | bytes 41943040 | tf_op jit(solution)/shard_map/project/pallas_call | solution.py:910
  158.7 1.2 copy-done.14
  160.0 0.7 all-gather.8.cloned.1.call-update
  160.6 0.2 reduce-scatter.4.cloned.1.call-start
  161.1 1.6 copy-done.11
  162.7 1.6 copy-done.12
  164.2 72.4 %attend.1 = (bf16[512,2048]{1,0:T(8,128)(2,1)S(1)}, f32[4,4,8,512]{3,2,1,0:T(8,128)S(1)}, bf16[4,512,2048]{2,1,0:T(8,128)(2,1)}) custom-call(bf16[512,2048]{1,0:T(8,128)(2,1)S(1)} %copy-done.12, bf16[4096,256]{1,0:T(8,128)(2,1)S(1)} %bitcast.65, s32[512,128]{1,0:T(8,128)S(1)} %broadcast_in_dim.11.low_ref, bf16[512,2048]{1,0:T(8,128)(2,1)S(1)} %copy-done.2), custom_call_target="tpu_custom_call" | custom-call | flops 62914560000 | bytes 16777216 | tf_op jit(solution)/shard_map/attend/pallas_call | solution.py:413
  236.7 6.1 multiply_reduce_fusion.2
  242.8 3.9 multiply_convert_fusion.x_ref
  246.8 34.2 %all-gather.8.cloned.1.call-done.up_ref = bf16[1408,2048]{1,0:T(8,128)(2,1)} async-done(((bf16[176,2048]{1,0:T(8,128)(2,1)}), bf16[1408,2048]{1,0:T(8,128)(2,1)}) %all-gather.8.cloned.1.call-update) | async-done | bytes 5767184 | tf_op jit(solution)/shard_map/all_gather | solution.py:1429
  281.0 138.2 %feed_forward.1 = (bf16[4,512,2048]{2,1,0:T(8,128)(2,1)}, bf16[4,512,1408]{2,1,0:T(8,128)(2,1)}, bf16[4,512,1408]{2,1,0:T(8,128)(2,1)}, bf16[4,512,1408]{2,1,0:T...) custom-call(bf16[512,2048]{1,0:T(8,128)(2,1)} %multiply_convert_fusi, ...), custom_call_target="tpu_custom_call" | custom-call | flops 59055800320 | bytes 41943040 | tf_op jit(solution)/shard_map/feed_forward/pallas_call | solution.py:284
  419.2 2.3 convert_element_type.95
  421.6 0.5 copy-done.24
  422.2 0.7 fusion.5
  422.9 1.6 pad_maximum_fusion.2
  424.5 1.6 pad_maximum_fusion.1
  426.1 1.0 slice-done.2
  427.1 0.4 slice-done.5
  427.5 1.4 slice-done.3
  428.9 14.1 %bitcast_convert_fusion.1 = bf16[1408,2048]{1,0:T(8,128)(2,1)} fusion(bf16[4,512,1408]{2,1,0:T(8,128)(2,1)S(1)} %bitcast.82, bf16[4,512,2048]{2,1,0:T(8,128)(2,1)S(1)} %bitcast.80), kind=kOutput, calls=%fused_computation.1 | convolution fusion | flops 11814043648 | bytes 19922944 | tf_op jit(solution)/shard_map/dot_general | solution.py:30
  443.1 0.6 collective-permute-start.1
  443.7 1.5 collective-permute-start
  445.2 44.0 %collective-permute-done.1 = bf16[512,2048]{1,0:T(8,128)(2,1)} collective-permute-done((bf16[512,2048]{1,0:T(8,128)(2,1)}, bf16[512,2048]{1,0:T(8,128)(2,1)}, u32[]{:S(2)}, u32[]{:S(2)}) %collective-permute-start.1) | collective-permute-done | bytes 2097184 | tf_op jit(solution)/shard_map/ppermute | solution.py:1416
  489.2 0.3 collective-permute-done
  489.4 18.4 %bitcast_convert_fusion = bf16[1408,2048]{1,0:T(8,128)(2,1)} fusion(bf16[4,512,1408]{2,1,0:T(8,128)(2,1)} %get-tuple-element.81, bf16[4,512,2048]{2,1,0:T(8,128)(2,1)} %get-tuple-element.75), kind=kOutput, calls=%fused_computation | convolution fusion | flops 11814043648 | bytes 19922944 | tf_op jit(solution)/shard_map/dot_general | solution.py:30
  507.9 17.9 %convolution_convert_fusion = bf16[1408,2048]{1,0:T(8,128)(2,1)} fusion(bf16[2048,1408]{1,0:T(8,128)(2,1)} %bitcast.77, bf16[2048,2048]{1,0:T(8,128)(2,1)} %bitcast.76), kind=kOutput, calls=%fused_computation.2 | convolution fusion | flops 11814043648 | bytes 19922944 | tf_op jit(solution)/shard_map/dot_general | solution.py:30
  525.9 5.3 multiply_reduce_fusion
  531.2 6.0 fusion.11
  537.3 6.1 convolution_convert_fusion.1.d_mixed_ref
  543.4 0.5 convert_element_type.100
  544.0 1.0 copy-done.23
  545.1 0.6 copy-done.22
  545.8 0.7 fusion.1
  546.5 0.1 pad_maximum_fusion.4
  546.7 0.2 pad_maximum_fusion.3
  546.8 1.5 collective-permute-start.2
  548.4 0.6 collective-permute-start.3
  549.0 120.8 %attend_back.1 = (bf16[512,2048]{1,0:T(8,128)(2,1)S(1)}, bf16[4096,256]{1,0:T(8,128)(2,1)}, f32[256,2048]{1,0:T(8,128)}) custom-call(bf16[512,2048]{1,0:T(8,128)(2,1)} %get-tuple-element.54.q_ref, bf16[4096,256]{1,0:T(8,128)(2,1)} %bitcast.64, f32[512,128]{1,0:T(8,128)S(1)} %copy-done.5, f32[512,128]{1,0:T(8,128)S(1)} %copy-done.7, ...), custom_call_target="tpu_custom_call" | custom-call | flops 62914560000 | bytes 16777216 | tf_op jit(solution)/shard_map/attend_back/pallas_call | solution.py:572
  669.8 1.3 copy-done.15
  671.1 6.2 add_convert_fusion
  677.4 3.1 pad_maximum_fusion.ffn_ref
  680.5 0.6 broadcast_in_dim.13.term_ref
  681.1 148.1 %finish.1 = (f32[512,2048]{1,0:T(8,128)}, f32[256,2048]{1,0:T(8,128)}, f32[256,384]{1,0:T(8,128)}, bf16[4,3,176,2048]{3,2,1,0:T(8,128)(2,1)}) custom-call(bf16[512,2048]{1,0:T(8,128)(2,1)} %get-tuple-element.61.normed_ref, bf16[512,2048]{1,0:T(8,128)(2,1)} %copy-done.15, bf16[512,2048]{1,0:T(8,128)(2,1)} %tokens_ref.3, ...), custom_call_target="tpu_custom_call" | custom-call | flops 214748364800 | bytes 41943040 | tf_op jit(solution)/shard_map/finish/pallas_call | solution.py:1382
  829.3 1.7 fusion.13
  830.9 1.8 slice_reduce_fusion
  832.7 3.9 fusion.12
  836.6 3.5 bitcast_convert_fusion.2
  840.1 3.5 convert_bitcast_fusion
  843.6 3.5 convert_bitcast_fusion.1
  847.1 2.1 copy.37
  849.2 1.0 copy-done.20
  850.2 1.3 copy.38
  851.5 1.0 copy-done.19
  852.5 1.3 copy.39
  (90 shorter events, 1.0 us)
Async XLA Ops:
  7.2 1.8 copy-start
  7.2 153.7 %all-gather.4.cloned.1.call-start = ((), (), s32[]{:S(2)}) async-start(), calls=%async_computation.3 | async-start | bytes 6488064 | tf_op jit(solution)/shard_map/all_gather | solution.py:1429
  9.9 7.4 copy-start.9
  9.9 236.8 %all-gather.6.cloned.1.call-start = ((), (), s32[]{:S(2)}) async-start(), calls=%async_computation.4 | async-start | bytes 6488064 | tf_op jit(solution)/shard_map/all_gather | solution.py:1429
  11.5 5.8 copy-start.10
  13.3 147.6 %copy-start.26 = (s32[512]{0:T(512)}, s32[512]{0:T(512)S(1)}, u32[]{:S(2)}) copy-start(s32[512]{0:T(512)S(1)} %get-tuple-element.117) | copy-start | bytes 6148
  14.5 144.2 %copy-start.4 = (f32[512,128]{1,0:T(8,128)}, f32[512,128]{1,0:T(8,128)S(1)}, u32[]{:S(2)}) copy-start(f32[512,128]{1,0:T(8,128)S(1)} %get-tuple-element.121.cos_ref) | copy-start | bytes 786436
  14.5 144.2 %copy-start.6 = (f32[512,128]{1,0:T(8,128)}, f32[512,128]{1,0:T(8,128)S(1)}, u32[]{:S(2)}) copy-start(f32[512,128]{1,0:T(8,128)S(1)} %get-tuple-element.122.sin_ref) | copy-start | bytes 786436
  17.3 143.7 %copy-start.2 = (bf16[512,2048]{1,0:T(8,128)(2,1)S(1)}, bf16[512,2048]{1,0:T(8,128)(2,1)}, u32[]{:S(2)}) copy-start(bf16[512,2048]{1,0:T(8,128)(2,1)} %grads_ref) | copy-start | bytes 6291460
  158.7 1.2 copy-start.14
  159.9 76.8 %copy-start.8 = (f32[8,2048]{1,0:T(8,128)}, f32[8,2048]{1,0:T(8,128)S(1)}, u32[]{:S(2)}) copy-start(f32[8,2048]{1,0:T(8,128)S(1)} %get-tuple-element.59.gain_ref) | copy-start | bytes 196612
  159.9 121.1 %all-gather.8.cloned.1.call-start = ((), (), s32[]{:S(2)}) async-start(), calls=%async_computation.5 | async-start | bytes 6488064 | tf_op jit(solution)/shard_map/all_gather | solution.py:1429
  160.6 516.7 %reduce-scatter.4.cloned.1.call-start = ((), (), s32[]{:S(2)}) async-start(), calls=%async_computation.6 | async-start | bytes 6488064 | tf_op jit(solution)/shard_map/reduce_scatter | solution.py:1433
  161.1 1.6 copy-start.11
  162.7 1.6 copy-start.12
  164.2 72.4 %copy-start.28 = (bf16[512,2048]{1,0:T(8,128)(2,1)S(1)}, bf16[512,2048]{1,0:T(8,128)(2,1)}, u32[]{:S(2)}) copy-start(bf16[512,2048]{1,0:T(8,128)(2,1)} %tokens_ref.3) | copy-start | bytes 6291460
  164.2 72.4 %copy-start.29 = (bf16[8,256,2048]{2,1,0:T(8,128)(2,1)S(1)}, bf16[8,256,2048]{2,1,0:T(8,128)(2,1)}, u32[]{:S(2)}) copy-start(bf16[8,256,2048]{2,1,0:T(8,128)(2,1)} %get-tuple-element.58) | copy-start | bytes 25165828
  236.7 6.2 copy-start.13
  419.2 2.3 copy-start.25
  419.2 2.8 copy-start.24
  422.1 4.0 slice-start.4
  422.2 4.9 slice-start.2
  422.2 5.3 slice-start.5
  422.9 6.0 slice-start.3
  443.0 234.3 %reduce-scatter.6.cloned.1.call-start = ((), (), s32[]{:S(2)}) async-start(), calls=%async_computation.7 | async-start | bytes 6488064 | tf_op jit(solution)/shard_map/reduce_scatter | solution.py:1433
  443.1 46.1 %collective-permute-start.1 = (bf16[512,2048]{1,0:T(8,128)(2,1)}, bf16[512,2048]{1,0:T(8,128)(2,1)}, u32[]{:S(2)}, u32[]{:S(2)}) collective-permute-start(bf16[512,2048]{1,0:T(8,128)(2,1)} %pad_maximum_fusion.2), channel_id=1, source_target_pairs={{0,16},{8,24},{16,0},{24,8},{1,17},{9,25},{17,1},{25,9},{2,18},{10... | collective-permute-start | bytes 6291464 | tf_op jit(solution)/shard_map/ppermute | solution.py:1416
  443.7 45.7 %collective-permute-start = (bf16[512,2048]{1,0:T(8,128)(2,1)}, bf16[512,2048]{1,0:T(8,128)(2,1)}, u32[]{:S(2)}, u32[]{:S(2)}) collective-permute-start(bf16[512,2048]{1,0:T(8,128)(2,1)} %pad_maximum_fusion.1), channel_id=1, source_target_pairs={{0,8},{8,0},{16,24},{24,16},{1,9},{9,1},{17,25},{25,17},{2,10},{10... | collective-permute-start | bytes 6291464 | tf_op jit(solution)/shard_map/ppermute | solution.py:1416
  507.9 169.5 %reduce-scatter.8.cloned.1.call-start = ((), (), s32[]{:S(2)}) async-start(), calls=%async_computation.8 | async-start | bytes 6488064 | tf_op jit(solution)/shard_map/reduce_scatter | solution.py:1433
  525.9 5.3 copy-start.3
  525.9 11.3 %slice-start = ((s8[8388608]{0:T(1024)(128)(4,1)}), s8[4194304]{0:T(1024)(128)(4,1)S(1)}, s32[]{:S(2)}) async-start(s8[8388608]{0:T(1024)(128)(4,1)} %bitcast.73), calls=%async_computation.9 | async-start | bytes 8388608
  531.2 6.0 slice-start.1
  537.2 6.2 copy-start.18
  537.2 6.2 copy-start.17
  543.4 1.6 copy-start.23
  543.4 2.3 copy-start.22
  546.5 2.5 copy-start.27
  546.5 2.5 copy-start.5
  546.5 2.5 copy-start.7
  546.8 124.3 %collective-permute-start.2 = (bf16[512,2048]{1,0:T(8,128)(2,1)S(1)}, bf16[512,2048]{1,0:T(8,128)(2,1)}, u32[]{:S(2)}, u32[]{:S(2)}) collective-permute-start(bf16[512,2048]{1,0:T(8,128)(2,1)S(1)} %pad_maximum_fusion.3), channel_id=1, source_target_pairs={{0,8},{8,0},{16,24},{24,16},{1,9},{9,1},{17,25},{25,17},{2,10},{10... | collective-permute-start | bytes 6291464 | tf_op jit(solution)/shard_map/ppermute | solution.py:1416
  548.4 122.7 %collective-permute-start.3 = (bf16[512,2048]{1,0:T(8,128)(2,1)S(1)}, bf16[512,2048]{1,0:T(8,128)(2,1)}, u32[]{:S(2)}, u32[]{:S(2)}) collective-permute-start(bf16[512,2048]{1,0:T(8,128)(2,1)S(1)} %pad_maximum_fusion.4), channel_id=1, source_target_pairs={{0,16},{8,24},{16,0},{24,8},{1,17},{9,25},{17,1},{25,9},{2,18},{10... | collective-permute-start | bytes 6291464 | tf_op jit(solution)/shard_map/ppermute | solution.py:1416
  549.0 122.1 %copy-start.21 = (bf16[512,2048]{1,0:T(8,128)(2,1)S(1)}, bf16[512,2048]{1,0:T(8,128)(2,1)}, u32[]{:S(2)}) copy-start(bf16[512,2048]{1,0:T(8,128)(2,1)} %get-tuple-element.64) | copy-start | bytes 6291460
  669.8 1.3 copy-start.15
  843.6 3.5 copy-start.16
  847.1 3.1 copy-start.20
  847.1 6.8 copy-start.1
  850.2 2.3 copy-start.19
Sparse Core Ops, SparseCore 0:
  10.2 85.6 all-gather.3
  160.0 59.6 all-gather.5
  221.9 59.0 all-gather.7
  443.2 62.6 reduce-scatter.3
  508.5 63.2 reduce-scatter.5
  574.5 70.7 reduce-scatter.7
